TPU v7x, 32 devices: a whole 2x2x4 slice. The times are simulated.
32 devices in a mesh: ctx: 4 (over z), fsdp: 8 (over y, x, core).
Axes of the slice: x: 2, y: 2, z: 4, core: 2. Of those that a mesh axis runs over, the one named last changes fastest.
Arguments:
- tokens: bfloat16 [8, 1024, 1024], P('fsdp', 'ctx'), may hold values from -10 to 10
- segment_ids: int32 [8, 1024], P('fsdp', 'ctx'), may hold values from 0 to 7, never falling along the last dimension, each value on 1 to 512 neighbouring positions
- cotangent: bfloat16 [8, 1024, 1024], P('fsdp', 'ctx'), may hold values from -6 to 6
- query_weight: bfloat16 [1024, 1024], P('fsdp'), may hold values from -0.1875 to 0.1875
- query_bias: bfloat16 [1024], P('fsdp'), may hold values from -3 to 3
- key_weight: bfloat16 [1024, 1024], P('fsdp'), may hold values from -0.1875 to 0.1875
- value_weight: bfloat16 [1024, 1024], P('fsdp'), may hold values from -0.1875 to 0.1875
- value_bias: bfloat16 [1024], P('fsdp'), may hold values from -3 to 3
- out_weight: bfloat16 [1024, 1024], P('fsdp'), may hold values from -0.75 to 0.75
- out_bias: bfloat16 [1024], P('fsdp'), may hold values from -3 to 3
- attn_gain: bfloat16 [1024], P('fsdp'), may hold values from 0.25 to 1.75
- attn_shift: bfloat16 [1024], P('fsdp'), may hold values from -2 to 2
- up_weight: bfloat16 [1024, 4096], P('fsdp'), may hold values from -0.1875 to 0.1875
- up_bias: bfloat16 [4096], P('fsdp'), may hold values from -3 to 3
- down_weight: bfloat16 [4096, 1024], P('fsdp'), may hold values from -0.09375 to 0.09375
- down_bias: bfloat16 [1024], P('fsdp'), may hold values from -3 to 3
- mlp_gain: bfloat16 [1024], P('fsdp'), may hold values from 0.25 to 1.75
- mlp_shift: bfloat16 [1024], P('fsdp'), may hold values from -2 to 2
Outputs:
- output: bfloat16 [8, 1024, 1024], P('fsdp', 'ctx')
- input_grad: float32 [8, 1024, 1024], P('fsdp', 'ctx')
- grad_query_weight: float32 [1024, 1024], P('fsdp')
- grad_query_bias: float32 [1024], P('fsdp')
- grad_key_weight: float32 [1024, 1024], P('fsdp')
- grad_value_weight: float32 [1024, 1024], P('fsdp')
- grad_value_bias: float32 [1024], P('fsdp')
- grad_out_weight: float32 [1024, 1024], P('fsdp')
- grad_out_bias: float32 [1024], P('fsdp')
- grad_attn_gain: float32 [1024], P('fsdp')
- grad_attn_shift: float32 [1024], P('fsdp')
- grad_up_weight: float32 [1024, 4096], P('fsdp')
- grad_up_bias: float32 [4096], P('fsdp')
- grad_down_weight: float32 [4096, 1024], P('fsdp')
- grad_down_bias: float32 [1024], P('fsdp')
- grad_mlp_gain: float32 [1024], P('fsdp')
- grad_mlp_shift: float32 [1024], P('fsdp')
- rms_stream: float32 [], replicated
- rms_attn: float32 [], replicated
- rms_mlp: float32 [], replicated
Inputs may be any that keep to these rules, and one draw needn't show every extreme that they name: `segment_ids`: each of the 8 sequences holds segments 0 to 7 in order, each of 1 to 512 tokens, one of exactly 512; tokens of segment 8 - 1 are padding.
All inputs are finite; a program needn't handle non-finite values.
Results may differ from a plain program's by a relative error of at most 0.019.
The roundings to bfloat16 on the way count: a program that leaves them out, or rounds other values in their place, can miss the bound.
Values may be sent and summed in bfloat16 or wider, within the bound.
No kernel may reach another device: no remote copies, remote signals or barrier semaphores. Data moves between devices by JAX's collectives and lax.ppermute only.
A program may use at most 192 MiB of HBM per device.

v0:
```python
from functools import partial

import jax
import jax.numpy as jnp
from jax import lax
from jax.sharding import PartitionSpec as P

HEADS = 16
HEAD_DIM = 64
SEGS = 8


EPSILON = 1e-05
MASKED = -1000000000.0


def matmul(layer_activations, weight_matrix):
    return jnp.einsum(
        "akz,zm->akm", layer_activations, weight_matrix, preferred_element_type=jnp.float32
    )


def product_pullback(layer_activations, weight_matrix):
    return jnp.einsum(
        "utg,yg->uty", layer_activations, weight_matrix, preferred_element_type=jnp.float32
    )


def outer_sum(left_operand, right_operand):
    return jnp.einsum(
        "xbh,xbp->hp", left_operand, right_operand, preferred_element_type=jnp.float32
    )


def token_total(values_in):
    return jnp.sum(values_in.astype(jnp.float32), axis=(0, 1))


def norm_forward(hidden, gain_vector, shift_vector):
    centre = hidden - jnp.mean(hidden, axis=-1, keepdims=True)
    inverse = lax.rsqrt(jnp.mean(centre * centre, axis=-1, keepdims=True) + EPSILON)
    scaled = centre * inverse
    return (scaled * gain_vector + shift_vector, scaled, inverse)


def norm_backward(upstream, scaled, inverse, gain_vector):
    grad_scaled = upstream * gain_vector
    return inverse * (
        grad_scaled
        - jnp.mean(grad_scaled, axis=-1, keepdims=True)
        - scaled * jnp.mean(grad_scaled * scaled, axis=-1, keepdims=True)
    )


def add_rows(gathered_rows, addition, first_row):
    current = lax.dynamic_slice_in_dim(gathered_rows, first_row, addition.shape[1], 1)
    return lax.dynamic_update_slice_in_dim(gathered_rows, current + addition, first_row, 1)


def per_device(
    tokens,
    segment_ids,
    cotangent,
    query_weight,
    query_bias,
    key_weight,
    value_weight,
    value_bias,
    out_weight,
    out_bias,
    attn_gain,
    attn_shift,
    up_weight,
    up_bias,
    down_weight,
    down_bias,
    mlp_gain,
    mlp_shift,
):
    seqs_here, rows_here, width_all = tokens.shape
    scale_factor = HEAD_DIM ** (-0.5)
    groups = lax.axis_size("ctx")
    (
        query_full,
        key_full,
        value_full,
        out_full,
        query_bias_full,
        value_bias_full,
        out_bias_full,
        attn_gain_full,
        attn_shift_full,
    ) = (
        lax.all_gather(query_weight, "fsdp", axis=0, tiled=True),
        lax.all_gather(key_weight, "fsdp", axis=0, tiled=True),
        lax.all_gather(value_weight, "fsdp", axis=0, tiled=True),
        lax.all_gather(out_weight, "fsdp", axis=0, tiled=True),
        lax.all_gather(query_bias, "fsdp", axis=0, tiled=True),
        lax.all_gather(value_bias, "fsdp", axis=0, tiled=True),
        lax.all_gather(out_bias, "fsdp", axis=0, tiled=True),
        lax.all_gather(attn_gain, "fsdp", axis=0, tiled=True),
        lax.all_gather(attn_shift, "fsdp", axis=0, tiled=True),
    )
    token_float = tokens.astype(jnp.float32)
    queries = (matmul(tokens, query_full) + query_bias_full.astype(jnp.float32)).astype(
        jnp.bfloat16
    )
    keys_local = matmul(tokens, key_full).astype(jnp.bfloat16)
    values_local = (matmul(tokens, value_full) + value_bias_full.astype(jnp.float32)).astype(
        jnp.bfloat16
    )
    queries_split = queries.reshape(seqs_here, rows_here, HEADS, HEAD_DIM)

    def score_block(keys_piece, labels_piece):
        keys_split = keys_piece.reshape(seqs_here, keys_piece.shape[1], HEADS, HEAD_DIM)
        scores = (
            jnp.einsum(
                "sqhd,skhd->shqk", queries_split, keys_split, preferred_element_type=jnp.float32
            )
            * scale_factor
        )
        matches = (segment_ids[:, :, None] == labels_piece[:, None, :])[:, None]
        return (jnp.where(matches, scores, MASKED), matches, keys_split)

    def in_blocks(block_fn, running, pieces, first_row):
        covered = pieces[2].shape[1]
        for offset in range(0, covered, rows_here):
            section = tuple(
                (lax.slice_in_dim(member, offset, offset + rows_here, axis=1) for member in pieces)
            )
            running = block_fn(running, section, first_row + offset)
        return running

    def forward_block(running, pieces, first_row):
        run_max, run_total, accumulated = running
        keys_piece, values_piece, labels_piece = pieces
        scores, matches, keys_split = score_block(keys_piece, labels_piece)
        values_split = values_piece.reshape(seqs_here, values_piece.shape[1], HEADS, HEAD_DIM)
        new_max = jnp.maximum(run_max, jnp.max(scores, axis=-1))
        probabilities = jnp.where(matches, jnp.exp(scores - new_max[..., None]), 0.0)
        rescale = jnp.exp(run_max - new_max)
        run_total = run_total * rescale + jnp.sum(probabilities, axis=-1)
        accumulated = accumulated * jnp.transpose(rescale, (0, 2, 1))[..., None] + jnp.einsum(
            "shqk,skhd->sqhd",
            probabilities.astype(jnp.bfloat16),
            values_split,
            preferred_element_type=jnp.float32,
        )
        return (new_max, run_total, accumulated)

    init_max = jnp.full((seqs_here, HEADS, rows_here), MASKED, jnp.float32)
    init_total = jnp.zeros((seqs_here, HEADS, rows_here), jnp.float32)
    init_accum = jnp.zeros((seqs_here, rows_here, HEADS, HEAD_DIM), jnp.float32)
    run_max, run_total, accumulated = in_blocks(
        forward_block,
        (init_max, init_total, init_accum),
        (
            lax.all_gather(keys_local, "ctx", axis=1, tiled=True),
            lax.all_gather(values_local, "ctx", axis=1, tiled=True),
            lax.all_gather(segment_ids, "ctx", axis=1, tiled=True),
        ),
        jnp.int32(0),
    )
    mixed_full = accumulated / jnp.transpose(run_total, (0, 2, 1))[..., None]
    log_total = run_max + jnp.log(run_total)
    mixed = mixed_full.reshape(seqs_here, rows_here, width_all).astype(jnp.bfloat16)
    attn_branch = matmul(mixed, out_full) + out_bias_full.astype(jnp.float32)
    attn_gain_float = attn_gain_full.astype(jnp.float32)
    normed, attn_scaled, attn_inverse = norm_forward(
        token_float + attn_branch, attn_gain_float, attn_shift_full.astype(jnp.float32)
    )
    up_full, down_full, up_bias_full, down_bias_full, mlp_gain_full, mlp_shift_full = (
        lax.all_gather(up_weight, "fsdp", axis=0, tiled=True),
        lax.all_gather(down_weight, "fsdp", axis=0, tiled=True),
        lax.all_gather(up_bias, "fsdp", axis=0, tiled=True),
        lax.all_gather(down_bias, "fsdp", axis=0, tiled=True),
        lax.all_gather(mlp_gain, "fsdp", axis=0, tiled=True),
        lax.all_gather(mlp_shift, "fsdp", axis=0, tiled=True),
    )
    normed_low = normed.astype(jnp.bfloat16)
    gate_pre = matmul(normed_low, up_full) + up_bias_full.astype(jnp.float32)
    hidden = jax.nn.gelu(gate_pre, approximate=False).astype(jnp.bfloat16)
    mlp_branch = matmul(hidden, down_full) + down_bias_full.astype(jnp.float32)
    mlp_gain_float = mlp_gain_full.astype(jnp.float32)
    result, mlp_scaled, mlp_inverse = norm_forward(
        normed + mlp_branch, mlp_gain_float, mlp_shift_full.astype(jnp.float32)
    )
    valid_mask = (segment_ids != SEGS - 1).astype(jnp.float32)
    weighted = valid_mask[..., None]
    statistics = lax.psum(
        (
            jnp.sum(weighted * token_float * token_float),
            jnp.sum(weighted * attn_branch * attn_branch),
            jnp.sum(weighted * mlp_branch * mlp_branch),
            jnp.sum(valid_mask),
        ),
        ("ctx", "fsdp"),
    )
    denominator = statistics[3] * width_all
    rms_stream = jnp.sqrt(statistics[0] / denominator)
    rms_attn = jnp.sqrt(statistics[1] / denominator)
    rms_mlp = jnp.sqrt(statistics[2] / denominator)
    upstream = cotangent.astype(jnp.float32) * weighted
    grad_mlp_gain = jnp.sum(upstream * mlp_scaled, axis=(0, 1))
    grad_mlp_shift = jnp.sum(upstream, axis=(0, 1))
    grad_second = norm_backward(upstream, mlp_scaled, mlp_inverse, mlp_gain_float)
    grad_mlp_low = grad_second.astype(jnp.bfloat16)
    grad_down = outer_sum(hidden, grad_mlp_low)
    grad_down_bias = token_total(grad_mlp_low)
    grad_hidden = product_pullback(grad_mlp_low, down_full)
    unused_value, gelu_pull = jax.vjp(partial(jax.nn.gelu, approximate=False), gate_pre)
    grad_gate = gelu_pull(grad_hidden)[0].astype(jnp.bfloat16)
    grad_up = outer_sum(normed_low, grad_gate)
    grad_up_bias = token_total(grad_gate)
    grad_normed = grad_second + product_pullback(grad_gate, up_full)
    mlp_terms = (grad_up, grad_down, grad_up_bias, grad_down_bias, grad_mlp_gain, grad_mlp_shift)
    mlp_parts = (
        lax.psum_scatter(mlp_terms[0], "fsdp", scatter_dimension=0, tiled=True),
        lax.psum_scatter(mlp_terms[1], "fsdp", scatter_dimension=0, tiled=True),
        lax.psum_scatter(mlp_terms[2], "fsdp", scatter_dimension=0, tiled=True),
        lax.psum_scatter(mlp_terms[3], "fsdp", scatter_dimension=0, tiled=True),
        lax.psum_scatter(mlp_terms[4], "fsdp", scatter_dimension=0, tiled=True),
        lax.psum_scatter(mlp_terms[5], "fsdp", scatter_dimension=0, tiled=True),
    )
    mlp_shares = (
        lax.psum(mlp_parts[0].astype(jnp.bfloat16), "ctx").astype(jnp.float32),
        lax.psum(mlp_parts[1].astype(jnp.bfloat16), "ctx").astype(jnp.float32),
        lax.psum(mlp_parts[2].astype(jnp.bfloat16), "ctx").astype(jnp.float32),
        lax.psum(mlp_parts[3].astype(jnp.bfloat16), "ctx").astype(jnp.float32),
        lax.psum(mlp_parts[4].astype(jnp.bfloat16), "ctx").astype(jnp.float32),
        lax.psum(mlp_parts[5].astype(jnp.bfloat16), "ctx").astype(jnp.float32),
    )
    grad_attn_gain = jnp.sum(grad_normed * attn_scaled, axis=(0, 1))
    grad_attn_shift = jnp.sum(grad_normed, axis=(0, 1))
    grad_first = norm_backward(grad_normed, attn_scaled, attn_inverse, attn_gain_float)
    grad_attn_low = grad_first.astype(jnp.bfloat16)
    grad_out = outer_sum(mixed, grad_attn_low)
    grad_out_bias = token_total(grad_attn_low)
    grad_mixed = product_pullback(grad_attn_low, out_full).astype(jnp.bfloat16)
    grad_mixed_split = grad_mixed.reshape(seqs_here, rows_here, HEADS, HEAD_DIM)
    row_delta = jnp.einsum("sqhd,sqhd->shq", grad_mixed_split.astype(jnp.float32), mixed_full)

    def backward_block(running, pieces, first_row):
        grad_query_acc, grad_keys_all, grad_values_all = running
        keys_piece, values_piece, labels_piece = pieces
        covered = keys_piece.shape[1]
        scores, matches, keys_split = score_block(keys_piece, labels_piece)
        values_split = values_piece.reshape(seqs_here, covered, HEADS, HEAD_DIM)
        probabilities = jnp.where(matches, jnp.exp(scores - log_total[..., None]), 0.0)
        value_gradient_portion = jnp.einsum(
            "shqk,sqhd->skhd",
            probabilities.astype(jnp.bfloat16),
            grad_mixed_split,
            preferred_element_type=jnp.float32,
        )
        grad_probs = jnp.einsum(
            "sqhd,skhd->shqk", grad_mixed_split, values_split, preferred_element_type=jnp.float32
        )
        grad_scores = (probabilities * (grad_probs - row_delta[..., None])).astype(jnp.bfloat16)
        grad_query_acc = (
            grad_query_acc
            + jnp.einsum(
                "shqk,skhd->sqhd", grad_scores, keys_split, preferred_element_type=jnp.float32
            )
            * scale_factor
        )
        grad_keys_piece = (
            jnp.einsum(
                "shqk,sqhd->skhd", grad_scores, queries_split, preferred_element_type=jnp.float32
            )
            * scale_factor
        )
        grad_keys_all = add_rows(
            grad_keys_all, grad_keys_piece.reshape(seqs_here, covered, width_all), first_row
        )
        grad_values_all = add_rows(
            grad_values_all,
            value_gradient_portion.reshape(seqs_here, covered, width_all),
            first_row,
        )
        return (grad_query_acc, grad_keys_all, grad_values_all)

    seq_total = rows_here * groups
    init_back = (
        jnp.zeros((seqs_here, rows_here, HEADS, HEAD_DIM), jnp.float32),
        jnp.zeros((seqs_here, seq_total, width_all), jnp.float32),
        jnp.zeros((seqs_here, seq_total, width_all), jnp.float32),
    )
    grad_query_acc, grad_keys_all, grad_values_all = in_blocks(
        backward_block,
        init_back,
        (
            lax.all_gather(keys_local, "ctx", axis=1, tiled=True),
            lax.all_gather(values_local, "ctx", axis=1, tiled=True),
            lax.all_gather(segment_ids, "ctx", axis=1, tiled=True),
        ),
        jnp.int32(0),
    )
    grad_keys_mine, grad_values_mine = (
        lax.psum_scatter(
            grad_keys_all.astype(jnp.bfloat16), "ctx", scatter_dimension=1, tiled=True
        ).astype(jnp.float32),
        lax.psum_scatter(
            grad_values_all.astype(jnp.bfloat16), "ctx", scatter_dimension=1, tiled=True
        ).astype(jnp.float32),
    )
    grad_query_low = grad_query_acc.reshape(seqs_here, rows_here, width_all).astype(jnp.bfloat16)
    grad_keys_low = grad_keys_mine.astype(jnp.bfloat16)
    grad_values_low = grad_values_mine.astype(jnp.bfloat16)
    grad_query_w = outer_sum(tokens, grad_query_low)
    grad_key_w = outer_sum(tokens, grad_keys_low)
    grad_value_w = outer_sum(tokens, grad_values_low)
    grad_query_b = token_total(grad_query_low)
    grad_value_b = token_total(grad_values_low)
    input_grad = (
        grad_first
        + product_pullback(grad_query_low, query_full)
        + product_pullback(grad_keys_low, key_full)
        + product_pullback(grad_values_low, value_full)
    )
    attn_terms = (
        grad_query_w,
        grad_key_w,
        grad_value_w,
        grad_out,
        grad_query_b,
        grad_value_b,
        grad_out_bias,
        grad_attn_gain,
        grad_attn_shift,
    )
    attn_parts = (
        lax.psum_scatter(attn_terms[0], "fsdp", scatter_dimension=0, tiled=True),
        lax.psum_scatter(attn_terms[1], "fsdp", scatter_dimension=0, tiled=True),
        lax.psum_scatter(attn_terms[2], "fsdp", scatter_dimension=0, tiled=True),
        lax.psum_scatter(attn_terms[3], "fsdp", scatter_dimension=0, tiled=True),
        lax.psum_scatter(attn_terms[4], "fsdp", scatter_dimension=0, tiled=True),
        lax.psum_scatter(attn_terms[5], "fsdp", scatter_dimension=0, tiled=True),
        lax.psum_scatter(attn_terms[6], "fsdp", scatter_dimension=0, tiled=True),
        lax.psum_scatter(attn_terms[7], "fsdp", scatter_dimension=0, tiled=True),
        lax.psum_scatter(attn_terms[8], "fsdp", scatter_dimension=0, tiled=True),
    )
    attn_shares = (
        lax.psum(attn_parts[0].astype(jnp.bfloat16), "ctx").astype(jnp.float32),
        lax.psum(attn_parts[1].astype(jnp.bfloat16), "ctx").astype(jnp.float32),
        lax.psum(attn_parts[2].astype(jnp.bfloat16), "ctx").astype(jnp.float32),
        lax.psum(attn_parts[3].astype(jnp.bfloat16), "ctx").astype(jnp.float32),
        lax.psum(attn_parts[4].astype(jnp.bfloat16), "ctx").astype(jnp.float32),
        lax.psum(attn_parts[5].astype(jnp.bfloat16), "ctx").astype(jnp.float32),
        lax.psum(attn_parts[6].astype(jnp.bfloat16), "ctx").astype(jnp.float32),
        lax.psum(attn_parts[7].astype(jnp.bfloat16), "ctx").astype(jnp.float32),
        lax.psum(attn_parts[8].astype(jnp.bfloat16), "ctx").astype(jnp.float32),
    )
    return (
        result.astype(jnp.bfloat16),
        input_grad,
        attn_shares[0],
        attn_shares[4],
        attn_shares[1],
        attn_shares[2],
        attn_shares[5],
        attn_shares[3],
        attn_shares[6],
        attn_shares[7],
        attn_shares[8],
        mlp_shares[0],
        mlp_shares[2],
        mlp_shares[1],
        mlp_shares[3],
        mlp_shares[4],
        mlp_shares[5],
        rms_stream,
        rms_attn,
        rms_mlp,
    )


def solution(mesh):
    placed = (
        P("fsdp", "ctx", None),
        P("fsdp", "ctx"),
        P("fsdp", "ctx", None),
        P("fsdp", None),
        P("fsdp"),
        P("fsdp", None),
        P("fsdp", None),
        P("fsdp"),
        P("fsdp", None),
        P("fsdp"),
        P("fsdp"),
        P("fsdp"),
        P("fsdp", None),
        P("fsdp"),
        P("fsdp", None),
        P("fsdp"),
        P("fsdp"),
        P("fsdp"),
    )
    return jax.shard_map(
        per_device,
        mesh=mesh,
        in_specs=placed,
        out_specs=(
            P("fsdp", "ctx", None),
            P("fsdp", "ctx", None),
            P("fsdp", None),
            P("fsdp"),
            P("fsdp", None),
            P("fsdp", None),
            P("fsdp"),
            P("fsdp", None),
            P("fsdp"),
            P("fsdp"),
            P("fsdp"),
            P("fsdp", None),
            P("fsdp"),
            P("fsdp", None),
            P("fsdp"),
            P("fsdp"),
            P("fsdp"),
            P(),
            P(),
            P(),
        ),
        check_vma=False,
    )
```

profile of v0, /device:TPU:0, one launch (start us, length us, event | category | flops | bytes accessed | tf_op | source)
XLA Modules:
  0.0 1078.2 jit_solution(9047605718650336814)
XLA Ops:
  9.5 10.3 all-gather.3
  19.8 20.8 %all-gather.24.cloned.1.call-done = bf16[1024,1024]{1,0:T(8,128)(2,1)} async-done(((bf16[128,1024]{1,0:T(8,128)(2,1)}), bf16[1024,1024]{1,0:T(8,128)(2,1)}) %all-gather.24.cloned.1.call-update) | async-done | bytes 2097168 | tf_op jit(solution)/shard_map/all_gather | solution.py:96
  40.6 3.3 fusion.86
  44.0 26.4 %all-gather.22.cloned.1.call-done = bf16[1024,1024]{1,0:T(8,128)(2,1)} async-done(((bf16[128,1024]{1,0:T(8,128)(2,1)}), bf16[1024,1024]{1,0:T(8,128)(2,1)}) %all-gather.22.cloned.1.call-update) | async-done | bytes 2097168 | tf_op jit(solution)/shard_map/all_gather | solution.py:95
  70.4 3.1 convolution_convert_fusion.1
  75.6 8.7 all-gather.2
  84.4 7.8 all-gather.4
  92.2 8.7 all-gather.5
  100.8 7.8 all-gather.6
  108.6 8.7 all-gather.8
  117.9 7.8 all-gather.9
  125.7 8.7 all-gather.10
  135.0 7.9 all-gather.7
  143.5 10.9 %all_gather.57 = s32[1,1024]{1,0:T(1,128)S(1)} all-gather(s32[1,256]{1,0:T(1,128)S(1)} %copy-done.50), channel_id=1, replica_groups=mesh['ctx'=4,'fsdp'=8] {'ctx'}, dimensions={1}, use_global_device_ids=true | all-gather | bytes 5120 | tf_op jit(solution)/shard_map/all_gather | solution.py:160
  163.6 31.2 %all-gather.32.cloned.1.call-done = bf16[1024,1024]{1,0:T(8,128)(2,1)} async-done(((bf16[256,1024]{1,0:T(8,128)(2,1)}), bf16[1024,1024]{1,0:T(8,128)(2,1)}) %all-gather.32.cloned.1.call-update) | async-done | bytes 2097168 | tf_op jit(solution)/shard_map/all_gather | solution.py:158
  194.8 2.5 fusion.173
  213.3 10.2 all-gather.26.cloned.1.call-done
  223.5 3.3 fusion.169
  227.7 52.1 %all-gather.28.cloned.1.call-done = bf16[1024,4096]{1,0:T(8,128)(2,1)} async-done(((bf16[128,4096]{1,0:T(8,128)(2,1)}), bf16[1024,4096]{1,0:T(8,128)(2,1)}) %all-gather.28.cloned.1.call-update) | async-done | bytes 8388624 | tf_op jit(solution)/shard_map/all_gather | solution.py:173
  279.8 16.4 %multiply_convert_fusion.4 = (bf16[256,4096]{1,0:T(8,128)(2,1)}, f32[256,4096]{1,0:T(8,128)}, f32[256,4096]{1,0:T(8,128)}) fusion(f32[4096]{0:T(1024)S(1)} %bitcast.424, bf16[1024,4096]{1,0:T(8,128)(2,1)} %all-gather.28.cloned.1.call-done, f32[1,256,1024]{2,1,0:T(8,128)S(1)} %get-tuple-element.128, f32[1024]{0:T(1024)S(1)} %bitcast.414, ...), kind=kOutput, calls=%fused_computation.13 | convolution fusion | flops 2218000384 | bytes 19949568 | tf_op jit(solution)/shard_map/akz,zm->akm/dot_general | solution.py:18
  296.3 39.9 %all-gather.30.cloned.1.call-done = bf16[4096,1024]{1,0:T(8,128)(2,1)} async-done(((bf16[512,1024]{1,0:T(8,128)(2,1)}), bf16[4096,1024]{1,0:T(8,128)(2,1)}) %all-gather.30.cloned.1.call-update) | async-done | bytes 8388624 | tf_op jit(solution)/shard_map/all_gather | solution.py:174
  336.2 7.4 fusion.167
  346.5 11.4 %convert_reduce_fusion = (f32[4096]{0:T(1024)S(1)}, bf16[256,4096]{1,0:T(8,128)(2,1)S(1)}) fusion(f32[256,4096]{1,0:T(8,128)S(1)} %copy-done.62, f32[256,4096]{1,0:T(8,128)} %get-tuple-element.166, bf16[4096,1024]{1,0:T(8,128)(2,1)} %all-gather.30.cloned.1.call-done, f32[1,256,1024]{2,1,0:T(8,128)S(1)} %get-tuple-element.120), kind=kOutput, calls=%fused_computation.3 | convolution fusion | flops 2164518912 | bytes 19939328 | tf_op jit(solution)/shard_map/utg,yg->uty/dot_general | solution.py:24
  357.9 6.9 multiply_reduce_fusion.1
  368.8 3.6 fusion.24
  382.7 4.0 multiply_convert_fusion.3
  404.0 2.8 fusion.107
  412.4 2.7 convolution_bitcast_fusion.2
  415.1 9.9 reduce-scatter.11.cloned.1.call-done
  425.0 3.7 convolution_bitcast_fusion
  428.8 41.6 %reduce-scatter.9.cloned.1.call-done = bf16[1,256,1024]{1,2,0:T(8,128)(2,1)} async-done(((bf16[1,1024,1024]{1,2,0:T(8,128)(2,1)}), bf16[1,256,1024]{1,2,0:T(8,128)(2,1)}) %reduce-scatter.9.cloned.1.call-update) | async-done | bytes 524304 | tf_op jit(solution)/shard_map/reduce_scatter | solution.py:300
  470.4 3.7 convolution_bitcast_fusion.1
  474.1 11.2 %fusion.164 = f32[1024,4096]{1,0:T(8,128)} fusion(bf16[256,4096]{1,0:T(8,128)(2,1)} %copy-done.35, f32[1,256,1024]{2,1,0:T(8,128)S(1)} %get-tuple-element.128, f32[1024]{0:T(1024)S(1)} %bitcast.416, f32[1024]{0:T(1024)S(1)} %bitcast.413, f32[256]{0:T(256)S(1)} %copy-done.45, f32[256]{0:T(256)S(1)} %broadcast_multiply_fusion.5), kind=kOutput, calls=%fused_computation.243 | convolution fusion | flops 2148794368 | bytes 19933184 | tf_op jit(solution)/shard_map/xbh,xbp->hp/dot_general | solution.py:30
  486.7 10.3 fusion.110
  497.1 27.4 %reduce-scatter.19.cloned.1.call-done = f32[128,1024]{1,0:T(8,128)} async-done(((f32[1024,1024]{1,0:T(8,128)}), f32[128,1024]{1,0:T(8,128)}) %reduce-scatter.19.cloned.1.call-update) | async-done | bytes 524304 | tf_op jit(solution)/shard_map/reduce_scatter | solution.py:336
  526.2 53.2 %reduce-scatter.13.cloned.1.call-done = f32[128,1024]{0,1:T(8,128)} async-done(((f32[1024,1024]{0,1:T(8,128)}), f32[128,1024]{0,1:T(8,128)}) %reduce-scatter.13.cloned.1.call-update) | async-done | bytes 524304 | tf_op jit(solution)/shard_map/reduce_scatter | solution.py:333
  581.2 52.9 %reduce-scatter.17.cloned.1.call-done = f32[128,1024]{0,1:T(8,128)} async-done(((f32[1024,1024]{0,1:T(8,128)}), f32[128,1024]{0,1:T(8,128)}) %reduce-scatter.17.cloned.1.call-update) | async-done | bytes 524304 | tf_op jit(solution)/shard_map/reduce_scatter | solution.py:335
  635.9 53.2 %reduce-scatter.15.cloned.1.call-done = f32[128,1024]{0,1:T(8,128)} async-done(((f32[1024,1024]{0,1:T(8,128)}), f32[128,1024]{0,1:T(8,128)}) %reduce-scatter.15.cloned.1.call-update) | async-done | bytes 524304 | tf_op jit(solution)/shard_map/reduce_scatter | solution.py:334
  690.8 117.6 %reduce-scatter.21.cloned.1.call-done = f32[128,4096]{1,0:T(8,128)} async-done(((f32[1024,4096]{1,0:T(8,128)}), f32[128,4096]{1,0:T(8,128)}) %reduce-scatter.21.cloned.1.call-update) | async-done | bytes 2097168 | tf_op jit(solution)/shard_map/reduce_scatter | solution.py:218
  808.4 2.7 convert_element_type.331
  811.1 116.7 %reduce-scatter.23.cloned.1.call-done = f32[512,1024]{1,0:T(8,128)} async-done(((f32[4096,1024]{1,0:T(8,128)}), f32[512,1024]{1,0:T(8,128)}) %reduce-scatter.23.cloned.1.call-update) | async-done | bytes 2097168 | tf_op jit(solution)/shard_map/reduce_scatter | solution.py:219
  927.8 2.7 convert_element_type.336
  935.3 43.0 %all-reduce.11 = (f32[]{:T(128)}, f32[]{:T(128)}, f32[]{:T(128)}, f32[]{:T(128)}) all-reduce(f32[]{:T(128)} %get-tuple-element.90, f32[]{:T(128)} %fusion.161, f32[]{:T(128)} %get-tuple-element.89, f32[]{:T(128)} %get-tuple-element.88), channel_id=1, replica_groups=mesh['ctx'=4,'fsdp'=8] {'ctx','fsdp'}, use_global_device_ids=true, to_apply=%region_58.59 | all-reduce | flops 4 | bytes 32 | tf_op jit(solution)/shard_map/psum | solution.py:190
  981.3 24.5 %all-reduce.12 = (bf16[1024]{0:T(1024)(128)(2,1)S(1)}, bf16[1024]{0:T(1024)(128)(2,1)S(1)}, bf16[1024]{0:T(1024)(128)(2,1)S(1)}, bf16[1024]{0:T(1024)(128)(2,1)S...) all-reduce(f32[1024]{0:T(1024)S(1)} %reduce_sum.252, ...), channel_id=7, replica_groups=mesh['ctx'=4,'fsdp'=8] {'fsdp'}, use_global_device_ids=true, to_apply=%region_21.22.clone | all-reduce | flops 12288 | bytes 73728
  1006.5 12.7 %all-reduce.13 = (bf16[128]{0:T(256)(128)(2,1)S(1)}, bf16[128]{0:T(256)(128)(2,1)S(1)}, bf16[128]{0:T(256)(128)(2,1)S(1)}, bf16[128]{0:T(256)(128)(2,1)S(1)}, bf...) all-reduce(bf16[128]{0:T(256)(128)(2,1)S(1)} %dynamic-slice.35, ...), channel_id=1, replica_groups=mesh['ctx'=4,'fsdp'=8] {'ctx'}, use_global_device_ids=true, to_apply=%region_22.23 | all-reduce | flops 1536 | bytes 6144 | tf_op jit(solution)/shard_map/psum | solution.py:348
  1023.8 2.5 convolution_bitcast_fusion.4
  1030.6 25.3 %all-reduce.17.cloned.1.call-done = (bf16[128,1024]{0,1:T(8,128)(2,1)}, bf16[128,1024]{0,1:T(8,128)(2,1)}, bf16[128,1024]{0,1:T(8,128)(2,1)}, bf16[128,1024]{1,0...) async-done(((bf16[128,1024]{0,1:T(8,128)(2,1)}, bf16[128,1024]{0,1:T(8,128)(2,1)}, bf16[128,1024]{0,1:T(8,128)(2,1)}, bf16[128,1024]{1,0:T(8,128)(2,1)}, ...) | async-done | bytes 3145744 | tf_op jit(solution)/shard_map/psum | solution.py:344
  1063.5 2.8 convert_element_type.332
  (273 shorter events, 102.7 us)
Async XLA Ops:
  7.2 63.2 %copy-start.10 = (bf16[1,256,1024]{2,1,0:T(8,128)(2,1)S(1)}, bf16[1,256,1024]{2,1,0:T(8,128)(2,1)}, u32[]{:S(2)}) copy-start(bf16[1,256,1024]{2,1,0:T(8,128)(2,1)} %param.18) | copy-start | bytes 1572868
  7.2 33.4 %all-gather.24.cloned.1.call-start = ((), (), s32[]{:S(2)}) async-start(), calls=%async_computation.10 | async-start | bytes 2359296 | tf_op jit(solution)/shard_map/all_gather | solution.py:96
  7.9 62.4 %all-gather.22.cloned.1.call-start = ((), (), s32[]{:S(2)}) async-start(), calls=%async_computation.9 | async-start | bytes 2359296 | tf_op jit(solution)/shard_map/all_gather | solution.py:95
  8.7 146.6 %all-gather.20.cloned.1.call-start = ((), (), s32[]{:S(2)}) async-start(), calls=%async_computation.8 | async-start | bytes 2359296 | tf_op jit(solution)/shard_map/all_gather | solution.py:94
  9.4 148.5 %all-gather.34.cloned.1.call-start = ((), (), s32[]{:S(2)}) async-start(), calls=%async_computation.23 | async-start | bytes 2621440 | tf_op jit(solution)/shard_map/all_gather | solution.py:159
  43.8 31.8 %copy-start.53 = (bf16[512]{0:T(512)(128)(2,1)S(1)}, bf16[512]{0:T(512)(128)(2,1)}, u32[]{:S(2)}) copy-start(bf16[512]{0:T(512)(128)(2,1)} %param.31) | copy-start | bytes 3076
  43.8 31.8 %copy-start.54 = (bf16[128]{0:T(256)(128)(2,1)S(1)}, bf16[128]{0:T(256)(128)(2,1)}, u32[]{:S(2)}) copy-start(bf16[128]{0:T(256)(128)(2,1)} %param.22) | copy-start | bytes 772
  43.8 40.5 %copy-start.55 = (bf16[128]{0:T(256)(128)(2,1)S(1)}, bf16[128]{0:T(256)(128)(2,1)}, u32[]{:S(2)}) copy-start(bf16[128]{0:T(256)(128)(2,1)} %param.27) | copy-start | bytes 772
  43.8 48.3 %copy-start.56 = (bf16[128]{0:T(256)(128)(2,1)S(1)}, bf16[128]{0:T(256)(128)(2,1)}, u32[]{:S(2)}) copy-start(bf16[128]{0:T(256)(128)(2,1)} %param.28) | copy-start | bytes 772
  43.8 57.0 %copy-start.57 = (bf16[128]{0:T(256)(128)(2,1)S(1)}, bf16[128]{0:T(256)(128)(2,1)}, u32[]{:S(2)}) copy-start(bf16[128]{0:T(256)(128)(2,1)} %param.29) | copy-start | bytes 772
  43.9 64.8 %copy-start.58 = (bf16[128]{0:T(256)(128)(2,1)S(1)}, bf16[128]{0:T(256)(128)(2,1)}, u32[]{:S(2)}) copy-start(bf16[128]{0:T(256)(128)(2,1)} %param.33) | copy-start | bytes 772
  43.9 74.1 %copy-start.59 = (bf16[128]{0:T(256)(128)(2,1)S(1)}, bf16[128]{0:T(256)(128)(2,1)}, u32[]{:S(2)}) copy-start(bf16[128]{0:T(256)(128)(2,1)} %param.34) | copy-start | bytes 772
  43.9 81.8 %copy-start.60 = (bf16[128]{0:T(256)(128)(2,1)S(1)}, bf16[128]{0:T(256)(128)(2,1)}, u32[]{:S(2)}) copy-start(bf16[128]{0:T(256)(128)(2,1)} %param.35) | copy-start | bytes 772
  43.9 99.7 %copy-start.50 = (s32[1,256]{1,0:T(1,128)S(1)}, s32[1,256]{1,0:T(1,128)}, u32[]{:S(2)}) copy-start(s32[1,256]{1,0:T(1,128)} %param.19) | copy-start | bytes 3076
  43.9 150.9 %all-gather.32.cloned.1.call-start = ((), (), s32[]{:S(2)}) async-start(), calls=%async_computation.22 | async-start | bytes 2621440 | tf_op jit(solution)/shard_map/all_gather | solution.py:158
  73.5 150.0 %all-gather.26.cloned.1.call-start = ((), (), s32[]{:S(2)}) async-start(), calls=%async_computation.11 | async-start | bytes 2359296 | tf_op jit(solution)/shard_map/all_gather | solution.py:97
  74.1 205.8 %all-gather.28.cloned.1.call-start = ((), (), s32[]{:S(2)}) async-start(), calls=%async_computation.12 | async-start | bytes 9437184 | tf_op jit(solution)/shard_map/all_gather | solution.py:173
  74.8 261.3 %all-gather.30.cloned.1.call-start = ((), (), s32[]{:S(2)}) async-start(), calls=%async_computation.13 | async-start | bytes 9437184 | tf_op jit(solution)/shard_map/all_gather | solution.py:174
  75.6 349.4 %reduce-scatter.11.cloned.1.call-start = ((), (), s32[]{:S(2)}) async-start(), calls=%async_computation.15 | async-start | bytes 2621440 | tf_op jit(solution)/shard_map/reduce_scatter | solution.py:303
  200.3 7.1 copy-start.8
  201.2 7.5 copy-start.5
  202.0 9.1 copy-start
  202.9 7.0 copy-start.3
  213.3 83.0 %copy-start.33 = (bf16[1,256,16,64]{1,3,2,0:T(8,128)(2,1)}, bf16[1,256,16,64]{1,3,2,0:T(8,128)(2,1)S(1)}, u32[]{:S(2)}) copy-start(bf16[1,256,16,64]{1,3,2,0:T(8,128)(2,1)S(1)} %get-tuple-element.163) | copy-start | bytes 1572868
  213.3 66.6 %copy-start.49 = (f32[8,1,512]{2,1,0:T(1,128)S(1)}, f32[8,1,512]{2,1,0:T(1,128)}, u32[]{:S(2)}) copy-start(f32[8,1,512]{2,1,0:T(1,128)} %convert_element_type.352) | copy-start | bytes 49156
  227.1 69.2 %copy-start.44 = (f32[256]{0:T(256)}, f32[256]{0:T(256)S(1)}, u32[]{:S(2)}) copy-start(f32[256]{0:T(256)S(1)} %add_rsqrt_fusion.1) | copy-start | bytes 3076
  279.8 56.3 %copy-start.52 = (f32[8,1,128]{2,1,0:T(1,128)S(1)}, f32[8,1,128]{2,1,0:T(1,128)}, u32[]{:S(2)}) copy-start(f32[8,1,128]{2,1,0:T(1,128)} %convert_element_type.353) | copy-start | bytes 12292
  336.1 7.7 copy-start.32
  336.1 7.7 copy-start.46
  336.2 9.0 copy-start.47
  346.5 11.4 %copy-start.26 = (f32[1,256,1024]{2,1,0:T(8,128)}, f32[1,256,1024]{2,1,0:T(8,128)S(1)}, u32[]{:S(2)}) copy-start(f32[1,256,1024]{2,1,0:T(8,128)S(1)} %get-tuple-element.120) | copy-start | bytes 3145732
  346.5 11.4 %copy-start.45 = (f32[256]{0:T(256)S(1)}, f32[256]{0:T(256)}, u32[]{:S(2)}) copy-start(f32[256]{0:T(256)} %copy-done.44) | copy-start | bytes 3076
  357.8 6.9 copy-start.35
  357.9 7.3 copy-start.12
  381.0 89.4 %reduce-scatter.9.cloned.1.call-start = ((), (), s32[]{:S(2)}) async-start(), calls=%async_computation.14 | async-start | bytes 2621440 | tf_op jit(solution)/shard_map/reduce_scatter | solution.py:300
  404.0 120.5 %reduce-scatter.19.cloned.1.call-start = ((), (), s32[]{:S(2)}) async-start(), calls=%async_computation.19 | async-start | bytes 4718592 | tf_op jit(solution)/shard_map/reduce_scatter | solution.py:336
  406.8 172.6 %reduce-scatter.13.cloned.1.call-start = ((), (), s32[]{:S(2)}) async-start(), calls=%async_computation.16 | async-start | bytes 4718592 | tf_op jit(solution)/shard_map/reduce_scatter | solution.py:333
  415.1 219.0 %reduce-scatter.17.cloned.1.call-start = ((), (), s32[]{:S(2)}) async-start(), calls=%async_computation.18 | async-start | bytes 4718592 | tf_op jit(solution)/shard_map/reduce_scatter | solution.py:335
  428.7 260.3 %reduce-scatter.15.cloned.1.call-start = ((), (), s32[]{:S(2)}) async-start(), calls=%async_computation.17 | async-start | bytes 4718592 | tf_op jit(solution)/shard_map/reduce_scatter | solution.py:334
  474.1 334.3 %reduce-scatter.21.cloned.1.call-start = ((), (), s32[]{:S(2)}) async-start(), calls=%async_computation.20 | async-start | bytes 18874368 | tf_op jit(solution)/shard_map/reduce_scatter | solution.py:218
  485.4 442.4 %reduce-scatter.23.cloned.1.call-start = ((), (), s32[]{:S(2)}) async-start(), calls=%async_computation.21 | async-start | bytes 18874368 | tf_op jit(solution)/shard_map/reduce_scatter | solution.py:219
  497.0 558.9 %all-reduce.17.cloned.1.call-start = ((), (), s32[]{:S(2)}) async-start(), calls=%async_computation.24 | async-start | bytes 6291456 | tf_op jit(solution)/shard_map/psum | solution.py:344
  690.8 239.8 %copy-start.61 = (u32[32]{0:T(128)S(1)}, u32[32]{0:T(128)}, u32[]{:S(2)}) copy-start(u32[32]{0:T(128)} %constant.108) | copy-start | bytes 388
  690.8 241.7 %copy-start.51 = (s32[1,256]{1,0:T(1,128)S(1)}, s32[1,256]{1,0:T(1,128)}, u32[]{:S(2)}) copy-start(s32[1,256]{1,0:T(1,128)} %param.19) | copy-start | bytes 3076
  690.8 242.3 %copy-start.28 = (f32[256,1024]{1,0:T(8,128)S(1)}, f32[256,1024]{1,0:T(8,128)}, u32[]{:S(2)}) copy-start(f32[256,1024]{1,0:T(8,128)} %get-tuple-element.165) | copy-start | bytes 3145732
  811.1 169.9 %copy-start.19 = (bf16[1,256,1024]{1,2,0:T(8,128)(2,1)S(1)}, bf16[1,256,1024]{1,2,0:T(8,128)(2,1)}, u32[]{:S(2)}) copy-start(bf16[1,256,1024]{1,2,0:T(8,128)(2,1)} %reduce-scatter.11.cloned.1.call-done) | copy-start | bytes 1572868
  1019.1 9.6 copy-start.31
  1055.9 10.3 copy-start.36
  (32 other events, 89.1 us)
Sparse Core Ops, SparseCore 0:
  9.9 30.5 all-gather.23
  42.4 27.8 all-gather.21
  72.3 27.8 all-gather.19
  102.2 45.9 all-gather.33
  150.2 44.6 all-gather.31
  196.6 26.8 all-gather.25
  225.4 54.3 all-gather.27
  281.7 54.3 all-gather.29
  381.1 43.8 reduce-scatter.10
  427.3 43.0 reduce-scatter.8
  473.7 50.6 reduce-scatter.18
  528.0 51.3 reduce-scatter.12
  582.7 51.3 reduce-scatter.16
  637.7 51.3 reduce-scatter.14
  692.5 115.9 reduce-scatter.20
  811.9 115.9 reduce-scatter.22
  931.7 124.2 all-reduce.16
where the time goes:
time: 1090 us; the launch traced here: 1080 us
  waiting for transfers between devices  683 us (63%)
  blocking collectives  167 us (15%)
  matrix products  130 us (12%)
  other arithmetic  43.5 us (4%)
  local copies, waits for them, and re-layouts  31.1 us (3%)
  between operations  22.9 us (2%)
    reduce_scatter x1, waiting for transfers between devices, per_device(): lax.psum_scatter(mlp_terms[0], 'fsdp', scatter_dimension=0, tiled=True)  118 us
    reduce_scatter x1, waiting for transfers between devices, per_device(): lax.psum_scatter(mlp_terms[1], 'fsdp', scatter_dimension=0, tiled=True)  117 us
    reduce_scatter x1, waiting for transfers between devices, per_device(): lax.psum_scatter(attn_terms[1], 'fsdp', scatter_dimension=0, tiled=True)  53.2 us
    reduce_scatter x1, waiting for transfers between devices, per_device(): lax.psum_scatter(attn_terms[0], 'fsdp', scatter_dimension=0, tiled=True)  53.2 us
    reduce_scatter x1, waiting for transfers between devices, per_device(): lax.psum_scatter(attn_terms[2], 'fsdp', scatter_dimension=0, tiled=True)  52.9 us
    all_gather x1, waiting for transfers between devices, per_device(): lax.all_gather(up_weight, 'fsdp', axis=0, tiled=True)  52.1 us
    psum x1, blocking collectives, per_device(): lax.psum((jnp.sum(weighted * token_float * token_float), jnp.sum(weighted...  43 us
    reduce_scatter x1, waiting for transfers between devices, per_device(): lax.psum_scatter(grad_keys_all.astype(jnp.bfloat16), 'ctx', scatter_dimen...  41.6 us
  transfers between devices with their start and end apart: 17, of which 15 were waited for; matrix products, arithmetic and copies ran while one was open for 13% of the time, Pallas kernels for 0%

commit v1 on v0

v1 whole, which is shorter than its diff:
```python
from functools import partial

import jax
import jax.numpy as jnp
from jax import lax
from jax.experimental import pallas as pl
from jax.experimental.pallas import tpu as pltpu
from jax.sharding import PartitionSpec as P

HEADS = 16
HEAD_DIM = 64
SEGS = 8
EPSILON = 1e-05
MASKED = -1000000000.0
SCALE = HEAD_DIM ** (-0.5)
BF = jnp.bfloat16
F32 = jnp.float32

CHUNK = 256
HERE = 4
WIDE = HERE * HEAD_DIM
SHARDS = 8
ROWS = 128
PARAMS = pltpu.CompilerParams(vmem_limit_bytes=60 * 1024 * 1024)


def dot(a, b, dims=((1,), (0,))):
    return lax.dot_general(a, b, (dims, ((), ())), preferred_element_type=F32)


def vec(small_ref, row, start, size):
    return jnp.concatenate(
        [small_ref[f, row : row + 1, start : start + size].astype(F32) for f in range(SHARDS)],
        axis=1,
    )


def any_spec(shape):
    return pl.BlockSpec(shape, lambda *a: (0,) * len(shape))


def segment_setup(z, xs, segr, segc, ends):
    for k in range(4):
        a = lax.rem(z - k + 4, 4)
        row = xs[k][CHUNK : CHUNK + 16, 0:CHUNK].astype(F32)[0:1, :]
        segr[a] = jnp.broadcast_to(row, (8, CHUNK))
        segc[a] = jnp.transpose(jnp.broadcast_to(row, (128, CHUNK)))
        ends[0, a] = jnp.min(row).astype(jnp.int32)
        ends[1, a] = jnp.max(row).astype(jnp.int32)


def key_range(ends, i):
    low = jnp.int32(0)
    high = jnp.int32(4)
    for j in range(4):
        low = low + (ends[1, j] < ends[0, i]).astype(jnp.int32)
        high = high - (ends[0, j] > ends[1, i]).astype(jnp.int32)
    return low, high


def attn_fwd_kernel(
    sc, x0, x1, x2, x3, w, m0, m1, m2, m3, mixf, lse, qkv, segr, segc, ends
):
    z = sc[0]
    xs = (x0, x1, x2, x3)
    segment_setup(z, xs, segr, segc, ends)
    weight = w[:, 0:ROWS, :].reshape(SHARDS * ROWS, 3 * WIDE)
    first = w[2 * z, ROWS : ROWS + 16, :].astype(F32)
    second = w[2 * z + 1, ROWS : ROWS + 16, :].astype(F32)
    qb = jnp.concatenate([first[0:1, 0:128], second[0:1, 0:128]], axis=1)
    vb = jnp.concatenate([first[0:1, 128:256], second[0:1, 128:256]], axis=1)
    for k in range(4):
        a = pl.multiple_of(lax.rem(z - k + 4, 4) * CHUNK, CHUNK)
        prod = dot(xs[k][0:CHUNK, :], weight)
        q = ((prod[:, 0:WIDE] + qb).astype(BF).astype(F32) * SCALE).astype(BF)
        kk = prod[:, WIDE : 2 * WIDE].astype(BF)
        v = (prod[:, 2 * WIDE :] + vb).astype(BF)
        for n, part in enumerate((q, kk, v)):
            for h in range(HERE):
                qkv[n * HERE + h, pl.ds(a, CHUNK), :] = part[:, h * HEAD_DIM : (h + 1) * HEAD_DIM]

    def q_chunk(i, carry):
        rows = pl.ds(pl.multiple_of(i * CHUNK, CHUNK), CHUNK)
        low, high = key_range(ends, i)
        col = segc[i]
        col2 = jnp.concatenate([col, col], axis=1)
        qs = [qkv[h, rows, :] for h in range(HERE)]

        def key_chunk(j, state):
            keys = pl.ds(pl.multiple_of(j * CHUNK, CHUNK), CHUNK)
            mask = col2 == segr[j][0:1, :]
            new = []
            for h in range(HERE):
                m, l, acc = state[h]
                s = dot(qs[h], qkv[HERE + h, keys, :], ((1,), (1,)))
                s = jnp.where(mask, s, MASKED)
                m_new = jnp.maximum(m, jnp.max(s, axis=1, keepdims=True))
                p = jnp.exp(s - m_new)
                fix = jnp.exp(m - m_new)
                l = l * fix + jnp.sum(p, axis=1, keepdims=True)
                acc = acc * fix + dot(p.astype(BF), qkv[2 * HERE + h, keys, :])
                new.append((m_new, l, acc))
            return tuple(new)

        init = tuple(
            (
                jnp.full((CHUNK, 1), MASKED, F32),
                jnp.zeros((CHUNK, 1), F32),
                jnp.zeros((CHUNK, HEAD_DIM), F32),
            )
            for _ in range(HERE)
        )
        state = lax.fori_loop(low, high, key_chunk, init)
        lane = lax.broadcasted_iota(jnp.int32, (CHUNK, 128), 1)
        logs = jnp.zeros((CHUNK, 128), F32)
        for h in range(HERE):
            m, l, acc = state[h]
            mixf[rows, h * HEAD_DIM : (h + 1) * HEAD_DIM] = acc / l
            logs = jnp.where(lane == h, m + jnp.log(l), logs)
        lse[rows, :] = logs
        return carry

    lax.fori_loop(0, 4, q_chunk, 0)
    for k, out in enumerate((m0, m1, m2, m3)):
        a = pl.multiple_of(lax.rem(z - k + 4, 4) * CHUNK, CHUNK)
        out[...] = mixf[pl.ds(a, CHUNK), :].astype(BF)


SMEM_SPEC = pl.BlockSpec(memory_space=pltpu.SMEM)
VMEM_SPEC = pl.BlockSpec(memory_space=pltpu.VMEM)


def attn_fwd(scalars, xs, pack):
    shape = jax.ShapeDtypeStruct
    return pl.pallas_call(
        attn_fwd_kernel,
        name="attn_fwd",
        out_shape=(shape((CHUNK, WIDE), BF),) * 4
        + (
            shape((4 * CHUNK, WIDE), F32),
            shape((4 * CHUNK, 128), F32),
            shape((3 * HERE, 4 * CHUNK, HEAD_DIM), BF),
        ),
        in_specs=[SMEM_SPEC] + [VMEM_SPEC] * 5,
        out_specs=(VMEM_SPEC,) * 7,
        scratch_shapes=[
            pltpu.VMEM((4, 8, CHUNK), F32),
            pltpu.VMEM((4, CHUNK, 128), F32),
            pltpu.SMEM((2, 4), jnp.int32),
        ],
        compiler_params=PARAMS,
    )(scalars, *xs, pack)


def normalise(h):
    centre = h - jnp.mean(h, axis=-1, keepdims=True)
    inverse = lax.rsqrt(jnp.mean(centre * centre, axis=-1, keepdims=True) + EPSILON)
    return centre * inverse, inverse


def norm_pullback(upstream, scaled, inverse, gain):
    e = upstream * gain
    return inverse * (
        e
        - jnp.mean(e, axis=-1, keepdims=True)
        - scaled * jnp.mean(e * scaled, axis=-1, keepdims=True)
    )


def out_kernel(sc, tok, r0, r1, r2, r3, w, small, valid, normed, low, scaled, inv, mixed, stats):
    z = sc[0]
    acc = jnp.zeros((CHUNK, 1024), F32)
    for k, r in enumerate((r0, r1, r2, r3)):
        a = lax.rem(z + k, 4)
        rows = w[pl.ds(2 * a, 2)].reshape(WIDE, 1024)
        acc = acc + dot(r[...], rows)
        mixed[:, pl.ds(pl.multiple_of(a * WIDE, WIDE), WIDE)] = r[...]
    branch = acc + vec(small, 0, 256, 128)
    x = tok[...].astype(F32)
    n, inverse = normalise(x + branch)
    y = n * vec(small, 0, 384, 128) + vec(small, 0, 512, 128)
    normed[...] = y
    low[...] = y.astype(BF)
    scaled[...] = n
    inv[...] = jnp.broadcast_to(inverse, (CHUNK, 128))
    ok = valid[...]
    lane = lax.broadcasted_iota(jnp.int32, (8, 128), 1)
    stats[...] = jnp.where(
        lane == 0,
        jnp.sum(ok * x * x),
        jnp.where(lane == 1, jnp.sum(ok * branch * branch), jnp.where(lane == 3, jnp.sum(ok), 0.0)),
    )


def out_project(scalars, tok, parts, big, pack, valid):
    shape = jax.ShapeDtypeStruct
    full = lambda *s: any_spec(s)
    return pl.pallas_call(
        out_kernel,
        name="out_project",
        grid=(1,),
        out_shape=(
            shape((CHUNK, 1024), F32),
            shape((CHUNK, 1024), BF),
            shape((CHUNK, 1024), F32),
            shape((CHUNK, 128), F32),
            shape((CHUNK, 1024), BF),
            shape((8, 128), F32),
        ),
        in_specs=[SMEM_SPEC, full(CHUNK, 1024)]
        + [full(CHUNK, WIDE)] * 4
        + [
            pl.BlockSpec((SHARDS, ROWS, 1024), lambda j: (0, 8, 0)),
            pl.BlockSpec((SHARDS, 16, 768), lambda j: (0, 8, 0)),
            full(CHUNK, 1),
        ],
        out_specs=(
            full(CHUNK, 1024),
            full(CHUNK, 1024),
            full(CHUNK, 1024),
            full(CHUNK, 128),
            full(CHUNK, 1024),
            full(8, 128),
        ),
        compiler_params=PARAMS,
    )(scalars, tok, *parts, big, pack, valid)


def mlp_fwd_kernel(
    normed, low, up, down, small, cot, valid, hidden, slope, out, gh2, gm, sums, stats, acc
):
    j = pl.program_id(0)
    gate = dot(low[...], up[...].reshape(SHARDS * ROWS, 512))
    gate = gate + small[j, 1:2, 256:768].astype(F32)
    cdf = 0.5 * (1.0 + lax.erf(gate * (2.0 ** -0.5)))
    h = (gate * cdf).astype(BF)
    hidden[...] = h
    slope[...] = cdf + gate * (jnp.exp(-0.5 * gate * gate) * 0.3989422804014327)
    part = dot(h, down[...].reshape(512, 1024))

    @pl.when(j == 0)
    def _():
        acc[...] = part

    @pl.when(j > 0)
    def _():
        acc[...] += part

    @pl.when(j == SHARDS - 1)
    def _():
        branch = acc[...] + vec(small, 0, 640, 128)
        n, inverse = normalise(normed[...] + branch)
        gain = vec(small, 1, 0, 128)
        out[...] = (n * gain + vec(small, 1, 128, 128)).astype(BF)
        ok = valid[...]
        u = cot[...].astype(F32) * ok
        g = norm_pullback(u, n, inverse, gain)
        gh2[...] = g
        g_low = g.astype(BF)
        gm[...] = g_low
        sums[0:1, :] = jnp.sum(u * n, axis=0, keepdims=True)
        sums[1:2, :] = jnp.sum(u, axis=0, keepdims=True)
        sums[2:3, :] = jnp.sum(g_low.astype(F32), axis=0, keepdims=True)
        sums[3:8, :] = jnp.zeros((5, 1024), F32)
        lane = lax.broadcasted_iota(jnp.int32, (8, 128), 1)
        stats[...] = jnp.where(lane == 2, jnp.sum(ok * branch * branch), 0.0)


def mlp_fwd(normed, low, big, pack, cot, valid):
    shape = jax.ShapeDtypeStruct
    full = lambda *s: any_spec(s)
    return pl.pallas_call(
        mlp_fwd_kernel,
        name="mlp_fwd",
        grid=(SHARDS,),
        out_shape=(
            shape((CHUNK, 4096), BF),
            shape((CHUNK, 4096), F32),
            shape((CHUNK, 1024), BF),
            shape((CHUNK, 1024), F32),
            shape((CHUNK, 1024), BF),
            shape((8, 1024), F32),
            shape((8, 128), F32),
        ),
        in_specs=[
            full(CHUNK, 1024),
            full(CHUNK, 1024),
            pl.BlockSpec((SHARDS, ROWS, 512), lambda j: (0, 4 + j // 2, j % 2)),
            pl.BlockSpec((1, 512, 1024), lambda j: (j, 0, 0)),
            pl.BlockSpec((SHARDS, 16, 768), lambda j: (0, 8, 0)),
            full(CHUNK, 1024),
            full(CHUNK, 1),
        ],
        out_specs=(
            pl.BlockSpec((CHUNK, 512), lambda j: (0, j)),
            pl.BlockSpec((CHUNK, 512), lambda j: (0, j)),
            full(CHUNK, 1024),
            full(CHUNK, 1024),
            full(CHUNK, 1024),
            full(8, 1024),
            full(8, 128),
        ),
        scratch_shapes=[pltpu.VMEM((CHUNK, 1024), F32)],
        compiler_params=PARAMS,
    )(normed, low, big, big, pack, cot, valid)


ORDER = (3, 1, 2, 0)


def step_shard(j, sc):
    half = j // 2
    rel = jnp.where(half == 0, 3, jnp.where(half == 3, 0, half))
    return 2 * jnp.bitwise_xor(sc[1], rel) + jnp.bitwise_xor(sc[2], 1 - j % 2)


def step_rel(j):
    half = j // 2
    return jnp.where(half == 0, 3, jnp.where(half == 3, 0, half))


def mlp_bwd_kernel(
    sc,
    gm,
    hidden,
    slope,
    up,
    down,
    low,
    gh2,
    scaled,
    inv,
    small,
    mixed,
    wout,
    gd_keep,
    gd_send,
    gu_keep,
    gu_send,
    go_keep,
    go_send,
    gh1,
    g0,
    g1,
    g2,
    g3,
    sums,
    ub,
    acc,
    low_t,
):
    j = pl.program_id(0)
    f = step_shard(j, sc)
    chip, core, z = sc[1], sc[2], sc[0]

    @pl.when(j == 0)
    def _():
        low_t[...] = jnp.transpose(low[...])

    grad = gm[...]
    dh = dot(grad, down[...].reshape(512, 1024), ((1,), (1,)))
    gg = dh * slope[...]
    gg_low = gg.astype(BF)
    ub[pl.ds(f, 1)] = jnp.sum(gg_low.astype(F32), axis=0, keepdims=True).reshape(1, 1, 512)
    gd = dot(hidden[...], grad, ((0,), (0,))).astype(BF)

    @pl.when(j % 2 == 0)
    def _():
        gd_send[...] = gd.reshape(1, 512, 1024)

    @pl.when(j % 2 == 1)
    def _():
        gd_keep[...] = gd.reshape(1, 512, 1024)

    for r in range(4):
        rows = 2 * jnp.bitwise_xor(chip, r)
        at = pl.multiple_of((rows + core) * ROWS, ROWS)
        gu_keep[r] = dot(low_t[pl.ds(at, ROWS), :], gg_low).astype(BF)
        at = pl.multiple_of((rows + 1 - core) * ROWS, ROWS)
        gu_send[r] = dot(low_t[pl.ds(at, ROWS), :], gg_low).astype(BF)
    part = dot(gg_low, up[...].reshape(SHARDS * ROWS, 512), ((1,), (1,)))

    @pl.when(j == 0)
    def _():
        acc[...] = part

    @pl.when(j > 0)
    def _():
        acc[...] += part

    @pl.when(j == SHARDS - 1)
    def _():
        u = gh2[...] + acc[...]
        n = scaled[...]
        g = norm_pullback(u, n, inv[:, 0:1], vec(small, 0, 384, 128))
        gh1[...] = g
        g_low = g.astype(BF)
        sums[0:1, :] = jnp.sum(u * n, axis=0, keepdims=True)
        sums[1:2, :] = jnp.sum(u, axis=0, keepdims=True)
        sums[2:3, :] = jnp.sum(g_low.astype(F32), axis=0, keepdims=True)
        sums[3:8, :] = jnp.zeros((5, 1024), F32)
        go = dot(mixed[...], g_low, ((0,), (0,)))
        acc_o = go.astype(BF).reshape(SHARDS, ROWS, 1024)
        low_t[...] = jnp.zeros_like(low_t)
        for f_at in range(SHARDS):
            rel = jnp.bitwise_xor(chip, f_at // 2)

            @pl.when(core == f_at % 2)
            def _():
                go_keep[rel] = acc_o[f_at]

            @pl.when(core != f_at % 2)
            def _():
                go_send[rel] = acc_o[f_at]

        for k, out in enumerate((g0, g1, g2, g3)):
            a = lax.rem(z + k, 4)
            rows = wout[pl.ds(2 * a, 2)].reshape(WIDE, 1024)
            out[...] = dot(g_low, rows, ((1,), (1,))).astype(BF)


def mlp_bwd(scalars, gm, hidden, slope, big, low, gh2, scaled, inv, pack, mixed):
    shape = jax.ShapeDtypeStruct
    full = lambda *s: pl.BlockSpec(s, lambda j, sc: (0,) * len(s))
    keep_down = pl.BlockSpec((1, 512, 1024), lambda j, sc: (step_rel(j), 0, 0))

    def up_at(j, sc):
        f = step_shard(j, sc)
        return (0, f // 2, f % 2)

    keep_up = pl.BlockSpec((4, ROWS, 512), up_at)
    return pl.pallas_call(
        mlp_bwd_kernel,
        name="mlp_bwd",
        grid_spec=pltpu.PrefetchScalarGridSpec(
            num_scalar_prefetch=1,
            grid=(SHARDS,),
            in_specs=[
                full(CHUNK, 1024),
                pl.BlockSpec((CHUNK, 512), lambda j, sc: (0, step_shard(j, sc))),
                pl.BlockSpec((CHUNK, 512), lambda j, sc: (0, step_shard(j, sc))),
                pl.BlockSpec(
                    (SHARDS, ROWS, 512),
                    lambda j, sc: (0, 4 + step_shard(j, sc) // 2, step_shard(j, sc) % 2),
                ),
                pl.BlockSpec((1, 512, 1024), lambda j, sc: (step_shard(j, sc), 0, 0)),
                full(CHUNK, 1024),
                full(CHUNK, 1024),
                full(CHUNK, 1024),
                full(CHUNK, 128),
                pl.BlockSpec((SHARDS, 16, 768), lambda j, sc: (0, 8, 0)),
                full(CHUNK, 1024),
                pl.BlockSpec((SHARDS, ROWS, 1024), lambda j, sc: (0, 8, 0)),
            ],
            out_specs=(
                keep_down,
                keep_down,
                keep_up,
                keep_up,
                full(4, ROWS, 1024),
                full(4, ROWS, 1024),
                full(CHUNK, 1024),
            )
            + (full(CHUNK, WIDE),) * 4
            + (full(8, 1024), full(SHARDS, 1, 512)),
            scratch_shapes=[pltpu.VMEM((CHUNK, 1024), F32), pltpu.VMEM((1024, CHUNK), BF)],
        ),
        out_shape=(
            shape((4, 512, 1024), BF),
            shape((4, 512, 1024), BF),
            shape((4, 512, 1024), BF),
            shape((4, 512, 1024), BF),
            shape((4, ROWS, 1024), BF),
            shape((4, ROWS, 1024), BF),
            shape((CHUNK, 1024), F32),
        )
        + (shape((CHUNK, WIDE), BF),) * 4
        + (shape((8, 1024), F32), shape((SHARDS, 1, 512), F32)),
        compiler_params=PARAMS,
    )(scalars, gm, hidden, slope, big, big, low, gh2, scaled, inv, pack, mixed, big)


def attn_bwd_kernel(
    sc,
    x0,
    x1,
    x2,
    x3,
    w,
    qkv,
    mixf,
    lse,
    g0,
    g1,
    g2,
    g3,
    own,
    s1,
    s2,
    s3,
    gw_keep,
    gw_send,
    sums,
    segr,
    segc,
    ends,
    gs,
    dq,
    dk,
    dv,
    delta,
    dall,
    gw,
):
    z, chip, core = sc[0], sc[1], sc[2]
    xs = (x0, x1, x2, x3)
    segment_setup(z, xs, segr, segc, ends)
    dk[...] = jnp.zeros_like(dk)
    dv[...] = jnp.zeros_like(dv)
    lane = lax.broadcasted_iota(jnp.int32, (CHUNK, 128), 1)
    for k, g in enumerate((g0, g1, g2, g3)):
        rows = pl.ds(pl.multiple_of(lax.rem(z - k + 4, 4) * CHUNK, CHUNK), CHUNK)
        prod = g[...].astype(F32) * mixf[rows, :]
        d = jnp.zeros((CHUNK, 128), F32)
        for h in range(HERE):
            at = slice(h * HEAD_DIM, (h + 1) * HEAD_DIM)
            gs[h, rows, :] = g[:, at]
            d = jnp.where(lane == h, jnp.sum(prod[:, at], axis=1, keepdims=True), d)
        delta[rows, :] = d

    def q_chunk(i, carry):
        rows = pl.ds(pl.multiple_of(i * CHUNK, CHUNK), CHUNK)
        low, high = key_range(ends, i)
        col = segc[i]
        col2 = jnp.concatenate([col, col], axis=1)
        logs = lse[rows, :]
        deltas = delta[rows, :]
        dq[...] = jnp.zeros_like(dq)

        def key_chunk(j, inner):
            keys = pl.ds(pl.multiple_of(j * CHUNK, CHUNK), CHUNK)
            mask = col2 == segr[j][0:1, :]
            for h in range(HERE):
                q = qkv[h, rows, :]
                kk = qkv[HERE + h, keys, :]
                v = qkv[2 * HERE + h, keys, :]
                g = gs[h, rows, :]
                s = dot(q, kk, ((1,), (1,)))
                p = jnp.where(mask, jnp.exp(s - logs[:, h : h + 1]), 0.0)
                dp = dot(g, v, ((1,), (1,)))
                ds = (p * (dp - deltas[:, h : h + 1])).astype(BF)
                dv[h, keys, :] += dot(p.astype(BF), g, ((0,), (0,)))
                dk[h, keys, :] += dot(ds, q, ((0,), (0,)))
                dq[h] += dot(ds, kk)
            return inner

        lax.fori_loop(low, high, key_chunk, 0)
        for h in range(HERE):
            dall[rows, h * HEAD_DIM : (h + 1) * HEAD_DIM] = (dq[h] * SCALE).astype(BF)
        return carry

    lax.fori_loop(0, 4, q_chunk, 0)
    for h in range(HERE):
        at = WIDE + h * HEAD_DIM
        dall[:, at : at + HEAD_DIM] = dk[h].astype(BF)
        at = 2 * WIDE + h * HEAD_DIM
        dall[:, at : at + HEAD_DIM] = dv[h].astype(BF)
    sums[0:1, :] = jnp.sum(dall[:, 0:WIDE].astype(F32), axis=0, keepdims=True)
    sums[1:2, :] = jnp.sum(dall[:, 2 * WIDE :].astype(F32), axis=0, keepdims=True)
    sums[2:8, :] = jnp.zeros((6, WIDE), F32)
    weight = w[:, 0:ROWS, :].reshape(SHARDS * ROWS, 3 * WIDE)
    for k, out in enumerate((own, s1, s2, s3)):
        rows = pl.ds(pl.multiple_of(lax.rem(z - k + 4, 4) * CHUNK, CHUNK), CHUNK)
        d = dall[rows, :]
        out[...] = dot(d, weight, ((1,), (1,))).astype(out.dtype)
        part = dot(xs[k][0:CHUNK, :], d, ((0,), (0,)))
        if k == 0:
            gw[...] = part
        else:
            gw[...] += part
    for r in range(4):
        at = 2 * jnp.bitwise_xor(chip, r)
        gw_keep[r] = gw[pl.ds(pl.multiple_of((at + core) * ROWS, ROWS), ROWS), :].astype(BF)
        gw_send[r] = gw[pl.ds(pl.multiple_of((at + 1 - core) * ROWS, ROWS), ROWS), :].astype(BF)


def attn_bwd(scalars, xs, pack, qkv, mixf, lse, gs):
    shape = jax.ShapeDtypeStruct
    return pl.pallas_call(
        attn_bwd_kernel,
        name="attn_bwd",
        out_shape=(shape((CHUNK, 1024), F32),)
        + (shape((CHUNK, 1024), BF),) * 3
        + (shape((4, ROWS, 768), BF),) * 2
        + (shape((8, WIDE), F32),),
        in_specs=[SMEM_SPEC] + [VMEM_SPEC] * 12,
        out_specs=(VMEM_SPEC,) * 7,
        scratch_shapes=[
            pltpu.VMEM((4, 8, CHUNK), F32),
            pltpu.VMEM((4, CHUNK, 128), F32),
            pltpu.SMEM((2, 4), jnp.int32),
            pltpu.VMEM((HERE, 4 * CHUNK, HEAD_DIM), BF),
            pltpu.VMEM((HERE, CHUNK, HEAD_DIM), F32),
            pltpu.VMEM((HERE, 4 * CHUNK, HEAD_DIM), F32),
            pltpu.VMEM((HERE, 4 * CHUNK, HEAD_DIM), F32),
            pltpu.VMEM((4 * CHUNK, 128), F32),
            pltpu.VMEM((4 * CHUNK, 768), BF),
            pltpu.VMEM((1024, 768), F32),
        ],
        compiler_params=PARAMS,
    )(scalars, *xs, pack, qkv, mixf, lse, *gs)


def shift(x, k):
    n = lax.axis_size("ctx")
    return lax.ppermute(x, "ctx", [(i, (i + k) % n) for i in range(n)])


def swap(x, bits):
    return lax.ppermute(x, "fsdp", [(i, i ^ bits) for i in range(lax.axis_size("fsdp"))])


def gather_rows(x):
    full = lax.all_gather(x, "fsdp", axis=0, tiled=False)
    owners = full.shape[0]
    return full if owners == SHARDS else full


def add(*terms):
    total = terms[0].astype(F32)
    for term in terms[1:]:
        total = total + term.astype(F32)
    return total


def plane_sum(keep, send, direct):
    got = swap(send, 1)
    rows = keep.shape[1]
    part = lambda r, a, b: add(keep[r, a:b], got[r, a:b])
    if direct:
        far = swap(part(3, 0, rows).astype(BF), 6)
        along = swap(part(1, 0, rows).astype(BF), 2)
        across = swap(part(2, 0, rows).astype(BF), 4)
        return add(part(0, 0, rows), along, across, far)
    half = rows // 2
    from_x = swap(part(3, 0, half).astype(BF), 2)
    from_y = swap(part(3, half, rows).astype(BF), 4)
    to_y = jnp.concatenate([add(part(2, 0, half), from_x), part(2, half, rows)]).astype(BF)
    to_x = jnp.concatenate([part(1, 0, half), add(part(1, half, rows), from_y)]).astype(BF)
    return add(part(0, 0, rows), swap(to_x, 2), swap(to_y, 4))


def line_sum(x):
    index = lax.axis_index("ctx")
    mine = x.astype(BF)
    pair = add(mine, lax.ppermute(mine, "ctx", [(0, 1), (3, 2)])).astype(BF)
    whole = add(pair, lax.ppermute(pair, "ctx", [(1, 2), (2, 1)])).astype(BF)
    back = lax.ppermute(whole, "ctx", [(1, 0), (2, 3)])
    inner = (index == 1) | (index == 2)
    return jnp.where(inner, whole, back).astype(F32)


def everyone_sum(x):
    owners = lax.axis_size("fsdp")
    step = 1
    while step < owners:
        x = x + swap(x, step)
        step *= 2
    x = x + lax.ppermute(x, "ctx", [(0, 1), (1, 0), (2, 3), (3, 2)])
    return x + lax.ppermute(x, "ctx", [(0, 2), (2, 0), (1, 3), (3, 1)])


def per_device(
    tokens,
    segment_ids,
    cotangent,
    query_weight,
    query_bias,
    key_weight,
    value_weight,
    value_bias,
    out_weight,
    out_bias,
    attn_gain,
    attn_shift,
    up_weight,
    up_bias,
    down_weight,
    down_bias,
    mlp_gain,
    mlp_shift,
):
    owners = lax.axis_size("fsdp")
    plane = owners == SHARDS
    z = lax.axis_index("ctx")
    f = lax.axis_index("fsdp")
    if plane:
        chip, core = f // 2, f % 2
    else:
        chip, core = jnp.int32(0), jnp.int32(0)
    scalars = jnp.stack([z, chip, core, z]).astype(jnp.int32)
    tok = tokens[0]
    seg_row = jnp.pad(segment_ids.astype(BF), ((0, 15), (0, 1024 - CHUNK)))
    packed = jnp.concatenate([tok, seg_row])
    xs = [packed] + [shift(packed, k) for k in (1, 2, 3)]
    valid = (segment_ids[0] != SEGS - 1).astype(F32)[:, None]

    quarter = jnp.concatenate(
        [
            lax.dynamic_slice_in_dim(m, z * WIDE, WIDE, 1)
            for m in (query_weight, key_weight, value_weight)
        ],
        axis=1,
    )
    if plane:
        line0 = jnp.concatenate(
            [query_bias, value_bias, out_bias, attn_gain, attn_shift, down_bias]
        )
        line1 = jnp.concatenate([mlp_gain, mlp_shift, up_bias])
        lines = jnp.pad(jnp.stack([line0, line1]), ((0, 14), (0, 0)))
        pack = lax.all_gather(jnp.concatenate([quarter, lines]), "fsdp", axis=0)
        ups = [up_weight[:, 1024 * b : 1024 * (b + 1)] for b in range(4)]
        big = lax.all_gather(
            jnp.concatenate([down_weight] + ups + [out_weight]), "fsdp", axis=0
        )
    else:
        whole = lambda m: lax.all_gather(m, "fsdp", axis=0, tiled=True)
        split = lambda m: whole(m).reshape(SHARDS, -1)
        line0 = jnp.concatenate(
            [split(m) for m in (query_bias, value_bias, out_bias, attn_gain, attn_shift, down_bias)],
            axis=1,
        )
        line1 = jnp.concatenate([split(m) for m in (mlp_gain, mlp_shift, up_bias)], axis=1)
        lines = jnp.pad(jnp.stack([line0, line1], axis=1), ((0, 0), (0, 14), (0, 0)))
        pack = jnp.concatenate([whole(quarter).reshape(SHARDS, ROWS, 768), lines], axis=1)
        up = whole(up_weight).reshape(SHARDS, ROWS, 4, 1024).swapaxes(1, 2)
        big = jnp.concatenate(
            [
                whole(down_weight).reshape(SHARDS, 512, 1024),
                up.reshape(SHARDS, 512, 1024),
                whole(out_weight).reshape(SHARDS, ROWS, 1024),
            ],
            axis=1,
        )

    m0, m1, m2, m3, mixf, lse, qkv = attn_fwd(scalars, xs, pack)
    parts = [m0] + [shift(m, -k) for k, m in ((1, m1), (2, m2), (3, m3))]
    normed, low, scaled, inv, mixed, stats_a = out_project(scalars, tok, parts, big, pack, valid)
    hidden, slope, result, gh2, gm, sums_m, stats_m = mlp_fwd(
        normed, low, big, pack, cotangent[0], valid
    )
    (
        gd_keep,
        gd_send,
        gu_keep,
        gu_send,
        go_keep,
        go_send,
        gh1,
        g0,
        g1,
        g2,
        g3,
        sums_a,
        ub,
    ) = mlp_bwd(scalars, gm, hidden, slope, big, low, gh2, scaled, inv, pack, mixed)
    gs = [g0] + [shift(g, k) for k, g in ((1, g1), (2, g2), (3, g3))]
    own, s1, s2, s3, gw_keep, gw_send, sums_q = attn_bwd(scalars, xs, pack, qkv, mixf, lse, gs)
    input_grad = gh1 + add(own, *[shift(s, -k) for k, s in ((1, s1), (2, s2), (3, s3))])

    place = lambda row: lax.dynamic_update_slice(
        jnp.zeros((1, 1024), F32), row, (0, z * WIDE)
    )
    smalls = jnp.concatenate(
        [
            sums_m[0:3],
            sums_a[0:3],
            place(sums_q[0:1]),
            place(sums_q[1:2]),
            ub.reshape(4, 1024),
            jnp.pad(stats_a[0:1] + stats_m[0:1], ((0, 3), (0, 1024 - 128))),
        ]
    )
    if plane:
        smalls = everyone_sum(smalls)
    else:
        smalls = lax.psum(smalls, ("ctx", "fsdp"))
    size = 1024 // owners
    mine = lambda row: lax.dynamic_slice(smalls, (row, f * size), (1, size)).reshape(size)
    up_bias_grad = lax.dynamic_slice(
        smalls[8:12].reshape(4096), (f * (4096 // owners),), (4096 // owners,)
    )
    counted = smalls[12, 3] * 1024
    rms = [jnp.sqrt(smalls[12, n] / counted) for n in range(3)]

    if plane:
        down_own = plane_sum(gd_keep, gd_send, False)
        up_own = plane_sum(gu_keep, gu_send, False)
        out_own = plane_sum(go_keep, go_send, True)
        q_own = plane_sum(gw_keep, gw_send, True)
        grad_down = line_sum(down_own)
        rest = line_sum(jnp.concatenate([up_own, out_own]))
        grad_up = jnp.concatenate([rest[ROWS * b : ROWS * (b + 1)] for b in range(4)], axis=1)
        grad_out = rest[512:]
    else:
        both = lambda keep, send: jnp.stack([keep, send], axis=1)
        scatter = lambda m: lax.psum_scatter(m, "fsdp", scatter_dimension=0, tiled=True)
        down_own = scatter(both(gd_keep, gd_send).reshape(4096, 1024))
        up_own = scatter(
            both(gu_keep, gu_send)
            .reshape(SHARDS, 4, ROWS, 1024)
            .swapaxes(1, 2)
            .reshape(1024, 4096)
        )
        out_own = scatter(both(go_keep, go_send).reshape(1024, 1024))
        q_own = scatter(both(gw_keep, gw_send).reshape(1024, 768))
        grad_down, grad_up, grad_out = line_sum(down_own), line_sum(up_own), line_sum(out_own)
    q_low = q_own.astype(BF)
    pieces = [q_low] + [shift(q_low, k) for k in (1, 2, 3)]
    table = jnp.stack(pieces)
    table = jnp.take(table, (z - jnp.arange(4)) % 4, axis=0).astype(F32)
    cols = lambda n: jnp.concatenate(
        [table[a, :, n * WIDE : (n + 1) * WIDE] for a in range(4)], axis=1
    )
    return (
        result[None],
        input_grad[None],
        cols(0),
        mine(6),
        cols(1),
        cols(2),
        mine(7),
        grad_out,
        mine(5),
        mine(3),
        mine(4),
        grad_up,
        up_bias_grad,
        grad_down,
        mine(2),
        mine(0),
        mine(1),
        rms[0],
        rms[1],
        rms[2],
    )


def solution(mesh):
    matrix, vector = P("fsdp", None), P("fsdp")
    stream = P("fsdp", "ctx", None)
    placed = (
        stream,
        P("fsdp", "ctx"),
        stream,
        matrix,
        vector,
        matrix,
        matrix,
        vector,
        matrix,
        vector,
        vector,
        vector,
        matrix,
        vector,
        matrix,
        vector,
        vector,
        vector,
    )
    return jax.shard_map(
        per_device,
        mesh=mesh,
        in_specs=placed,
        out_specs=(
            stream,
            stream,
            matrix,
            vector,
            matrix,
            matrix,
            vector,
            matrix,
            vector,
            vector,
            vector,
            matrix,
            vector,
            matrix,
            vector,
            vector,
            vector,
            P(),
            P(),
            P(),
        ),
        check_vma=False,
    )
```

time: 1090 us -> 515 us (0.47)
  waiting for transfers between devices: 683 us -> 274 us
  blocking collectives: 167 us -> 0 us
  matrix products: 130 us -> 0 us
  Pallas kernels: 0 us -> 100 us
  starting transfers between devices: 1.15 us -> 65.1 us
  local copies, waits for them, and re-layouts: 31.1 us -> 17.1 us
    reduce_scatter x8 -> x0, waiting for transfers between devices: 472 us -> none  [the longest x1 118 us: per_device(): lax.psum_scatter(mlp_terms[0], 'fsdp', scatter_dimension=0, tiled=True)]
    ppermute x0 -> x44, waiting for transfers between devices: none -> 238 us  [the longest x15 110 us: shift(): return lax.ppermute(x, 'ctx', [(i, (i + k) % n) for i in range(n)])]
    all_gather x8 -> x2, waiting for transfers between devices: 181 us -> 36.2 us  [the longest x1 36.2 us: per_device(): lax.all_gather(jnp.concatenate([down_weight] + ups + [out_weight]), 'fsdp...]
    dot_general x42 -> x0, matrix products: 130 us -> none  [the longest x6 35.9 us: matmul(): jnp.einsum('akz,zm->akm', layer_activations, weight_matrix, preferred_ele...]
    pallas_call x0 -> x5, Pallas kernels: none -> 100 us  [the longest x1 30.7 us: attn_bwd(): pl.pallas_call(attn_bwd_kernel, name='attn_bwd', out_shape=(shape((CHUNK,...]
    all_gather x10 -> x0, blocking collectives: 87.2 us -> none  [the longest x1 10.9 us: per_device(): lax.all_gather(segment_ids, 'ctx', axis=1, tiled=True)]
    ppermute x0 -> x44, starting transfers between devices: none -> 65 us  [the longest x15 36.1 us: shift(): return lax.ppermute(x, 'ctx', [(i, (i + k) % n) for i in range(n)])]
    psum x2 -> x0, blocking collectives: 55.6 us -> none  [the longest x1 43 us: per_device(): lax.psum((jnp.sum(weighted * token_float * token_float), jnp.sum(weighted...]
  transfers between devices with their start and end apart: 17 -> 46, of which waited for: 15 -> 24; matrix products, arithmetic and copies ran while one was open for 13% -> 8% of each run, Pallas kernels for 0% -> 10%
where the time goes in v1:
time: 515 us; the launch traced here: 514 us
  waiting for transfers between devices  274 us (53%)
  Pallas kernels  100 us (19%)
  starting transfers between devices  65.1 us (13%)
  other arithmetic  36.2 us (7%)
  between operations  20.9 us (4%)
  local copies, waits for them, and re-layouts  17.1 us (3%)
    ppermute x15, waiting for transfers between devices, shift(): return lax.ppermute(x, 'ctx', [(i, (i + k) % n) for i in range(n)])  110 us
    ppermute x21, waiting for transfers between devices, swap(): lax.ppermute(x, 'fsdp', [(i, i ^ bits) for i in range(lax.axis_size('fsdp...  58.2 us
    all_gather x1, waiting for transfers between devices, per_device(): lax.all_gather(jnp.concatenate([down_weight] + ups + [out_weight]), 'fsdp...  36.2 us
    ppermute x15, starting transfers between devices, shift(): return lax.ppermute(x, 'ctx', [(i, (i + k) % n) for i in range(n)])  36.1 us
    ppermute x1, waiting for transfers between devices, everyone_sum(): x = x + lax.ppermute(x, 'ctx', [(0, 1), (1, 0), (2, 3), (3, 2)])  32.4 us
    pallas_call x1, Pallas kernels, attn_bwd(): pl.pallas_call(attn_bwd_kernel, name='attn_bwd', out_shape=(shape((CHUNK,...  30.7 us
    pallas_call x1, Pallas kernels, mlp_bwd(): pl.pallas_call(mlp_bwd_kernel, name='mlp_bwd', grid_spec=pltpu.PrefetchSc...  27.5 us
    ppermute x1, waiting for transfers between devices, everyone_sum(): return x + lax.ppermute(x, 'ctx', [(0, 2), (2, 0), (1, 3), (3, 1)])  21.1 us
  transfers between devices with their start and end apart: 46, of which 24 were waited for; matrix products, arithmetic and copies ran while one was open for 8% of the time, Pallas kernels for 10%

profile of v1, /device:TPU:0, one launch (start us, length us, event | category | flops | bytes accessed | tf_op | source)
XLA Modules:
  0.0 513.6 jit_solution(12761382910768724215)
XLA Ops:
  18.0 3.1 collective-permute-start
  21.1 2.6 collective-permute-start.1
  25.6 11.1 %collective-permute-done.x1 = bf16[272,1024]{1,0:T(8,128)(2,1)S(1)} collective-permute-done((bf16[272,1024]{1,0:T(8,128)(2,1)S(1)}, bf16[272,1024]{1,0:T(8,128)(2,1)S(1)}, u32[]{:S(2)}, u32[]{:S(2)}) %collective-permute-start) | collective-permute-done | bytes 557088 | tf_op jit(solution)/shard_map/ppermute | solution.py:616
  36.7 23.0 %collective-permute-done.1.x2 = bf16[272,1024]{1,0:T(8,128)(2,1)S(1)} collective-permute-done((bf16[272,1024]{1,0:T(8,128)(2,1)S(1)}, bf16[272,1024]{1,0:T(8,128)(2,1)S(1)}, u32[]{:S(2)}, u32[]{:S(2)}) %collective-permute-start.1) | collective-permute-done | bytes 557088 | tf_op jit(solution)/shard_map/ppermute | solution.py:616
  60.8 20.9 %attn_fwd.1 = (bf16[256,256]{1,0:T(8,128)(2,1)}, bf16[256,256]{1,0:T(8,128)(2,1)}, bf16[256,256]{1,0:T(8,128)(2,1)}, bf16[256,256]{1,0:T(8,128)(2,1)}, f32[1024,...) custom-call(s32[4]{0:T(128)} %pad_add_fusion.sc, bf16[272,1024]{1,0:T(8,128)(2,1)} %copy-done.2, ...), custom_call_target="tpu_custom_call" | custom-call | tf_op jit(solution)/shard_map/attn_fwd/pallas_call | solution.py:135
  81.6 14.5 %collective-permute-start.3 = (bf16[256,256]{1,0:T(8,128)(2,1)}, bf16[256,256]{1,0:T(8,128)(2,1)S(1)}, u32[]{:S(2)}, u32[]{:S(2)}) collective-permute-start(bf16[256,256]{1,0:T(8,128)(2,1)} %get-tuple-element.61), channel_id=1, source_target_pairs={{0,24},{8,0},{16,8},{24,16},{1,25},{9,1},{17,9},{25,17},{2,26},{10... | collective-permute-start | bytes 393224 | tf_op jit(solution)/shard_map/ppermute | solution.py:616
  97.5 2.8 collective-permute-done.3.r1
  100.3 8.2 %collective-permute-done.4.r2 = bf16[256,256]{1,0:T(8,128)(2,1)S(1)} collective-permute-done((bf16[256,256]{1,0:T(8,128)(2,1)}, bf16[256,256]{1,0:T(8,128)(2,1)S(1)}, u32[]{:S(2)}, u32[]{:S(2)}) %collective-permute-start.4) | collective-permute-done | bytes 131104 | tf_op jit(solution)/shard_map/ppermute | solution.py:616
  108.5 36.2 %all-gather.7.cloned.1.call-done = bf16[9216,1024]{1,0:T(8,128)(2,1)} async-done(((bf16[1152,1024]{1,0:T(8,128)(2,1)}), bf16[9216,1024]{1,0:T(8,128)(2,1)}) %all-gather.7.cloned.1.call-update) | async-done | bytes 18874384 | tf_op jit(solution)/shard_map/all_gather | solution.py:723
  144.7 5.0 out_project.1
  149.7 16.2 %mlp_fwd.1 = (bf16[256,4096]{1,0:T(8,128)(2,1)}, f32[256,4096]{1,0:T(8,128)}, bf16[256,1024]{1,0:T(8,128)(2,1)}, f32[256,1024]{1,0:T(8,128)}, bf16[256,1024]{1,0...) custom-call(f32[256,1024]{1,0:T(8,128)} %get-tuple-element.64.normed, bf16[256,1024]{1,0:T(8,128)(2,1)} %get-tuple-element.65.low, ...), custom_call_target="tpu_custom_call" | custom-call | tf_op jit(solution)/shard_map/mlp_fwd/pallas_call | solution.py:272
  165.9 27.5 %mlp_bwd.1 = (bf16[4,512,1024]{2,1,0:T(8,128)(2,1)}, bf16[4,512,1024]{2,1,0:T(8,128)(2,1)}, bf16[4,512,1024]{2,1,0:T(8,128)(2,1)}, bf16[4,512,1024]{2,1,0:T(8,12...) custom-call(s32[4]{0:T(128)} %pad_add_fusion.sc, ...), custom_call_target="tpu_custom_call" | custom-call | tf_op jit(solution)/shard_map/mlp_bwd/pallas_call | solution.py:432
  194.2 1.5 collective-permute-start.6
  195.7 2.4 collective-permute-start.7
  198.1 2.7 collective-permute-done.24
  200.8 4.1 fusion.10
  205.6 2.7 collective-permute-done.29
  208.3 1.5 collective-permute-start.27
  211.9 7.2 %collective-permute-done.25 = bf16[256,1024]{1,0:T(8,128)(2,1)S(1)} collective-permute-done((bf16[256,1024]{1,0:T(8,128)(2,1)S(1)}, bf16[256,1024]{1,0:T(8,128)(2,1)S(1)}, u32[]{:S(2)}, u32[]{:S(2)}) %collective-permute-start.25) | collective-permute-done | bytes 524320 | tf_op jit(solution)/shard_map/ppermute | solution.py:620
  219.7 3.4 collective-permute-done.27
  223.1 1.5 collective-permute-start.39
  224.5 1.8 fusion.8
  227.5 10.4 %collective-permute-done.37 = bf16[256,1024]{1,0:T(8,128)(2,1)S(1)} collective-permute-done((bf16[256,1024]{1,0:T(8,128)(2,1)S(1)}, bf16[256,1024]{1,0:T(8,128)(2,1)S(1)}, u32[]{:S(2)}, u32[]{:S(2)}) %collective-permute-start.37) | collective-permute-done | bytes 524320 | tf_op jit(solution)/shard_map/ppermute | solution.py:620
  239.3 1.5 collective-permute-start.26
  243.3 3.6 collective-permute-start.8
  251.3 18.3 %collective-permute-done.31 = bf16[128,1024]{1,0:T(8,128)(2,1)S(1)} collective-permute-done((bf16[128,1024]{1,0:T(8,128)(2,1)S(1)}, bf16[128,1024]{1,0:T(8,128)(2,1)S(1)}, u32[]{:S(2)}, u32[]{:S(2)}) %collective-permute-start.31) | collective-permute-done | bytes 262176 | tf_op jit(solution)/shard_map/ppermute | solution.py:620
  269.7 1.5 collective-permute-start.30
  272.0 30.7 %attn_bwd.1 = (f32[256,1024]{1,0:T(8,128)}, bf16[256,1024]{1,0:T(8,128)(2,1)}, bf16[256,1024]{1,0:T(8,128)(2,1)}, bf16[256,1024]{1,0:T(8,128)(2,1)}, bf16[4,128,...) custom-call(s32[4]{0:T(128)} %pad_add_fusion.sc, bf16[272,1024]{1,0:T(8,128)(2,1)} %copy-done.2, ...), custom_call_target="tpu_custom_call" | custom-call | tf_op jit(solution)/shard_map/attn_bwd/pallas_call | solution.py:589
  304.1 2.4 fusion.3
  307.7 4.5 collective-permute-start.33
  312.1 3.1 fusion.1
  320.2 3.5 collective-permute-done.20
  324.4 3.7 collective-permute-done.21
  328.2 32.4 %collective-permute-done.22 = f32[16,1024]{1,0:T(8,128)S(1)} collective-permute-done((f32[16,1024]{1,0:T(8,128)S(1)}, f32[16,1024]{1,0:T(8,128)S(1)}, u32[]{:S(2)}, u32[]{:S(2)}) %collective-permute-start.22) | collective-permute-done | bytes 65568 | tf_op jit(solution)/shard_map/ppermute | solution.py:669
  360.6 3.4 collective-permute-start.23
  364.1 2.0 collective-permute-start.10
  366.2 21.1 %collective-permute-done.23 = f32[16,1024]{1,0:T(8,128)S(1)} collective-permute-done((f32[16,1024]{1,0:T(8,128)S(1)}, f32[16,1024]{1,0:T(8,128)S(1)}, u32[]{:S(2)}, u32[]{:S(2)}) %collective-permute-start.23) | collective-permute-done | bytes 65568 | tf_op jit(solution)/shard_map/ppermute | solution.py:670
  389.0 1.8 add_convert_fusion.1
  396.4 2.1 collective-permute-done.10
  398.9 8.3 %collective-permute-done.9 = bf16[256,1024]{1,0:T(8,128)(2,1)S(1)} collective-permute-done((bf16[256,1024]{1,0:T(8,128)(2,1)}, bf16[256,1024]{1,0:T(8,128)(2,1)S(1)}, u32[]{:S(2)}, u32[]{:S(2)}) %collective-permute-start.9) | collective-permute-done | bytes 524320 | tf_op jit(solution)/shard_map/ppermute | solution.py:616
  409.8 4.3 collective-permute-done.13
  414.2 3.7 collective-permute-start.18
  422.4 52.4 %collective-permute-done.17 = bf16[128,768]{1,0:T(8,128)(2,1)S(1)} collective-permute-done((bf16[128,768]{1,0:T(8,128)(2,1)S(1)}, bf16[128,768]{1,0:T(8,128)(2,1)S(1)}, u32[]{:S(2)}, u32[]{:S(2)}) %collective-permute-start.17) | collective-permute-done | bytes 196640 | tf_op jit(solution)/shard_map/ppermute | solution.py:616
  475.7 1.7 gather_fusion
  480.4 2.7 select_convert_fusion.1
  483.1 16.4 %collective-permute-done.35 = bf16[640,1024]{1,0:T(8,128)(2,1)} collective-permute-done((bf16[640,1024]{1,0:T(8,128)(2,1)S(1)}, bf16[640,1024]{1,0:T(8,128)(2,1)}, u32[]{:S(2)}, u32[]{:S(2)}) %collective-permute-start.35) | collective-permute-done | bytes 1310752 | tf_op jit(solution)/shard_map/ppermute | solution.py:658
  499.4 1.5 select_convert_fusion
  501.9 1.5 pad_maximum_fusion
  (197 shorter events, 54.4 us)
Async XLA Ops:
  7.2 52.6 %all-gather.5.cloned.1.call-start = ((), (), s32[]{:S(2)}) async-start(), calls=%async_computation | async-start | bytes 1990656 | tf_op jit(solution)/shard_map/all_gather | solution.py:721
  14.7 130.0 %all-gather.7.cloned.1.call-start = ((), (), s32[]{:S(2)}) async-start(), calls=%async_computation.1 | async-start | bytes 21233664 | tf_op jit(solution)/shard_map/all_gather | solution.py:723
  18.0 41.8 %copy-start.2 = (bf16[272,1024]{1,0:T(8,128)(2,1)}, bf16[272,1024]{1,0:T(8,128)(2,1)S(1)}, u32[]{:S(2)}) copy-start(bf16[272,1024]{1,0:T(8,128)(2,1)S(1)} %fusion.9.x0) | copy-start | bytes 1671172
  18.0 18.7 %collective-permute-start = (bf16[272,1024]{1,0:T(8,128)(2,1)S(1)}, bf16[272,1024]{1,0:T(8,128)(2,1)S(1)}, u32[]{:S(2)}, u32[]{:S(2)}) collective-permute-start(bf16[272,1024]{1,0:T(8,128)(2,1)S(1)} %fusion.9.x0), channel_id=1, source_target_pairs={{0,8},{8,16},{16,24},{24,0},{1,9},{9,17},{17,25},{25,1},{2,10},{10... | collective-permute-start | bytes 1671176 | tf_op jit(solution)/shard_map/ppermute | solution.py:616
  21.1 38.7 %collective-permute-start.1 = (bf16[272,1024]{1,0:T(8,128)(2,1)S(1)}, bf16[272,1024]{1,0:T(8,128)(2,1)S(1)}, u32[]{:S(2)}, u32[]{:S(2)}) collective-permute-start(bf16[272,1024]{1,0:T(8,128)(2,1)S(1)} %fusion.9.x0), channel_id=1, source_target_pairs={{0,16},{8,24},{16,0},{24,8},{1,17},{9,25},{17,1},{25,9},{2,18},{10... | collective-permute-start | bytes 1671176 | tf_op jit(solution)/shard_map/ppermute | solution.py:616
  23.7 36.1 %collective-permute-start.2 = (bf16[272,1024]{1,0:T(8,128)(2,1)S(1)}, bf16[272,1024]{1,0:T(8,128)(2,1)S(1)}, u32[]{:S(2)}, u32[]{:S(2)}) collective-permute-start(bf16[272,1024]{1,0:T(8,128)(2,1)S(1)} %fusion.9.x0), channel_id=1, source_target_pairs={{0,24},{8,0},{16,8},{24,16},{1,25},{9,1},{17,9},{25,17},{2,26},{10... | collective-permute-start | bytes 1671176 | tf_op jit(solution)/shard_map/ppermute | solution.py:616
  81.6 18.7 %collective-permute-start.3 = (bf16[256,256]{1,0:T(8,128)(2,1)}, bf16[256,256]{1,0:T(8,128)(2,1)S(1)}, u32[]{:S(2)}, u32[]{:S(2)}) collective-permute-start(bf16[256,256]{1,0:T(8,128)(2,1)} %get-tuple-element.61), channel_id=1, source_target_pairs={{0,24},{8,0},{16,8},{24,16},{1,25},{9,1},{17,9},{25,17},{2,26},{10... | collective-permute-start | bytes 393224 | tf_op jit(solution)/shard_map/ppermute | solution.py:616
  96.1 12.4 %collective-permute-start.4 = (bf16[256,256]{1,0:T(8,128)(2,1)}, bf16[256,256]{1,0:T(8,128)(2,1)S(1)}, u32[]{:S(2)}, u32[]{:S(2)}) collective-permute-start(bf16[256,256]{1,0:T(8,128)(2,1)} %get-tuple-element.62), channel_id=1, source_target_pairs={{0,16},{8,24},{16,0},{24,8},{1,17},{9,25},{17,1},{25,9},{2,18},{10... | collective-permute-start | bytes 393224 | tf_op jit(solution)/shard_map/ppermute | solution.py:616
  96.4 12.1 %collective-permute-start.5 = (bf16[256,256]{1,0:T(8,128)(2,1)}, bf16[256,256]{1,0:T(8,128)(2,1)S(1)}, u32[]{:S(2)}, u32[]{:S(2)}) collective-permute-start(bf16[256,256]{1,0:T(8,128)(2,1)} %get-tuple-element.63), channel_id=1, source_target_pairs={{0,8},{8,16},{16,24},{24,0},{1,9},{9,17},{17,25},{25,1},{2,10},{10... | collective-permute-start | bytes 393224 | tf_op jit(solution)/shard_map/ppermute | solution.py:616
  100.3 44.4 %copy-start.25 = (bf16[256,256]{1,0:T(8,128)(2,1)}, bf16[256,256]{1,0:T(8,128)(2,1)S(1)}, u32[]{:S(2)}) copy-start(bf16[256,256]{1,0:T(8,128)(2,1)S(1)} %collective-permute-done.3.r1) | copy-start | bytes 393220
  193.4 7.4 %collective-permute-start.24 = (bf16[4,512,1024]{2,1,0:T(8,128)(2,1)}, bf16[4,512,1024]{2,1,0:T(8,128)(2,1)S(1)}, u32[]{:S(2)}, u32[]{:S(2)}) collective-permute-start(bf16[4,512,1024]{2,1,0:T(8,128)(2,1)} %get-tuple-element.95), channel_id=1, source_target_pairs={{0,1},{1,0},{2,3},{3,2},{4,5},{5,4},{6,7},{7,6},{8,9},{9,8},{10,11... | collective-permute-start | bytes 12582920 | tf_op jit(solution)/shard_map/ppermute | solution.py:620
  193.7 16.4 %collective-permute-start.36 = (bf16[4,512,1024]{2,1,0:T(8,128)(2,1)}, bf16[4,512,1024]{2,1,0:T(8,128)(2,1)S(1)}, u32[]{:S(2)}, u32[]{:S(2)}) collective-permute-start(bf16[4,512,1024]{2,1,0:T(8,128)(2,1)} %get-tuple-element.99), channel_id=1, source_target_pairs={{0,1},{1,0},{2,3},{3,2},{4,5},{5,4},{6,7},{7,6},{8,9},{9,8},{10,11... | collective-permute-start | bytes 12582920 | tf_op jit(solution)/shard_map/ppermute | solution.py:620
  194.0 14.4 %collective-permute-start.29 = (bf16[4,128,1024]{2,1,0:T(8,128)(2,1)}, bf16[4,128,1024]{2,1,0:T(8,128)(2,1)S(1)}, u32[]{:S(2)}, u32[]{:S(2)}) collective-permute-start(bf16[4,128,1024]{2,1,0:T(8,128)(2,1)} %get-tuple-element.97), channel_id=1, source_target_pairs={{0,1},{1,0},{2,3},{3,2},{4,5},{5,4},{6,7},{7,6},{8,9},{9,8},{10,11... | collective-permute-start | bytes 3145736 | tf_op jit(solution)/shard_map/ppermute | solution.py:620
  194.2 47.2 %collective-permute-start.6 = (bf16[256,256]{1,0:T(8,128)(2,1)}, bf16[256,256]{1,0:T(8,128)(2,1)S(1)}, u32[]{:S(2)}, u32[]{:S(2)}) collective-permute-start(bf16[256,256]{1,0:T(8,128)(2,1)} %get-tuple-element.79), channel_id=1, source_target_pairs={{0,8},{8,16},{16,24},{24,0},{1,9},{9,17},{17,25},{25,1},{2,10},{10... | collective-permute-start | bytes 393224 | tf_op jit(solution)/shard_map/ppermute | solution.py:616
  195.7 47.6 %collective-permute-start.7 = (bf16[256,256]{1,0:T(8,128)(2,1)}, bf16[256,256]{1,0:T(8,128)(2,1)S(1)}, u32[]{:S(2)}, u32[]{:S(2)}) collective-permute-start(bf16[256,256]{1,0:T(8,128)(2,1)} %get-tuple-element.80), channel_id=1, source_target_pairs={{0,16},{8,24},{16,0},{24,8},{1,17},{9,25},{17,1},{25,9},{2,18},{10... | collective-permute-start | bytes 393224 | tf_op jit(solution)/shard_map/ppermute | solution.py:616
  204.9 14.2 %collective-permute-start.25 = (bf16[256,1024]{1,0:T(8,128)(2,1)S(1)}, bf16[256,1024]{1,0:T(8,128)(2,1)S(1)}, u32[]{:S(2)}, u32[]{:S(2)}) collective-permute-start(bf16[256,1024]{1,0:T(8,128)(2,1)S(1)} %get-tuple-element.109), channel_id=1, source_target_pairs={{0,4},{1,5},{2,6},{3,7},{4,0},{5,1},{6,2},{7,3},{8,12},{9,13},{10,... | collective-permute-start | bytes 1572872 | tf_op jit(solution)/shard_map/ppermute | solution.py:620
  208.3 14.8 %collective-permute-start.27 = (bf16[256,1024]{1,0:T(8,128)(2,1)S(1)}, bf16[256,1024]{1,0:T(8,128)(2,1)S(1)}, u32[]{:S(2)}, u32[]{:S(2)}) collective-permute-start(bf16[256,1024]{1,0:T(8,128)(2,1)S(1)} %get-tuple-element.108), channel_id=1, source_target_pairs={{0,2},{1,3},{2,0},{3,1},{4,6},{5,7},{6,4},{7,5},{8,10},{9,11},{10,... | collective-permute-start | bytes 1572872 | tf_op jit(solution)/shard_map/ppermute | solution.py:620
  210.1 40.7 %collective-permute-start.32 = (bf16[128,1024]{1,0:T(8,128)(2,1)S(1)}, bf16[128,1024]{1,0:T(8,128)(2,1)S(1)}, u32[]{:S(2)}, u32[]{:S(2)}) collective-permute-start(bf16[128,1024]{1,0:T(8,128)(2,1)S(1)} %get-tuple-element.118), channel_id=1, source_target_pairs={{0,6},{1,7},{2,4},{3,5},{4,2},{5,3},{6,0},{7,1},{8,14},{9,15},{10,... | collective-permute-start | bytes 786440 | tf_op jit(solution)/shard_map/ppermute | solution.py:620
  219.1 18.9 %collective-permute-start.37 = (bf16[256,1024]{1,0:T(8,128)(2,1)S(1)}, bf16[256,1024]{1,0:T(8,128)(2,1)S(1)}, u32[]{:S(2)}, u32[]{:S(2)}) collective-permute-start(bf16[256,1024]{1,0:T(8,128)(2,1)S(1)} %get-tuple-element.103), channel_id=1, source_target_pairs={{0,4},{1,5},{2,6},{3,7},{4,0},{5,1},{6,2},{7,3},{8,12},{9,13},{10,... | collective-permute-start | bytes 1572872 | tf_op jit(solution)/shard_map/ppermute | solution.py:620
  223.1 16.2 %collective-permute-start.39 = (bf16[256,1024]{1,0:T(8,128)(2,1)S(1)}, bf16[256,1024]{1,0:T(8,128)(2,1)S(1)}, u32[]{:S(2)}, u32[]{:S(2)}) collective-permute-start(bf16[256,1024]{1,0:T(8,128)(2,1)S(1)} %get-tuple-element.102), channel_id=1, source_target_pairs={{0,2},{1,3},{2,0},{3,1},{4,6},{5,7},{6,4},{7,5},{8,10},{9,11},{10,... | collective-permute-start | bytes 1572872 | tf_op jit(solution)/shard_map/ppermute | solution.py:620
  237.9 66.1 %collective-permute-start.28 = (bf16[512,1024]{1,0:T(8,128)(2,1)S(1)}, bf16[512,1024]{1,0:T(8,128)(2,1)S(1)}, u32[]{:S(2)}, u32[]{:S(2)}) collective-permute-start(bf16[512,1024]{1,0:T(8,128)(2,1)S(1)} %pad_maximum_fusion.3), channel_id=1, source_target_pairs={{0,4},{1,5},{2,6},{3,7},{4,0},{5,1},{6,2},{7,3},{8,12},{9,13},{10,... | collective-permute-start | bytes 3145736 | tf_op jit(solution)/shard_map/ppermute | solution.py:620
  239.3 64.7 %collective-permute-start.26 = (bf16[512,1024]{1,0:T(8,128)(2,1)}, bf16[512,1024]{1,0:T(8,128)(2,1)S(1)}, u32[]{:S(2)}, u32[]{:S(2)}) collective-permute-start(bf16[512,1024]{1,0:T(8,128)(2,1)} %pad_maximum_fusion.2), channel_id=1, source_target_pairs={{0,2},{1,3},{2,0},{3,1},{4,6},{5,7},{6,4},{7,5},{8,10},{9,11},{10,... | collective-permute-start | bytes 3145736 | tf_op jit(solution)/shard_map/ppermute | solution.py:620
  241.5 28.2 %collective-permute-start.31 = (bf16[128,1024]{1,0:T(8,128)(2,1)S(1)}, bf16[128,1024]{1,0:T(8,128)(2,1)S(1)}, u32[]{:S(2)}, u32[]{:S(2)}) collective-permute-start(bf16[128,1024]{1,0:T(8,128)(2,1)S(1)} %get-tuple-element.119), channel_id=1, source_target_pairs={{0,4},{1,5},{2,6},{3,7},{4,0},{5,1},{6,2},{7,3},{8,12},{9,13},{10,... | collective-permute-start | bytes 786440 | tf_op jit(solution)/shard_map/ppermute | solution.py:620
  243.3 6.1 %collective-permute-start.8 = (bf16[256,256]{1,0:T(8,128)(2,1)S(1)}, bf16[256,256]{1,0:T(8,128)(2,1)S(1)}, u32[]{:S(2)}, u32[]{:S(2)}) collective-permute-start(bf16[256,256]{1,0:T(8,128)(2,1)S(1)} %copy-done.32), channel_id=1, source_target_pairs={{0,24},{8,0},{16,8},{24,16},{1,25},{9,1},{17,9},{25,17},{2,26},{10... | collective-permute-start | bytes 393224 | tf_op jit(solution)/shard_map/ppermute | solution.py:616
  249.4 62.7 %collective-permute-start.40 = (bf16[512,1024]{1,0:T(8,128)(2,1)}, bf16[512,1024]{1,0:T(8,128)(2,1)}, u32[]{:S(2)}, u32[]{:S(2)}) collective-permute-start(bf16[512,1024]{1,0:T(8,128)(2,1)} %pad_maximum_fusion.5), channel_id=1, source_target_pairs={{0,4},{1,5},{2,6},{3,7},{4,0},{5,1},{6,2},{7,3},{8,12},{9,13},{10,... | collective-permute-start | bytes 3145736 | tf_op jit(solution)/shard_map/ppermute | solution.py:620
  250.8 61.4 %collective-permute-start.38 = (bf16[512,1024]{1,0:T(8,128)(2,1)}, bf16[512,1024]{1,0:T(8,128)(2,1)}, u32[]{:S(2)}, u32[]{:S(2)}) collective-permute-start(bf16[512,1024]{1,0:T(8,128)(2,1)} %pad_maximum_fusion.4), channel_id=1, source_target_pairs={{0,2},{1,3},{2,0},{3,1},{4,6},{5,7},{6,4},{7,5},{8,10},{9,11},{10,... | collective-permute-start | bytes 3145736 | tf_op jit(solution)/shard_map/ppermute | solution.py:620
  269.7 33.0 %collective-permute-start.30 = (bf16[128,1024]{1,0:T(8,128)(2,1)S(1)}, bf16[128,1024]{1,0:T(8,128)(2,1)}, u32[]{:S(2)}, u32[]{:S(2)}) collective-permute-start(bf16[128,1024]{1,0:T(8,128)(2,1)S(1)} %get-tuple-element.117), channel_id=1, source_target_pairs={{0,2},{1,3},{2,0},{3,1},{4,6},{5,7},{6,4},{7,5},{8,10},{9,11},{10,... | collective-permute-start | bytes 786440 | tf_op jit(solution)/shard_map/ppermute | solution.py:620
  307.7 80.2 %collective-permute-start.33 = (bf16[640,1024]{1,0:T(8,128)(2,1)}, bf16[640,1024]{1,0:T(8,128)(2,1)}, u32[]{:S(2)}, u32[]{:S(2)}) collective-permute-start(bf16[640,1024]{1,0:T(8,128)(2,1)} %pad_maximum_fusion.1), channel_id=1, source_target_pairs={{0,8},{24,16},{1,9},{25,17},{2,10},{26,18},{3,11},{27,19},{4,12},{... | collective-permute-start | bytes 3932168 | tf_op jit(solution)/shard_map/ppermute | solution.py:656
  315.2 72.1 %collective-permute-start.41 = (bf16[512,1024]{1,0:T(8,128)(2,1)S(1)}, bf16[512,1024]{1,0:T(8,128)(2,1)S(1)}, u32[]{:S(2)}, u32[]{:S(2)}) collective-permute-start(bf16[512,1024]{1,0:T(8,128)(2,1)S(1)} %fusion.1), channel_id=1, source_target_pairs={{0,8},{24,16},{1,9},{25,17},{2,10},{26,18},{3,11},{27,19},{4,12},{... | collective-permute-start | bytes 3145736 | tf_op jit(solution)/shard_map/ppermute | solution.py:656
  318.1 1.3 collective-permute-start.19
  319.4 4.3 collective-permute-start.20
  323.7 4.3 collective-permute-start.21
  328.1 32.5 %collective-permute-start.22 = (f32[16,1024]{1,0:T(8,128)S(1)}, f32[16,1024]{1,0:T(8,128)S(1)}, u32[]{:S(2)}, u32[]{:S(2)}) collective-permute-start(f32[16,1024]{1,0:T(8,128)S(1)} %add.280), channel_id=1, source_target_pairs={{0,8},{8,0},{16,24},{24,16},{1,9},{9,1},{17,25},{25,17},{2,10},{10... | collective-permute-start | bytes 196616 | tf_op jit(solution)/shard_map/ppermute | solution.py:669
  360.6 26.7 %collective-permute-start.23 = (f32[16,1024]{1,0:T(8,128)S(1)}, f32[16,1024]{1,0:T(8,128)S(1)}, u32[]{:S(2)}, u32[]{:S(2)}) collective-permute-start(f32[16,1024]{1,0:T(8,128)S(1)} %add.281), channel_id=1, source_target_pairs={{0,16},{16,0},{8,24},{24,8},{1,17},{17,1},{9,25},{25,9},{2,18},{18... | collective-permute-start | bytes 196616 | tf_op jit(solution)/shard_map/ppermute | solution.py:670
  364.1 32.3 %collective-permute-start.11 = (bf16[256,1024]{1,0:T(8,128)(2,1)}, bf16[256,1024]{1,0:T(8,128)(2,1)S(1)}, u32[]{:S(2)}, u32[]{:S(2)}) collective-permute-start(bf16[256,1024]{1,0:T(8,128)(2,1)} %get-tuple-element.85), channel_id=1, source_target_pairs={{0,8},{8,16},{16,24},{24,0},{1,9},{9,17},{17,25},{25,1},{2,10},{10... | collective-permute-start | bytes 1572872 | tf_op jit(solution)/shard_map/ppermute | solution.py:616
  364.1 34.5 %collective-permute-start.10 = (bf16[256,1024]{1,0:T(8,128)(2,1)}, bf16[256,1024]{1,0:T(8,128)(2,1)S(1)}, u32[]{:S(2)}, u32[]{:S(2)}) collective-permute-start(bf16[256,1024]{1,0:T(8,128)(2,1)} %get-tuple-element.84), channel_id=1, source_target_pairs={{0,16},{8,24},{16,0},{24,8},{1,17},{9,25},{17,1},{25,9},{2,18},{10... | collective-permute-start | bytes 1572872 | tf_op jit(solution)/shard_map/ppermute | solution.py:616
  387.3 3.5 collective-permute-start.12
  387.3 19.9 %collective-permute-start.9 = (bf16[256,1024]{1,0:T(8,128)(2,1)}, bf16[256,1024]{1,0:T(8,128)(2,1)S(1)}, u32[]{:S(2)}, u32[]{:S(2)}) collective-permute-start(bf16[256,1024]{1,0:T(8,128)(2,1)} %get-tuple-element.83), channel_id=1, source_target_pairs={{0,24},{8,0},{16,8},{24,16},{1,25},{9,1},{17,9},{25,17},{2,26},{10... | collective-permute-start | bytes 1572872 | tf_op jit(solution)/shard_map/ppermute | solution.py:616
  387.9 30.7 %collective-permute-start.42 = (bf16[512,1024]{1,0:T(8,128)(2,1)S(1)}, bf16[512,1024]{1,0:T(8,128)(2,1)S(1)}, u32[]{:S(2)}, u32[]{:S(2)}) collective-permute-start(bf16[512,1024]{1,0:T(8,128)(2,1)S(1)} %add_convert_fusion.3), channel_id=1, source_target_pairs={{8,16},{16,8},{9,17},{17,9},{10,18},{18,10},{11,19},{19,11},{12,20... | collective-permute-start | bytes 3145736 | tf_op jit(solution)/shard_map/ppermute | solution.py:657
  390.8 29.4 %collective-permute-start.34 = (bf16[640,1024]{1,0:T(8,128)(2,1)S(1)}, bf16[640,1024]{1,0:T(8,128)(2,1)S(1)}, u32[]{:S(2)}, u32[]{:S(2)}) collective-permute-start(bf16[640,1024]{1,0:T(8,128)(2,1)S(1)} %add_convert_fusion.1), channel_id=1, source_target_pairs={{8,16},{16,8},{9,17},{17,9},{10,18},{18,10},{11,19},{19,11},{12,20... | collective-permute-start | bytes 3932168 | tf_op jit(solution)/shard_map/ppermute | solution.py:657
  396.4 13.4 %collective-permute-start.15 = (bf16[128,768]{1,0:T(8,128)(2,1)S(1)}, bf16[128,768]{1,0:T(8,128)(2,1)S(1)}, u32[]{:S(2)}, u32[]{:S(2)}) collective-permute-start(bf16[128,768]{1,0:T(8,128)(2,1)S(1)} %get-tuple-element.133), channel_id=1, source_target_pairs={{0,6},{1,7},{2,4},{3,5},{4,2},{5,3},{6,0},{7,1},{8,14},{9,15},{10,... | collective-permute-start | bytes 589832 | tf_op jit(solution)/shard_map/ppermute | solution.py:620
  398.6 11.2 %collective-permute-start.14 = (bf16[128,768]{1,0:T(8,128)(2,1)S(1)}, bf16[128,768]{1,0:T(8,128)(2,1)S(1)}, u32[]{:S(2)}, u32[]{:S(2)}) collective-permute-start(bf16[128,768]{1,0:T(8,128)(2,1)S(1)} %get-tuple-element.134), channel_id=1, source_target_pairs={{0,4},{1,5},{2,6},{3,7},{4,0},{5,1},{6,2},{7,3},{8,12},{9,13},{10,... | collective-permute-start | bytes 589832 | tf_op jit(solution)/shard_map/ppermute | solution.py:620
  407.2 6.9 %collective-permute-start.13 = (bf16[128,768]{1,0:T(8,128)(2,1)S(1)}, bf16[128,768]{1,0:T(8,128)(2,1)S(1)}, u32[]{:S(2)}, u32[]{:S(2)}) collective-permute-start(bf16[128,768]{1,0:T(8,128)(2,1)S(1)} %get-tuple-element.132), channel_id=1, source_target_pairs={{0,2},{1,3},{2,0},{3,1},{4,6},{5,7},{6,4},{7,5},{8,10},{9,11},{10,... | collective-permute-start | bytes 589832 | tf_op jit(solution)/shard_map/ppermute | solution.py:620
  414.2 8.2 %collective-permute-start.18 = (bf16[128,768]{1,0:T(8,128)(2,1)S(1)}, bf16[128,768]{1,0:T(8,128)(2,1)S(1)}, u32[]{:S(2)}, u32[]{:S(2)}) collective-permute-start(bf16[128,768]{1,0:T(8,128)(2,1)S(1)} %fusion.23), channel_id=1, source_target_pairs={{0,24},{8,0},{16,8},{24,16},{1,25},{9,1},{17,9},{25,17},{2,26},{10... | collective-permute-start | bytes 589832 | tf_op jit(solution)/shard_map/ppermute | solution.py:616
  417.9 56.8 %collective-permute-start.17 = (bf16[128,768]{1,0:T(8,128)(2,1)S(1)}, bf16[128,768]{1,0:T(8,128)(2,1)S(1)}, u32[]{:S(2)}, u32[]{:S(2)}) collective-permute-start(bf16[128,768]{1,0:T(8,128)(2,1)S(1)} %fusion.23), channel_id=1, source_target_pairs={{0,16},{8,24},{16,0},{24,8},{1,17},{9,25},{17,1},{25,9},{2,18},{10... | collective-permute-start | bytes 589832 | tf_op jit(solution)/shard_map/ppermute | solution.py:616
  417.9 56.8 %collective-permute-start.16 = (bf16[128,768]{1,0:T(8,128)(2,1)S(1)}, bf16[128,768]{1,0:T(8,128)(2,1)S(1)}, u32[]{:S(2)}, u32[]{:S(2)}) collective-permute-start(bf16[128,768]{1,0:T(8,128)(2,1)S(1)} %fusion.23), channel_id=1, source_target_pairs={{0,8},{8,16},{16,24},{24,0},{1,9},{9,17},{17,25},{25,1},{2,10},{10... | collective-permute-start | bytes 589832 | tf_op jit(solution)/shard_map/ppermute | solution.py:616
  419.0 61.4 %collective-permute-start.43 = (bf16[512,1024]{1,0:T(8,128)(2,1)S(1)}, bf16[512,1024]{1,0:T(8,128)(2,1)}, u32[]{:S(2)}, u32[]{:S(2)}) collective-permute-start(bf16[512,1024]{1,0:T(8,128)(2,1)S(1)} %add_convert_fusion.2), channel_id=1, source_target_pairs={{8,0},{16,24},{9,1},{17,25},{10,2},{18,26},{11,3},{19,27},{12,4},{... | collective-permute-start | bytes 3145736 | tf_op jit(solution)/shard_map/ppermute | solution.py:658
  420.9 78.6 %collective-permute-start.35 = (bf16[640,1024]{1,0:T(8,128)(2,1)S(1)}, bf16[640,1024]{1,0:T(8,128)(2,1)}, u32[]{:S(2)}, u32[]{:S(2)}) collective-permute-start(bf16[640,1024]{1,0:T(8,128)(2,1)S(1)} %add_convert_fusion), channel_id=1, source_target_pairs={{8,0},{16,24},{9,1},{17,25},{10,2},{18,26},{11,3},{19,27},{12,4},{... | collective-permute-start | bytes 3932168 | tf_op jit(solution)/shard_map/ppermute | solution.py:658
  (31 other events, 467.2 us)
Sparse Core Ops, SparseCore 0:
  14.8 29.2 all-gather.4
  45.9 98.7 all-gather.6

commit v2 on v1

v2 whole, which is shorter than its diff:
```python
from functools import partial

import jax
import jax.numpy as jnp
from jax import lax
from jax.experimental import pallas as pl
from jax.experimental.pallas import tpu as pltpu
from jax.sharding import PartitionSpec as P

HEADS = 16
HEAD_DIM = 64
SEGS = 8
EPSILON = 1e-05
MASKED = -1000000000.0
SCALE = HEAD_DIM ** (-0.5)
BF = jnp.bfloat16
F32 = jnp.float32

CHUNK = 256
HERE = 4
WIDE = HERE * HEAD_DIM
SHARDS = 8
ROWS = 128
PACK = 2 * ROWS + 16
PARAMS = pltpu.CompilerParams(vmem_limit_bytes=60 * 1024 * 1024)


SMEM_SPEC = pl.BlockSpec(memory_space=pltpu.SMEM)
VMEM_SPEC = pl.BlockSpec(memory_space=pltpu.VMEM)


def dot(a, b, dims=((1,), (0,))):
    return lax.dot_general(a, b, (dims, ((), ())), preferred_element_type=F32)


def vec(small_ref, row, start, size):
    return jnp.concatenate(
        [small_ref[f, row : row + 1, start : start + size].astype(F32) for f in range(SHARDS)],
        axis=1,
    )


def any_spec(shape):
    return pl.BlockSpec(shape, lambda *a: (0,) * len(shape))


def pack_kernel(sc, tok, seg, wq, wk, wv, wout, qb, vb, ob, ag, sh, db, mg, ms, ub, xp, pk):
    z = sc[0]
    cols = pl.ds(pl.multiple_of(z * WIDE, WIDE), WIDE)
    xp[0:CHUNK] = tok[...]
    xp[CHUNK:] = jnp.zeros((16, 1024), BF)
    xp[CHUNK : CHUNK + 1, 0:CHUNK] = seg[...].astype(F32).astype(BF)
    pk[0:ROWS] = wout[...]
    for n, w in enumerate((wq, wk, wv)):
        pk[ROWS : 2 * ROWS, WIDE * n : WIDE * n + WIDE] = w[:, cols]
    pk[ROWS : 2 * ROWS, 3 * WIDE :] = jnp.zeros((ROWS, 1024 - 3 * WIDE), BF)
    pk[2 * ROWS :] = jnp.zeros((16, 1024), BF)
    at = slice(2 * ROWS, 2 * ROWS + 1)
    for n, vector in enumerate((qb, vb, ob, ag, sh, db)):
        pk[at, 128 * n : 128 * n + 128] = vector[...]
    at = slice(2 * ROWS + 1, 2 * ROWS + 2)
    for n, vector in enumerate((mg, ms)):
        pk[at, 128 * n : 128 * n + 128] = vector[...]
    pk[at, 256:768] = ub[...]


def pack_inputs(scalars, tok, seg, weights, vectors):
    shape = jax.ShapeDtypeStruct
    return pl.pallas_call(
        pack_kernel,
        name="pack_inputs",
        in_specs=[SMEM_SPEC] + [VMEM_SPEC] * 15,
        out_specs=(VMEM_SPEC,) * 2,
        out_shape=(shape((CHUNK + 16, 1024), BF), shape((PACK, 1024), BF)),
        compiler_params=PARAMS,
    )(scalars, tok, seg, *weights, *[v[None] for v in vectors])


def segment_setup(rows, segc, ends):
    for a in range(4):
        row = rows[a][0:1, :]
        segc[a] = jnp.transpose(jnp.broadcast_to(row, (128, CHUNK)))
        ends[0, a] = jnp.min(row).astype(jnp.int32)
        ends[1, a] = jnp.max(row).astype(jnp.int32)


def key_range(ends, i):
    low = jnp.int32(0)
    high = jnp.int32(4)
    for j in range(4):
        low = low + (ends[1, j] < ends[0, i]).astype(jnp.int32)
        high = high - (ends[0, j] > ends[1, i]).astype(jnp.int32)
    return low, high


def attn_fwd_kernel(
    sc,
    x0,
    right,
    left,
    x2,
    far,
    w,
    small,
    m0,
    m1,
    m2,
    m3,
    mixf,
    lse,
    qkv,
    xall,
    segr,
    segc,
    ends,
):
    z = sc[0]

    def place(k, src):
        a = lax.rem(z - k + 4, 4)
        xall[a] = src[0:CHUNK, :]
        segr[a] = jnp.broadcast_to(
            src[CHUNK : CHUNK + 16, 0:CHUNK].astype(F32)[0:1, :], (8, CHUNK)
        )

    place(0, x0)
    place(2, x2)
    for k, usual, end in ((1, right, 0), (3, left, 3)):
        pl.when(z == end)(partial(place, k, far))
        pl.when(z != end)(partial(place, k, usual))
    segment_setup(segr, segc, ends)
    weight = w[...].reshape(SHARDS * ROWS, 3 * WIDE)
    first = small[2 * z].astype(F32)
    second = small[2 * z + 1].astype(F32)
    qb = jnp.concatenate([first[0:1, 0:128], second[0:1, 0:128]], axis=1)
    vb = jnp.concatenate([first[0:1, 128:256], second[0:1, 128:256]], axis=1)
    for n in range(4):
        a = n * CHUNK
        prod = dot(xall[n], weight)
        q = ((prod[:, 0:WIDE] + qb).astype(BF).astype(F32) * SCALE).astype(BF)
        kk = prod[:, WIDE : 2 * WIDE].astype(BF)
        v = (prod[:, 2 * WIDE :] + vb).astype(BF)
        for at, part in enumerate((q, kk, v)):
            for h in range(HERE):
                qkv[at * HERE + h, a : a + CHUNK, :] = part[:, h * HEAD_DIM : (h + 1) * HEAD_DIM]

    def q_chunk(i, carry):
        rows = pl.ds(pl.multiple_of(i * CHUNK, CHUNK), CHUNK)
        low, high = key_range(ends, i)
        col = segc[i]
        col2 = jnp.concatenate([col, col], axis=1)
        qs = [qkv[h, rows, :] for h in range(HERE)]

        def key_chunk(j, state):
            keys = pl.ds(pl.multiple_of(j * CHUNK, CHUNK), CHUNK)
            mask = col2 == segr[j][0:1, :]
            new = []
            for h in range(HERE):
                m, l, acc = state[h]
                s = dot(qs[h], qkv[HERE + h, keys, :], ((1,), (1,)))
                s = jnp.where(mask, s, MASKED)
                m_new = jnp.maximum(m, jnp.max(s, axis=1, keepdims=True))
                p = jnp.exp(s - m_new)
                fix = jnp.exp(m - m_new)
                l = l * fix + jnp.sum(p, axis=1, keepdims=True)
                acc = acc * fix + dot(p.astype(BF), qkv[2 * HERE + h, keys, :])
                new.append((m_new, l, acc))
            return tuple(new)

        init = tuple(
            (
                jnp.full((CHUNK, 1), MASKED, F32),
                jnp.zeros((CHUNK, 1), F32),
                jnp.zeros((CHUNK, HEAD_DIM), F32),
            )
            for _ in range(HERE)
        )
        state = lax.fori_loop(low, high, key_chunk, init)
        lane = lax.broadcasted_iota(jnp.int32, (CHUNK, 128), 1)
        logs = jnp.zeros((CHUNK, 128), F32)
        for h in range(HERE):
            m, l, acc = state[h]
            mixf[rows, h * HEAD_DIM : (h + 1) * HEAD_DIM] = acc / l
            logs = jnp.where(lane == h, m + jnp.log(l), logs)
        lse[rows, :] = logs
        return carry

    lax.fori_loop(0, 4, q_chunk, 0)
    for k, out in enumerate((m0, m1, m2, m3)):
        a = pl.multiple_of(lax.rem(z - k + 4, 4) * CHUNK, CHUNK)
        out[...] = mixf[pl.ds(a, CHUNK), :].astype(BF)


OUT_SPEC = pl.BlockSpec((SHARDS, ROWS, 1024), lambda *a: (0, 0, 0))
QKV_SPEC = pl.BlockSpec((SHARDS, ROWS, 3 * WIDE), lambda *a: (0, 1, 0))
SMALL_SPEC = pl.BlockSpec((SHARDS, 16, 3 * WIDE), lambda *a: (0, 2 * ROWS // 16, 0))


def attn_fwd(scalars, xs, pack):
    shape = jax.ShapeDtypeStruct
    return pl.pallas_call(
        attn_fwd_kernel,
        name="attn_fwd",
        out_shape=(shape((CHUNK, WIDE), BF),) * 4
        + (
            shape((4 * CHUNK, WIDE), F32),
            shape((4 * CHUNK, 128), F32),
            shape((3 * HERE, 4 * CHUNK, HEAD_DIM), BF),
            shape((4, CHUNK, 1024), BF),
            shape((4, 8, CHUNK), F32),
        ),
        grid=(1,),
        in_specs=[SMEM_SPEC] + [any_spec((CHUNK + 16, 1024))] * 5 + [QKV_SPEC, SMALL_SPEC],
        out_specs=(any_spec((CHUNK, WIDE)),) * 4
        + (
            any_spec((4 * CHUNK, WIDE)),
            any_spec((4 * CHUNK, 128)),
            any_spec((3 * HERE, 4 * CHUNK, HEAD_DIM)),
            any_spec((4, CHUNK, 1024)),
            any_spec((4, 8, CHUNK)),
        ),
        scratch_shapes=[
            pltpu.VMEM((4, CHUNK, 128), F32),
            pltpu.SMEM((2, 4), jnp.int32),
        ],
        compiler_params=PARAMS,
    )(scalars, *xs, pack, pack)


def normalise(h):
    centre = h - jnp.mean(h, axis=-1, keepdims=True)
    inverse = lax.rsqrt(jnp.mean(centre * centre, axis=-1, keepdims=True) + EPSILON)
    return centre * inverse, inverse


def norm_pullback(upstream, scaled, inverse, gain):
    e = upstream * gain
    return inverse * (
        e
        - jnp.mean(e, axis=-1, keepdims=True)
        - scaled * jnp.mean(e * scaled, axis=-1, keepdims=True)
    )


def relative(f, sc):
    return 2 * jnp.bitwise_xor(sc[1], f // 2) + jnp.bitwise_xor(sc[2], f % 2)


def out_kernel(sc, tok, r0, r1, r2, r3, w, small, valid, normed, low, low_rel, scaled, inv, mixed, stats):
    z = sc[0]
    acc = jnp.zeros((CHUNK, 1024), F32)
    for k, r in enumerate((r0, r1, r2, r3)):
        a = lax.rem(z + k, 4)
        rows = w[pl.ds(2 * a, 2)].reshape(WIDE, 1024)
        acc = acc + dot(r[...], rows)
        mixed[:, pl.ds(pl.multiple_of(a * WIDE, WIDE), WIDE)] = r[...]
    branch = acc + vec(small, 0, 256, 128)
    x = tok[...].astype(F32)
    n, inverse = normalise(x + branch)
    y = n * vec(small, 0, 384, 128) + vec(small, 0, 512, 128)
    normed[...] = y
    y_low = y.astype(BF)
    low[...] = y_low
    for f in range(SHARDS):
        at = relative(f, sc)
        low_rel[:, pl.ds(pl.multiple_of(at * ROWS, ROWS), ROWS)] = y_low[:, ROWS * f : ROWS * f + ROWS]
    scaled[...] = n
    inv[...] = jnp.broadcast_to(inverse, (CHUNK, 128))
    ok = valid[...]
    lane = lax.broadcasted_iota(jnp.int32, (8, 128), 1)
    stats[...] = jnp.where(
        lane == 0,
        jnp.sum(ok * x * x),
        jnp.where(lane == 1, jnp.sum(ok * branch * branch), jnp.where(lane == 3, jnp.sum(ok), 0.0)),
    )


def out_project(scalars, tok, parts, pack, valid):
    shape = jax.ShapeDtypeStruct
    full = lambda *s: any_spec(s)
    return pl.pallas_call(
        out_kernel,
        name="out_project",
        grid=(1,),
        out_shape=(
            shape((CHUNK, 1024), F32),
            shape((CHUNK, 1024), BF),
            shape((CHUNK, 1024), BF),
            shape((CHUNK, 1024), F32),
            shape((CHUNK, 128), F32),
            shape((CHUNK, 1024), BF),
            shape((8, 128), F32),
        ),
        in_specs=[SMEM_SPEC, full(CHUNK, 1024)]
        + [full(CHUNK, WIDE)] * 4
        + [OUT_SPEC, SMALL_SPEC, full(CHUNK, 1)],
        out_specs=(
            full(CHUNK, 1024),
            full(CHUNK, 1024),
            full(CHUNK, 1024),
            full(CHUNK, 1024),
            full(CHUNK, 128),
            full(CHUNK, 1024),
            full(8, 128),
        ),
        compiler_params=PARAMS,
    )(scalars, tok, *parts, pack, pack, valid)


def mlp_fwd_kernel(normed, low, low_rel, mixed, *refs):
    ups = refs[0:SHARDS]
    down, small, cot, valid, acts, slope, out, gh2, sums, stats, acc = refs[SHARDS:]
    j = pl.program_id(0)
    gate = dot(low_rel[...], jnp.concatenate([u[...] for u in ups]))
    gate = gate + small[j, 1:2, 256:768].astype(F32)
    cdf = 0.5 * (1.0 + lax.erf(gate * (2.0 ** -0.5)))
    h = (gate * cdf).astype(BF)
    for b in range(4):
        for half in range(2):

            @pl.when(j == 2 * b + half)
            def _():
                acts[b, :, 512 * half : 512 * half + 512] = h

    slope[...] = cdf + gate * (jnp.exp(-0.5 * gate * gate) * 0.3989422804014327)
    part = dot(h, down[...].reshape(512, 1024))

    @pl.when(j == 0)
    def _():
        acc[...] = part

    @pl.when(j > 0)
    def _():
        acc[...] += part

    @pl.when(j == SHARDS - 1)
    def _():
        branch = acc[...] + vec(small, 0, 640, 128)
        n, inverse = normalise(normed[...] + branch)
        gain = vec(small, 1, 0, 128)
        out[...] = (n * gain + vec(small, 1, 128, 128)).astype(BF)
        ok = valid[...]
        u = cot[...].astype(F32) * ok
        g = norm_pullback(u, n, inverse, gain)
        gh2[...] = g
        g_low = g.astype(BF)
        acts[4] = low[...]
        acts[5] = mixed[...]
        acts[6] = g_low
        sums[0:1, :] = jnp.sum(u * n, axis=0, keepdims=True)
        sums[1:2, :] = jnp.sum(u, axis=0, keepdims=True)
        sums[2:3, :] = jnp.sum(g_low.astype(F32), axis=0, keepdims=True)
        sums[3:8, :] = jnp.zeros((5, 1024), F32)
        lane = lax.broadcasted_iota(jnp.int32, (8, 128), 1)
        stats[...] = jnp.where(lane == 2, jnp.sum(ok * branch * branch), 0.0)


UP_SPECS = [pl.BlockSpec((ROWS, 512), lambda j: (0, j))] * SHARDS


def mlp_fwd(normed, low, low_rel, mixed, ups, down, pack, cot, valid):
    shape = jax.ShapeDtypeStruct
    full = lambda *s: any_spec(s)
    return pl.pallas_call(
        mlp_fwd_kernel,
        name="mlp_fwd",
        grid=(SHARDS,),
        out_shape=(
            shape((7, CHUNK, 1024), BF),
            shape((CHUNK, 4096), F32),
            shape((CHUNK, 1024), BF),
            shape((CHUNK, 1024), F32),
            shape((8, 1024), F32),
            shape((8, 128), F32),
        ),
        in_specs=[
            full(CHUNK, 1024),
            full(CHUNK, 1024),
            full(CHUNK, 1024),
            full(CHUNK, 1024),
        ]
        + UP_SPECS
        + [
            pl.BlockSpec((1, 512, 1024), lambda j: (j, 0, 0)),
            SMALL_SPEC,
            full(CHUNK, 1024),
            full(CHUNK, 1),
        ],
        out_specs=(
            full(7, CHUNK, 1024),
            pl.BlockSpec((CHUNK, 512), lambda j: (0, j)),
            full(CHUNK, 1024),
            full(CHUNK, 1024),
            full(8, 1024),
            full(8, 128),
        ),
        scratch_shapes=[pltpu.VMEM((CHUNK, 1024), F32)],
        compiler_params=PARAMS,
    )(normed, low, low_rel, mixed, *ups, down, pack, cot, valid)


def mlp_bwd_kernel(sc, gm, slope, *refs):
    ups = refs[0:SHARDS]
    down, gh2, scaled, inv, small, wout = refs[SHARDS : SHARDS + 6]
    grads, gh1, g0, g1, g2, g3, sums, ub, acc, total = refs[SHARDS + 6 :]
    j = pl.program_id(0)
    z = sc[0]
    dh = dot(gm[0], down[...].reshape(512, 1024), ((1,), (1,)))
    gg = (dh * slope[...]).astype(BF)
    ub[pl.ds(j, 1)] = jnp.sum(gg.astype(F32), axis=0, keepdims=True).reshape(1, 1, 512)
    for b in range(4):
        for half in range(2):

            @pl.when(j == 2 * b + half)
            def _():
                grads[b, :, 512 * half : 512 * half + 512] = gg

    part = dot(gg, jnp.concatenate([u[...] for u in ups]), ((1,), (1,)))

    @pl.when(j == 0)
    def _():
        acc[...] = part

    @pl.when(j > 0)
    def _():
        acc[...] += part

    @pl.when(j == SHARDS - 1)
    def _():
        for f in range(SHARDS):
            at = pl.ds(pl.multiple_of(relative(f, sc) * ROWS, ROWS), ROWS)
            total[:, ROWS * f : ROWS * f + ROWS] = acc[:, at]
        u = gh2[...] + total[...]
        n = scaled[...]
        g = norm_pullback(u, n, inv[:, 0:1], vec(small, 0, 384, 128))
        gh1[...] = g
        g_low = g.astype(BF)
        grads[4] = g_low
        sums[0:1, :] = jnp.sum(u * n, axis=0, keepdims=True)
        sums[1:2, :] = jnp.sum(u, axis=0, keepdims=True)
        sums[2:3, :] = jnp.sum(g_low.astype(F32), axis=0, keepdims=True)
        sums[3:8, :] = jnp.zeros((5, 1024), F32)
        for k, out in enumerate((g0, g1, g2, g3)):
            a = lax.rem(z + k, 4)
            rows = wout[pl.ds(2 * a, 2)].reshape(WIDE, 1024)
            out[...] = dot(g_low, rows, ((1,), (1,))).astype(BF)


def mlp_bwd(scalars, acts, slope, ups, down, gh2, scaled, inv, pack):
    shape = jax.ShapeDtypeStruct
    full = lambda *s: any_spec(s)
    return pl.pallas_call(
        mlp_bwd_kernel,
        name="mlp_bwd",
        grid=(SHARDS,),
        in_specs=[
            SMEM_SPEC,
            pl.BlockSpec((1, CHUNK, 1024), lambda j: (6, 0, 0)),
            pl.BlockSpec((CHUNK, 512), lambda j: (0, j)),
        ]
        + UP_SPECS
        + [
            pl.BlockSpec((1, 512, 1024), lambda j: (j, 0, 0)),
            full(CHUNK, 1024),
            full(CHUNK, 1024),
            full(CHUNK, 128),
            SMALL_SPEC,
            OUT_SPEC,
        ],
        out_specs=(full(5, CHUNK, 1024), full(CHUNK, 1024))
        + (full(CHUNK, WIDE),) * 4
        + (full(8, 1024), full(SHARDS, 1, 512)),
        scratch_shapes=[pltpu.VMEM((CHUNK, 1024), F32)] * 2,
        out_shape=(shape((5, CHUNK, 1024), BF), shape((CHUNK, 1024), F32))
        + (shape((CHUNK, WIDE), BF),) * 4
        + (shape((8, 1024), F32), shape((SHARDS, 1, 512), F32)),
        compiler_params=PARAMS,
    )(scalars, acts, slope, *ups, down, gh2, scaled, inv, pack, pack)


REST = 640


def step_shard(j, sc):
    rel = jnp.where(j == 0, 3, jnp.where(j >= 3, 0, j))
    return 2 * jnp.bitwise_xor(sc[1], rel) + sc[2]


def down_kernel(sc, ho, hp, lo, lp, d3, d1, d2, d0, right):
    s = pl.program_id(0)

    @pl.when(s == 0)
    def _():
        right[0:CHUNK] = lo[0]
        right[CHUNK:] = lp[0]

    left = jnp.concatenate([ho[0], hp[0]])
    res = dot(left, right[...], ((0,), (0,))).astype(BF)
    for n, out in enumerate((d3, d1, d2, d0)):

        @pl.when(s == n)
        def _():
            out[...] = res


def down_grads(scalars, acts, acts_p):
    shape = jax.ShapeDtypeStruct
    full = lambda *s: pl.BlockSpec(s, lambda j, sc: (0,) * len(s))

    def hid(j, sc):
        f = step_shard(j, sc)
        return (f // 2, 0, f % 2)

    hidden = pl.BlockSpec((1, CHUNK, 512), hid)
    grad = pl.BlockSpec((1, CHUNK, 1024), lambda j, sc: (6, 0, 0))
    return pl.pallas_call(
        down_kernel,
        name="down_grads",
        grid_spec=pltpu.PrefetchScalarGridSpec(
            num_scalar_prefetch=1,
            grid=(4,),
            in_specs=[hidden, hidden, grad, grad],
            out_specs=(full(512, 1024),) * 4,
            scratch_shapes=[pltpu.VMEM((2 * CHUNK, 1024), BF)],
        ),
        out_shape=(shape((512, 1024), BF),) * 4,
        compiler_params=PARAMS,
    )(scalars, acts, acts_p, acts, acts_p)


def rest_kernel(sc, lo, lp, go, gp, r3, r1, r2, r0, low_sel, mix_sel):
    s = pl.program_id(0)
    chip, core = sc[1], sc[2]

    @pl.when(s == 0)
    def _():
        for r in range(4):
            at = pl.multiple_of((2 * jnp.bitwise_xor(chip, r) + core) * ROWS, ROWS)
            to = slice(ROWS * r, ROWS * r + ROWS)
            low_sel[0:CHUNK, to] = lo[0, :, pl.ds(at, ROWS)]
            low_sel[CHUNK:, to] = lp[0, :, pl.ds(at, ROWS)]
            mix_sel[0:CHUNK, to] = lo[1, :, pl.ds(at, ROWS)]
            mix_sel[CHUNK:, to] = lp[1, :, pl.ds(at, ROWS)]

    @pl.when(s == 4)
    def _():
        low_sel[...] = mix_sel[...]

    right = jnp.concatenate([go[0], gp[0]])
    res = dot(low_sel[...], right, ((0,), (0,))).astype(BF)
    for b in range(5):

        @pl.when(s == b)
        def _():
            for r, out in enumerate((r0, r1, r2, r3)):
                out[ROWS * b : ROWS * b + ROWS] = res[ROWS * r : ROWS * r + ROWS]


def rest_grads(scalars, acts, acts_p, grads, grads_p):
    shape = jax.ShapeDtypeStruct
    full = lambda *s: pl.BlockSpec(s, lambda j, sc: (0,) * len(s))
    flat = pl.BlockSpec((pl.Element(2), pl.Element(CHUNK), pl.Element(1024)), lambda j, sc: (4, 0, 0))
    grad = pl.BlockSpec((1, CHUNK, 1024), lambda j, sc: (j, 0, 0))
    return pl.pallas_call(
        rest_kernel,
        name="rest_grads",
        grid_spec=pltpu.PrefetchScalarGridSpec(
            num_scalar_prefetch=1,
            grid=(5,),
            in_specs=[flat, flat, grad, grad],
            out_specs=(full(REST, 1024),) * 4,
            scratch_shapes=[pltpu.VMEM((2 * CHUNK, 512), BF)] * 2,
        ),
        out_shape=(shape((REST, 1024), BF),) * 4,
        compiler_params=PARAMS,
    )(scalars, acts, acts_p, grads, grads_p)


def attn_bwd_kernel(
    sc,
    xall,
    segr,
    w,
    qkv,
    mixf,
    lse,
    g0,
    g1,
    g2,
    g3,
    sums_m,
    sums_a,
    ubt,
    stats_a,
    stats_m,
    ig,
    gw_out,
    small,
    segc,
    ends,
    gs,
    dq,
    dk,
    dv,
    delta,
    dall,
    gw,
):
    z = sc[0]
    segment_setup(segr, segc, ends)
    dk[...] = jnp.zeros_like(dk)
    dv[...] = jnp.zeros_like(dv)
    lane = lax.broadcasted_iota(jnp.int32, (CHUNK, 128), 1)
    for k, g in enumerate((g0, g1, g2, g3)):
        rows = pl.ds(pl.multiple_of(lax.rem(z - k + 4, 4) * CHUNK, CHUNK), CHUNK)
        prod = g[...].astype(F32) * mixf[rows, :]
        d = jnp.zeros((CHUNK, 128), F32)
        for h in range(HERE):
            at = slice(h * HEAD_DIM, (h + 1) * HEAD_DIM)
            gs[h, rows, :] = g[:, at]
            d = jnp.where(lane == h, jnp.sum(prod[:, at], axis=1, keepdims=True), d)
        delta[rows, :] = d

    def q_chunk(i, carry):
        rows = pl.ds(pl.multiple_of(i * CHUNK, CHUNK), CHUNK)
        low, high = key_range(ends, i)
        col = segc[i]
        col2 = jnp.concatenate([col, col], axis=1)
        logs = lse[rows, :]
        deltas = delta[rows, :]
        dq[...] = jnp.zeros_like(dq)

        def key_chunk(j, inner):
            keys = pl.ds(pl.multiple_of(j * CHUNK, CHUNK), CHUNK)
            mask = col2 == segr[j][0:1, :]
            for h in range(HERE):
                q = qkv[h, rows, :]
                kk = qkv[HERE + h, keys, :]
                v = qkv[2 * HERE + h, keys, :]
                g = gs[h, rows, :]
                s = dot(q, kk, ((1,), (1,)))
                p = jnp.where(mask, jnp.exp(s - logs[:, h : h + 1]), 0.0)
                dp = dot(g, v, ((1,), (1,)))
                ds = (p * (dp - deltas[:, h : h + 1])).astype(BF)
                dv[h, keys, :] += dot(p.astype(BF), g, ((0,), (0,)))
                dk[h, keys, :] += dot(ds, q, ((0,), (0,)))
                dq[h] += dot(ds, kk)
            return inner

        lax.fori_loop(low, high, key_chunk, 0)
        for h in range(HERE):
            dall[rows, h * HEAD_DIM : (h + 1) * HEAD_DIM] = (dq[h] * SCALE).astype(BF)
        return carry

    lax.fori_loop(0, 4, q_chunk, 0)
    for h in range(HERE):
        at = WIDE + h * HEAD_DIM
        dall[:, at : at + HEAD_DIM] = dk[h].astype(BF)
        at = 2 * WIDE + h * HEAD_DIM
        dall[:, at : at + HEAD_DIM] = dv[h].astype(BF)
    here = pl.ds(pl.multiple_of(z * WIDE, WIDE), WIDE)
    small[...] = jnp.zeros_like(small)
    small[0:3, :] = sums_m[0:3, :]
    small[3:6, :] = sums_a[0:3, :]
    small[6:7, here] = jnp.sum(dall[:, 0:WIDE].astype(F32), axis=0, keepdims=True)
    small[7:8, here] = jnp.sum(dall[:, 2 * WIDE :].astype(F32), axis=0, keepdims=True)
    small[8:12, :] = ubt[...]
    every = lambda value: jnp.broadcast_to(value, (1, 1024))
    small[12:13, :] = every(stats_a[0:1, 0:1])
    small[13:14, :] = every(stats_a[0:1, 1:2])
    small[14:15, :] = every(stats_m[0:1, 2:3])
    count = stats_a[0:1, 3:4]
    high = jnp.floor(count * 0.0625)
    small[15:16, :] = every(high)
    small[16:17, :] = every(count - 16.0 * high)
    gw_out[:, 3 * WIDE :] = jnp.transpose(small[...]).astype(BF)
    weight = w[...].reshape(SHARDS * ROWS, 3 * WIDE)
    for k in range(4):
        rows = slice(CHUNK * k, CHUNK * k + CHUNK)
        d = dall[rows, :]
        ig[rows, :] = dot(d, weight, ((1,), (1,))).astype(BF)
        part = dot(xall[k], d, ((0,), (0,)))
        if k == 0:
            gw[...] = part
        else:
            gw[...] += part
    gw_out[:, 0 : 3 * WIDE] = gw[...].astype(BF)


def attn_bwd(scalars, xall, segr, pack, qkv, mixf, lse, gs, smalls):
    shape = jax.ShapeDtypeStruct
    return pl.pallas_call(
        attn_bwd_kernel,
        name="attn_bwd",
        out_shape=(shape((1024, 1024), BF), shape((1024, 3 * WIDE + 128), BF)),
        grid=(1,),
        in_specs=[SMEM_SPEC]
        + [
            any_spec((4, CHUNK, 1024)),
            any_spec((4, 8, CHUNK)),
            QKV_SPEC,
            any_spec((3 * HERE, 4 * CHUNK, HEAD_DIM)),
            any_spec((4 * CHUNK, WIDE)),
            any_spec((4 * CHUNK, 128)),
        ]
        + [any_spec((CHUNK, WIDE))] * 4
        + [any_spec((8, 1024)), any_spec((8, 1024)), any_spec((4, 1024))]
        + [any_spec((8, 128))] * 2,
        out_specs=(any_spec((1024, 1024)), any_spec((1024, 3 * WIDE + 128))),
        scratch_shapes=[
            pltpu.VMEM((128, 1024), F32),
            pltpu.VMEM((4, CHUNK, 128), F32),
            pltpu.SMEM((2, 4), jnp.int32),
            pltpu.VMEM((HERE, 4 * CHUNK, HEAD_DIM), BF),
            pltpu.VMEM((HERE, CHUNK, HEAD_DIM), F32),
            pltpu.VMEM((HERE, 4 * CHUNK, HEAD_DIM), F32),
            pltpu.VMEM((HERE, 4 * CHUNK, HEAD_DIM), F32),
            pltpu.VMEM((4 * CHUNK, 128), F32),
            pltpu.VMEM((4 * CHUNK, 768), BF),
            pltpu.VMEM((1024, 768), F32),
        ],
        compiler_params=PARAMS,
    )(scalars, xall, segr, pack, qkv, mixf, lse, *gs, *smalls)


def finish_kernel(sc, *refs):
    z = sc[0]
    pieces, (gq, gk, gv), vectors, ub, rms = refs[0:4], refs[4:7], refs[7:15], refs[15], refs[16:19]
    for k, piece in enumerate(pieces):
        cols = pl.ds(pl.multiple_of(lax.rem(z - k + 4, 4) * WIDE, WIDE), WIDE)
        for n, out in enumerate((gq, gk, gv)):
            out[:, cols] = piece[:, WIDE * n : WIDE * n + WIDE].astype(F32)
    extra = pieces[0][:, 3 * WIDE :].astype(F32)
    for piece in pieces[1:]:
        extra = extra + piece[:, 3 * WIDE :].astype(F32)
    extra = jnp.transpose(extra)
    for n, out in enumerate(vectors):
        out[...] = extra[n : n + 1, :]
    ub[...] = extra[8:12, :]
    counted = (16.0 * extra[15:16, 0:1] + extra[16:17, 0:1]) * 1024.0
    for n, out in enumerate(rms):
        out[...] = jnp.sqrt(extra[12 + n : 13 + n, 0:1] / counted)


def finish(scalars, pieces):
    shape = jax.ShapeDtypeStruct
    shapes = [(ROWS, 1024)] * 3 + [(1, ROWS)] * 8 + [(4, ROWS)] + [(1, 1)] * 3
    return pl.pallas_call(
        finish_kernel,
        name="finish",
        out_shape=tuple(shape(n, F32) for n in shapes),
        in_specs=[SMEM_SPEC] + [VMEM_SPEC] * 4,
        out_specs=(VMEM_SPEC,) * len(shapes),
        compiler_params=PARAMS,
    )(scalars, *pieces)


def line_gather(x):
    right = lax.ppermute(x, "ctx", [(0, 1), (1, 2), (2, 3)])
    left = lax.ppermute(x, "ctx", [(1, 0), (2, 1), (3, 2)])
    two = lax.ppermute(x, "ctx", [(0, 2), (1, 3), (2, 0), (3, 1)])
    return [x, right, left, two]


def line_forward(two):
    return lax.ppermute(two, "ctx", [(1, 0), (2, 3)])


def shift(x, k):
    n = lax.axis_size("ctx")
    return lax.ppermute(x, "ctx", [(i, (i + k) % n) for i in range(n)])


def swap(x, bits):
    return lax.ppermute(x, "fsdp", [(i, i ^ bits) for i in range(lax.axis_size("fsdp"))])


def add(*terms):
    total = terms[0].astype(F32)
    for term in terms[1:]:
        total = total + term.astype(F32)
    return total


def line_in(x):
    return lax.ppermute(x, "ctx", [(0, 1), (3, 2)])


def line_cross(x):
    return lax.ppermute(x, "ctx", [(1, 2), (2, 1)])


def line_out(x):
    return lax.ppermute(x, "ctx", [(1, 0), (2, 3)])


def line_sum(x):
    index = lax.axis_index("ctx")
    mine = x.astype(BF)
    pair = add(mine, line_in(mine)).astype(BF)
    whole = add(pair, line_cross(pair)).astype(BF)
    inner = (index == 1) | (index == 2)
    return jnp.where(inner, whole, line_out(whole)).astype(F32)


def per_device(
    tokens,
    segment_ids,
    cotangent,
    query_weight,
    query_bias,
    key_weight,
    value_weight,
    value_bias,
    out_weight,
    out_bias,
    attn_gain,
    attn_shift,
    up_weight,
    up_bias,
    down_weight,
    down_bias,
    mlp_gain,
    mlp_shift,
):
    owners = lax.axis_size("fsdp")
    plane = owners == SHARDS
    z = lax.axis_index("ctx")
    f = lax.axis_index("fsdp")
    if plane:
        chip, core = f // 2, f % 2
    else:
        chip, core = jnp.int32(0), jnp.int32(0)
    scalars = jnp.stack([z, chip, core, z]).astype(jnp.int32)
    tok = tokens[0]
    if plane:
        weights = (query_weight, key_weight, value_weight, out_weight)
        vectors = (query_bias, value_bias, out_bias, attn_gain, attn_shift, down_bias)
        vectors += (mlp_gain, mlp_shift, up_bias)
        packed, mine_pack = pack_inputs(scalars, tok, segment_ids, weights, vectors)
        pack = lax.all_gather(mine_pack, "fsdp", axis=0)
        xs = line_gather(packed)
        xs.append(line_forward(xs[3]))
        near_x, near_y = swap(up_weight, 2), swap(up_weight, 4)
        xs, near_x, near_y, after, pack = lax.optimization_barrier(
            (xs, near_x, near_y, down_weight, pack)
        )
        down = lax.all_gather(after, "fsdp", axis=0)
        half = up_weight.shape[1] // 2
        far = [swap(near_x[:, :half], 4), swap(near_y[:, half:], 2)]
    else:
        seg_row = jnp.pad(segment_ids.astype(BF), ((0, 15), (0, 1024 - CHUNK)))
        packed = jnp.concatenate([tok, seg_row])
        xs = line_gather(packed)
        xs.append(line_forward(xs[3]))
        quarter = jnp.concatenate(
            [
                lax.dynamic_slice_in_dim(m, z * WIDE, WIDE, 1)
                for m in (query_weight, key_weight, value_weight)
            ],
            axis=1,
        )
        whole = lambda m: lax.all_gather(m, "fsdp", axis=0, tiled=True)
        split = lambda m: whole(m).reshape(SHARDS, -1)
        line0 = jnp.concatenate(
            [split(m) for m in (query_bias, value_bias, out_bias, attn_gain, attn_shift, down_bias)],
            axis=1,
        )
        line1 = jnp.concatenate([split(m) for m in (mlp_gain, mlp_shift, up_bias)], axis=1)
        lines = jnp.pad(jnp.stack([line0, line1], axis=1), ((0, 0), (0, 14), (0, 0)))
        pack = jnp.concatenate([whole(quarter).reshape(SHARDS, ROWS, 768), lines], axis=1)
        out_rows = whole(out_weight).reshape(SHARDS, ROWS, 1024)
        wide = lambda m: jnp.pad(m, ((0, 0), (0, 0), (0, 1024 - m.shape[2])))
        pack = jnp.concatenate([out_rows, wide(pack)], axis=1)
        ups = list(whole(up_weight).reshape(SHARDS, ROWS, 4096))
        down = whole(down_weight).reshape(SHARDS, 512, 1024)
    valid = (segment_ids[0] != SEGS - 1).astype(F32)[:, None]

    m0, m1, m2, m3, mixf, lse, qkv, xall, segr = attn_fwd(scalars, xs, pack)
    parts = [m0] + [shift(m, -k) for k, m in ((1, m1), (2, m2), (3, m3))]
    if plane:
        far, m0 = lax.optimization_barrier((far, m0))
        far = jnp.concatenate(far, axis=1)
        ups = []
        for rows in (up_weight, near_x, near_y, far):
            ups += [rows, swap(rows, 1)]
    normed, low, low_rel, scaled, inv, mixed, stats_a = out_project(
        scalars, tok, parts, pack, valid
    )
    acts, slope, result, gh2, sums_m, stats_m = mlp_fwd(
        normed, low, low_rel, mixed, ups, down, pack, cotangent[0], valid
    )
    acts_p = swap(acts, 1)
    grads, gh1, g0, g1, g2, g3, sums_a, ub = mlp_bwd(
        scalars, acts, slope, ups, down, gh2, scaled, inv, pack
    )
    gs = [g0] + [shift(g, k) for k, g in ((1, g1), (2, g2), (3, g3))]
    grads_p = swap(grads, 1)
    d3, d1, d2, d0 = down_grads(scalars, acts, acts_p)
    if plane:
        d_far = swap(d3, 2)
    r3, r1, r2, r0 = rest_grads(scalars, acts, acts_p, grads, grads_p)
    gs, d1, r3, r1, r2, r0 = lax.optimization_barrier((gs, d1, r3, r1, r2, r0))
    if plane:
        r_far = swap(r3, 4)
        d_from_x, r_from_y = swap(d1, 2), swap(r2, 4)
    smalls = (sums_m, sums_a, ub.reshape(1024, 4).T, stats_a, stats_m)
    ig, gw = attn_bwd(scalars, xall, segr, pack, qkv, mixf, lse, gs, smalls)
    if plane:
        ig, gw, d_far, r_far, d_from_x = lax.optimization_barrier(
            (ig, gw, d_far, r_far, d_from_x)
        )
    gw_first = gw
    ig = lax.psum_scatter(ig, "ctx", scatter_dimension=0, tiled=True)
    ig, gw = lax.optimization_barrier((ig, gw))
    q_own = lax.psum_scatter(gw, "fsdp", scatter_dimension=0, tiled=True)
    input_grad = add(gh1, ig)
    q_low = q_own.astype(BF)

    if plane:
        cuts = ((0, 192, 0, 256), (192, 320, 256, 384), (320, 448, 384, 512), (448, 512, 512, 640))
        count = len(cuts)
        sent, pairs, wholes, parts = {}, {}, {}, {}
        q_pieces = None
        for wave in range(count + 3):
            out = {}
            if wave < count:
                a, b, c, d = cuts[wave]
                out["y"] = add(d2[a:b], d_far[a:b]).astype(BF)
                out["x"] = add(r1[c:d], r_far[c:d]).astype(BF)
            if 0 <= wave - 1 < count:
                a, b, c, d = cuts[wave - 1]
                from_y, from_x = sent.pop(wave - 1)
                total = [add(d0[a:b], d_from_x[a:b], from_y), add(r0[c:d], r_from_y[c:d], from_x)]
                out["one"] = jnp.concatenate(total).astype(BF)
            if 0 <= wave - 2 < count:
                out["two"] = pairs.pop(wave - 2)
            if 0 <= wave - 3 < count:
                out["three"] = wholes[wave - 3]
            if wave == 0:
                out["after"] = gw_first
            if wave == 2:
                out["after"] = ig
            if wave == 3:
                out["after"] = q_low
            if wave == count + 1:
                out["q"] = q_low
            out = lax.optimization_barrier(out)
            if "y" in out:
                sent[wave] = (swap(out["y"], 4), swap(out["x"], 2))
            if "one" in out:
                pairs[wave - 1] = add(out["one"], line_in(out["one"])).astype(BF)
            if "two" in out:
                wholes[wave - 2] = add(out["two"], line_cross(out["two"])).astype(BF)
            if "three" in out:
                inner = (z == 1) | (z == 2)
                back = line_out(out["three"])
                parts[wave - 3] = jnp.where(inner, out["three"], back).astype(F32)
            if "q" in out:
                q_pieces = [out["q"]] + [shift(out["q"], k) for k in (1, 2, 3)]
        parts_d = [parts[n][0 : cuts[n][1] - cuts[n][0]] for n in range(count)]
        parts_r = [parts[n][cuts[n][1] - cuts[n][0] :] for n in range(count)]
        parts_r = [parts_r[0][0:ROWS], parts_r[0][ROWS:]] + parts_r[1:]
        grad_down = jnp.concatenate(parts_d)
        grad_up = jnp.concatenate(parts_r[0:4], axis=1)
        grad_out = parts_r[4]
    else:
        other = scalars.at[2].set(1)
        sums_w = (d3, d1, d2, d0, r3, r1, r2, r0)
        second = down_grads(other, acts, acts_p) + rest_grads(other, acts, acts_p, grads, grads_p)
        rows_of = lambda t: ([t[3], t[1], t[2], t[0]], [t[7], t[5], t[6], t[4]])
        down_0, rest_0 = rows_of(sums_w)
        down_1, rest_1 = rows_of(second)
        down_all = 0.5 * jnp.stack([m.astype(F32) for p in zip(down_0, down_1) for m in p])
        rest_all = 0.5 * jnp.stack([m.astype(F32) for p in zip(rest_0, rest_1) for m in p])
        scatter = lambda m: lax.psum_scatter(
            m.astype(BF), "fsdp", scatter_dimension=0, tiled=True
        )
        grad_down = line_sum(scatter(down_all.reshape(4096, 1024)))
        grad_up = line_sum(
            scatter(
                rest_all[:, 0:512]
                .reshape(SHARDS, 4, ROWS, 1024)
                .swapaxes(1, 2)
                .reshape(1024, 4096)
            )
        )
        grad_out = line_sum(scatter(rest_all[:, 512:].reshape(1024, 1024)))
        q_pieces = [q_low] + [shift(q_low, k) for k in (1, 2, 3)]
    if plane:
        done = finish(scalars, q_pieces)
        grad_q, grad_k, grad_v = done[0:3]
        vectors = [v.reshape(-1) for v in done[3:11]]
        up_bias_grad = done[11].T.reshape(-1)
        rms = [v.reshape(()) for v in done[12:15]]
    else:
        table = jnp.take(jnp.stack(q_pieces), (z - jnp.arange(4)) % 4, axis=0)
        extra = add(*q_pieces)[:, 3 * WIDE :]
        cols = lambda n: jnp.concatenate(
            [table[a, :, n * WIDE : (n + 1) * WIDE].astype(F32) for a in range(4)], axis=1
        )
        grad_q, grad_k, grad_v = cols(0), cols(1), cols(2)
        vectors = [extra[:, n] for n in range(8)]
        up_bias_grad = extra[:, 8:12].reshape(-1)
        counted = (16.0 * extra[0, 15] + extra[0, 16]) * 1024
        rms = [jnp.sqrt(extra[0, 12 + n] / counted) for n in range(3)]
    return (
        result[None],
        input_grad[None],
        grad_q,
        vectors[6],
        grad_k,
        grad_v,
        vectors[7],
        grad_out,
        vectors[5],
        vectors[3],
        vectors[4],
        grad_up,
        up_bias_grad,
        grad_down,
        vectors[2],
        vectors[0],
        vectors[1],
        rms[0],
        rms[1],
        rms[2],
    )


def solution(mesh):
    matrix, vector = P("fsdp", None), P("fsdp")
    stream = P("fsdp", "ctx", None)
    placed = (
        stream,
        P("fsdp", "ctx"),
        stream,
        matrix,
        vector,
        matrix,
        matrix,
        vector,
        matrix,
        vector,
        vector,
        vector,
        matrix,
        vector,
        matrix,
        vector,
        vector,
        vector,
    )
    return jax.shard_map(
        per_device,
        mesh=mesh,
        in_specs=placed,
        out_specs=(
            stream,
            stream,
            matrix,
            vector,
            matrix,
            matrix,
            vector,
            matrix,
            vector,
            vector,
            vector,
            matrix,
            vector,
            matrix,
            vector,
            vector,
            vector,
            P(),
            P(),
            P(),
        ),
        check_vma=False,
    )
```

time: 515 us -> 407 us (0.79)
  waiting for transfers between devices: 274 us -> 158 us
  Pallas kernels: 100 us -> 117 us
  starting transfers between devices: 65.1 us -> 78.7 us
  other arithmetic: 36.2 us -> 23.1 us
  between operations: 20.9 us -> 14.6 us
    ppermute x15 -> x9, waiting for transfers between devices: 110 us -> 24.1 us  [shift(): return lax.ppermute(x, 'ctx', [(i, (i + k) % n) for i in range(n)])]
    ppermute x8 -> x16, starting transfers between devices: 13.8 us -> 43.9 us  [the longest x4 24 us: line_in(): return lax.ppermute(x, 'ctx', [(0, 1), (3, 2)])]
    all_gather x2, waiting for transfers between devices: 36.2 us -> 7.47 us  [the longest x1 4.1 us: per_device(): pack = lax.all_gather(mine_pack, 'fsdp', axis=0)]
    ppermute x15 -> x9, starting transfers between devices: 36.1 us -> 14.1 us  [shift(): return lax.ppermute(x, 'ctx', [(i, (i + k) % n) for i in range(n)])]
    pallas_call x2 -> x6, Pallas kernels: 58.2 us -> 71.6 us  [the longest x1 30.5 us: attn_bwd(): pl.pallas_call(attn_bwd_kernel, name='attn_bwd', out_shape=(shape((1024,...]
    concatenate x12 -> x6, other arithmetic: 9.91 us -> 3.08 us  [the longest x1 1.47 us: per_device(): grad_up = jnp.concatenate(parts_r[0:4], axis=1)]
    add x8 -> x0, other arithmetic: 5.84 us -> none  [the longest x2 5.1 us: add(): total = total + term.astype(F32)]
    ppermute x21 -> x22, starting transfers between devices: 15.2 us -> 20.5 us  [swap(): lax.ppermute(x, 'fsdp', [(i, i ^ bits) for i in range(lax.axis_size('fsdp...]
  transfers between devices with their start and end apart: 46 -> 51, of which waited for: 24 -> 24; matrix products, arithmetic and copies ran while one was open for 8% -> 7% of each run, Pallas kernels for 10% -> 24%
where the time goes in v2:
time: 407 us; the launch traced here: 406 us
  waiting for transfers between devices  158 us (39%)
  Pallas kernels  117 us (29%)
  starting transfers between devices  78.7 us (19%)
  other arithmetic  23.1 us (6%)
  local copies, waits for them, and re-layouts  14.8 us (4%)
  between operations  14.6 us (4%)
    ppermute x22, waiting for transfers between devices, swap(): lax.ppermute(x, 'fsdp', [(i, i ^ bits) for i in range(lax.axis_size('fsdp...  55.2 us
    pallas_call x1, Pallas kernels, attn_bwd(): pl.pallas_call(attn_bwd_kernel, name='attn_bwd', out_shape=(shape((1024,...  30.5 us
    ppermute x9, waiting for transfers between devices, shift(): return lax.ppermute(x, 'ctx', [(i, (i + k) % n) for i in range(n)])  24.1 us
    ppermute x4, starting transfers between devices, line_in(): return lax.ppermute(x, 'ctx', [(0, 1), (3, 2)])  24 us
    ppermute x4, waiting for transfers between devices, line_out(): return lax.ppermute(x, 'ctx', [(1, 0), (2, 3)])  23.7 us
    pallas_call x1, Pallas kernels, attn_fwd(): pl.pallas_call(attn_fwd_kernel, name='attn_fwd', out_shape=(shape((CHUNK,...  21.9 us
    ppermute x22, starting transfers between devices, swap(): lax.ppermute(x, 'fsdp', [(i, i ^ bits) for i in range(lax.axis_size('fsdp...  20.5 us
    ppermute x4, waiting for transfers between devices, line_in(): return lax.ppermute(x, 'ctx', [(0, 1), (3, 2)])  20.4 us
  transfers between devices with their start and end apart: 51, of which 24 were waited for; matrix products, arithmetic and copies ran while one was open for 7% of the time, Pallas kernels for 24%

profile of v2, /device:TPU:0, one launch (start us, length us, event | category | flops | bytes accessed | tf_op | source)
XLA Modules:
  0.0 405.5 jit_solution(1889218815568790301)
XLA Ops:
  9.2 2.5 pack_inputs.1
  11.8 4.1 %collective-permute-start.2 = (bf16[272,1024]{1,0:T(8,128)(2,1)}, bf16[272,1024]{1,0:T(8,128)(2,1)S(1)}, u32[]{:S(2)}, u32[]{:S(2)}) collective-permute-start(bf16[272,1024]{1,0:T(8,128)(2,1)} %get-tuple-element.126.x0), channel_id=1, source_target_pairs={{0,16},{8,24},{16,0},{24,8},{1,17},{9,25},{17,1},{25,9},{2,18},{10... | collective-permute-start | bytes 1671176 | tf_op jit(solution)/shard_map/ppermute | solution.py:761
  15.9 1.5 collective-permute-start.5
  17.4 1.5 collective-permute-start.4
  20.2 4.6 %collective-permute-start = (bf16[272,1024]{1,0:T(8,128)(2,1)}, bf16[272,1024]{1,0:T(8,128)(2,1)S(1)}, u32[]{:S(2)}, u32[]{:S(2)}) collective-permute-start(bf16[272,1024]{1,0:T(8,128)(2,1)} %get-tuple-element.126.x0), channel_id=1, source_target_pairs={{0,8},{8,16},{16,24},{1,9},{9,17},{17,25},{2,10},{10,18},{18,26},{... | collective-permute-start | bytes 1671176 | tf_op jit(solution)/shard_map/ppermute | solution.py:759
  24.7 16.8 %collective-permute-done.2.x2 = bf16[272,1024]{1,0:T(8,128)(2,1)S(1)} collective-permute-done((bf16[272,1024]{1,0:T(8,128)(2,1)}, bf16[272,1024]{1,0:T(8,128)(2,1)S(1)}, u32[]{:S(2)}, u32[]{:S(2)}) %collective-permute-start.2) | collective-permute-done | bytes 557088 | tf_op jit(solution)/shard_map/ppermute | solution.py:761
  42.8 3.2 collective-permute-done.1.left
  46.0 4.2 %collective-permute-done.5.refs_4_ = bf16[128,4096]{1,0:T(8,128)(2,1)S(1)} collective-permute-done((bf16[128,4096]{1,0:T(8,128)(2,1)}, bf16[128,4096]{1,0:T(8,128)(2,1)S(1)}, u32[]{:S(2)}, u32[]{:S(2)}) %collective-permute-start.5) | collective-permute-done | bytes 1048608 | tf_op jit(solution)/shard_map/ppermute | solution.py:775
  50.2 2.7 collective-permute-done.4.refs_2_
  52.9 4.4 %collective-permute-done.3.far = bf16[272,1024]{1,0:T(8,128)(2,1)} collective-permute-done((bf16[272,1024]{1,0:T(8,128)(2,1)S(1)}, bf16[272,1024]{1,0:T(8,128)(2,1)}, u32[]{:S(2)}, u32[]{:S(2)}) %collective-permute-start.3) | collective-permute-done | bytes 557088 | tf_op jit(solution)/shard_map/ppermute | solution.py:766
  57.3 4.1 %all-gather.5.cloned.1.call-done = bf16[2176,1024]{1,0:T(8,128)(2,1)} async-done(((bf16[272,1024]{1,0:T(8,128)(2,1)}), bf16[2176,1024]{1,0:T(8,128)(2,1)}) %all-gather.5.cloned.1.call-update) | async-done | bytes 4456464 | tf_op jit(solution)/shard_map/all_gather | solution.py:841
  63.1 1.5 collective-permute-start.13
  65.7 21.9 %attn_fwd.1 = (bf16[256,256]{1,0:T(8,128)(2,1)}, bf16[256,256]{1,0:T(8,128)(2,1)}, bf16[256,256]{1,0:T(8,128)(2,1)}, bf16[256,256]{1,0:T(8,128)(2,1)}, f32[1024,...) custom-call(s32[4]{0:T(128)} %pad_add_fusion.sc, ...), custom_call_target="tpu_custom_call" | custom-call | tf_op jit(solution)/shard_map/attn_fwd/pallas_call | solution.py:201
  90.8 4.2 %collective-permute-done.6.r1 = bf16[256,256]{1,0:T(8,128)(2,1)S(1)} collective-permute-done((bf16[256,256]{1,0:T(8,128)(2,1)S(1)}, bf16[256,256]{1,0:T(8,128)(2,1)S(1)}, u32[]{:S(2)}, u32[]{:S(2)}) %collective-permute-start.6) | collective-permute-done | bytes 131104 | tf_op jit(solution)/shard_map/ppermute | solution.py:771
  95.5 7.8 %collective-permute-done.7.r2 = bf16[256,256]{1,0:T(8,128)(2,1)S(1)} collective-permute-done((bf16[256,256]{1,0:T(8,128)(2,1)S(1)}, bf16[256,256]{1,0:T(8,128)(2,1)S(1)}, u32[]{:S(2)}, u32[]{:S(2)}) %collective-permute-start.7) | collective-permute-done | bytes 131104 | tf_op jit(solution)/shard_map/ppermute | solution.py:771
  104.1 6.2 %collective-permute-done.8.r3 = bf16[256,256]{1,0:T(8,128)(2,1)S(1)} collective-permute-done((bf16[256,256]{1,0:T(8,128)(2,1)}, bf16[256,256]{1,0:T(8,128)(2,1)S(1)}, u32[]{:S(2)}, u32[]{:S(2)}) %collective-permute-start.8) | collective-permute-done | bytes 131104 | tf_op jit(solution)/shard_map/ppermute | solution.py:771
  110.9 5.0 %out_project.1 = (f32[256,1024]{1,0:T(8,128)}, bf16[256,1024]{1,0:T(8,128)(2,1)}, bf16[256,1024]{1,0:T(8,128)(2,1)}, f32[256,1024]{1,0:T(8,128)}, f32[256,128]{1...) custom-call(s32[4]{0:T(128)} %pad_add_fusion.sc, bf16[256,1024]{1,0:T(8,128)(2,1)} %bitcast.44, ...), custom_call_target="tpu_custom_call" | custom-call | tf_op jit(solution)/shard_map/out_project/pallas_call | solution.py:281
  116.0 3.4 all-gather.7.cloned.1.call-done
  119.3 18.3 %mlp_fwd.1 = (bf16[7,256,1024]{2,1,0:T(8,128)(2,1)}, f32[256,4096]{1,0:T(8,128)}, bf16[256,1024]{1,0:T(8,128)(2,1)}, f32[256,1024]{1,0:T(8,128)}, f32[8,1024]{1,0:T(8,128)}, /*index=5*/f32[8,128]{1,0:T(8,128)}) custom-call(f32[256,1024]{1,0:T(8,128)} %get-tuple-element.136.normed, bf16[256,1024]{1,0:T(8,128)(2,1)} %get-tuple-element.137.low, ...), custom_call_target="tpu_custom_call" | custom-call | tf_op jit(solution)/shard_map/mlp_fwd/pallas_call | solution.py:364
  138.0 17.9 %mlp_bwd.1 = (bf16[5,256,1024]{2,1,0:T(8,128)(2,1)}, f32[256,1024]{1,0:T(8,128)}, bf16[256,256]{1,0:T(8,128)(2,1)}, bf16[256,256]{1,0:T(8,128)(2,1)}, bf16[256,2...) custom-call(s32[4]{0:T(128)} %pad_add_fusion.sc, ...), custom_call_target="tpu_custom_call" | custom-call | tf_op jit(solution)/shard_map/mlp_bwd/pallas_call | solution.py:452
  156.2 1.5 collective-permute-start.15
  157.7 2.4 collective-permute-start.16
  161.5 1.8 copy-done
  163.3 7.8 %down_grads.1 = (bf16[512,1024]{1,0:T(8,128)(2,1)}, bf16[512,1024]{1,0:T(8,128)(2,1)}, bf16[512,1024]{1,0:T(8,128)(2,1)}, bf16[512,1024]{1,0:T(8,128)(2,1)}) custom-call(s32[4]{0:T(128)} %pad_add_fusion.sc, bf16[7,256,1024]{2,1,0:T(8,128)(2,1)} %get-tuple-element.146.gm.ho.lo, bf16[7,256,1024]{2,1,0:T(8,128)(2,1)} %copy-done, ...), custom_call_target="tpu_custom_call" | custom-call | tf_op jit(solution)/shard_map/down_grads/pallas_call | solution.py:516
  171.2 10.4 %rest_grads.1 = (bf16[640,1024]{1,0:T(8,128)(2,1)}, bf16[640,1024]{1,0:T(8,128)(2,1)}, bf16[640,1024]{1,0:T(8,128)(2,1)}, bf16[640,1024]{1,0:T(8,128)(2,1)}) custom-call(s32[4]{0:T(128)} %pad_add_fusion.sc, bf16[7,256,1024]{2,1,0:T(8,128)(2,1)} %get-tuple-element.146.gm.ho.lo, bf16[7,256,1024]{2,1,0:T(8,128)(2,1)} %copy-done, ...), custom_call_target="tpu_custom_call" | custom-call | tf_op jit(solution)/shard_map/rest_grads/pallas_call | solution.py:564
  186.2 30.5 %attn_bwd.1 = (bf16[1024,1024]{1,0:T(8,128)(2,1)}, bf16[1024,896]{1,0:T(8,128)(2,1)}) custom-call(s32[4]{0:T(128)} %pad_add_fusion.sc, bf16[4,256,1024]{2,1,0:T(8,128)(2,1)} %get-tuple-element.152.xall, f32[4,8,256]{2,1,0:T(8,128)} %get-tuple-element.153.segr, bf16[8,272,1024]{2,1,0:T(8,128)(2,1)} %bitcast.40, bf16[12,1024,64]{2,1,0:T(8,128)(2,1)} %get-tuple-element.154.qkv, ...), custom_call_target="tpu_custom_call" | custom-call | tf_op jit(solution)/shard_map/attn_bwd/pallas_call | solution.py:692
  216.7 13.1 %collective-permute-done.20 = bf16[512,1024]{1,0:T(8,128)(2,1)} collective-permute-done((bf16[512,1024]{1,0:T(8,128)(2,1)}, bf16[512,1024]{1,0:T(8,128)(2,1)}, u32[]{:S(2)}, u32[]{:S(2)}) %collective-permute-start.20) | collective-permute-done | bytes 1048608 | tf_op jit(solution)/shard_map/ppermute | solution.py:775
  234.4 2.0 add_convert_fusion.16
  236.7 30.7 %collective-permute-done.23 = bf16[192,1024]{1,0:T(8,128)(2,1)S(1)} collective-permute-done((bf16[192,1024]{1,0:T(8,128)(2,1)S(1)}, bf16[192,1024]{1,0:T(8,128)(2,1)S(1)}, u32[]{:S(2)}, u32[]{:S(2)}) %collective-permute-start.23) | collective-permute-done | bytes 393248 | tf_op jit(solution)/shard_map/ppermute | solution.py:775
  271.5 2.7 collective-permute-start.28
  276.7 4.4 %collective-permute-done.26 = bf16[128,1024]{1,0:T(8,128)(2,1)S(1)} collective-permute-done((bf16[128,1024]{1,0:T(8,128)(2,1)S(1)}, bf16[128,1024]{1,0:T(8,128)(2,1)S(1)}, u32[]{:S(2)}, u32[]{:S(2)}) %collective-permute-start.26) | collective-permute-done | bytes 262176 | tf_op jit(solution)/shard_map/ppermute | solution.py:775
  283.5 9.0 %collective-permute-done.28 = bf16[448,1024]{1,0:T(8,128)(2,1)S(1)} collective-permute-done((bf16[448,1024]{1,0:T(8,128)(2,1)S(1)}, bf16[448,1024]{1,0:T(8,128)(2,1)S(1)}, u32[]{:S(2)}, u32[]{:S(2)}) %collective-permute-start.28) | collective-permute-done | bytes 917536 | tf_op jit(solution)/shard_map/ppermute | solution.py:786
  292.9 1.6 collective-permute-start.29
  297.6 8.5 %collective-permute-start.32 = (bf16[256,1024]{1,0:T(8,128)(2,1)S(1)}, bf16[256,1024]{1,0:T(8,128)(2,1)S(1)}, u32[]{:S(2)}, u32[]{:S(2)}) collective-permute-start(bf16[256,1024]{1,0:T(8,128)(2,1)S(1)} %pad_maximum_fusion.3), channel_id=1, source_target_pairs={{0,8},{24,16},{1,9},{25,17},{2,10},{26,18},{3,11},{27,19},{4,12},{... | collective-permute-start | bytes 1572872 | tf_op jit(solution)/shard_map/ppermute | solution.py:786
  308.4 7.2 %collective-permute-done.32 = bf16[256,1024]{1,0:T(8,128)(2,1)S(1)} collective-permute-done((bf16[256,1024]{1,0:T(8,128)(2,1)S(1)}, bf16[256,1024]{1,0:T(8,128)(2,1)S(1)}, u32[]{:S(2)}, u32[]{:S(2)}) %collective-permute-start.32) | collective-permute-done | bytes 524320 | tf_op jit(solution)/shard_map/ppermute | solution.py:786
  316.1 1.9 reduce-scatter.5.cloned.1.call-done.refs_0_
  320.8 8.4 %collective-permute-start.36 = (bf16[256,1024]{1,0:T(8,128)(2,1)S(1)}, bf16[256,1024]{1,0:T(8,128)(2,1)S(1)}, u32[]{:S(2)}, u32[]{:S(2)}) collective-permute-start(bf16[256,1024]{1,0:T(8,128)(2,1)S(1)} %pad_maximum_fusion.4), channel_id=1, source_target_pairs={{0,8},{24,16},{1,9},{25,17},{2,10},{26,18},{3,11},{27,19},{4,12},{... | collective-permute-start | bytes 1572872 | tf_op jit(solution)/shard_map/ppermute | solution.py:786
  333.0 4.2 %collective-permute-done.36 = bf16[256,1024]{1,0:T(8,128)(2,1)S(1)} collective-permute-done((bf16[256,1024]{1,0:T(8,128)(2,1)S(1)}, bf16[256,1024]{1,0:T(8,128)(2,1)S(1)}, u32[]{:S(2)}, u32[]{:S(2)}) %collective-permute-start.36) | collective-permute-done | bytes 524320 | tf_op jit(solution)/shard_map/ppermute | solution.py:786
  337.4 4.4 %collective-permute-start.38 = (bf16[192,1024]{1,0:T(8,128)(2,1)S(1)}, bf16[192,1024]{1,0:T(8,128)(2,1)S(1)}, u32[]{:S(2)}, u32[]{:S(2)}) collective-permute-start(bf16[192,1024]{1,0:T(8,128)(2,1)S(1)} %pad_maximum_fusion.5), channel_id=1, source_target_pairs={{0,8},{24,16},{1,9},{25,17},{2,10},{26,18},{3,11},{27,19},{4,12},{... | collective-permute-start | bytes 1179656 | tf_op jit(solution)/shard_map/ppermute | solution.py:786
  344.9 9.5 %collective-permute-done.44 = bf16[448,1024]{1,0:T(8,128)(2,1)S(1)} collective-permute-done((bf16[448,1024]{1,0:T(8,128)(2,1)S(1)}, bf16[448,1024]{1,0:T(8,128)(2,1)S(1)}, u32[]{:S(2)}, u32[]{:S(2)}) %collective-permute-start.44) | collective-permute-done | bytes 917536 | tf_op jit(solution)/shard_map/ppermute | solution.py:794
  356.0 3.7 collective-permute-start.41
  359.7 2.9 collective-permute-start.40
  364.4 8.6 %collective-permute-done.45 = bf16[256,1024]{1,0:T(8,128)(2,1)S(1)} collective-permute-done((bf16[256,1024]{1,0:T(8,128)(2,1)S(1)}, bf16[256,1024]{1,0:T(8,128)(2,1)S(1)}, u32[]{:S(2)}, u32[]{:S(2)}) %collective-permute-start.45) | collective-permute-done | bytes 524320 | tf_op jit(solution)/shard_map/ppermute | solution.py:794
  374.4 5.9 %collective-permute-done.41.refs_3_ = bf16[128,896]{1,0:T(8,128)(2,1)S(1)} collective-permute-done((bf16[128,896]{1,0:T(8,128)(2,1)S(1)}, bf16[128,896]{1,0:T(8,128)(2,1)S(1)}, u32[]{:S(2)}, u32[]{:S(2)}) %collective-permute-start.41) | collective-permute-done | bytes 229408 | tf_op jit(solution)/shard_map/ppermute | solution.py:771
  381.8 2.5 finish.1
  388.2 3.1 collective-permute-done.46
  392.5 1.5 pad_maximum_fusion
  394.0 2.6 collective-permute-done.43
  (179 shorter events, 62.5 us)
Async XLA Ops:
  7.2 54.2 %all-gather.5.cloned.1.call-start = ((), (), s32[]{:S(2)}) async-start(), calls=%async_computation.4 | async-start | bytes 5013504 | tf_op jit(solution)/shard_map/all_gather | solution.py:841
  11.7 107.6 %all-gather.7.cloned.1.call-start = ((), (), s32[]{:S(2)}) async-start(), calls=%async_computation.5 | async-start | bytes 9437184 | tf_op jit(solution)/shard_map/all_gather | solution.py:848
  11.8 29.7 %collective-permute-start.2 = (bf16[272,1024]{1,0:T(8,128)(2,1)}, bf16[272,1024]{1,0:T(8,128)(2,1)S(1)}, u32[]{:S(2)}, u32[]{:S(2)}) collective-permute-start(bf16[272,1024]{1,0:T(8,128)(2,1)} %get-tuple-element.126.x0), channel_id=1, source_target_pairs={{0,16},{8,24},{16,0},{24,8},{1,17},{9,25},{17,1},{25,9},{2,18},{10... | collective-permute-start | bytes 1671176 | tf_op jit(solution)/shard_map/ppermute | solution.py:761
  15.9 34.4 %collective-permute-start.5 = (bf16[128,4096]{1,0:T(8,128)(2,1)}, bf16[128,4096]{1,0:T(8,128)(2,1)S(1)}, u32[]{:S(2)}, u32[]{:S(2)}) collective-permute-start(bf16[128,4096]{1,0:T(8,128)(2,1)} %refs_0_.3), channel_id=1, source_target_pairs={{0,4},{1,5},{2,6},{3,7},{4,0},{5,1},{6,2},{7,3},{8,12},{9,13},{10,... | collective-permute-start | bytes 3145736 | tf_op jit(solution)/shard_map/ppermute | solution.py:775
  17.4 35.5 %collective-permute-start.4 = (bf16[128,4096]{1,0:T(8,128)(2,1)}, bf16[128,4096]{1,0:T(8,128)(2,1)S(1)}, u32[]{:S(2)}, u32[]{:S(2)}) collective-permute-start(bf16[128,4096]{1,0:T(8,128)(2,1)} %refs_0_.3), channel_id=1, source_target_pairs={{0,2},{1,3},{2,0},{3,1},{4,6},{5,7},{6,4},{7,5},{8,10},{9,11},{10,... | collective-permute-start | bytes 3145736 | tf_op jit(solution)/shard_map/ppermute | solution.py:775
  18.9 27.1 %collective-permute-start.1 = (bf16[272,1024]{1,0:T(8,128)(2,1)}, bf16[272,1024]{1,0:T(8,128)(2,1)S(1)}, u32[]{:S(2)}, u32[]{:S(2)}) collective-permute-start(bf16[272,1024]{1,0:T(8,128)(2,1)} %get-tuple-element.126.x0), channel_id=1, source_target_pairs={{8,0},{16,8},{24,16},{9,1},{17,9},{25,17},{10,2},{18,10},{26,18},{... | collective-permute-start | bytes 1671176 | tf_op jit(solution)/shard_map/ppermute | solution.py:760
  20.2 25.9 %collective-permute-start = (bf16[272,1024]{1,0:T(8,128)(2,1)}, bf16[272,1024]{1,0:T(8,128)(2,1)S(1)}, u32[]{:S(2)}, u32[]{:S(2)}) collective-permute-start(bf16[272,1024]{1,0:T(8,128)(2,1)} %get-tuple-element.126.x0), channel_id=1, source_target_pairs={{0,8},{8,16},{16,24},{1,9},{9,17},{17,25},{2,10},{10,18},{18,26},{... | collective-permute-start | bytes 1671176 | tf_op jit(solution)/shard_map/ppermute | solution.py:759
  41.5 15.8 %collective-permute-start.3 = (bf16[272,1024]{1,0:T(8,128)(2,1)S(1)}, bf16[272,1024]{1,0:T(8,128)(2,1)}, u32[]{:S(2)}, u32[]{:S(2)}) collective-permute-start(bf16[272,1024]{1,0:T(8,128)(2,1)S(1)} %collective-permute-done.2.x2), channel_id=1, source_target_pairs={{8,0},{16,24},{9,1},{17,25},{10,2},{18,26},{11,3},{19,27},{12,4},{... | collective-permute-start | bytes 1671176 | tf_op jit(solution)/shard_map/ppermute | solution.py:766
  61.4 210.0 %reduce-scatter.3.cloned.1.call-start = ((), (), s32[]{:S(2)}) async-start(), calls=%async_computation.2 | async-start | bytes 2621440 | tf_op jit(solution)/shard_map/reduce_scatter | solution.py:914
  63.1 24.5 %collective-permute-start.13 = (bf16[128,2048]{1,0:T(8,128)(2,1)}, bf16[128,2048]{1,0:T(8,128)(2,1)S(1)}, u32[]{:S(2)}, u32[]{:S(2)}) collective-permute-start(bf16[128,2048]{1,0:T(8,128)(2,1)} %slice.133), channel_id=1, source_target_pairs={{0,2},{1,3},{2,0},{3,1},{4,6},{5,7},{6,4},{7,5},{8,10},{9,11},{10,... | collective-permute-start | bytes 1572872 | tf_op jit(solution)/shard_map/ppermute | solution.py:775
  64.6 23.0 %collective-permute-start.12 = (bf16[128,2048]{1,0:T(8,128)(2,1)}, bf16[128,2048]{1,0:T(8,128)(2,1)}, u32[]{:S(2)}, u32[]{:S(2)}) collective-permute-start(bf16[128,2048]{1,0:T(8,128)(2,1)} %slice.132), channel_id=1, source_target_pairs={{0,4},{1,5},{2,6},{3,7},{4,0},{5,1},{6,2},{7,3},{8,12},{9,13},{10,... | collective-permute-start | bytes 1572872 | tf_op jit(solution)/shard_map/ppermute | solution.py:775
  65.1 50.8 %collective-permute-start.9 = (bf16[128,4096]{1,0:T(8,128)(2,1)}, bf16[128,4096]{1,0:T(8,128)(2,1)}, u32[]{:S(2)}, u32[]{:S(2)}) collective-permute-start(bf16[128,4096]{1,0:T(8,128)(2,1)} %refs_0_.3), channel_id=1, source_target_pairs={{0,1},{1,0},{2,3},{3,2},{4,5},{5,4},{6,7},{7,6},{8,9},{9,8},{10,11... | collective-permute-start | bytes 3145736 | tf_op jit(solution)/shard_map/ppermute | solution.py:775
  65.1 50.8 %collective-permute-start.10 = (bf16[128,4096]{1,0:T(8,128)(2,1)S(1)}, bf16[128,4096]{1,0:T(8,128)(2,1)}, u32[]{:S(2)}, u32[]{:S(2)}) collective-permute-start(bf16[128,4096]{1,0:T(8,128)(2,1)S(1)} %collective-permute-done.4.refs_2_), channel_id=1, source_target_pairs={{0,1},{1,0},{2,3},{3,2},{4,5},{5,4},{6,7},{7,6},{8,9},{9,8},{10,11... | collective-permute-start | bytes 3145736 | tf_op jit(solution)/shard_map/ppermute | solution.py:775
  65.6 50.3 %collective-permute-start.11 = (bf16[128,4096]{1,0:T(8,128)(2,1)S(1)}, bf16[128,4096]{1,0:T(8,128)(2,1)}, u32[]{:S(2)}, u32[]{:S(2)}) collective-permute-start(bf16[128,4096]{1,0:T(8,128)(2,1)S(1)} %collective-permute-done.5.refs_4_), channel_id=1, source_target_pairs={{0,1},{1,0},{2,3},{3,2},{4,5},{5,4},{6,7},{7,6},{8,9},{9,8},{10,11... | collective-permute-start | bytes 3145736 | tf_op jit(solution)/shard_map/ppermute | solution.py:775
  88.8 27.1 %collective-permute-start.14 = (bf16[128,4096]{1,0:T(8,128)(2,1)S(1)}, bf16[128,4096]{1,0:T(8,128)(2,1)}, u32[]{:S(2)}, u32[]{:S(2)}) collective-permute-start(bf16[128,4096]{1,0:T(8,128)(2,1)S(1)} %constant_dynamic-update-slice_fusion.refs_6_), channel_id=1, source_target_pairs={{0,1},{1,0},{2,3},{3,2},{4,5},{5,4},{6,7},{7,6},{8,9},{9,8},{10,11... | collective-permute-start | bytes 3145736 | tf_op jit(solution)/shard_map/ppermute | solution.py:775
  95.0 8.3 %collective-permute-start.7 = (bf16[256,256]{1,0:T(8,128)(2,1)S(1)}, bf16[256,256]{1,0:T(8,128)(2,1)S(1)}, u32[]{:S(2)}, u32[]{:S(2)}) collective-permute-start(bf16[256,256]{1,0:T(8,128)(2,1)S(1)} %copy-done.28), channel_id=1, source_target_pairs={{0,16},{8,24},{16,0},{24,8},{1,17},{9,25},{17,1},{25,9},{2,18},{10... | collective-permute-start | bytes 393224 | tf_op jit(solution)/shard_map/ppermute | solution.py:771
  137.7 23.9 %collective-permute-start.18 = (bf16[7,256,1024]{2,1,0:T(8,128)(2,1)}, bf16[7,256,1024]{2,1,0:T(8,128)(2,1)S(1)}, u32[]{:S(2)}, u32[]{:S(2)}) collective-permute-start(bf16[7,256,1024]{2,1,0:T(8,128)(2,1)} %get-tuple-element.146.gm.ho.lo), channel_id=1, source_target_pairs={{0,1},{1,0},{2,3},{3,2},{4,5},{5,4},{6,7},{7,6},{8,9},{9,8},{10,11... | collective-permute-start | bytes 11010056 | tf_op jit(solution)/shard_map/ppermute | solution.py:775
  155.9 15.3 %collective-permute-start.19 = (bf16[5,256,1024]{2,1,0:T(8,128)(2,1)}, bf16[5,256,1024]{2,1,0:T(8,128)(2,1)}, u32[]{:S(2)}, u32[]{:S(2)}) collective-permute-start(bf16[5,256,1024]{2,1,0:T(8,128)(2,1)} %get-tuple-element.162.go), channel_id=1, source_target_pairs={{0,1},{1,0},{2,3},{3,2},{4,5},{5,4},{6,7},{7,6},{8,9},{9,8},{10,11... | collective-permute-start | bytes 7864328 | tf_op jit(solution)/shard_map/ppermute | solution.py:775
  156.2 25.3 %collective-permute-start.15 = (bf16[256,256]{1,0:T(8,128)(2,1)}, bf16[256,256]{1,0:T(8,128)(2,1)S(1)}, u32[]{:S(2)}, u32[]{:S(2)}) collective-permute-start(bf16[256,256]{1,0:T(8,128)(2,1)} %get-tuple-element.158), channel_id=1, source_target_pairs={{0,8},{8,16},{16,24},{24,0},{1,9},{9,17},{17,25},{25,1},{2,10},{10... | collective-permute-start | bytes 393224 | tf_op jit(solution)/shard_map/ppermute | solution.py:771
  157.7 23.9 %collective-permute-start.16 = (bf16[256,256]{1,0:T(8,128)(2,1)}, bf16[256,256]{1,0:T(8,128)(2,1)S(1)}, u32[]{:S(2)}, u32[]{:S(2)}) collective-permute-start(bf16[256,256]{1,0:T(8,128)(2,1)} %get-tuple-element.159), channel_id=1, source_target_pairs={{0,16},{8,24},{16,0},{24,8},{1,17},{9,25},{17,1},{25,9},{2,18},{10... | collective-permute-start | bytes 393224 | tf_op jit(solution)/shard_map/ppermute | solution.py:771
  160.1 21.5 %collective-permute-start.17 = (bf16[256,256]{1,0:T(8,128)(2,1)}, bf16[256,256]{1,0:T(8,128)(2,1)S(1)}, u32[]{:S(2)}, u32[]{:S(2)}) collective-permute-start(bf16[256,256]{1,0:T(8,128)(2,1)} %get-tuple-element.160), channel_id=1, source_target_pairs={{0,24},{8,0},{16,8},{24,16},{1,25},{9,1},{17,9},{25,17},{2,26},{10... | collective-permute-start | bytes 393224 | tf_op jit(solution)/shard_map/ppermute | solution.py:771
  181.6 48.2 %collective-permute-start.21 = (bf16[640,1024]{1,0:T(8,128)(2,1)}, bf16[640,1024]{1,0:T(8,128)(2,1)S(1)}, u32[]{:S(2)}, u32[]{:S(2)}) collective-permute-start(bf16[640,1024]{1,0:T(8,128)(2,1)} %get-tuple-element.179), channel_id=1, source_target_pairs={{0,4},{1,5},{2,6},{3,7},{4,0},{5,1},{6,2},{7,3},{8,12},{9,13},{10,... | collective-permute-start | bytes 3932168 | tf_op jit(solution)/shard_map/ppermute | solution.py:775
  182.8 33.9 %collective-permute-start.22 = (bf16[512,1024]{1,0:T(8,128)(2,1)}, bf16[512,1024]{1,0:T(8,128)(2,1)}, u32[]{:S(2)}, u32[]{:S(2)}) collective-permute-start(bf16[512,1024]{1,0:T(8,128)(2,1)} %get-tuple-element.180), channel_id=1, source_target_pairs={{0,2},{1,3},{2,0},{3,1},{4,6},{5,7},{6,4},{7,5},{8,10},{9,11},{10,... | collective-permute-start | bytes 3145736 | tf_op jit(solution)/shard_map/ppermute | solution.py:775
  183.7 46.1 %collective-permute-start.20 = (bf16[512,1024]{1,0:T(8,128)(2,1)}, bf16[512,1024]{1,0:T(8,128)(2,1)}, u32[]{:S(2)}, u32[]{:S(2)}) collective-permute-start(bf16[512,1024]{1,0:T(8,128)(2,1)} %get-tuple-element.178), channel_id=1, source_target_pairs={{0,2},{1,3},{2,0},{3,1},{4,6},{5,7},{6,4},{7,5},{8,10},{9,11},{10,... | collective-permute-start | bytes 3145736 | tf_op jit(solution)/shard_map/ppermute | solution.py:775
  229.8 88.3 %reduce-scatter.5.cloned.1.call-start = ((), (), s32[]{:S(2)}) async-start(), calls=%async_computation.3 | async-start | bytes 2064384 | tf_op jit(solution)/shard_map/reduce_scatter | solution.py:916
  229.8 38.9 %collective-permute-start.24 = (bf16[640,1024]{1,0:T(8,128)(2,1)}, bf16[640,1024]{1,0:T(8,128)(2,1)S(1)}, u32[]{:S(2)}, u32[]{:S(2)}) collective-permute-start(bf16[640,1024]{1,0:T(8,128)(2,1)} %get-tuple-element.193), channel_id=1, source_target_pairs={{0,4},{1,5},{2,6},{3,7},{4,0},{5,1},{6,2},{7,3},{8,12},{9,13},{10,... | collective-permute-start | bytes 3932168 | tf_op jit(solution)/shard_map/ppermute | solution.py:775
  232.3 35.1 %collective-permute-start.23 = (bf16[192,1024]{1,0:T(8,128)(2,1)S(1)}, bf16[192,1024]{1,0:T(8,128)(2,1)S(1)}, u32[]{:S(2)}, u32[]{:S(2)}) collective-permute-start(bf16[192,1024]{1,0:T(8,128)(2,1)S(1)} %add_convert_fusion.11), channel_id=1, source_target_pairs={{0,4},{1,5},{2,6},{3,7},{4,0},{5,1},{6,2},{7,3},{8,12},{9,13},{10,... | collective-permute-start | bytes 1179656 | tf_op jit(solution)/shard_map/ppermute | solution.py:775
  233.5 35.3 %collective-permute-start.25 = (bf16[256,1024]{1,0:T(8,128)(2,1)S(1)}, bf16[256,1024]{1,0:T(8,128)(2,1)S(1)}, u32[]{:S(2)}, u32[]{:S(2)}) collective-permute-start(bf16[256,1024]{1,0:T(8,128)(2,1)S(1)} %add_convert_fusion.7), channel_id=1, source_target_pairs={{0,2},{1,3},{2,0},{3,1},{4,6},{5,7},{6,4},{7,5},{8,10},{9,11},{10,... | collective-permute-start | bytes 1572872 | tf_op jit(solution)/shard_map/ppermute | solution.py:775
  271.5 21.0 %collective-permute-start.28 = (bf16[448,1024]{1,0:T(8,128)(2,1)S(1)}, bf16[448,1024]{1,0:T(8,128)(2,1)S(1)}, u32[]{:S(2)}, u32[]{:S(2)}) collective-permute-start(bf16[448,1024]{1,0:T(8,128)(2,1)S(1)} %pad_maximum_fusion.2), channel_id=1, source_target_pairs={{0,8},{24,16},{1,9},{25,17},{2,10},{26,18},{3,11},{27,19},{4,12},{... | collective-permute-start | bytes 2752520 | tf_op jit(solution)/shard_map/ppermute | solution.py:786
  275.2 7.0 %collective-permute-start.27 = (bf16[128,1024]{1,0:T(8,128)(2,1)S(1)}, bf16[128,1024]{1,0:T(8,128)(2,1)S(1)}, u32[]{:S(2)}, u32[]{:S(2)}) collective-permute-start(bf16[128,1024]{1,0:T(8,128)(2,1)S(1)} %get-tuple-element.196), channel_id=1, source_target_pairs={{0,2},{1,3},{2,0},{3,1},{4,6},{5,7},{6,4},{7,5},{8,10},{9,11},{10,... | collective-permute-start | bytes 786440 | tf_op jit(solution)/shard_map/ppermute | solution.py:775
  292.9 13.2 %collective-permute-start.29 = (bf16[128,1024]{1,0:T(8,128)(2,1)S(1)}, bf16[128,1024]{1,0:T(8,128)(2,1)S(1)}, u32[]{:S(2)}, u32[]{:S(2)}) collective-permute-start(bf16[128,1024]{1,0:T(8,128)(2,1)S(1)} %copy-done.14), channel_id=1, source_target_pairs={{0,4},{1,5},{2,6},{3,7},{4,0},{5,1},{6,2},{7,3},{8,12},{9,13},{10,... | collective-permute-start | bytes 786440 | tf_op jit(solution)/shard_map/ppermute | solution.py:775
  294.4 12.8 %collective-permute-start.30 = (bf16[128,1024]{1,0:T(8,128)(2,1)S(1)}, bf16[128,1024]{1,0:T(8,128)(2,1)S(1)}, u32[]{:S(2)}, u32[]{:S(2)}) collective-permute-start(bf16[128,1024]{1,0:T(8,128)(2,1)S(1)} %get-tuple-element.199), channel_id=1, source_target_pairs={{0,2},{1,3},{2,0},{3,1},{4,6},{5,7},{6,4},{7,5},{8,10},{9,11},{10,... | collective-permute-start | bytes 786440 | tf_op jit(solution)/shard_map/ppermute | solution.py:775
  295.9 19.9 %collective-permute-start.31 = (bf16[448,1024]{1,0:T(8,128)(2,1)S(1)}, bf16[448,1024]{1,0:T(8,128)(2,1)S(1)}, u32[]{:S(2)}, u32[]{:S(2)}) collective-permute-start(bf16[448,1024]{1,0:T(8,128)(2,1)S(1)} %add_convert_fusion.1), channel_id=1, source_target_pairs={{8,16},{16,8},{9,17},{17,9},{10,18},{18,10},{11,19},{19,11},{12,20... | collective-permute-start | bytes 2752520 | tf_op jit(solution)/shard_map/ppermute | solution.py:790
  297.6 18.0 %collective-permute-start.32 = (bf16[256,1024]{1,0:T(8,128)(2,1)S(1)}, bf16[256,1024]{1,0:T(8,128)(2,1)S(1)}, u32[]{:S(2)}, u32[]{:S(2)}) collective-permute-start(bf16[256,1024]{1,0:T(8,128)(2,1)S(1)} %pad_maximum_fusion.3), channel_id=1, source_target_pairs={{0,8},{24,16},{1,9},{25,17},{2,10},{26,18},{3,11},{27,19},{4,12},{... | collective-permute-start | bytes 1572872 | tf_op jit(solution)/shard_map/ppermute | solution.py:786
  318.1 12.4 %collective-permute-start.33 = (bf16[64,1024]{1,0:T(8,128)(2,1)S(1)}, bf16[64,1024]{1,0:T(8,128)(2,1)S(1)}, u32[]{:S(2)}, u32[]{:S(2)}) collective-permute-start(bf16[64,1024]{1,0:T(8,128)(2,1)S(1)} %add_convert_fusion.23), channel_id=1, source_target_pairs={{0,4},{1,5},{2,6},{3,7},{4,0},{5,1},{6,2},{7,3},{8,12},{9,13},{10,... | collective-permute-start | bytes 393224 | tf_op jit(solution)/shard_map/ppermute | solution.py:775
  319.5 12.0 %collective-permute-start.34 = (bf16[128,1024]{1,0:T(8,128)(2,1)S(1)}, bf16[128,1024]{1,0:T(8,128)(2,1)S(1)}, u32[]{:S(2)}, u32[]{:S(2)}) collective-permute-start(bf16[128,1024]{1,0:T(8,128)(2,1)S(1)} %get-tuple-element.203), channel_id=1, source_target_pairs={{0,2},{1,3},{2,0},{3,1},{4,6},{5,7},{6,4},{7,5},{8,10},{9,11},{10,... | collective-permute-start | bytes 786440 | tf_op jit(solution)/shard_map/ppermute | solution.py:775
  320.1 12.7 %collective-permute-start.35 = (bf16[256,1024]{1,0:T(8,128)(2,1)S(1)}, bf16[256,1024]{1,0:T(8,128)(2,1)S(1)}, u32[]{:S(2)}, u32[]{:S(2)}) collective-permute-start(bf16[256,1024]{1,0:T(8,128)(2,1)S(1)} %add_convert_fusion.5), channel_id=1, source_target_pairs={{8,16},{16,8},{9,17},{17,9},{10,18},{18,10},{11,19},{19,11},{12,20... | collective-permute-start | bytes 1572872 | tf_op jit(solution)/shard_map/ppermute | solution.py:790
  320.8 16.4 %collective-permute-start.36 = (bf16[256,1024]{1,0:T(8,128)(2,1)S(1)}, bf16[256,1024]{1,0:T(8,128)(2,1)S(1)}, u32[]{:S(2)}, u32[]{:S(2)}) collective-permute-start(bf16[256,1024]{1,0:T(8,128)(2,1)S(1)} %pad_maximum_fusion.4), channel_id=1, source_target_pairs={{0,8},{24,16},{1,9},{25,17},{2,10},{26,18},{3,11},{27,19},{4,12},{... | collective-permute-start | bytes 1572872 | tf_op jit(solution)/shard_map/ppermute | solution.py:786
  329.2 25.2 %collective-permute-start.44 = (bf16[448,1024]{1,0:T(8,128)(2,1)S(1)}, bf16[448,1024]{1,0:T(8,128)(2,1)S(1)}, u32[]{:S(2)}, u32[]{:S(2)}) collective-permute-start(bf16[448,1024]{1,0:T(8,128)(2,1)S(1)} %add_convert_fusion), channel_id=1, source_target_pairs={{8,0},{16,24},{9,1},{17,25},{10,2},{18,26},{11,3},{19,27},{12,4},{... | collective-permute-start | bytes 2752520 | tf_op jit(solution)/shard_map/ppermute | solution.py:794
  337.4 17.2 %collective-permute-start.38 = (bf16[192,1024]{1,0:T(8,128)(2,1)S(1)}, bf16[192,1024]{1,0:T(8,128)(2,1)S(1)}, u32[]{:S(2)}, u32[]{:S(2)}) collective-permute-start(bf16[192,1024]{1,0:T(8,128)(2,1)S(1)} %pad_maximum_fusion.5), channel_id=1, source_target_pairs={{0,8},{24,16},{1,9},{25,17},{2,10},{26,18},{3,11},{27,19},{4,12},{... | collective-permute-start | bytes 1179656 | tf_op jit(solution)/shard_map/ppermute | solution.py:786
  342.9 12.9 %collective-permute-start.37 = (bf16[256,1024]{1,0:T(8,128)(2,1)S(1)}, bf16[256,1024]{1,0:T(8,128)(2,1)S(1)}, u32[]{:S(2)}, u32[]{:S(2)}) collective-permute-start(bf16[256,1024]{1,0:T(8,128)(2,1)S(1)} %add_convert_fusion.3), channel_id=1, source_target_pairs={{8,16},{16,8},{9,17},{17,9},{10,18},{18,10},{11,19},{19,11},{12,20... | collective-permute-start | bytes 1572872 | tf_op jit(solution)/shard_map/ppermute | solution.py:790
  343.6 29.4 %collective-permute-start.45 = (bf16[256,1024]{1,0:T(8,128)(2,1)S(1)}, bf16[256,1024]{1,0:T(8,128)(2,1)S(1)}, u32[]{:S(2)}, u32[]{:S(2)}) collective-permute-start(bf16[256,1024]{1,0:T(8,128)(2,1)S(1)} %add_convert_fusion.4), channel_id=1, source_target_pairs={{8,0},{16,24},{9,1},{17,25},{10,2},{18,26},{11,3},{19,27},{12,4},{... | collective-permute-start | bytes 1572872 | tf_op jit(solution)/shard_map/ppermute | solution.py:794
  356.0 24.4 %collective-permute-start.41 = (bf16[128,896]{1,0:T(8,128)(2,1)S(1)}, bf16[128,896]{1,0:T(8,128)(2,1)S(1)}, u32[]{:S(2)}, u32[]{:S(2)}) collective-permute-start(bf16[128,896]{1,0:T(8,128)(2,1)S(1)} %copy-done.16), channel_id=1, source_target_pairs={{0,24},{8,0},{16,8},{24,16},{1,25},{9,1},{17,9},{25,17},{2,26},{10... | collective-permute-start | bytes 688136 | tf_op jit(solution)/shard_map/ppermute | solution.py:771
  359.7 20.7 %collective-permute-start.40 = (bf16[128,896]{1,0:T(8,128)(2,1)S(1)}, bf16[128,896]{1,0:T(8,128)(2,1)S(1)}, u32[]{:S(2)}, u32[]{:S(2)}) collective-permute-start(bf16[128,896]{1,0:T(8,128)(2,1)S(1)} %copy-done.16), channel_id=1, source_target_pairs={{0,16},{8,24},{16,0},{24,8},{1,17},{9,25},{17,1},{25,9},{2,18},{10... | collective-permute-start | bytes 688136 | tf_op jit(solution)/shard_map/ppermute | solution.py:771
  362.7 17.7 %collective-permute-start.39 = (bf16[128,896]{1,0:T(8,128)(2,1)S(1)}, bf16[128,896]{1,0:T(8,128)(2,1)S(1)}, u32[]{:S(2)}, u32[]{:S(2)}) collective-permute-start(bf16[128,896]{1,0:T(8,128)(2,1)S(1)} %copy-done.16), channel_id=1, source_target_pairs={{0,8},{8,16},{16,24},{24,0},{1,9},{9,17},{17,25},{25,1},{2,10},{10... | collective-permute-start | bytes 688136 | tf_op jit(solution)/shard_map/ppermute | solution.py:771
  363.0 22.8 %collective-permute-start.42 = (bf16[192,1024]{1,0:T(8,128)(2,1)S(1)}, bf16[192,1024]{1,0:T(8,128)(2,1)}, u32[]{:S(2)}, u32[]{:S(2)}) collective-permute-start(bf16[192,1024]{1,0:T(8,128)(2,1)S(1)} %add_convert_fusion.9), channel_id=1, source_target_pairs={{8,16},{16,8},{9,17},{17,9},{10,18},{18,10},{11,19},{19,11},{12,20... | collective-permute-start | bytes 1179656 | tf_op jit(solution)/shard_map/ppermute | solution.py:790
  373.0 18.3 %collective-permute-start.46 = (bf16[256,1024]{1,0:T(8,128)(2,1)S(1)}, bf16[256,1024]{1,0:T(8,128)(2,1)}, u32[]{:S(2)}, u32[]{:S(2)}) collective-permute-start(bf16[256,1024]{1,0:T(8,128)(2,1)S(1)} %add_convert_fusion.2), channel_id=1, source_target_pairs={{8,0},{16,24},{9,1},{17,25},{10,2},{18,26},{11,3},{19,27},{12,4},{... | collective-permute-start | bytes 1572872 | tf_op jit(solution)/shard_map/ppermute | solution.py:794
  386.9 9.7 %collective-permute-start.43 = (bf16[192,1024]{1,0:T(8,128)(2,1)S(1)}, bf16[192,1024]{1,0:T(8,128)(2,1)S(1)}, u32[]{:S(2)}, u32[]{:S(2)}) collective-permute-start(bf16[192,1024]{1,0:T(8,128)(2,1)S(1)} %add_convert_fusion.8), channel_id=1, source_target_pairs={{8,0},{16,24},{9,1},{17,25},{10,2},{18,26},{11,3},{19,27},{12,4},{... | collective-permute-start | bytes 1179656 | tf_op jit(solution)/shard_map/ppermute | solution.py:794
  (34 other events, 316.2 us)
Sparse Core Ops, SparseCore 0:
  11.8 49.5 all-gather.4
  63.3 55.9 all-gather.6
  229.9 41.4 reduce-scatter.2
  275.0 43.0 reduce-scatter.4

commit v3 on v2

v3 whole, which is shorter than its diff:
```python
from functools import partial

import jax
import jax.numpy as jnp
from jax import lax
from jax.experimental import pallas as pl
from jax.experimental.pallas import tpu as pltpu
from jax.sharding import PartitionSpec as P

HEADS = 16
HEAD_DIM = 64
SEGS = 8
EPSILON = 1e-05
MASKED = -1000000000.0
SCALE = HEAD_DIM ** (-0.5)
BF = jnp.bfloat16
F32 = jnp.float32

CHUNK = 256
HERE = 4
WIDE = HERE * HEAD_DIM
SHARDS = 8
ROWS = 128
PACK = 2 * ROWS + 16
PARAMS = pltpu.CompilerParams(vmem_limit_bytes=60 * 1024 * 1024)


SMEM_SPEC = pl.BlockSpec(memory_space=pltpu.SMEM)
VMEM_SPEC = pl.BlockSpec(memory_space=pltpu.VMEM)


def dot(a, b, dims=((1,), (0,))):
    return lax.dot_general(a, b, (dims, ((), ())), preferred_element_type=F32)


def vec(small_ref, row, start, size):
    return jnp.concatenate(
        [small_ref[f, row : row + 1, start : start + size].astype(F32) for f in range(SHARDS)],
        axis=1,
    )


def any_spec(shape):
    return pl.BlockSpec(shape, lambda *a: (0,) * len(shape))


def pack_kernel(sc, tok, seg, wq, wk, wv, wout, qb, vb, ob, ag, sh, db, mg, ms, ub, xp, pk):
    z = sc[0]
    cols = pl.ds(pl.multiple_of(z * WIDE, WIDE), WIDE)
    xp[0:CHUNK] = tok[...]
    xp[CHUNK:] = jnp.zeros((16, 1024), BF)
    xp[CHUNK : CHUNK + 1, 0:CHUNK] = seg[...].astype(F32).astype(BF)
    pk[0:ROWS] = wout[...]
    for n, w in enumerate((wq, wk, wv)):
        pk[ROWS : 2 * ROWS, WIDE * n : WIDE * n + WIDE] = w[:, cols]
    pk[ROWS : 2 * ROWS, 3 * WIDE :] = jnp.zeros((ROWS, 1024 - 3 * WIDE), BF)
    pk[2 * ROWS :] = jnp.zeros((16, 1024), BF)
    at = slice(2 * ROWS, 2 * ROWS + 1)
    for n, vector in enumerate((qb, vb, ob, ag, sh, db)):
        pk[at, 128 * n : 128 * n + 128] = vector[...]
    at = slice(2 * ROWS + 1, 2 * ROWS + 2)
    for n, vector in enumerate((mg, ms)):
        pk[at, 128 * n : 128 * n + 128] = vector[...]
    pk[at, 256:768] = ub[...]


def pack_inputs(scalars, tok, seg, weights, vectors):
    shape = jax.ShapeDtypeStruct
    return pl.pallas_call(
        pack_kernel,
        name="pack_inputs",
        in_specs=[SMEM_SPEC] + [VMEM_SPEC] * 15,
        out_specs=(VMEM_SPEC,) * 2,
        out_shape=(shape((CHUNK + 16, 1024), BF), shape((PACK, 1024), BF)),
        compiler_params=PARAMS,
    )(scalars, tok, seg, *weights, *[v[None] for v in vectors])


def segment_setup(rows, segc, ends):
    for a in range(4):
        row = rows[a][0:1, :]
        segc[a] = jnp.transpose(jnp.broadcast_to(row, (128, CHUNK)))
        ends[0, a] = jnp.min(row).astype(jnp.int32)
        ends[1, a] = jnp.max(row).astype(jnp.int32)


def key_range(ends, i):
    low = jnp.int32(0)
    high = jnp.int32(4)
    for j in range(4):
        low = low + (ends[1, j] < ends[0, i]).astype(jnp.int32)
        high = high - (ends[0, j] > ends[1, i]).astype(jnp.int32)
    return low, high


def one_head(x, h):
    pair = x[:, 128 * (h // 2) : 128 * (h // 2) + 128]
    lane = lax.broadcasted_iota(jnp.int32, pair.shape, 1)
    return jnp.where((lane < HEAD_DIM) == (h % 2 == 0), pair, jnp.zeros_like(pair))


def attn_fwd_kernel(
    sc,
    x0,
    right,
    left,
    x2,
    far,
    w,
    small,
    m0,
    m1,
    m2,
    m3,
    mixt,
    lse,
    qm,
    kv,
    kt,
    xall,
    segr,
    vt,
    acc,
    scores,
    probs,
    segc,
    ends,
):
    z = sc[0]

    def place(k, src):
        a = lax.rem(z - k + 4, 4)
        xall[a] = src[0:CHUNK, :]
        segr[a] = jnp.broadcast_to(
            src[CHUNK : CHUNK + 16, 0:CHUNK].astype(F32)[0:1, :], (8, CHUNK)
        )

    place(0, x0)
    place(2, x2)
    for k, usual, end in ((1, right, 0), (3, left, 3)):
        pl.when(z == end)(partial(place, k, far))
        pl.when(z != end)(partial(place, k, usual))
    segment_setup(segr, segc, ends)
    weight = w[...].reshape(SHARDS * ROWS, 3 * WIDE)
    first = small[2 * z].astype(F32)
    second = small[2 * z + 1].astype(F32)
    qb = jnp.concatenate([first[0:1, 0:128], second[0:1, 0:128]], axis=1)
    vb = jnp.concatenate([first[0:1, 128:256], second[0:1, 128:256]], axis=1)
    for n in range(4):
        at = slice(n * CHUNK, (n + 1) * CHUNK)
        prod = dot(xall[n], weight)
        q = ((prod[:, 0:WIDE] + qb).astype(BF).astype(F32) * SCALE).astype(BF)
        kk = prod[:, WIDE : 2 * WIDE].astype(BF)
        v = (prod[:, 2 * WIDE :] + vb).astype(BF)
        for h in range(HERE):
            qm[h, at, :] = one_head(q, h)
        kv[at, 0:WIDE] = kk
        kv[at, WIDE:] = v
        kt[:, at] = jnp.transpose(kk)
        vt[:, at] = jnp.transpose(v)

    def q_chunk(i, carry):
        rows = pl.ds(pl.multiple_of(i * CHUNK, CHUNK), CHUNK)
        low, high = key_range(ends, i)
        row = segr[i][0:1, :]

        acc[...] = jnp.zeros_like(acc)

        def key_chunk(j, state):
            keys = pl.ds(pl.multiple_of(j * CHUNK, CHUNK), CHUNK)
            col = segc[j]
            mask = jnp.concatenate([col, col], axis=1) == row
            new, fixes = [], []
            for h in range(HERE):
                pair = slice(128 * (h // 2), 128 * (h // 2) + 128)
                s = dot(kv[keys, pair], qm[h, rows, :], ((1,), (1,)))
                s = jnp.where(mask, s, MASKED)
                scores[h] = s
                new.append(jnp.maximum(state[h][0], jnp.max(s, axis=0, keepdims=True)))
            out = []
            for h in range(HERE):
                m, l = state[h]
                total = jnp.zeros((1, CHUNK), F32)
                for t in range(4):
                    tile = slice(64 * t, 64 * t + 64)
                    p = jnp.exp(scores[h, tile, :] - new[h])
                    total = total + jnp.sum(p, axis=0, keepdims=True)
                    probs[h, tile, :] = p.astype(BF)
                fixes.append(jnp.exp(m - new[h]))
                out.append((new[h], l * fixes[h] + total))
            for h in range(HERE):
                head = slice(h * HEAD_DIM, (h + 1) * HEAD_DIM)
                acc[head, :] = acc[head, :] * fixes[h] + dot(vt[head, keys], probs[h])
            return tuple(out)

        init = tuple(
            (jnp.full((1, CHUNK), MASKED, F32), jnp.zeros((1, CHUNK), F32)) for _ in range(HERE)
        )
        state = lax.fori_loop(low, high, key_chunk, init)
        for h in range(HERE):
            m, l = state[h]
            head = slice(h * HEAD_DIM, (h + 1) * HEAD_DIM)
            mixt[head, rows] = acc[head, :] / l
            lse[h : h + 1, rows] = m + jnp.log(l)
        return carry

    lax.fori_loop(0, 4, q_chunk, 0)
    for k, out in enumerate((m0, m1, m2, m3)):
        a = pl.multiple_of(lax.rem(z - k + 4, 4) * CHUNK, CHUNK)
        out[...] = jnp.transpose(mixt[:, pl.ds(a, CHUNK)].astype(BF))


OUT_SPEC = pl.BlockSpec((SHARDS, ROWS, 1024), lambda *a: (0, 0, 0))
QKV_SPEC = pl.BlockSpec((SHARDS, ROWS, 3 * WIDE), lambda *a: (0, 1, 0))
SMALL_SPEC = pl.BlockSpec((SHARDS, 16, 3 * WIDE), lambda *a: (0, 2 * ROWS // 16, 0))


def attn_fwd(scalars, xs, pack):
    shape = jax.ShapeDtypeStruct
    return pl.pallas_call(
        attn_fwd_kernel,
        name="attn_fwd",
        out_shape=(shape((CHUNK, WIDE), BF),) * 4
        + (
            shape((WIDE, 4 * CHUNK), F32),
            shape((8, 4 * CHUNK), F32),
            shape((HERE, 4 * CHUNK, 128), BF),
            shape((4 * CHUNK, 2 * WIDE), BF),
            shape((WIDE, 4 * CHUNK), BF),
            shape((4, CHUNK, 1024), BF),
            shape((4, 8, CHUNK), F32),
        ),
        grid=(1,),
        in_specs=[SMEM_SPEC] + [any_spec((CHUNK + 16, 1024))] * 5 + [QKV_SPEC, SMALL_SPEC],
        out_specs=(any_spec((CHUNK, WIDE)),) * 4
        + (
            any_spec((WIDE, 4 * CHUNK)),
            any_spec((8, 4 * CHUNK)),
            any_spec((HERE, 4 * CHUNK, 128)),
            any_spec((4 * CHUNK, 2 * WIDE)),
            any_spec((WIDE, 4 * CHUNK)),
            any_spec((4, CHUNK, 1024)),
            any_spec((4, 8, CHUNK)),
        ),
        scratch_shapes=[
            pltpu.VMEM((WIDE, 4 * CHUNK), BF),
            pltpu.VMEM((WIDE, CHUNK), F32),
            pltpu.VMEM((HERE, CHUNK, CHUNK), F32),
            pltpu.VMEM((HERE, CHUNK, CHUNK), BF),
            pltpu.VMEM((4, CHUNK, 128), F32),
            pltpu.SMEM((2, 4), jnp.int32),
        ],
        compiler_params=PARAMS,
    )(scalars, *xs, pack, pack)


def normalise(h):
    centre = h - jnp.mean(h, axis=-1, keepdims=True)
    inverse = lax.rsqrt(jnp.mean(centre * centre, axis=-1, keepdims=True) + EPSILON)
    return centre * inverse, inverse


def norm_pullback(upstream, scaled, inverse, gain):
    e = upstream * gain
    return inverse * (
        e
        - jnp.mean(e, axis=-1, keepdims=True)
        - scaled * jnp.mean(e * scaled, axis=-1, keepdims=True)
    )


def relative(f, sc):
    return 2 * jnp.bitwise_xor(sc[1], f // 2) + jnp.bitwise_xor(sc[2], f % 2)


TILE = 16


def eight(x):
    return jnp.sum(x.reshape(TILE // 8, 8, x.shape[1]), axis=0)


def out_kernel(
    sc, tok, r0, r1, r2, r3, w, small, valid, normed, low, low_rel, scaled, inv, mixed, stats, acc
):
    z = sc[0]
    for k, r in enumerate((r0, r1, r2, r3)):
        a = lax.rem(z + k, 4)
        mixed[:, pl.ds(pl.multiple_of(a * WIDE, WIDE), WIDE)] = r[...]
    acc[...] = dot(mixed[...], w[...].reshape(1024, 1024))
    bias, gain, shift_by = vec(small, 0, 256, 128), vec(small, 0, 384, 128), vec(small, 0, 512, 128)

    def tile(t, carry):
        rows = pl.ds(pl.multiple_of(t * TILE, TILE), TILE)
        branch = acc[rows, :] + bias
        x = tok[rows, :].astype(F32)
        n, inverse = normalise(x + branch)
        y = n * gain + shift_by
        normed[rows, :] = y
        low[rows, :] = y.astype(BF)
        scaled[rows, :] = n
        inv[rows, :] = jnp.broadcast_to(inverse, (TILE, 128))
        ok = valid[rows, :]
        return carry[0] + eight(ok * x * x), carry[1] + eight(ok * branch * branch)

    zero = jnp.zeros((8, 1024), F32)
    stream, branch = lax.fori_loop(0, CHUNK // TILE, tile, (zero, zero), unroll=4)
    for f in range(SHARDS):
        at = pl.multiple_of(relative(f, sc) * ROWS, ROWS)
        low_rel[:, pl.ds(at, ROWS)] = low[:, ROWS * f : ROWS * f + ROWS]
    lane = lax.broadcasted_iota(jnp.int32, (8, 128), 1)
    stats[...] = jnp.where(
        lane == 0,
        jnp.sum(stream),
        jnp.where(
            lane == 1, jnp.sum(branch), jnp.where(lane == 3, jnp.sum(valid[...]), 0.0)
        ),
    )


def out_project(scalars, tok, parts, pack, valid):
    shape = jax.ShapeDtypeStruct
    full = lambda *s: any_spec(s)
    return pl.pallas_call(
        out_kernel,
        name="out_project",
        grid=(1,),
        out_shape=(
            shape((CHUNK, 1024), F32),
            shape((CHUNK, 1024), BF),
            shape((CHUNK, 1024), BF),
            shape((CHUNK, 1024), F32),
            shape((CHUNK, 128), F32),
            shape((CHUNK, 1024), BF),
            shape((8, 128), F32),
        ),
        in_specs=[SMEM_SPEC, full(CHUNK, 1024)]
        + [full(CHUNK, WIDE)] * 4
        + [OUT_SPEC, SMALL_SPEC, full(CHUNK, 1)],
        out_specs=(
            full(CHUNK, 1024),
            full(CHUNK, 1024),
            full(CHUNK, 1024),
            full(CHUNK, 1024),
            full(CHUNK, 128),
            full(CHUNK, 1024),
            full(8, 128),
        ),
        scratch_shapes=[pltpu.VMEM((CHUNK, 1024), F32)],
        compiler_params=PARAMS,
    )(scalars, tok, *parts, pack, pack, valid)


UP_SPECS = [pl.BlockSpec((ROWS, 512), lambda j: (0, j))] * SHARDS


def gate_kernel(low, low_rel, mixed, *refs):
    ups = refs[0:SHARDS]
    small, acts, slope, pre = refs[SHARDS:]
    j = pl.program_id(0)
    pre[...] = dot(low_rel[...], jnp.concatenate([u[...] for u in ups]))
    bias = small[j, 1:2, 256:768].astype(F32)
    cols = pl.ds(pl.multiple_of((j % 2) * 512, 512), 512)
    for t in range(CHUNK // TILE):
        rows = slice(TILE * t, TILE * t + TILE)
        gate = pre[rows, :] + bias
        cdf = 0.5 * (1.0 + lax.erf(gate * (2.0 ** -0.5)))
        acts[j // 2, rows, cols] = (gate * cdf).astype(BF)
        slope[rows, :] = cdf + gate * (jnp.exp(-0.5 * gate * gate) * 0.3989422804014327)

    @pl.when(j == 0)
    def _():
        acts[4] = low[...]
        acts[5] = mixed[...]


def mlp_gate(low, low_rel, mixed, ups, pack):
    shape = jax.ShapeDtypeStruct
    full = lambda *s: any_spec(s)
    return pl.pallas_call(
        gate_kernel,
        name="mlp_gate",
        grid=(SHARDS,),
        out_shape=(shape((6, CHUNK, 1024), BF), shape((CHUNK, 4096), F32)),
        in_specs=[full(CHUNK, 1024)] * 3 + UP_SPECS + [SMALL_SPEC],
        out_specs=(full(6, CHUNK, 1024), pl.BlockSpec((CHUNK, 512), lambda j: (0, j))),
        scratch_shapes=[pltpu.VMEM((CHUNK, 512), F32)],
        compiler_params=PARAMS,
    )(low, low_rel, mixed, *ups, pack)


def mlp_tail_kernel(sc, acts, down_cols, down_rows, slope, small, valid, inv, *refs):
    far = refs[0 : SHARDS + 4]
    (
        out,
        grads,
        gh1,
        g0,
        g1,
        g2,
        g3,
        sums_m,
        stats,
        sums_a,
        ub,
        acc,
        gh2,
        gm,
        gg_all,
        pre,
        total,
        held,
        normed,
        cot,
        scaled,
        wout,
        sems,
    ) = refs[SHARDS + 4 :]
    s = pl.program_id(0)
    z = sc[0]
    targets = [normed, cot, scaled, wout] + [held.at[n] for n in range(SHARDS)]
    sources = [far[0], far[1], far[2], far[3].at[:, 0:ROWS, :]] + list(far[4:])
    copies = [
        pltpu.make_async_copy(src, dst, sems.at[n])
        for n, (src, dst) in enumerate(zip(sources, targets))
    ]
    zero = jnp.zeros((8, 1024), F32)

    def tiles(body, count):
        totals = lax.fori_loop(0, CHUNK // TILE, body, (zero,) * count, unroll=4)
        return [jnp.sum(t, axis=0, keepdims=True) for t in totals]

    @pl.when(s == 0)
    def _():
        for copy in copies:
            copy.start()

    @pl.when(s < 4)
    def _():
        hidden = jnp.concatenate([acts[b] for b in range(4)], axis=1)
        cols = pl.ds(pl.multiple_of(jnp.minimum(s, 3) * 256, 256), 256)
        acc[:, cols] = dot(hidden, down_cols[...].reshape(4096, 256))

    @pl.when(s == 3)
    def _():
        for copy in copies[0:2]:
            copy.wait()
        bias, gain, shift_by = vec(small, 0, 640, 128), vec(small, 1, 0, 128), vec(small, 1, 128, 128)

        def tile(t, carry):
            rows = pl.ds(pl.multiple_of(t * TILE, TILE), TILE)
            branch = acc[rows, :] + bias
            unit, inverse = normalise(normed[rows, :] + branch)
            out[rows, :] = (unit * gain + shift_by).astype(BF)
            ok = valid[rows, :]
            u = cot[rows, :].astype(F32) * ok
            g = norm_pullback(u, unit, inverse, gain)
            gh2[rows, :] = g
            g_low = g.astype(BF)
            gm[rows, :] = g_low
            terms = (u * unit, u, g_low.astype(F32), ok * branch * branch)
            return tuple(c + eight(v) for c, v in zip(carry, terms))

        totals = tiles(tile, 4)
        sums_m[...] = jnp.zeros_like(sums_m)
        for at in range(3):
            sums_m[at : at + 1, :] = totals[at]
        lane = lax.broadcasted_iota(jnp.int32, (8, 128), 1)
        stats[...] = jnp.where(lane == 2, jnp.sum(totals[3]), 0.0)

    @pl.when((s >= 4) & (s < 12))
    def _():
        j = jnp.clip(s - 4, 0, SHARDS - 1)
        pre[...] = dot(gm[...], down_rows[...].reshape(512, 1024), ((1,), (1,)))
        cols = pl.ds(pl.multiple_of((j % 2) * 512, 512), 512)
        total_ub = jnp.zeros((8, 512), F32)
        for t in range(CHUNK // TILE):
            rows = slice(TILE * t, TILE * t + TILE)
            gg = (pre[rows, :] * slope[rows, :]).astype(BF)
            gg_all[j // 2, rows, cols] = gg
            grads[0, rows, cols] = gg
            total_ub = total_ub + eight(gg.astype(F32))
        ub[pl.ds(j, 1)] = jnp.sum(total_ub, axis=0, keepdims=True).reshape(1, 1, 512)

    @pl.when(s == 12)
    def _():
        grads[0] = gm[...]
        for copy in copies[2:]:
            copy.wait()

    @pl.when(s >= 12)
    def _():
        j = jnp.clip(s - 12, 0, 3)
        rows = held[pl.ds(2 * j, 2)].reshape(2 * ROWS, 4096)
        gg = jnp.concatenate([gg_all[b] for b in range(4)], axis=1)
        part = dot(gg, rows, ((1,), (1,)))
        pair = jnp.bitwise_xor(sc[1], j)
        for t in range(2):
            f = 2 * pair + jnp.bitwise_xor(sc[2], t)
            to = pl.ds(pl.multiple_of(f * ROWS, ROWS), ROWS)
            total[:, to] = part[:, ROWS * t : ROWS * t + ROWS]

    @pl.when(s == 15)
    def _():
        gain = vec(small, 0, 384, 128)

        def tile(t, carry):
            rows = pl.ds(pl.multiple_of(t * TILE, TILE), TILE)
            u = gh2[rows, :] + total[rows, :]
            n = scaled[rows, :]
            g = norm_pullback(u, n, inv[rows, 0:1], gain)
            gh1[rows, :] = g
            g_low = g.astype(BF)
            grads[0, rows, :] = g_low
            terms = (u * n, u, g_low.astype(F32))
            return tuple(c + eight(v) for c, v in zip(carry, terms))

        totals = tiles(tile, 3)
        sums_a[...] = jnp.zeros_like(sums_a)
        for at in range(3):
            sums_a[at : at + 1, :] = totals[at]
        g_low = grads[0]
        for k, g_out in enumerate((g0, g1, g2, g3)):
            a = lax.rem(z + k, 4)
            rows = wout[pl.ds(2 * a, 2)].reshape(WIDE, 1024)
            g_out[...] = dot(g_low, rows, ((1,), (1,))).astype(BF)


def mlp_tail(scalars, acts, slope, ups, down, normed, scaled, inv, pack, cot, valid):
    shape = jax.ShapeDtypeStruct
    full = lambda *s: any_spec(s)
    block = lambda s: jnp.clip(s - 4, 0, SHARDS - 1)

    def grads_at(s):
        return (jnp.where(s < 12, block(s) // 2, jnp.where(s < 15, 5, 4)), 0, 0)

    return pl.pallas_call(
        mlp_tail_kernel,
        name="mlp_tail",
        grid=(16,),
        in_specs=[
            SMEM_SPEC,
            full(4, CHUNK, 1024),
            pl.BlockSpec((SHARDS, 512, 256), lambda s: (0, 0, jnp.minimum(s, 3))),
            pl.BlockSpec((1, 512, 1024), lambda s: (block(s), 0, 0)),
            pl.BlockSpec((CHUNK, 512), lambda s: (0, block(s))),
            SMALL_SPEC,
            full(CHUNK, 1),
            full(CHUNK, 128),
        ]
        + [pl.BlockSpec(memory_space=pl.ANY)] * (SHARDS + 4),
        out_specs=(
            full(CHUNK, 1024),
            pl.BlockSpec((1, CHUNK, 1024), grads_at),
            full(CHUNK, 1024),
        )
        + (full(CHUNK, WIDE),) * 4
        + (full(8, 1024), full(8, 128), full(8, 1024), full(SHARDS, 1, 512)),
        out_shape=(
            shape((CHUNK, 1024), BF),
            shape((6, CHUNK, 1024), BF),
            shape((CHUNK, 1024), F32),
        )
        + (shape((CHUNK, WIDE), BF),) * 4
        + (
            shape((8, 1024), F32),
            shape((8, 128), F32),
            shape((8, 1024), F32),
            shape((SHARDS, 1, 512), F32),
        ),
        scratch_shapes=[
            pltpu.VMEM((CHUNK, 1024), F32),
            pltpu.VMEM((CHUNK, 1024), F32),
            pltpu.VMEM((CHUNK, 1024), BF),
            pltpu.VMEM((4, CHUNK, 1024), BF),
            pltpu.VMEM((CHUNK, 512), F32),
            pltpu.VMEM((CHUNK, 1024), F32),
            pltpu.VMEM((SHARDS, ROWS, 4096), BF),
            pltpu.VMEM((CHUNK, 1024), F32),
            pltpu.VMEM((CHUNK, 1024), BF),
            pltpu.VMEM((CHUNK, 1024), F32),
            pltpu.VMEM((SHARDS, ROWS, 1024), BF),
            pltpu.SemaphoreType.DMA((SHARDS + 4,)),
        ],
        compiler_params=PARAMS,
    )(scalars, acts, down, down, slope, pack, valid, inv, normed, cot, scaled, pack, *ups)


REST = 640


def step_shard(j, sc):
    rel = jnp.where(j == 0, 3, jnp.where(j >= 3, 0, j))
    return 2 * jnp.bitwise_xor(sc[1], rel) + sc[2]


def product(left, right, res):
    for n in range(4):
        cols = slice(256 * n, 256 * n + 256)
        res[:, cols] = dot(left[...], right[:, cols]).astype(BF)


def down_kernel(sc, ho, hp, go, gp, d3, d1, d2, d0, left, right, res):
    s = pl.program_id(0)

    @pl.when(s == 0)
    def _():
        right[0:CHUNK] = go[0]
        right[CHUNK:] = gp[0]

    left[:, 0:CHUNK] = jnp.transpose(ho[0])
    left[:, CHUNK:] = jnp.transpose(hp[0])
    product(left, right, res)
    for n, out in enumerate((d3, d1, d2, d0)):

        @pl.when(s == n)
        def _():
            out[...] = res[...]


def down_grads(scalars, acts, acts_p, grads, grads_p):
    shape = jax.ShapeDtypeStruct
    full = lambda *s: pl.BlockSpec(s, lambda j, sc: (0,) * len(s))

    def hid(j, sc):
        f = step_shard(j, sc)
        return (f // 2, 0, f % 2)

    hidden = pl.BlockSpec((1, CHUNK, 512), hid)
    grad = pl.BlockSpec((1, CHUNK, 1024), lambda j, sc: (5, 0, 0))
    return pl.pallas_call(
        down_kernel,
        name="down_grads",
        grid_spec=pltpu.PrefetchScalarGridSpec(
            num_scalar_prefetch=1,
            grid=(4,),
            in_specs=[hidden, hidden, grad, grad],
            out_specs=(full(512, 1024),) * 4,
            scratch_shapes=[
                pltpu.VMEM((512, 2 * CHUNK), BF),
                pltpu.VMEM((2 * CHUNK, 1024), BF),
                pltpu.VMEM((512, 1024), BF),
            ],
        ),
        out_shape=(shape((512, 1024), BF),) * 4,
        compiler_params=PARAMS,
    )(scalars, acts, acts_p, grads, grads_p)


def rest_kernel(sc, lo, lp, go, gp, r3, r1, r2, r0, low_sel, mix_sel, right, res):
    s = pl.program_id(0)
    chip, core = sc[1], sc[2]

    @pl.when(s == 0)
    def _():
        for r in range(4):
            at = pl.multiple_of((2 * jnp.bitwise_xor(chip, r) + core) * ROWS, ROWS)
            to = slice(ROWS * r, ROWS * r + ROWS)
            for n, out in enumerate((low_sel, mix_sel)):
                out[to, 0:CHUNK] = jnp.transpose(lo[n, :, pl.ds(at, ROWS)])
                out[to, CHUNK:] = jnp.transpose(lp[n, :, pl.ds(at, ROWS)])

    @pl.when(s == 4)
    def _():
        low_sel[...] = mix_sel[...]

    right[0:CHUNK] = go[0]
    right[CHUNK:] = gp[0]
    product(low_sel, right, res)
    for r, out in enumerate((r0, r1, r2, r3)):
        out[...] = res[ROWS * r : ROWS * r + ROWS, :]


def rest_grads(scalars, acts, acts_p, grads, grads_p):
    shape = jax.ShapeDtypeStruct
    full = lambda *s: pl.BlockSpec(s, lambda j, sc: (0,) * len(s))
    flat = pl.BlockSpec((pl.Element(2), pl.Element(CHUNK), pl.Element(1024)), lambda j, sc: (4, 0, 0))
    grad = pl.BlockSpec((1, CHUNK, 1024), lambda j, sc: (j, 0, 0))
    return pl.pallas_call(
        rest_kernel,
        name="rest_grads",
        grid_spec=pltpu.PrefetchScalarGridSpec(
            num_scalar_prefetch=1,
            grid=(5,),
            in_specs=[flat, flat, grad, grad],
            out_specs=(pl.BlockSpec((ROWS, 1024), lambda j, sc: (j, 0)),) * 4,
            scratch_shapes=[
                pltpu.VMEM((512, 2 * CHUNK), BF),
                pltpu.VMEM((512, 2 * CHUNK), BF),
                pltpu.VMEM((2 * CHUNK, 1024), BF),
                pltpu.VMEM((512, 1024), BF),
            ],
        ),
        out_shape=(shape((REST, 1024), BF),) * 4,
        compiler_params=PARAMS,
    )(scalars, acts, acts_p, grads, grads_p)


def attn_bwd_kernel(
    sc,
    xall,
    segr,
    w,
    qm,
    kv,
    kt,
    mixt,
    lse,
    g0,
    g1,
    g2,
    g3,
    sums_m,
    sums_a,
    ubt,
    stats_a,
    stats_m,
    ig,
    gw_out,
    small,
    segc,
    ends,
    gs,
    dq,
    dqt,
    dk,
    dv,
    delta,
    dall,
    gw,
    scores,
    slopes,
    probs,
    pulls,
):
    z = sc[0]
    segment_setup(segr, segc, ends)
    dk[...] = jnp.zeros_like(dk)
    dv[...] = jnp.zeros_like(dv)
    for k, g in enumerate((g0, g1, g2, g3)):
        rows = pl.ds(pl.multiple_of(lax.rem(z - k + 4, 4) * CHUNK, CHUNK), CHUNK)
        turned = jnp.transpose(g[...])
        for h in range(HERE):
            head = slice(h * HEAD_DIM, (h + 1) * HEAD_DIM)
            gs[h, rows, :] = one_head(g[...], h)
            prod = turned[head, :].astype(F32) * mixt[head, rows]
            delta[h : h + 1, rows] = jnp.sum(prod, axis=0, keepdims=True)

    def q_chunk(i, carry):
        rows = pl.ds(pl.multiple_of(i * CHUNK, CHUNK), CHUNK)
        low, high = key_range(ends, i)
        row = segr[i][0:1, :]
        dqt[...] = jnp.zeros_like(dqt)

        def key_chunk(j, inner):
            keys = pl.ds(pl.multiple_of(j * CHUNK, CHUNK), CHUNK)
            col = segc[j]
            mask = jnp.concatenate([col, col], axis=1) == row
            for h in range(HERE):
                low_lane = 128 * (h // 2)
                pair = slice(low_lane, low_lane + 128)
                scores[h] = dot(kv[keys, pair], qm[h, rows, :], ((1,), (1,)))
                wide = slice(WIDE + low_lane, WIDE + low_lane + 128)
                slopes[h] = dot(kv[keys, wide], gs[h, rows, :], ((1,), (1,)))
            for h in range(HERE):
                log, shift_by = lse[h : h + 1, rows], delta[h : h + 1, rows]
                for t in range(4):
                    tile = slice(64 * t, 64 * t + 64)
                    p = jnp.where(mask[tile, :], jnp.exp(scores[h, tile, :] - log), 0.0)
                    probs[h, tile, :] = p.astype(BF)
                    pulls[h, tile, :] = (p * (slopes[h, tile, :] - shift_by)).astype(BF)
            for h in range(HERE):
                head = slice(h * HEAD_DIM, (h + 1) * HEAD_DIM)
                pair = slice(128 * (h // 2), 128 * (h // 2) + 128)
                dv[keys, pair] += dot(probs[h], gs[h, rows, :])
                dk[keys, pair] += dot(pulls[h], qm[h, rows, :])
                dqt[head, :] += dot(kt[head, keys], pulls[h])
            return inner

        lax.fori_loop(low, high, key_chunk, 0)
        dq[...] = (dqt[...] * SCALE).astype(BF)
        dall[rows, 0:WIDE] = jnp.transpose(dq[...])
        return carry

    lax.fori_loop(0, 4, q_chunk, 0)
    dall[:, WIDE : 2 * WIDE] = dk[...].astype(BF)
    dall[:, 2 * WIDE :] = dv[...].astype(BF)
    here = pl.ds(pl.multiple_of(z * WIDE, WIDE), WIDE)
    small[...] = jnp.zeros_like(small)
    small[0:3, :] = sums_m[0:3, :]
    small[3:6, :] = sums_a[0:3, :]
    small[6:7, here] = jnp.sum(dall[:, 0:WIDE].astype(F32), axis=0, keepdims=True)
    small[7:8, here] = jnp.sum(dall[:, 2 * WIDE :].astype(F32), axis=0, keepdims=True)
    small[8:12, :] = ubt[...]
    every = lambda value: jnp.broadcast_to(value, (1, 1024))
    small[12:13, :] = every(stats_a[0:1, 0:1])
    small[13:14, :] = every(stats_a[0:1, 1:2])
    small[14:15, :] = every(stats_m[0:1, 2:3])
    count = stats_a[0:1, 3:4]
    high = jnp.floor(count * 0.0625)
    small[15:16, :] = every(high)
    small[16:17, :] = every(count - 16.0 * high)
    gw_out[:, 3 * WIDE :] = jnp.transpose(small[...]).astype(BF)
    weight = w[...].reshape(SHARDS * ROWS, 3 * WIDE)
    for k in range(4):
        rows = slice(CHUNK * k, CHUNK * k + CHUNK)
        d = dall[rows, :]
        ig[rows, :] = dot(d, weight, ((1,), (1,))).astype(BF)
        part = dot(xall[k], d, ((0,), (0,)))
        if k == 0:
            gw[...] = part
        else:
            gw[...] += part
    gw_out[:, 0 : 3 * WIDE] = gw[...].astype(BF)


def attn_bwd(scalars, xall, segr, pack, qm, kv, kt, mixt, lse, gs, smalls):
    shape = jax.ShapeDtypeStruct
    return pl.pallas_call(
        attn_bwd_kernel,
        name="attn_bwd",
        out_shape=(shape((1024, 1024), BF), shape((1024, 3 * WIDE + 128), BF)),
        grid=(1,),
        in_specs=[SMEM_SPEC]
        + [
            any_spec((4, CHUNK, 1024)),
            any_spec((4, 8, CHUNK)),
            QKV_SPEC,
            any_spec((HERE, 4 * CHUNK, 128)),
            any_spec((4 * CHUNK, 2 * WIDE)),
            any_spec((WIDE, 4 * CHUNK)),
            any_spec((WIDE, 4 * CHUNK)),
            any_spec((8, 4 * CHUNK)),
        ]
        + [any_spec((CHUNK, WIDE))] * 4
        + [any_spec((8, 1024)), any_spec((8, 1024)), any_spec((4, 1024))]
        + [any_spec((8, 128))] * 2,
        out_specs=(any_spec((1024, 1024)), any_spec((1024, 3 * WIDE + 128))),
        scratch_shapes=[
            pltpu.VMEM((128, 1024), F32),
            pltpu.VMEM((4, CHUNK, 128), F32),
            pltpu.SMEM((2, 4), jnp.int32),
            pltpu.VMEM((HERE, 4 * CHUNK, 128), BF),
            pltpu.VMEM((WIDE, CHUNK), BF),
            pltpu.VMEM((WIDE, CHUNK), F32),
            pltpu.VMEM((4 * CHUNK, WIDE), F32),
            pltpu.VMEM((4 * CHUNK, WIDE), F32),
            pltpu.VMEM((8, 4 * CHUNK), F32),
            pltpu.VMEM((4 * CHUNK, 768), BF),
            pltpu.VMEM((1024, 768), F32),
            pltpu.VMEM((HERE, CHUNK, CHUNK), F32),
            pltpu.VMEM((HERE, CHUNK, CHUNK), F32),
            pltpu.VMEM((HERE, CHUNK, CHUNK), BF),
            pltpu.VMEM((HERE, CHUNK, CHUNK), BF),
        ],
        compiler_params=PARAMS,
    )(scalars, xall, segr, pack, qm, kv, kt, mixt, lse, *gs, *smalls)


def finish_kernel(sc, *refs):
    z = sc[0]
    pieces, (gq, gk, gv), vectors, ub, rms = refs[0:4], refs[4:7], refs[7:15], refs[15], refs[16:19]
    for k, piece in enumerate(pieces):
        cols = pl.ds(pl.multiple_of(lax.rem(z - k + 4, 4) * WIDE, WIDE), WIDE)
        for n, out in enumerate((gq, gk, gv)):
            out[:, cols] = piece[:, WIDE * n : WIDE * n + WIDE].astype(F32)
    extra = pieces[0][:, 3 * WIDE :].astype(F32)
    for piece in pieces[1:]:
        extra = extra + piece[:, 3 * WIDE :].astype(F32)
    extra = jnp.transpose(extra)
    for n, out in enumerate(vectors):
        out[...] = extra[n : n + 1, :]
    ub[...] = extra[8:12, :]
    counted = (16.0 * extra[15:16, 0:1] + extra[16:17, 0:1]) * 1024.0
    for n, out in enumerate(rms):
        out[...] = jnp.sqrt(extra[12 + n : 13 + n, 0:1] / counted)


def finish(scalars, pieces):
    shape = jax.ShapeDtypeStruct
    shapes = [(ROWS, 1024)] * 3 + [(1, ROWS)] * 8 + [(4, ROWS)] + [(1, 1)] * 3
    return pl.pallas_call(
        finish_kernel,
        name="finish",
        out_shape=tuple(shape(n, F32) for n in shapes),
        in_specs=[SMEM_SPEC] + [VMEM_SPEC] * 4,
        out_specs=(VMEM_SPEC,) * len(shapes),
        compiler_params=PARAMS,
    )(scalars, *pieces)


def line_gather(x):
    right = lax.ppermute(x, "ctx", [(0, 1), (1, 2), (2, 3)])
    left = lax.ppermute(x, "ctx", [(1, 0), (2, 1), (3, 2)])
    two = lax.ppermute(x, "ctx", [(0, 2), (1, 3), (2, 0), (3, 1)])
    return [x, right, left, two]


def line_forward(two):
    return lax.ppermute(two, "ctx", [(1, 0), (2, 3)])


def shift(x, k):
    n = lax.axis_size("ctx")
    return lax.ppermute(x, "ctx", [(i, (i + k) % n) for i in range(n)])


def swap(x, bits):
    return lax.ppermute(x, "fsdp", [(i, i ^ bits) for i in range(lax.axis_size("fsdp"))])


def add(*terms):
    total = terms[0].astype(F32)
    for term in terms[1:]:
        total = total + term.astype(F32)
    return total


def neighbour(x, bits):
    return lax.ppermute(x, "ctx", [(i, i ^ bits) for i in range(4)])


def half_sum(terms, which):
    half = terms[0].shape[0] // 2
    return add(*[lax.dynamic_slice_in_dim(t, which * half, half, 0) for t in terms])


class LineSum:
    def __init__(self, *terms):
        self.terms = terms
        self.odd = lax.axis_index("ctx") % 2

    def first(self):
        return half_sum(self.terms, 1 - self.odd).astype(BF)

    def second(self, got):
        self.pair = add(half_sum(self.terms, self.odd), got).astype(BF)
        return self.pair

    def third(self, got):
        self.whole = add(self.pair, got).astype(BF)
        return self.whole

    def result(self, got):
        even = self.odd == 0
        low = jnp.where(even, self.whole, got)
        return jnp.concatenate([low, jnp.where(even, got, self.whole)]).astype(F32)


def line_sum(*terms):
    parts = LineSum(*terms)
    got = neighbour(parts.first(), 1)
    got = neighbour(parts.second(got), 2)
    return parts.result(neighbour(parts.third(got), 1))


def per_device(
    tokens,
    segment_ids,
    cotangent,
    query_weight,
    query_bias,
    key_weight,
    value_weight,
    value_bias,
    out_weight,
    out_bias,
    attn_gain,
    attn_shift,
    up_weight,
    up_bias,
    down_weight,
    down_bias,
    mlp_gain,
    mlp_shift,
):
    owners = lax.axis_size("fsdp")
    plane = owners == SHARDS
    z = lax.axis_index("ctx")
    f = lax.axis_index("fsdp")
    if plane:
        chip, core = f // 2, f % 2
    else:
        chip, core = jnp.int32(0), jnp.int32(0)
    scalars = jnp.stack([z, chip, core, z]).astype(jnp.int32)
    tok = tokens[0]
    if plane:
        weights = (query_weight, key_weight, value_weight, out_weight)
        vectors = (query_bias, value_bias, out_bias, attn_gain, attn_shift, down_bias)
        vectors += (mlp_gain, mlp_shift, up_bias)
        packed, mine_pack = pack_inputs(scalars, tok, segment_ids, weights, vectors)
        pack = lax.all_gather(mine_pack, "fsdp", axis=0)
        xs = line_gather(packed)
        xs.append(line_forward(xs[3]))
        near_x, near_y = swap(up_weight, 2), swap(up_weight, 4)
        xs, near_x, near_y, after, pack = lax.optimization_barrier(
            (xs, near_x, near_y, down_weight, pack)
        )
        down = lax.all_gather(after, "fsdp", axis=0)
        half = up_weight.shape[1] // 2
        far = [swap(near_x[:, :half], 4), swap(near_y[:, half:], 2)]
    else:
        seg_row = jnp.pad(segment_ids.astype(BF), ((0, 15), (0, 1024 - CHUNK)))
        packed = jnp.concatenate([tok, seg_row])
        xs = line_gather(packed)
        xs.append(line_forward(xs[3]))
        quarter = jnp.concatenate(
            [
                lax.dynamic_slice_in_dim(m, z * WIDE, WIDE, 1)
                for m in (query_weight, key_weight, value_weight)
            ],
            axis=1,
        )
        whole = lambda m: lax.all_gather(m, "fsdp", axis=0, tiled=True)
        split = lambda m: whole(m).reshape(SHARDS, -1)
        line0 = jnp.concatenate(
            [split(m) for m in (query_bias, value_bias, out_bias, attn_gain, attn_shift, down_bias)],
            axis=1,
        )
        line1 = jnp.concatenate([split(m) for m in (mlp_gain, mlp_shift, up_bias)], axis=1)
        lines = jnp.pad(jnp.stack([line0, line1], axis=1), ((0, 0), (0, 14), (0, 0)))
        pack = jnp.concatenate([whole(quarter).reshape(SHARDS, ROWS, 768), lines], axis=1)
        out_rows = whole(out_weight).reshape(SHARDS, ROWS, 1024)
        wide = lambda m: jnp.pad(m, ((0, 0), (0, 0), (0, 1024 - m.shape[2])))
        pack = jnp.concatenate([out_rows, wide(pack)], axis=1)
        ups = list(whole(up_weight).reshape(SHARDS, ROWS, 4096))
        down = whole(down_weight).reshape(SHARDS, 512, 1024)
    valid = (segment_ids[0] != SEGS - 1).astype(F32)[:, None]

    m0, m1, m2, m3, mixt, lse, qm, kv, kt, xall, segr = attn_fwd(scalars, xs, pack)
    parts = [m0] + [shift(m, -k) for k, m in ((1, m1), (2, m2), (3, m3))]
    if plane:
        ups = [up_weight, swap(up_weight, 1)]
        parts, near_x, near_y, far = lax.optimization_barrier((parts, near_x, near_y, far))
        for rows in (near_x, near_y, jnp.concatenate(far, axis=1)):
            ups += [rows, swap(rows, 1)]
    normed, low, low_rel, scaled, inv, mixed, stats_a = out_project(
        scalars, tok, parts, pack, valid
    )
    acts, slope = mlp_gate(low, low_rel, mixed, ups, pack)
    acts_p = swap(acts, 1)
    result, grads, gh1, g0, g1, g2, g3, sums_m, stats_m, sums_a, ub = mlp_tail(
        scalars, acts, slope, ups, down, normed, scaled, inv, pack, cotangent[0], valid
    )
    gs = [g0] + [shift(g, k) for k, g in ((1, g1), (2, g2), (3, g3))]
    grads_p = swap(grads, 1)
    d3, d1, d2, d0 = down_grads(scalars, acts, acts_p, grads, grads_p)
    if plane:
        d_far = swap(d3, 2)
    r3, r1, r2, r0 = rest_grads(scalars, acts, acts_p, grads, grads_p)
    gs, r3, r1, r2, r0 = lax.optimization_barrier((gs, r3, r1, r2, r0))
    if plane:
        r_far = swap(r3, 4)
    smalls = (sums_m, sums_a, ub.reshape(1024, 4).T, stats_a, stats_m)
    ig, gw = attn_bwd(scalars, xall, segr, pack, qm, kv, kt, mixt, lse, gs, smalls)
    tie = lax.optimization_barrier
    if plane:
        ig, gw, d_far, r_far = tie((ig, gw, d_far, r_far))
    ig = lax.psum_scatter(ig, "ctx", scatter_dimension=0, tiled=True)
    if plane:
        to_y, to_x = add(d2, d_far).astype(BF), add(r1, r_far).astype(BF)
        to_y, to_x, d1, r2 = tie((to_y, to_x, d1, r2))
        r_from_x, r_from_y = swap(to_x, 2), swap(r2, 4)
        d_from_x, d_from_y = swap(d1, 2), swap(to_y, 4)
        r_sum = LineSum(r0, r_from_x, r_from_y)
        got_r = neighbour(r_sum.first(), 1)
        ig, gw, _ = tie((ig, gw, got_r))
    q_own = lax.psum_scatter(gw, "fsdp", scatter_dimension=0, tiled=True)
    q_low = q_own.astype(BF)

    if plane:
        r_second = r_sum.second(got_r)
        got_r = neighbour(r_second, 2)
        d_from_x, d_from_y, _ = tie((d_from_x, d_from_y, r_second))
        d_sum = LineSum(d0, d_from_x, d_from_y)
        got = neighbour(d_sum.first(), 1)
        r_third = r_sum.third(got_r)
        got_r = neighbour(r_third, 1)
        got, _ = tie((got, r_third))
        d_second = d_sum.second(got)
        got = neighbour(d_second, 2)
        q_low, _ = tie((q_low, d_second))
        q_pieces = [q_low] + [shift(q_low, k) for k in (1, 2, 3)]
        rest = r_sum.result(got_r)
        grad_down = d_sum.result(neighbour(d_sum.third(got), 1))
        input_grad = add(gh1, ig)
        grad_up = jnp.concatenate([rest[ROWS * b : ROWS * b + ROWS] for b in range(4)], axis=1)
        grad_out = rest[4 * ROWS :]
    else:
        other = scalars.at[2].set(1)
        sums_w = (d3, d1, d2, d0, r3, r1, r2, r0)
        second = down_grads(other, acts, acts_p, grads, grads_p)
        second += rest_grads(other, acts, acts_p, grads, grads_p)
        rows_of = lambda t: ([t[3], t[1], t[2], t[0]], [t[7], t[5], t[6], t[4]])
        down_0, rest_0 = rows_of(sums_w)
        down_1, rest_1 = rows_of(second)
        down_all = 0.5 * jnp.stack([m.astype(F32) for p in zip(down_0, down_1) for m in p])
        rest_all = 0.5 * jnp.stack([m.astype(F32) for p in zip(rest_0, rest_1) for m in p])
        scatter = lambda m: lax.psum_scatter(
            m.astype(BF), "fsdp", scatter_dimension=0, tiled=True
        )
        grad_down = line_sum(scatter(down_all.reshape(4096, 1024)))
        grad_up = line_sum(
            scatter(
                rest_all[:, 0:512]
                .reshape(SHARDS, 4, ROWS, 1024)
                .swapaxes(1, 2)
                .reshape(1024, 4096)
            )
        )
        grad_out = line_sum(scatter(rest_all[:, 512:].reshape(1024, 1024)))
        q_pieces = [q_low] + [shift(q_low, k) for k in (1, 2, 3)]
        input_grad = add(gh1, ig)
    if plane:
        done = finish(scalars, q_pieces)
        grad_q, grad_k, grad_v = done[0:3]
        vectors = [v.reshape(-1) for v in done[3:11]]
        up_bias_grad = done[11].T.reshape(-1)
        rms = [v.reshape(()) for v in done[12:15]]
    else:
        table = jnp.take(jnp.stack(q_pieces), (z - jnp.arange(4)) % 4, axis=0)
        extra = add(*q_pieces)[:, 3 * WIDE :]
        cols = lambda n: jnp.concatenate(
            [table[a, :, n * WIDE : (n + 1) * WIDE].astype(F32) for a in range(4)], axis=1
        )
        grad_q, grad_k, grad_v = cols(0), cols(1), cols(2)
        vectors = [extra[:, n] for n in range(8)]
        up_bias_grad = extra[:, 8:12].reshape(-1)
        counted = (16.0 * extra[0, 15] + extra[0, 16]) * 1024
        rms = [jnp.sqrt(extra[0, 12 + n] / counted) for n in range(3)]
    return (
        result[None],
        input_grad[None],
        grad_q,
        vectors[6],
        grad_k,
        grad_v,
        vectors[7],
        grad_out,
        vectors[5],
        vectors[3],
        vectors[4],
        grad_up,
        up_bias_grad,
        grad_down,
        vectors[2],
        vectors[0],
        vectors[1],
        rms[0],
        rms[1],
        rms[2],
    )


def solution(mesh):
    matrix, vector = P("fsdp", None), P("fsdp")
    stream = P("fsdp", "ctx", None)
    placed = (
        stream,
        P("fsdp", "ctx"),
        stream,
        matrix,
        vector,
        matrix,
        matrix,
        vector,
        matrix,
        vector,
        vector,
        vector,
        matrix,
        vector,
        matrix,
        vector,
        vector,
        vector,
    )
    return jax.shard_map(
        per_device,
        mesh=mesh,
        in_specs=placed,
        out_specs=(
            stream,
            stream,
            matrix,
            vector,
            matrix,
            matrix,
            vector,
            matrix,
            vector,
            vector,
            vector,
            matrix,
            vector,
            matrix,
            vector,
            vector,
            vector,
            P(),
            P(),
            P(),
        ),
        check_vma=False,
    )
```

time: 407 us -> 365 us (0.90)
  starting transfers between devices: 78.7 us -> 43 us
  waiting for transfers between devices: 158 us -> 176 us
  Pallas kernels: 117 us -> 99.6 us
  other arithmetic: 23.1 us -> 18 us
    ppermute x12 -> x6, waiting for transfers between devices: 44.1 us -> 72.1 us  [neighbour(): return lax.ppermute(x, 'ctx', [(i, i ^ bits) for i in range(4)])]
    ppermute x12 -> x6, starting transfers between devices: 32.7 us -> 8.57 us  [neighbour(): return lax.ppermute(x, 'ctx', [(i, i ^ bits) for i in range(4)])]
    ppermute x22 -> x16, waiting for transfers between devices: 55.2 us -> 37.2 us  [swap(): lax.ppermute(x, 'fsdp', [(i, i ^ bits) for i in range(lax.axis_size('fsdp...]
    pallas_call x1, Pallas kernels: 30.5 us -> 18.6 us  [attn_bwd(): pl.pallas_call(attn_bwd_kernel, name='attn_bwd', out_shape=(shape((1024,...]
    another operation x8 -> x0, other arithmetic: 9.28 us -> none
    ppermute x22 -> x16, starting transfers between devices: 20.5 us -> 13.1 us  [swap(): lax.ppermute(x, 'fsdp', [(i, i ^ bits) for i in range(lax.axis_size('fsdp...]
    pallas_call x1, Pallas kernels: 21.9 us -> 15.2 us  [attn_fwd(): pl.pallas_call(attn_fwd_kernel, name='attn_fwd', out_shape=(shape((CHUNK,...]
    convert_element_type x17 -> x10, other arithmetic: 8.9 us -> 14.6 us  [the longest x2 4.64 us: per_device(): to_y, to_x = (add(d2, d_far).astype(BF), add(r1, r_far).astype(BF))]
  transfers between devices with their start and end apart: 51 -> 39, of which waited for: 24 -> 20; matrix products, arithmetic and copies ran while one was open for 7% -> 6% of each run, Pallas kernels for 24% -> 26%
where the time goes in v3:
time: 365 us; the launch traced here: 362 us
  waiting for transfers between devices  176 us (48%)
  Pallas kernels  99.6 us (27%)
  starting transfers between devices  43 us (12%)
  other arithmetic  18 us (5%)
  between operations  14.2 us (4%)
  local copies, waits for them, and re-layouts  11.6 us (3%)
    ppermute x6, waiting for transfers between devices, neighbour(): return lax.ppermute(x, 'ctx', [(i, i ^ bits) for i in range(4)])  72.1 us
    ppermute x16, waiting for transfers between devices, swap(): lax.ppermute(x, 'fsdp', [(i, i ^ bits) for i in range(lax.axis_size('fsdp...  37.2 us
    pallas_call x1, Pallas kernels, mlp_tail(): pl.pallas_call(mlp_tail_kernel, name='mlp_tail', grid=(16,), in_specs=[SM...  27 us
    ppermute x9, waiting for transfers between devices, shift(): return lax.ppermute(x, 'ctx', [(i, (i + k) % n) for i in range(n)])  25.9 us
    pallas_call x1, Pallas kernels, attn_bwd(): pl.pallas_call(attn_bwd_kernel, name='attn_bwd', out_shape=(shape((1024,...  18.6 us
    ppermute x1, waiting for transfers between devices, line_gather(): two = lax.ppermute(x, 'ctx', [(0, 2), (1, 3), (2, 0), (3, 1)])  17.8 us
    pallas_call x1, Pallas kernels, attn_fwd(): pl.pallas_call(attn_fwd_kernel, name='attn_fwd', out_shape=(shape((CHUNK,...  15.2 us
    ppermute x16, starting transfers between devices, swap(): lax.ppermute(x, 'fsdp', [(i, i ^ bits) for i in range(lax.axis_size('fsdp...  13.1 us
  transfers between devices with their start and end apart: 39, of which 20 were waited for; matrix products, arithmetic and copies ran while one was open for 6% of the time, Pallas kernels for 26%

profile of v3, /device:TPU:0, one launch (start us, length us, event | category | flops | bytes accessed | tf_op | source)
XLA Modules:
  0.0 362.5 jit_solution(5998902576055222535)
XLA Ops:
  9.1 2.5 pack_inputs.1
  11.7 4.1 %collective-permute-start.2 = (bf16[272,1024]{1,0:T(8,128)(2,1)}, bf16[272,1024]{1,0:T(8,128)(2,1)S(1)}, u32[]{:S(2)}, u32[]{:S(2)}) collective-permute-start(bf16[272,1024]{1,0:T(8,128)(2,1)} %get-tuple-element.119.x0), channel_id=1, source_target_pairs={{0,16},{8,24},{16,0},{24,8},{1,17},{9,25},{17,1},{25,9},{2,18},{10... | collective-permute-start | bytes 1671176 | tf_op jit(solution)/shard_map/ppermute | solution.py:895
  15.8 1.5 collective-permute-start.4
  17.3 1.5 collective-permute-start.5
  18.8 3.5 collective-permute-start
  23.6 17.8 %collective-permute-done.2.x2 = bf16[272,1024]{1,0:T(8,128)(2,1)S(1)} collective-permute-done((bf16[272,1024]{1,0:T(8,128)(2,1)}, bf16[272,1024]{1,0:T(8,128)(2,1)S(1)}, u32[]{:S(2)}, u32[]{:S(2)}) %collective-permute-start.2) | collective-permute-done | bytes 557088 | tf_op jit(solution)/shard_map/ppermute | solution.py:895
  42.8 8.0 %collective-permute-done.1.left = bf16[272,1024]{1,0:T(8,128)(2,1)S(1)} collective-permute-done((bf16[272,1024]{1,0:T(8,128)(2,1)}, bf16[272,1024]{1,0:T(8,128)(2,1)S(1)}, u32[]{:S(2)}, u32[]{:S(2)}) %collective-permute-start.1) | collective-permute-done | bytes 557088 | tf_op jit(solution)/shard_map/ppermute | solution.py:894
  50.8 2.1 collective-permute-done.5.refs_4_.refs_8_
  52.9 7.6 %collective-permute-done.3.far = bf16[272,1024]{1,0:T(8,128)(2,1)} collective-permute-done((bf16[272,1024]{1,0:T(8,128)(2,1)S(1)}, bf16[272,1024]{1,0:T(8,128)(2,1)}, u32[]{:S(2)}, u32[]{:S(2)}) %collective-permute-start.3) | collective-permute-done | bytes 557088 | tf_op jit(solution)/shard_map/ppermute | solution.py:900
  63.8 1.5 collective-permute-start.9
  65.3 15.2 %attn_fwd.1 = (bf16[256,256]{1,0:T(8,128)(2,1)}, bf16[256,256]{1,0:T(8,128)(2,1)}, bf16[256,256]{1,0:T(8,128)(2,1)}, bf16[256,256]{1,0:T(8,128)(2,1)}, f32[256,1...) custom-call(s32[4]{0:T(128)} %pad_add_fusion.sc, ...), custom_call_target="tpu_custom_call" | custom-call | tf_op jit(solution)/shard_map/attn_fwd/pallas_call | solution.py:220
  80.5 1.4 collective-permute-start.6
  81.9 1.7 collective-permute-start.7
  83.6 2.6 collective-permute-done.6.r1
  86.2 9.1 %collective-permute-done.7.r2 = bf16[256,256]{1,0:T(8,128)(2,1)S(1)} collective-permute-done((bf16[256,256]{1,0:T(8,128)(2,1)}, bf16[256,256]{1,0:T(8,128)(2,1)S(1)}, u32[]{:S(2)}, u32[]{:S(2)}) %collective-permute-start.7) | collective-permute-done | bytes 131104 | tf_op jit(solution)/shard_map/ppermute | solution.py:905
  98.0 5.6 %out_project.1 = (f32[256,1024]{1,0:T(8,128)}, bf16[256,1024]{1,0:T(8,128)(2,1)}, bf16[256,1024]{1,0:T(8,128)(2,1)}, f32[256,1024]{1,0:T(8,128)}, f32[256,128]{1...) custom-call(s32[4]{0:T(128)} %pad_add_fusion.sc, bf16[256,1024]{1,0:T(8,128)(2,1)} %bitcast.44, ...), custom_call_target="tpu_custom_call" | custom-call | tf_op jit(solution)/shard_map/out_project/pallas_call | solution.py:324
  103.7 11.4 %mlp_gate.1 = (bf16[6,256,1024]{2,1,0:T(8,128)(2,1)}, f32[256,4096]{1,0:T(8,128)}) custom-call(bf16[256,1024]{1,0:T(8,128)(2,1)} %get-tuple-element.135.low, bf16[256,1024]{1,0:T(8,128)(2,1)} %get-tuple-element.136.low_rel, bf16[256,1024]{1,0:T(8,128)(2,1)} %get-tuple-element.137.mixed, bf16[128,4096]{1,0:T(8,128)(2,1)} %refs_4_.1, ...), custom_call_target="tpu_custom_call" | custom-call | tf_op jit(solution)/shard_map/mlp_gate/pallas_call | solution.py:380
  115.7 6.3 %all-gather.7.cloned.1.call-done = bf16[4096,1024]{1,0:T(8,128)(2,1)} async-done(((bf16[512,1024]{1,0:T(8,128)(2,1)}), bf16[4096,1024]{1,0:T(8,128)(2,1)}) %all-gather.7.cloned.1.call-update) | async-done | bytes 8388624 | tf_op jit(solution)/shard_map/all_gather | solution.py:999
  122.0 27.0 %mlp_tail.1 = (bf16[256,1024]{1,0:T(8,128)(2,1)}, bf16[6,256,1024]{2,1,0:T(8,128)(2,1)}, f32[256,1024]{1,0:T(8,128)}, bf16[256,256]{1,0:T(8,128)(2,1)}, bf16[256...) custom-call(s32[4]{0:T(128)} %pad_add_fusion.sc, ...), custom_call_target="tpu_custom_call" | custom-call | tf_op jit(solution)/shard_map/mlp_tail/pallas_call | solution.py:537
  150.0 1.6 collective-permute-start.16
  151.6 1.5 collective-permute-start.17
  153.1 1.9 collective-permute-done.19.gp
  155.0 9.0 %rest_grads.1 = (bf16[640,1024]{1,0:T(8,128)(2,1)}, bf16[640,1024]{1,0:T(8,128)(2,1)}, bf16[640,1024]{1,0:T(8,128)(2,1)}, bf16[640,1024]{1,0:T(8,128)(2,1)}) custom-call(s32[4]{0:T(128)} %pad_add_fusion.sc, bf16[6,256,1024]{2,1,0:T(8,128)(2,1)} %get-tuple-element.142.acts.lo.ho, bf16[6,256,1024]{2,1,0:T(8,128)(2,1)} %copy-done, ...), custom_call_target="tpu_custom_call" | custom-call | tf_op jit(solution)/shard_map/rest_grads/pallas_call | solution.py:679
  164.9 7.9 %down_grads.1 = (bf16[512,1024]{1,0:T(8,128)(2,1)}, bf16[512,1024]{1,0:T(8,128)(2,1)}, bf16[512,1024]{1,0:T(8,128)(2,1)}, bf16[512,1024]{1,0:T(8,128)(2,1)}) custom-call(s32[4]{0:T(128)} %pad_add_fusion.sc, bf16[6,256,1024]{2,1,0:T(8,128)(2,1)} %get-tuple-element.142.acts.lo.ho, bf16[6,256,1024]{2,1,0:T(8,128)(2,1)} %copy-done, ...), custom_call_target="tpu_custom_call" | custom-call | tf_op jit(solution)/shard_map/down_grads/pallas_call | solution.py:631
  175.2 18.6 %attn_bwd.1 = (bf16[1024,1024]{1,0:T(8,128)(2,1)}, bf16[1024,896]{1,0:T(8,128)(2,1)}) custom-call(s32[4]{0:T(128)} %pad_add_fusion.sc, bf16[4,256,1024]{2,1,0:T(8,128)(2,1)} %get-tuple-element.150.xall, f32[4,8,256]{2,1,0:T(8,128)} %get-tuple-element.151.segr, bf16[8,272,1024]{2,1,0:T(8,128)(2,1)} %bitcast.40, bf16[4,1024,128]{2,1,0:T(8,128)(2,1)} %get-tuple-element.152.qm, ...), custom_call_target="tpu_custom_call" | custom-call | tf_op jit(solution)/shard_map/attn_bwd/pallas_call | solution.py:819
  193.8 3.9 %collective-permute-done.20 = bf16[512,1024]{1,0:T(8,128)(2,1)S(1)} collective-permute-done((bf16[512,1024]{1,0:T(8,128)(2,1)}, bf16[512,1024]{1,0:T(8,128)(2,1)S(1)}, u32[]{:S(2)}, u32[]{:S(2)}) %collective-permute-start.20) | collective-permute-done | bytes 1048608 | tf_op jit(solution)/shard_map/ppermute | solution.py:909
  199.4 3.0 add_convert_fusion.1
  202.5 1.6 add_convert_fusion
  206.1 27.5 %collective-permute-done.22 = bf16[640,1024]{1,0:T(8,128)(2,1)S(1)} collective-permute-done((bf16[640,1024]{1,0:T(8,128)(2,1)}, bf16[640,1024]{1,0:T(8,128)(2,1)S(1)}, u32[]{:S(2)}, u32[]{:S(2)}) %collective-permute-start.22) | collective-permute-done | bytes 1310752 | tf_op jit(solution)/shard_map/ppermute | solution.py:909
  234.2 1.4 add_convert_fusion.4
  237.8 1.5 collective-permute-start.26
  239.3 15.5 %collective-permute-done.24 = bf16[320,1024]{1,0:T(8,128)(2,1)} collective-permute-done((bf16[320,1024]{1,0:T(8,128)(2,1)S(1)}, bf16[320,1024]{1,0:T(8,128)(2,1)}, u32[]{:S(2)}, u32[]{:S(2)}) %collective-permute-start.24) | collective-permute-done | bytes 655392 | tf_op jit(solution)/shard_map/ppermute | solution.py:920
  254.7 1.8 add_convert_fusion.3
  256.5 2.9 collective-permute-start.28
  260.5 1.6 add_convert_fusion.7
  262.2 1.7 collective-permute-start.27
  263.9 23.5 %collective-permute-done.28 = bf16[320,1024]{1,0:T(8,128)(2,1)} collective-permute-done((bf16[320,1024]{1,0:T(8,128)(2,1)S(1)}, bf16[320,1024]{1,0:T(8,128)(2,1)}, u32[]{:S(2)}, u32[]{:S(2)}) %collective-permute-start.28) | collective-permute-done | bytes 655392 | tf_op jit(solution)/shard_map/ppermute | solution.py:920
  288.9 1.7 add_convert_fusion.6
  290.7 2.9 collective-permute-start.32
  293.5 21.6 %collective-permute-done.33 = bf16[256,1024]{1,0:T(8,128)(2,1)S(1)} collective-permute-done((bf16[256,1024]{1,0:T(8,128)(2,1)S(1)}, bf16[256,1024]{1,0:T(8,128)(2,1)S(1)}, u32[]{:S(2)}, u32[]{:S(2)}) %collective-permute-start.33) | collective-permute-done | bytes 524320 | tf_op jit(solution)/shard_map/ppermute | solution.py:920
  315.4 3.7 %collective-permute-done.32 = bf16[320,1024]{1,0:T(8,128)(2,1)S(1)} collective-permute-done((bf16[320,1024]{1,0:T(8,128)(2,1)S(1)}, bf16[320,1024]{1,0:T(8,128)(2,1)S(1)}, u32[]{:S(2)}, u32[]{:S(2)}) %collective-permute-start.32) | collective-permute-done | bytes 655392 | tf_op jit(solution)/shard_map/ppermute | solution.py:920
  320.6 1.5 pad_maximum_fusion
  322.0 7.7 %collective-permute-done.34 = bf16[256,1024]{1,0:T(8,128)(2,1)S(1)} collective-permute-done((bf16[256,1024]{1,0:T(8,128)(2,1)S(1)}, bf16[256,1024]{1,0:T(8,128)(2,1)S(1)}, u32[]{:S(2)}, u32[]{:S(2)}) %collective-permute-start.34) | collective-permute-done | bytes 524320 | tf_op jit(solution)/shard_map/ppermute | solution.py:920
  329.9 1.6 maximum_convert_fusion.1
  331.7 2.4 collective-permute-start.30
  336.4 5.7 %collective-permute-done.29.refs_1_ = bf16[128,896]{1,0:T(8,128)(2,1)S(1)} collective-permute-done((bf16[128,896]{1,0:T(8,128)(2,1)}, bf16[128,896]{1,0:T(8,128)(2,1)S(1)}, u32[]{:S(2)}, u32[]{:S(2)}) %collective-permute-start.29) | collective-permute-done | bytes 229408 | tf_op jit(solution)/shard_map/ppermute | solution.py:905
  342.1 8.4 %collective-permute-done.30.refs_2_ = bf16[128,896]{1,0:T(8,128)(2,1)S(1)} collective-permute-done((bf16[128,896]{1,0:T(8,128)(2,1)}, bf16[128,896]{1,0:T(8,128)(2,1)S(1)}, u32[]{:S(2)}, u32[]{:S(2)}) %collective-permute-start.30) | collective-permute-done | bytes 229408 | tf_op jit(solution)/shard_map/ppermute | solution.py:905
  351.9 2.5 finish.1
  (123 shorter events, 31.7 us)
Async XLA Ops:
  7.2 54.3 %all-gather.5.cloned.1.call-start = ((), (), s32[]{:S(2)}) async-start(), calls=%async_computation.4 | async-start | bytes 5013504 | tf_op jit(solution)/shard_map/all_gather | solution.py:992
  11.7 110.3 %all-gather.7.cloned.1.call-start = ((), (), s32[]{:S(2)}) async-start(), calls=%async_computation.5 | async-start | bytes 9437184 | tf_op jit(solution)/shard_map/all_gather | solution.py:999
  11.7 29.7 %collective-permute-start.2 = (bf16[272,1024]{1,0:T(8,128)(2,1)}, bf16[272,1024]{1,0:T(8,128)(2,1)S(1)}, u32[]{:S(2)}, u32[]{:S(2)}) collective-permute-start(bf16[272,1024]{1,0:T(8,128)(2,1)} %get-tuple-element.119.x0), channel_id=1, source_target_pairs={{0,16},{8,24},{16,0},{24,8},{1,17},{9,25},{17,1},{25,9},{2,18},{10... | collective-permute-start | bytes 1671176 | tf_op jit(solution)/shard_map/ppermute | solution.py:895
  15.8 35.0 %collective-permute-start.4 = (bf16[128,4096]{1,0:T(8,128)(2,1)}, bf16[128,4096]{1,0:T(8,128)(2,1)S(1)}, u32[]{:S(2)}, u32[]{:S(2)}) collective-permute-start(bf16[128,4096]{1,0:T(8,128)(2,1)} %refs_4_.1), channel_id=1, source_target_pairs={{0,2},{1,3},{2,0},{3,1},{4,6},{5,7},{6,4},{7,5},{8,10},{9,11},{10,... | collective-permute-start | bytes 3145736 | tf_op jit(solution)/shard_map/ppermute | solution.py:909
  17.3 35.6 %collective-permute-start.5 = (bf16[128,4096]{1,0:T(8,128)(2,1)}, bf16[128,4096]{1,0:T(8,128)(2,1)S(1)}, u32[]{:S(2)}, u32[]{:S(2)}) collective-permute-start(bf16[128,4096]{1,0:T(8,128)(2,1)} %refs_4_.1), channel_id=1, source_target_pairs={{0,4},{1,5},{2,6},{3,7},{4,0},{5,1},{6,2},{7,3},{8,12},{9,13},{10,... | collective-permute-start | bytes 3145736 | tf_op jit(solution)/shard_map/ppermute | solution.py:909
  18.8 23.9 %collective-permute-start = (bf16[272,1024]{1,0:T(8,128)(2,1)}, bf16[272,1024]{1,0:T(8,128)(2,1)S(1)}, u32[]{:S(2)}, u32[]{:S(2)}) collective-permute-start(bf16[272,1024]{1,0:T(8,128)(2,1)} %get-tuple-element.119.x0), channel_id=1, source_target_pairs={{0,8},{8,16},{16,24},{1,9},{9,17},{17,25},{2,10},{10,18},{18,26},{... | collective-permute-start | bytes 1671176 | tf_op jit(solution)/shard_map/ppermute | solution.py:893
  22.3 28.4 %collective-permute-start.1 = (bf16[272,1024]{1,0:T(8,128)(2,1)}, bf16[272,1024]{1,0:T(8,128)(2,1)S(1)}, u32[]{:S(2)}, u32[]{:S(2)}) collective-permute-start(bf16[272,1024]{1,0:T(8,128)(2,1)} %get-tuple-element.119.x0), channel_id=1, source_target_pairs={{8,0},{16,8},{24,16},{9,1},{17,9},{25,17},{10,2},{18,10},{26,18},{... | collective-permute-start | bytes 1671176 | tf_op jit(solution)/shard_map/ppermute | solution.py:894
  41.5 23.8 %copy-start.11 = (bf16[272,1024]{1,0:T(8,128)(2,1)}, bf16[272,1024]{1,0:T(8,128)(2,1)S(1)}, u32[]{:S(2)}) copy-start(bf16[272,1024]{1,0:T(8,128)(2,1)S(1)} %collective-permute-done.2.x2) | copy-start | bytes 1671172
  41.5 19.0 %collective-permute-start.3 = (bf16[272,1024]{1,0:T(8,128)(2,1)S(1)}, bf16[272,1024]{1,0:T(8,128)(2,1)}, u32[]{:S(2)}, u32[]{:S(2)}) collective-permute-start(bf16[272,1024]{1,0:T(8,128)(2,1)S(1)} %collective-permute-done.2.x2), channel_id=1, source_target_pairs={{8,0},{16,24},{9,1},{17,25},{10,2},{18,26},{11,3},{19,27},{12,4},{... | collective-permute-start | bytes 1671176 | tf_op jit(solution)/shard_map/ppermute | solution.py:900
  42.8 22.5 %copy-start.12 = (bf16[272,1024]{1,0:T(8,128)(2,1)}, bf16[272,1024]{1,0:T(8,128)(2,1)S(1)}, u32[]{:S(2)}) copy-start(bf16[272,1024]{1,0:T(8,128)(2,1)S(1)} %collective-permute-done.right) | copy-start | bytes 1671172
  50.8 45.8 %copy-start.1 = (bf16[128,4096]{1,0:T(8,128)(2,1)}, bf16[128,4096]{1,0:T(8,128)(2,1)S(1)}, u32[]{:S(2)}) copy-start(bf16[128,4096]{1,0:T(8,128)(2,1)S(1)} %collective-permute-done.4.refs_2_.refs_6_) | copy-start | bytes 3145732
  52.9 44.2 %copy-start.2 = (bf16[128,4096]{1,0:T(8,128)(2,1)}, bf16[128,4096]{1,0:T(8,128)(2,1)S(1)}, u32[]{:S(2)}) copy-start(bf16[128,4096]{1,0:T(8,128)(2,1)S(1)} %collective-permute-done.5.refs_4_.refs_8_) | copy-start | bytes 3145732
  61.5 227.3 %reduce-scatter.3.cloned.1.call-start = ((), (), s32[]{:S(2)}) async-start(), calls=%async_computation.2 | async-start | bytes 2621440 | tf_op jit(solution)/shard_map/reduce_scatter | solution.py:1059
  62.4 32.9 %collective-permute-start.10 = (bf16[128,2048]{1,0:T(8,128)(2,1)}, bf16[128,2048]{1,0:T(8,128)(2,1)S(1)}, u32[]{:S(2)}, u32[]{:S(2)}) collective-permute-start(bf16[128,2048]{1,0:T(8,128)(2,1)} %slice.22), channel_id=1, source_target_pairs={{0,2},{1,3},{2,0},{3,1},{4,6},{5,7},{6,4},{7,5},{8,10},{9,11},{10,... | collective-permute-start | bytes 1572872 | tf_op jit(solution)/shard_map/ppermute | solution.py:909
  63.8 31.5 %collective-permute-start.9 = (bf16[128,2048]{1,0:T(8,128)(2,1)}, bf16[128,2048]{1,0:T(8,128)(2,1)}, u32[]{:S(2)}, u32[]{:S(2)}) collective-permute-start(bf16[128,2048]{1,0:T(8,128)(2,1)} %slice.21), channel_id=1, source_target_pairs={{0,4},{1,5},{2,6},{3,7},{4,0},{5,1},{6,2},{7,3},{8,12},{9,13},{10,... | collective-permute-start | bytes 1572872 | tf_op jit(solution)/shard_map/ppermute | solution.py:909
  80.5 16.7 %copy-start.25 = (s32[1,256]{1,0:T(1,128)S(1)}, s32[1,256]{1,0:T(1,128)}, u32[]{:S(2)}) copy-start(s32[1,256]{1,0:T(1,128)} %seg.1) | copy-start | bytes 3076
  80.5 5.7 %collective-permute-start.6 = (bf16[256,256]{1,0:T(8,128)(2,1)}, bf16[256,256]{1,0:T(8,128)(2,1)S(1)}, u32[]{:S(2)}, u32[]{:S(2)}) collective-permute-start(bf16[256,256]{1,0:T(8,128)(2,1)} %get-tuple-element.126), channel_id=1, source_target_pairs={{0,24},{8,0},{16,8},{24,16},{1,25},{9,1},{17,9},{25,17},{2,26},{10... | collective-permute-start | bytes 393224 | tf_op jit(solution)/shard_map/ppermute | solution.py:905
  81.9 13.4 %collective-permute-start.7 = (bf16[256,256]{1,0:T(8,128)(2,1)}, bf16[256,256]{1,0:T(8,128)(2,1)S(1)}, u32[]{:S(2)}, u32[]{:S(2)}) collective-permute-start(bf16[256,256]{1,0:T(8,128)(2,1)} %get-tuple-element.127), channel_id=1, source_target_pairs={{0,16},{8,24},{16,0},{24,8},{1,17},{9,25},{17,1},{25,9},{2,18},{10... | collective-permute-start | bytes 393224 | tf_op jit(solution)/shard_map/ppermute | solution.py:905
  83.6 11.7 %collective-permute-start.8 = (bf16[256,256]{1,0:T(8,128)(2,1)}, bf16[256,256]{1,0:T(8,128)(2,1)S(1)}, u32[]{:S(2)}, u32[]{:S(2)}) collective-permute-start(bf16[256,256]{1,0:T(8,128)(2,1)} %get-tuple-element.128), channel_id=1, source_target_pairs={{0,8},{8,16},{16,24},{24,0},{1,9},{9,17},{17,25},{25,1},{2,10},{10... | collective-permute-start | bytes 393224 | tf_op jit(solution)/shard_map/ppermute | solution.py:905
  86.2 11.9 %copy-start.21 = (bf16[256,256]{1,0:T(8,128)(2,1)}, bf16[256,256]{1,0:T(8,128)(2,1)S(1)}, u32[]{:S(2)}) copy-start(bf16[256,256]{1,0:T(8,128)(2,1)S(1)} %collective-permute-done.6.r1) | copy-start | bytes 393220
  86.2 17.5 %collective-permute-start.11 = (bf16[128,4096]{1,0:T(8,128)(2,1)}, bf16[128,4096]{1,0:T(8,128)(2,1)}, u32[]{:S(2)}, u32[]{:S(2)}) collective-permute-start(bf16[128,4096]{1,0:T(8,128)(2,1)} %refs_4_.1), channel_id=1, source_target_pairs={{0,1},{1,0},{2,3},{3,2},{4,5},{5,4},{6,7},{7,6},{8,9},{9,8},{10,11... | collective-permute-start | bytes 3145736 | tf_op jit(solution)/shard_map/ppermute | solution.py:909
  96.5 7.2 %collective-permute-start.14 = (bf16[128,4096]{1,0:T(8,128)(2,1)S(1)}, bf16[128,4096]{1,0:T(8,128)(2,1)}, u32[]{:S(2)}, u32[]{:S(2)}) collective-permute-start(bf16[128,4096]{1,0:T(8,128)(2,1)S(1)} %constant_dynamic-update-slice_fusion.refs_6_.refs_10_), channel_id=1, source_target_pairs={{0,1},{1,0},{2,3},{3,2},{4,5},{5,4},{6,7},{7,6},{8,9},{9,8},{10,11... | collective-permute-start | bytes 3145736 | tf_op jit(solution)/shard_map/ppermute | solution.py:909
  96.6 7.1 %collective-permute-start.12 = (bf16[128,4096]{1,0:T(8,128)(2,1)S(1)}, bf16[128,4096]{1,0:T(8,128)(2,1)}, u32[]{:S(2)}, u32[]{:S(2)}) collective-permute-start(bf16[128,4096]{1,0:T(8,128)(2,1)S(1)} %collective-permute-done.4.refs_2_.refs_6_), channel_id=1, source_target_pairs={{0,1},{1,0},{2,3},{3,2},{4,5},{5,4},{6,7},{7,6},{8,9},{9,8},{10,11... | collective-permute-start | bytes 3145736 | tf_op jit(solution)/shard_map/ppermute | solution.py:909
  97.1 6.6 %collective-permute-start.13 = (bf16[128,4096]{1,0:T(8,128)(2,1)S(1)}, bf16[128,4096]{1,0:T(8,128)(2,1)}, u32[]{:S(2)}, u32[]{:S(2)}) collective-permute-start(bf16[128,4096]{1,0:T(8,128)(2,1)S(1)} %collective-permute-done.5.refs_4_.refs_8_), channel_id=1, source_target_pairs={{0,1},{1,0},{2,3},{3,2},{4,5},{5,4},{6,7},{7,6},{8,9},{9,8},{10,11... | collective-permute-start | bytes 3145736 | tf_op jit(solution)/shard_map/ppermute | solution.py:909
  115.1 38.1 %collective-permute-start.18 = (bf16[6,256,1024]{2,1,0:T(8,128)(2,1)}, bf16[6,256,1024]{2,1,0:T(8,128)(2,1)S(1)}, u32[]{:S(2)}, u32[]{:S(2)}) collective-permute-start(bf16[6,256,1024]{2,1,0:T(8,128)(2,1)} %get-tuple-element.142.acts.lo.ho), channel_id=1, source_target_pairs={{0,1},{1,0},{2,3},{3,2},{4,5},{5,4},{6,7},{7,6},{8,9},{9,8},{10,11... | collective-permute-start | bytes 9437192 | tf_op jit(solution)/shard_map/ppermute | solution.py:909
  149.0 6.1 %collective-permute-start.19 = (bf16[6,256,1024]{2,1,0:T(8,128)(2,1)}, bf16[6,256,1024]{2,1,0:T(8,128)(2,1)}, u32[]{:S(2)}, u32[]{:S(2)}) collective-permute-start(bf16[6,256,1024]{2,1,0:T(8,128)(2,1)} %get-tuple-element.161.go), channel_id=1, source_target_pairs={{0,1},{1,0},{2,3},{3,2},{4,5},{5,4},{6,7},{7,6},{8,9},{9,8},{10,11... | collective-permute-start | bytes 9437192 | tf_op jit(solution)/shard_map/ppermute | solution.py:909
  149.3 14.7 %collective-permute-start.15 = (bf16[256,256]{1,0:T(8,128)(2,1)}, bf16[256,256]{1,0:T(8,128)(2,1)S(1)}, u32[]{:S(2)}, u32[]{:S(2)}) collective-permute-start(bf16[256,256]{1,0:T(8,128)(2,1)} %get-tuple-element.158), channel_id=1, source_target_pairs={{0,8},{8,16},{16,24},{24,0},{1,9},{9,17},{17,25},{25,1},{2,10},{10... | collective-permute-start | bytes 393224 | tf_op jit(solution)/shard_map/ppermute | solution.py:905
  150.0 14.0 %collective-permute-start.16 = (bf16[256,256]{1,0:T(8,128)(2,1)}, bf16[256,256]{1,0:T(8,128)(2,1)S(1)}, u32[]{:S(2)}, u32[]{:S(2)}) collective-permute-start(bf16[256,256]{1,0:T(8,128)(2,1)} %get-tuple-element.159), channel_id=1, source_target_pairs={{0,16},{8,24},{16,0},{24,8},{1,17},{9,25},{17,1},{25,9},{2,18},{10... | collective-permute-start | bytes 393224 | tf_op jit(solution)/shard_map/ppermute | solution.py:905
  151.6 12.4 %collective-permute-start.17 = (bf16[256,256]{1,0:T(8,128)(2,1)}, bf16[256,256]{1,0:T(8,128)(2,1)S(1)}, u32[]{:S(2)}, u32[]{:S(2)}) collective-permute-start(bf16[256,256]{1,0:T(8,128)(2,1)} %get-tuple-element.160), channel_id=1, source_target_pairs={{0,24},{8,0},{16,8},{24,16},{1,25},{9,1},{17,9},{25,17},{2,26},{10... | collective-permute-start | bytes 393224 | tf_op jit(solution)/shard_map/ppermute | solution.py:905
  164.1 9.8 %copy-start.24 = (f32[8,1,512]{2,1,0:T(1,128)S(1)}, f32[8,1,512]{2,1,0:T(1,128)}, u32[]{:S(2)}) copy-start(f32[8,1,512]{2,1,0:T(1,128)} %get-tuple-element.172) | copy-start | bytes 49156
  164.1 33.6 %collective-permute-start.21 = (bf16[640,1024]{1,0:T(8,128)(2,1)}, bf16[640,1024]{1,0:T(8,128)(2,1)S(1)}, u32[]{:S(2)}, u32[]{:S(2)}) collective-permute-start(bf16[640,1024]{1,0:T(8,128)(2,1)} %get-tuple-element.178), channel_id=1, source_target_pairs={{0,4},{1,5},{2,6},{3,7},{4,0},{5,1},{6,2},{7,3},{8,12},{9,13},{10,... | collective-permute-start | bytes 3932168 | tf_op jit(solution)/shard_map/ppermute | solution.py:909
  172.9 24.8 %collective-permute-start.20 = (bf16[512,1024]{1,0:T(8,128)(2,1)}, bf16[512,1024]{1,0:T(8,128)(2,1)S(1)}, u32[]{:S(2)}, u32[]{:S(2)}) collective-permute-start(bf16[512,1024]{1,0:T(8,128)(2,1)} %get-tuple-element.177), channel_id=1, source_target_pairs={{0,2},{1,3},{2,0},{3,1},{4,6},{5,7},{6,4},{7,5},{8,10},{9,11},{10,... | collective-permute-start | bytes 3145736 | tf_op jit(solution)/shard_map/ppermute | solution.py:909
  199.2 132.3 %reduce-scatter.5.cloned.1.call-start = ((), (), s32[]{:S(2)}) async-start(), calls=%async_computation.3 | async-start | bytes 2064384 | tf_op jit(solution)/shard_map/reduce_scatter | solution.py:1068
  202.5 31.7 %copy-start.4 = (bf16[640,1024]{1,0:T(8,128)(2,1)S(1)}, bf16[640,1024]{1,0:T(8,128)(2,1)}, u32[]{:S(2)}) copy-start(bf16[640,1024]{1,0:T(8,128)(2,1)} %get-tuple-element.181) | copy-start | bytes 3932164
  204.1 29.5 %collective-permute-start.22 = (bf16[640,1024]{1,0:T(8,128)(2,1)}, bf16[640,1024]{1,0:T(8,128)(2,1)S(1)}, u32[]{:S(2)}, u32[]{:S(2)}) collective-permute-start(bf16[640,1024]{1,0:T(8,128)(2,1)} %add_convert_fusion), channel_id=1, source_target_pairs={{0,2},{1,3},{2,0},{3,1},{4,6},{5,7},{6,4},{7,5},{8,10},{9,11},{10,... | collective-permute-start | bytes 3932168 | tf_op jit(solution)/shard_map/ppermute | solution.py:909
  204.9 29.3 %collective-permute-start.23 = (bf16[640,1024]{1,0:T(8,128)(2,1)}, bf16[640,1024]{1,0:T(8,128)(2,1)}, u32[]{:S(2)}, u32[]{:S(2)}) collective-permute-start(bf16[640,1024]{1,0:T(8,128)(2,1)} %get-tuple-element.189), channel_id=1, source_target_pairs={{0,4},{1,5},{2,6},{3,7},{4,0},{5,1},{6,2},{7,3},{8,12},{9,13},{10,... | collective-permute-start | bytes 3932168 | tf_op jit(solution)/shard_map/ppermute | solution.py:909
  235.6 19.1 %collective-permute-start.24 = (bf16[320,1024]{1,0:T(8,128)(2,1)S(1)}, bf16[320,1024]{1,0:T(8,128)(2,1)}, u32[]{:S(2)}, u32[]{:S(2)}) collective-permute-start(bf16[320,1024]{1,0:T(8,128)(2,1)S(1)} %add_convert_fusion.4), channel_id=1, source_target_pairs={{0,8},{8,0},{16,24},{24,16},{1,9},{9,1},{17,25},{25,17},{2,10},{10... | collective-permute-start | bytes 1966088 | tf_op jit(solution)/shard_map/ppermute | solution.py:920
  236.6 22.8 %collective-permute-start.25 = (bf16[512,1024]{1,0:T(8,128)(2,1)}, bf16[512,1024]{1,0:T(8,128)(2,1)}, u32[]{:S(2)}, u32[]{:S(2)}) collective-permute-start(bf16[512,1024]{1,0:T(8,128)(2,1)} %get-tuple-element.193), channel_id=1, source_target_pairs={{0,2},{1,3},{2,0},{3,1},{4,6},{5,7},{6,4},{7,5},{8,10},{9,11},{10,... | collective-permute-start | bytes 3145736 | tf_op jit(solution)/shard_map/ppermute | solution.py:909
  237.8 22.8 %collective-permute-start.26 = (bf16[512,1024]{1,0:T(8,128)(2,1)}, bf16[512,1024]{1,0:T(8,128)(2,1)}, u32[]{:S(2)}, u32[]{:S(2)}) collective-permute-start(bf16[512,1024]{1,0:T(8,128)(2,1)} %add_convert_fusion.1), channel_id=1, source_target_pairs={{0,4},{1,5},{2,6},{3,7},{4,0},{5,1},{6,2},{7,3},{8,12},{9,13},{10,... | collective-permute-start | bytes 3145736 | tf_op jit(solution)/shard_map/ppermute | solution.py:909
  256.5 31.0 %collective-permute-start.28 = (bf16[320,1024]{1,0:T(8,128)(2,1)S(1)}, bf16[320,1024]{1,0:T(8,128)(2,1)}, u32[]{:S(2)}, u32[]{:S(2)}) collective-permute-start(bf16[320,1024]{1,0:T(8,128)(2,1)S(1)} %add_convert_fusion.3), channel_id=1, source_target_pairs={{0,16},{8,24},{16,0},{24,8},{1,17},{9,25},{17,1},{25,9},{2,18},{10... | collective-permute-start | bytes 1966088 | tf_op jit(solution)/shard_map/ppermute | solution.py:920
  262.2 26.6 %collective-permute-start.27 = (bf16[256,1024]{1,0:T(8,128)(2,1)S(1)}, bf16[256,1024]{1,0:T(8,128)(2,1)}, u32[]{:S(2)}, u32[]{:S(2)}) collective-permute-start(bf16[256,1024]{1,0:T(8,128)(2,1)S(1)} %add_convert_fusion.7), channel_id=1, source_target_pairs={{0,8},{8,0},{16,24},{24,16},{1,9},{9,1},{17,25},{25,17},{2,10},{10... | collective-permute-start | bytes 1572872 | tf_op jit(solution)/shard_map/ppermute | solution.py:920
  263.9 24.9 %copy-start.10 = (bf16[512,1024]{1,0:T(8,128)(2,1)S(1)}, bf16[512,1024]{1,0:T(8,128)(2,1)}, u32[]{:S(2)}) copy-start(bf16[512,1024]{1,0:T(8,128)(2,1)} %get-tuple-element.192) | copy-start | bytes 3145732
  290.6 24.5 %collective-permute-start.33 = (bf16[256,1024]{1,0:T(8,128)(2,1)S(1)}, bf16[256,1024]{1,0:T(8,128)(2,1)S(1)}, u32[]{:S(2)}, u32[]{:S(2)}) collective-permute-start(bf16[256,1024]{1,0:T(8,128)(2,1)S(1)} %add_convert_fusion.6), channel_id=1, source_target_pairs={{0,16},{8,24},{16,0},{24,8},{1,17},{9,25},{17,1},{25,9},{2,18},{10... | collective-permute-start | bytes 1572872 | tf_op jit(solution)/shard_map/ppermute | solution.py:920
  290.7 28.5 %collective-permute-start.32 = (bf16[320,1024]{1,0:T(8,128)(2,1)S(1)}, bf16[320,1024]{1,0:T(8,128)(2,1)S(1)}, u32[]{:S(2)}, u32[]{:S(2)}) collective-permute-start(bf16[320,1024]{1,0:T(8,128)(2,1)S(1)} %add_convert_fusion.2), channel_id=1, source_target_pairs={{0,8},{8,0},{16,24},{24,16},{1,9},{9,1},{17,25},{25,17},{2,10},{10... | collective-permute-start | bytes 1966088 | tf_op jit(solution)/shard_map/ppermute | solution.py:920
  315.3 14.5 %collective-permute-start.34 = (bf16[256,1024]{1,0:T(8,128)(2,1)S(1)}, bf16[256,1024]{1,0:T(8,128)(2,1)S(1)}, u32[]{:S(2)}, u32[]{:S(2)}) collective-permute-start(bf16[256,1024]{1,0:T(8,128)(2,1)S(1)} %add_convert_fusion.5), channel_id=1, source_target_pairs={{0,8},{8,0},{16,24},{24,16},{1,9},{9,1},{17,25},{25,17},{2,10},{10... | collective-permute-start | bytes 1572872 | tf_op jit(solution)/shard_map/ppermute | solution.py:920
  331.5 10.6 %collective-permute-start.29 = (bf16[128,896]{1,0:T(8,128)(2,1)}, bf16[128,896]{1,0:T(8,128)(2,1)S(1)}, u32[]{:S(2)}, u32[]{:S(2)}) collective-permute-start(bf16[128,896]{1,0:T(8,128)(2,1)} %reduce-scatter.5.cloned.1.call-done.refs_0_), channel_id=1, source_target_pairs={{0,8},{8,16},{16,24},{24,0},{1,9},{9,17},{17,25},{25,1},{2,10},{10... | collective-permute-start | bytes 688136 | tf_op jit(solution)/shard_map/ppermute | solution.py:905
  331.7 18.8 %collective-permute-start.30 = (bf16[128,896]{1,0:T(8,128)(2,1)}, bf16[128,896]{1,0:T(8,128)(2,1)S(1)}, u32[]{:S(2)}, u32[]{:S(2)}) collective-permute-start(bf16[128,896]{1,0:T(8,128)(2,1)} %reduce-scatter.5.cloned.1.call-done.refs_0_), channel_id=1, source_target_pairs={{0,16},{8,24},{16,0},{24,8},{1,17},{9,25},{17,1},{25,9},{2,18},{10... | collective-permute-start | bytes 688136 | tf_op jit(solution)/shard_map/ppermute | solution.py:905
  334.1 16.5 %collective-permute-start.31 = (bf16[128,896]{1,0:T(8,128)(2,1)}, bf16[128,896]{1,0:T(8,128)(2,1)S(1)}, u32[]{:S(2)}, u32[]{:S(2)}) collective-permute-start(bf16[128,896]{1,0:T(8,128)(2,1)} %reduce-scatter.5.cloned.1.call-done.refs_0_), channel_id=1, source_target_pairs={{0,24},{8,0},{16,8},{24,16},{1,25},{9,1},{17,9},{25,17},{2,26},{10... | collective-permute-start | bytes 688136 | tf_op jit(solution)/shard_map/ppermute | solution.py:905
  (17 other events, 72.5 us)
Sparse Core Ops, SparseCore 0:
  11.8 49.6 all-gather.4
  63.4 58.5 all-gather.6
  199.3 45.9 reduce-scatter.2
  289.0 39.9 reduce-scatter.4

commit v4 on v3

--- a/solution.py
+++ b/solution.py
@@ -61,7 +61,8 @@
     at = slice(2 * ROWS + 1, 2 * ROWS + 2)
     for n, vector in enumerate((mg, ms)):
         pk[at, 128 * n : 128 * n + 128] = vector[...]
-    pk[at, 256:768] = ub[...]
+    for n in range(4):
+        pk[at, 256 + 128 * n : 384 + 128 * n] = ub[n : n + 1, :]
 
 
 def pack_inputs(scalars, tok, seg, weights, vectors):
@@ -73,7 +74,7 @@
         out_specs=(VMEM_SPEC,) * 2,
         out_shape=(shape((CHUNK + 16, 1024), BF), shape((PACK, 1024), BF)),
         compiler_params=PARAMS,
-    )(scalars, tok, seg, *weights, *[v[None] for v in vectors])
+    )(scalars, tok, seg, *weights, *[v.reshape(-1, 128) for v in vectors])
 
 
 def segment_setup(rows, segc, ends):
@@ -119,6 +120,7 @@
     kt,
     xall,
     segr,
+    valid,
     vt,
     acc,
     scores,
@@ -141,6 +143,7 @@
         pl.when(z == end)(partial(place, k, far))
         pl.when(z != end)(partial(place, k, usual))
     segment_setup(segr, segc, ends)
+    valid[...] = (segc[z] != SEGS - 1).astype(F32)
     weight = w[...].reshape(SHARDS * ROWS, 3 * WIDE)
     first = small[2 * z].astype(F32)
     second = small[2 * z + 1].astype(F32)
@@ -229,6 +232,7 @@
             shape((WIDE, 4 * CHUNK), BF),
             shape((4, CHUNK, 1024), BF),
             shape((4, 8, CHUNK), F32),
+            shape((CHUNK, 128), F32),
         ),
         grid=(1,),
         in_specs=[SMEM_SPEC] + [any_spec((CHUNK + 16, 1024))] * 5 + [QKV_SPEC, SMALL_SPEC],
@@ -241,6 +245,7 @@
             any_spec((WIDE, 4 * CHUNK)),
             any_spec((4, CHUNK, 1024)),
             any_spec((4, 8, CHUNK)),
+            any_spec((CHUNK, 128)),
         ),
         scratch_shapes=[
             pltpu.VMEM((WIDE, 4 * CHUNK), BF),
@@ -300,7 +305,7 @@
         low[rows, :] = y.astype(BF)
         scaled[rows, :] = n
         inv[rows, :] = jnp.broadcast_to(inverse, (TILE, 128))
-        ok = valid[rows, :]
+        ok = valid[rows, 0:1]
         return carry[0] + eight(ok * x * x), carry[1] + eight(ok * branch * branch)
 
     zero = jnp.zeros((8, 1024), F32)
@@ -313,7 +318,7 @@
         lane == 0,
         jnp.sum(stream),
         jnp.where(
-            lane == 1, jnp.sum(branch), jnp.where(lane == 3, jnp.sum(valid[...]), 0.0)
+            lane == 1, jnp.sum(branch), jnp.where(lane == 3, jnp.sum(valid[:, 0:1]), 0.0)
         ),
     )
 
@@ -336,7 +341,7 @@
         ),
         in_specs=[SMEM_SPEC, full(CHUNK, 1024)]
         + [full(CHUNK, WIDE)] * 4
-        + [OUT_SPEC, SMALL_SPEC, full(CHUNK, 1)],
+        + [OUT_SPEC, SMALL_SPEC, full(CHUNK, 128)],
         out_specs=(
             full(CHUNK, 1024),
             full(CHUNK, 1024),
@@ -351,7 +356,7 @@
     )(scalars, tok, *parts, pack, pack, valid)
 
 
-UP_SPECS = [pl.BlockSpec((ROWS, 512), lambda j: (0, j))] * SHARDS
+UP_SPECS = [pl.BlockSpec((ROWS, 1024), lambda j: (0, j))] * SHARDS
 
 
 def gate_kernel(low, low_rel, mixed, *refs):
@@ -359,14 +364,17 @@
     small, acts, slope, pre = refs[SHARDS:]
     j = pl.program_id(0)
     pre[...] = dot(low_rel[...], jnp.concatenate([u[...] for u in ups]))
-    bias = small[j, 1:2, 256:768].astype(F32)
-    cols = pl.ds(pl.multiple_of((j % 2) * 512, 512), 512)
+    bias = jnp.concatenate(
+        [small[2 * j + n, 1:2, 256:768].astype(F32) for n in range(2)], axis=1
+    )
     for t in range(CHUNK // TILE):
         rows = slice(TILE * t, TILE * t + TILE)
-        gate = pre[rows, :] + bias
-        cdf = 0.5 * (1.0 + lax.erf(gate * (2.0 ** -0.5)))
-        acts[j // 2, rows, cols] = (gate * cdf).astype(BF)
-        slope[rows, :] = cdf + gate * (jnp.exp(-0.5 * gate * gate) * 0.3989422804014327)
+        for n in range(2):
+            cols = slice(512 * n, 512 * n + 512)
+            gate = pre[rows, cols] + bias[:, cols]
+            cdf = 0.5 * (1.0 + lax.erf(gate * (2.0 ** -0.5)))
+            acts[j, rows, cols] = (gate * cdf).astype(BF)
+            slope[rows, cols] = cdf + gate * (jnp.exp(-0.5 * gate * gate) * 0.3989422804014327)
 
     @pl.when(j == 0)
     def _():
@@ -380,11 +388,11 @@
     return pl.pallas_call(
         gate_kernel,
         name="mlp_gate",
-        grid=(SHARDS,),
+        grid=(4,),
         out_shape=(shape((6, CHUNK, 1024), BF), shape((CHUNK, 4096), F32)),
         in_specs=[full(CHUNK, 1024)] * 3 + UP_SPECS + [SMALL_SPEC],
-        out_specs=(full(6, CHUNK, 1024), pl.BlockSpec((CHUNK, 512), lambda j: (0, j))),
-        scratch_shapes=[pltpu.VMEM((CHUNK, 512), F32)],
+        out_specs=(full(6, CHUNK, 1024), pl.BlockSpec((CHUNK, 1024), lambda j: (0, j))),
+        scratch_shapes=[pltpu.VMEM((CHUNK, 1024), F32)],
         compiler_params=PARAMS,
     )(low, low_rel, mixed, *ups, pack)
 
@@ -435,13 +443,15 @@
         for copy in copies:
             copy.start()
 
-    @pl.when(s < 4)
+    @pl.when(s < 2)
     def _():
         hidden = jnp.concatenate([acts[b] for b in range(4)], axis=1)
-        cols = pl.ds(pl.multiple_of(jnp.minimum(s, 3) * 256, 256), 256)
-        acc[:, cols] = dot(hidden, down_cols[...].reshape(4096, 256))
-
-    @pl.when(s == 3)
+        for n in range(2):
+            cols = pl.ds(pl.multiple_of(jnp.minimum(s, 1) * 512 + 256 * n, 256), 256)
+            part = down_cols[:, :, 256 * n : 256 * n + 256].reshape(4096, 256)
+            acc[:, cols] = dot(hidden, part)
+
+    @pl.when(s == 1)
     def _():
         for copy in copies[0:2]:
             copy.wait()
@@ -452,7 +462,7 @@
             branch = acc[rows, :] + bias
             unit, inverse = normalise(normed[rows, :] + branch)
             out[rows, :] = (unit * gain + shift_by).astype(BF)
-            ok = valid[rows, :]
+            ok = valid[rows, 0:1]
             u = cot[rows, :].astype(F32) * ok
             g = norm_pullback(u, unit, inverse, gain)
             gh2[rows, :] = g
@@ -468,39 +478,44 @@
         lane = lax.broadcasted_iota(jnp.int32, (8, 128), 1)
         stats[...] = jnp.where(lane == 2, jnp.sum(totals[3]), 0.0)
 
-    @pl.when((s >= 4) & (s < 12))
+    @pl.when((s >= 2) & (s < 6))
     def _():
-        j = jnp.clip(s - 4, 0, SHARDS - 1)
-        pre[...] = dot(gm[...], down_rows[...].reshape(512, 1024), ((1,), (1,)))
-        cols = pl.ds(pl.multiple_of((j % 2) * 512, 512), 512)
-        total_ub = jnp.zeros((8, 512), F32)
-        for t in range(CHUNK // TILE):
-            rows = slice(TILE * t, TILE * t + TILE)
-            gg = (pre[rows, :] * slope[rows, :]).astype(BF)
-            gg_all[j // 2, rows, cols] = gg
-            grads[0, rows, cols] = gg
-            total_ub = total_ub + eight(gg.astype(F32))
-        ub[pl.ds(j, 1)] = jnp.sum(total_ub, axis=0, keepdims=True).reshape(1, 1, 512)
-
-    @pl.when(s == 12)
+        j = jnp.clip(s - 2, 0, 3)
+        pre[...] = dot(gm[...], down_rows[...].reshape(1024, 1024), ((1,), (1,)))
+        for n in range(2):
+            cols = slice(512 * n, 512 * n + 512)
+            total_ub = jnp.zeros((8, 512), F32)
+            for t in range(CHUNK // TILE):
+                rows = slice(TILE * t, TILE * t + TILE)
+                gg = (pre[rows, cols] * slope[rows, cols]).astype(BF)
+                gg_all[j, rows, cols] = gg
+                grads[0, rows, cols] = gg
+                total_ub = total_ub + eight(gg.astype(F32))
+            row = jnp.sum(total_ub, axis=0, keepdims=True)
+            for q in range(4):
+                to = pl.ds(pl.multiple_of((2 * j + n) * 128, 128), 128)
+                ub[q : q + 1, to] = row[:, 128 * q : 128 * q + 128]
+
+    @pl.when(s == 6)
     def _():
         grads[0] = gm[...]
         for copy in copies[2:]:
             copy.wait()
 
-    @pl.when(s >= 12)
+    @pl.when(s >= 6)
     def _():
-        j = jnp.clip(s - 12, 0, 3)
-        rows = held[pl.ds(2 * j, 2)].reshape(2 * ROWS, 4096)
         gg = jnp.concatenate([gg_all[b] for b in range(4)], axis=1)
-        part = dot(gg, rows, ((1,), (1,)))
-        pair = jnp.bitwise_xor(sc[1], j)
-        for t in range(2):
-            f = 2 * pair + jnp.bitwise_xor(sc[2], t)
-            to = pl.ds(pl.multiple_of(f * ROWS, ROWS), ROWS)
-            total[:, to] = part[:, ROWS * t : ROWS * t + ROWS]
-
-    @pl.when(s == 15)
+        for m in range(2):
+            j = jnp.clip(2 * (s - 6) + m, 0, 3)
+            rows = held[pl.ds(2 * j, 2)].reshape(2 * ROWS, 4096)
+            part = dot(gg, rows, ((1,), (1,)))
+            pair = jnp.bitwise_xor(sc[1], j)
+            for t in range(2):
+                f = 2 * pair + jnp.bitwise_xor(sc[2], t)
+                to = pl.ds(pl.multiple_of(f * ROWS, ROWS), ROWS)
+                total[:, to] = part[:, ROWS * t : ROWS * t + ROWS]
+
+    @pl.when(s == 7)
     def _():
         gain = vec(small, 0, 384, 128)
 
@@ -529,23 +544,23 @@
 def mlp_tail(scalars, acts, slope, ups, down, normed, scaled, inv, pack, cot, valid):
     shape = jax.ShapeDtypeStruct
     full = lambda *s: any_spec(s)
-    block = lambda s: jnp.clip(s - 4, 0, SHARDS - 1)
+    block = lambda s: jnp.clip(s - 2, 0, 3)
 
     def grads_at(s):
-        return (jnp.where(s < 12, block(s) // 2, jnp.where(s < 15, 5, 4)), 0, 0)
+        return (jnp.where(s < 6, block(s), jnp.where(s < 7, 5, 4)), 0, 0)
 
     return pl.pallas_call(
         mlp_tail_kernel,
         name="mlp_tail",
-        grid=(16,),
+        grid=(8,),
         in_specs=[
             SMEM_SPEC,
             full(4, CHUNK, 1024),
-            pl.BlockSpec((SHARDS, 512, 256), lambda s: (0, 0, jnp.minimum(s, 3))),
-            pl.BlockSpec((1, 512, 1024), lambda s: (block(s), 0, 0)),
-            pl.BlockSpec((CHUNK, 512), lambda s: (0, block(s))),
+            pl.BlockSpec((SHARDS, 512, 512), lambda s: (0, 0, jnp.minimum(s, 1))),
+            pl.BlockSpec((2, 512, 1024), lambda s: (block(s), 0, 0)),
+            pl.BlockSpec((CHUNK, 1024), lambda s: (0, block(s))),
             SMALL_SPEC,
-            full(CHUNK, 1),
+            full(CHUNK, 128),
             full(CHUNK, 128),
         ]
         + [pl.BlockSpec(memory_space=pl.ANY)] * (SHARDS + 4),
@@ -555,7 +570,7 @@
             full(CHUNK, 1024),
         )
         + (full(CHUNK, WIDE),) * 4
-        + (full(8, 1024), full(8, 128), full(8, 1024), full(SHARDS, 1, 512)),
+        + (full(8, 1024), full(8, 128), full(8, 1024), full(4, 1024)),
         out_shape=(
             shape((CHUNK, 1024), BF),
             shape((6, CHUNK, 1024), BF),
@@ -566,14 +581,14 @@
             shape((8, 1024), F32),
             shape((8, 128), F32),
             shape((8, 1024), F32),
-            shape((SHARDS, 1, 512), F32),
+            shape((4, 1024), F32),
         ),
         scratch_shapes=[
             pltpu.VMEM((CHUNK, 1024), F32),
             pltpu.VMEM((CHUNK, 1024), F32),
             pltpu.VMEM((CHUNK, 1024), BF),
             pltpu.VMEM((4, CHUNK, 1024), BF),
-            pltpu.VMEM((CHUNK, 512), F32),
+            pltpu.VMEM((CHUNK, 1024), F32),
             pltpu.VMEM((CHUNK, 1024), F32),
             pltpu.VMEM((SHARDS, ROWS, 4096), BF),
             pltpu.VMEM((CHUNK, 1024), F32),
@@ -698,7 +713,6 @@
 
 def attn_bwd_kernel(
     sc,
-    xall,
     segr,
     w,
     qm,
@@ -710,14 +724,8 @@
     g1,
     g2,
     g3,
-    sums_m,
-    sums_a,
-    ubt,
-    stats_a,
-    stats_m,
     ig,
-    gw_out,
-    small,
+    dall,
     segc,
     ends,
     gs,
@@ -726,8 +734,6 @@
     dk,
     dv,
     delta,
-    dall,
-    gw,
     scores,
     slopes,
     probs,
@@ -785,6 +791,21 @@
     lax.fori_loop(0, 4, q_chunk, 0)
     dall[:, WIDE : 2 * WIDE] = dk[...].astype(BF)
     dall[:, 2 * WIDE :] = dv[...].astype(BF)
+    weight = w[...].reshape(SHARDS * ROWS, 3 * WIDE)
+    for k in range(4):
+        rows = slice(CHUNK * k, CHUNK * k + CHUNK)
+        ig[rows, :] = dot(dall[rows, :], weight, ((1,), (1,))).astype(BF)
+
+
+def qkv_kernel(sc, xall, dall, sums_m, sums_a, ubt, stats_a, stats_m, out, small, acc):
+    z = sc[0]
+    for k in range(4):
+        part = dot(xall[k], dall[CHUNK * k : CHUNK * k + CHUNK, :], ((0,), (0,)))
+        if k == 0:
+            acc[...] = part
+        else:
+            acc[...] += part
+    out[:, 0 : 3 * WIDE] = acc[...].astype(BF)
     here = pl.ds(pl.multiple_of(z * WIDE, WIDE), WIDE)
     small[...] = jnp.zeros_like(small)
     small[0:3, :] = sums_m[0:3, :]
@@ -800,30 +821,30 @@
     high = jnp.floor(count * 0.0625)
     small[15:16, :] = every(high)
     small[16:17, :] = every(count - 16.0 * high)
-    gw_out[:, 3 * WIDE :] = jnp.transpose(small[...]).astype(BF)
-    weight = w[...].reshape(SHARDS * ROWS, 3 * WIDE)
-    for k in range(4):
-        rows = slice(CHUNK * k, CHUNK * k + CHUNK)
-        d = dall[rows, :]
-        ig[rows, :] = dot(d, weight, ((1,), (1,))).astype(BF)
-        part = dot(xall[k], d, ((0,), (0,)))
-        if k == 0:
-            gw[...] = part
-        else:
-            gw[...] += part
-    gw_out[:, 0 : 3 * WIDE] = gw[...].astype(BF)
-
-
-def attn_bwd(scalars, xall, segr, pack, qm, kv, kt, mixt, lse, gs, smalls):
+    out[:, 3 * WIDE :] = jnp.transpose(small[...]).astype(BF)
+
+
+def qkv_grads(scalars, xall, dall, smalls):
+    return pl.pallas_call(
+        qkv_kernel,
+        name="qkv_grads",
+        out_shape=jax.ShapeDtypeStruct((1024, 3 * WIDE + 128), BF),
+        in_specs=[SMEM_SPEC] + [VMEM_SPEC] * 7,
+        out_specs=VMEM_SPEC,
+        scratch_shapes=[pltpu.VMEM((128, 1024), F32), pltpu.VMEM((1024, 3 * WIDE), F32)],
+        compiler_params=PARAMS,
+    )(scalars, xall, dall, *smalls)
+
+
+def attn_bwd(scalars, segr, pack, qm, kv, kt, mixt, lse, gs):
     shape = jax.ShapeDtypeStruct
     return pl.pallas_call(
         attn_bwd_kernel,
         name="attn_bwd",
-        out_shape=(shape((1024, 1024), BF), shape((1024, 3 * WIDE + 128), BF)),
+        out_shape=(shape((1024, 1024), BF), shape((1024, 3 * WIDE), BF)),
         grid=(1,),
         in_specs=[SMEM_SPEC]
         + [
-            any_spec((4, CHUNK, 1024)),
             any_spec((4, 8, CHUNK)),
             QKV_SPEC,
             any_spec((HERE, 4 * CHUNK, 128)),
@@ -832,12 +853,9 @@
             any_spec((WIDE, 4 * CHUNK)),
             any_spec((8, 4 * CHUNK)),
         ]
-        + [any_spec((CHUNK, WIDE))] * 4
-        + [any_spec((8, 1024)), any_spec((8, 1024)), any_spec((4, 1024))]
-        + [any_spec((8, 128))] * 2,
-        out_specs=(any_spec((1024, 1024)), any_spec((1024, 3 * WIDE + 128))),
+        + [any_spec((CHUNK, WIDE))] * 4,
+        out_specs=(any_spec((1024, 1024)), any_spec((1024, 3 * WIDE))),
         scratch_shapes=[
-            pltpu.VMEM((128, 1024), F32),
             pltpu.VMEM((4, CHUNK, 128), F32),
             pltpu.SMEM((2, 4), jnp.int32),
             pltpu.VMEM((HERE, 4 * CHUNK, 128), BF),
@@ -846,15 +864,13 @@
             pltpu.VMEM((4 * CHUNK, WIDE), F32),
             pltpu.VMEM((4 * CHUNK, WIDE), F32),
             pltpu.VMEM((8, 4 * CHUNK), F32),
-            pltpu.VMEM((4 * CHUNK, 768), BF),
-            pltpu.VMEM((1024, 768), F32),
             pltpu.VMEM((HERE, CHUNK, CHUNK), F32),
             pltpu.VMEM((HERE, CHUNK, CHUNK), F32),
             pltpu.VMEM((HERE, CHUNK, CHUNK), BF),
             pltpu.VMEM((HERE, CHUNK, CHUNK), BF),
         ],
         compiler_params=PARAMS,
-    )(scalars, xall, segr, pack, qm, kv, kt, mixt, lse, *gs, *smalls)
+    )(scalars, segr, pack, qm, kv, kt, mixt, lse, *gs)
 
 
 def finish_kernel(sc, *refs):
@@ -993,12 +1009,12 @@
         xs = line_gather(packed)
         xs.append(line_forward(xs[3]))
         near_x, near_y = swap(up_weight, 2), swap(up_weight, 4)
+        half = up_weight.shape[1] // 2
+        far = [swap(near_x[:, :half], 4), swap(near_y[:, half:], 2)]
         xs, near_x, near_y, after, pack = lax.optimization_barrier(
             (xs, near_x, near_y, down_weight, pack)
         )
         down = lax.all_gather(after, "fsdp", axis=0)
-        half = up_weight.shape[1] // 2
-        far = [swap(near_x[:, :half], 4), swap(near_y[:, half:], 2)]
     else:
         seg_row = jnp.pad(segment_ids.astype(BF), ((0, 15), (0, 1024 - CHUNK)))
         packed = jnp.concatenate([tok, seg_row])
@@ -1025,14 +1041,15 @@
         pack = jnp.concatenate([out_rows, wide(pack)], axis=1)
         ups = list(whole(up_weight).reshape(SHARDS, ROWS, 4096))
         down = whole(down_weight).reshape(SHARDS, 512, 1024)
-    valid = (segment_ids[0] != SEGS - 1).astype(F32)[:, None]
-
-    m0, m1, m2, m3, mixt, lse, qm, kv, kt, xall, segr = attn_fwd(scalars, xs, pack)
+
+    m0, m1, m2, m3, mixt, lse, qm, kv, kt, xall, segr, valid = attn_fwd(scalars, xs, pack)
     parts = [m0] + [shift(m, -k) for k, m in ((1, m1), (2, m2), (3, m3))]
     if plane:
         ups = [up_weight, swap(up_weight, 1)]
+        far, _ = lax.optimization_barrier((far, m0))
+        far = jnp.concatenate(far, axis=1)
         parts, near_x, near_y, far = lax.optimization_barrier((parts, near_x, near_y, far))
-        for rows in (near_x, near_y, jnp.concatenate(far, axis=1)):
+        for rows in (near_x, near_y, far):
             ups += [rows, swap(rows, 1)]
     normed, low, low_rel, scaled, inv, mixed, stats_a = out_project(
         scalars, tok, parts, pack, valid
@@ -1051,27 +1068,32 @@
     gs, r3, r1, r2, r0 = lax.optimization_barrier((gs, r3, r1, r2, r0))
     if plane:
         r_far = swap(r3, 4)
-    smalls = (sums_m, sums_a, ub.reshape(1024, 4).T, stats_a, stats_m)
-    ig, gw = attn_bwd(scalars, xall, segr, pack, qm, kv, kt, mixt, lse, gs, smalls)
+    if not plane:
+        ub = ub.reshape(4, SHARDS, 128).swapaxes(0, 1).reshape(1024, 4).T
+    smalls = (sums_m, sums_a, ub, stats_a, stats_m)
+    ig, dall = attn_bwd(scalars, segr, pack, qm, kv, kt, mixt, lse, gs)
     tie = lax.optimization_barrier
     if plane:
-        ig, gw, d_far, r_far = tie((ig, gw, d_far, r_far))
+        ig, dall, d_far, r_far = tie((ig, dall, d_far, r_far))
     ig = lax.psum_scatter(ig, "ctx", scatter_dimension=0, tiled=True)
     if plane:
-        to_y, to_x = add(d2, d_far).astype(BF), add(r1, r_far).astype(BF)
-        to_y, to_x, d1, r2 = tie((to_y, to_x, d1, r2))
+        to_x = add(r1, r_far).astype(BF)
+        to_x, r2, dall, d_far = tie((to_x, r2, dall, d_far))
         r_from_x, r_from_y = swap(to_x, 2), swap(r2, 4)
+    gw = qkv_grads(scalars, xall, dall, smalls)
+    if plane:
+        to_y = add(d2, d_far).astype(BF)
+        r_sum = LineSum(r0, r_from_x, r_from_y)
+        r_first, gw, to_y, d1 = tie((r_sum.first(), gw, to_y, d1))
         d_from_x, d_from_y = swap(d1, 2), swap(to_y, 4)
-        r_sum = LineSum(r0, r_from_x, r_from_y)
-        got_r = neighbour(r_sum.first(), 1)
-        ig, gw, _ = tie((ig, gw, got_r))
+        got_r = neighbour(r_first, 1)
+        ig, gw, d_from_x, d_from_y, got_r = tie((ig, gw, d_from_x, d_from_y, got_r))
     q_own = lax.psum_scatter(gw, "fsdp", scatter_dimension=0, tiled=True)
     q_low = q_own.astype(BF)
 
     if plane:
-        r_second = r_sum.second(got_r)
-        got_r = neighbour(r_second, 2)
-        d_from_x, d_from_y, _ = tie((d_from_x, d_from_y, r_second))
+        d_from_x, d_from_y, got_r = tie((d_from_x, d_from_y, got_r))
+        got_r = neighbour(r_sum.second(got_r), 2)
         d_sum = LineSum(d0, d_from_x, d_from_y)
         got = neighbour(d_sum.first(), 1)
         r_third = r_sum.third(got_r)
@@ -1081,6 +1103,7 @@
         got = neighbour(d_second, 2)
         q_low, _ = tie((q_low, d_second))
         q_pieces = [q_low] + [shift(q_low, k) for k in (1, 2, 3)]
+        got, got_r, q_pieces = tie((got, got_r, q_pieces))
         rest = r_sum.result(got_r)
         grad_down = d_sum.result(neighbour(d_sum.third(got), 1))
         input_grad = add(gh1, ig)
@@ -1115,7 +1138,7 @@
         done = finish(scalars, q_pieces)
         grad_q, grad_k, grad_v = done[0:3]
         vectors = [v.reshape(-1) for v in done[3:11]]
-        up_bias_grad = done[11].T.reshape(-1)
+        up_bias_grad = done[11].reshape(-1)
         rms = [v.reshape(()) for v in done[12:15]]
     else:
         table = jnp.take(jnp.stack(q_pieces), (z - jnp.arange(4)) % 4, axis=0)

time: 365 us -> 348 us (0.953)
  waiting for transfers between devices: 176 us -> 164 us
  starting transfers between devices: 43 us -> 51.6 us
  local copies, waits for them, and re-layouts: 11.6 us -> 3.84 us
  Pallas kernels: 99.6 us -> 94.3 us
    ppermute x9, waiting for transfers between devices: 25.9 us -> 13.2 us  [shift(): return lax.ppermute(x, 'ctx', [(i, (i + k) % n) for i in range(n)])]
    ppermute x6, starting transfers between devices: 8.57 us -> 14.5 us  [neighbour(): return lax.ppermute(x, 'ctx', [(i, i ^ bits) for i in range(4)])]
    ppermute x16, waiting for transfers between devices: 37.2 us -> 33 us  [swap(): lax.ppermute(x, 'fsdp', [(i, i ^ bits) for i in range(lax.axis_size('fsdp...]
    pallas_call x2 -> x3, Pallas kernels: 38.4 us -> 35.7 us  [the longest x1 20.6 us: mlp_tail(): pl.pallas_call(mlp_tail_kernel, name='mlp_tail', grid=(8,), in_specs=[SME...]
  transfers between devices with their start and end apart: 39 -> 39, of which waited for: 20 -> 21; matrix products, arithmetic and copies ran while one was open for 6% -> 5% of each run, Pallas kernels for 26% -> 26%
where the time goes in v4:
time: 348 us; the launch traced here: 347 us
  waiting for transfers between devices  164 us (47%)
  Pallas kernels  94.3 us (27%)
  starting transfers between devices  51.6 us (15%)
  other arithmetic  19.5 us (6%)
  between operations  14.2 us (4%)
  local copies, waits for them, and re-layouts  3.84 us (1%)
    ppermute x6, waiting for transfers between devices, neighbour(): return lax.ppermute(x, 'ctx', [(i, i ^ bits) for i in range(4)])  71.8 us
    ppermute x16, waiting for transfers between devices, swap(): lax.ppermute(x, 'fsdp', [(i, i ^ bits) for i in range(lax.axis_size('fsdp...  33 us
    pallas_call x1, Pallas kernels, mlp_tail(): pl.pallas_call(mlp_tail_kernel, name='mlp_tail', grid=(8,), in_specs=[SME...  20.6 us
    ppermute x1, waiting for transfers between devices, line_gather(): two = lax.ppermute(x, 'ctx', [(0, 2), (1, 3), (2, 0), (3, 1)])  17.8 us
    pallas_call x1, Pallas kernels, attn_bwd(): pl.pallas_call(attn_bwd_kernel, name='attn_bwd', out_shape=(shape((1024,...  16.1 us
    pallas_call x1, Pallas kernels, attn_fwd(): pl.pallas_call(attn_fwd_kernel, name='attn_fwd', out_shape=(shape((CHUNK,...  15.2 us
    ppermute x6, starting transfers between devices, neighbour(): return lax.ppermute(x, 'ctx', [(i, i ^ bits) for i in range(4)])  14.5 us
    ppermute x9, starting transfers between devices, shift(): return lax.ppermute(x, 'ctx', [(i, (i + k) % n) for i in range(n)])  13.6 us
  transfers between devices with their start and end apart: 39, of which 21 were waited for; matrix products, arithmetic and copies ran while one was open for 5% of the time, Pallas kernels for 26%

profile of v4, /device:TPU:0, one launch (start us, length us, event | category | flops | bytes accessed | tf_op | source)
XLA Modules:
  0.0 347.0 jit_solution(14277448699896459374)
XLA Ops:
  7.9 2.5 pack_inputs.1
  10.4 4.1 %collective-permute-start.2 = (bf16[272,1024]{1,0:T(8,128)(2,1)}, bf16[272,1024]{1,0:T(8,128)(2,1)S(1)}, u32[]{:S(2)}, u32[]{:S(2)}) collective-permute-start(bf16[272,1024]{1,0:T(8,128)(2,1)} %get-tuple-element.135.x0), channel_id=1, source_target_pairs={{0,16},{8,24},{16,0},{24,8},{1,17},{9,25},{17,1},{25,9},{2,18},{10... | collective-permute-start | bytes 1671176 | tf_op jit(solution)/shard_map/ppermute | solution.py:911
  14.5 1.5 collective-permute-start.4
  16.0 1.5 collective-permute-start.5
  17.6 3.5 %collective-permute-start = (bf16[272,1024]{1,0:T(8,128)(2,1)}, bf16[272,1024]{1,0:T(8,128)(2,1)S(1)}, u32[]{:S(2)}, u32[]{:S(2)}) collective-permute-start(bf16[272,1024]{1,0:T(8,128)(2,1)} %get-tuple-element.135.x0), channel_id=1, source_target_pairs={{0,8},{8,16},{16,24},{1,9},{9,17},{17,25},{2,10},{10,18},{18,26},{... | collective-permute-start | bytes 1671176 | tf_op jit(solution)/shard_map/ppermute | solution.py:909
  22.4 17.8 %collective-permute-done.2.x2 = bf16[272,1024]{1,0:T(8,128)(2,1)S(1)} collective-permute-done((bf16[272,1024]{1,0:T(8,128)(2,1)}, bf16[272,1024]{1,0:T(8,128)(2,1)S(1)}, u32[]{:S(2)}, u32[]{:S(2)}) %collective-permute-start.2) | collective-permute-done | bytes 557088 | tf_op jit(solution)/shard_map/ppermute | solution.py:911
  41.5 8.0 %collective-permute-done.1.left = bf16[272,1024]{1,0:T(8,128)(2,1)S(1)} collective-permute-done((bf16[272,1024]{1,0:T(8,128)(2,1)}, bf16[272,1024]{1,0:T(8,128)(2,1)S(1)}, u32[]{:S(2)}, u32[]{:S(2)}) %collective-permute-start.1) | collective-permute-done | bytes 557088 | tf_op jit(solution)/shard_map/ppermute | solution.py:910
  49.5 2.1 collective-permute-done.5.refs_4_.refs_8_
  51.6 7.6 %collective-permute-done.3.far = bf16[272,1024]{1,0:T(8,128)(2,1)} collective-permute-done((bf16[272,1024]{1,0:T(8,128)(2,1)S(1)}, bf16[272,1024]{1,0:T(8,128)(2,1)}, u32[]{:S(2)}, u32[]{:S(2)}) %collective-permute-start.3) | collective-permute-done | bytes 557088 | tf_op jit(solution)/shard_map/ppermute | solution.py:916
  61.8 1.5 collective-permute-start.9
  63.3 15.2 %attn_fwd.1 = (bf16[256,256]{1,0:T(8,128)(2,1)}, bf16[256,256]{1,0:T(8,128)(2,1)}, bf16[256,256]{1,0:T(8,128)(2,1)}, bf16[256,256]{1,0:T(8,128)(2,1)}, f32[256,1...) custom-call(s32[4]{0:T(128)} %pad_add_fusion.sc, ...), custom_call_target="tpu_custom_call" | custom-call | tf_op jit(solution)/shard_map/attn_fwd/pallas_call | solution.py:223
  78.7 2.6 collective-permute-done.9
  81.3 2.9 collective-permute-start.7
  85.5 2.8 collective-permute-done.6.r1
  88.3 5.1 %collective-permute-done.7.r2 = bf16[256,256]{1,0:T(8,128)(2,1)S(1)} collective-permute-done((bf16[256,256]{1,0:T(8,128)(2,1)}, bf16[256,256]{1,0:T(8,128)(2,1)S(1)}, u32[]{:S(2)}, u32[]{:S(2)}) %collective-permute-start.7) | collective-permute-done | bytes 131104 | tf_op jit(solution)/shard_map/ppermute | solution.py:921
  94.1 5.6 %out_project.1 = (f32[256,1024]{1,0:T(8,128)}, bf16[256,1024]{1,0:T(8,128)(2,1)}, bf16[256,1024]{1,0:T(8,128)(2,1)}, f32[256,1024]{1,0:T(8,128)}, f32[256,128]{1...) custom-call(s32[4]{0:T(128)} %pad_add_fusion.sc, bf16[256,1024]{1,0:T(8,128)(2,1)} %bitcast.42, ...), custom_call_target="tpu_custom_call" | custom-call | tf_op jit(solution)/shard_map/out_project/pallas_call | solution.py:329
  99.8 9.6 %mlp_gate.1 = (bf16[6,256,1024]{2,1,0:T(8,128)(2,1)}, f32[256,4096]{1,0:T(8,128)}) custom-call(bf16[256,1024]{1,0:T(8,128)(2,1)} %get-tuple-element.154.low, bf16[256,1024]{1,0:T(8,128)(2,1)} %get-tuple-element.155.low_rel, bf16[256,1024]{1,0:T(8,128)(2,1)} %get-tuple-element.156.mixed, bf16[128,4096]{1,0:T(8,128)(2,1)} %refs_4_.1, ...), custom_call_target="tpu_custom_call" | custom-call | tf_op jit(solution)/shard_map/mlp_gate/pallas_call | solution.py:388
  110.0 8.4 %all-gather.7.cloned.1.call-done = bf16[4096,1024]{1,0:T(8,128)(2,1)} async-done(((bf16[512,1024]{1,0:T(8,128)(2,1)}), bf16[4096,1024]{1,0:T(8,128)(2,1)}) %all-gather.7.cloned.1.call-update) | async-done | bytes 8388624 | tf_op jit(solution)/shard_map/all_gather | solution.py:1017
  118.4 20.6 %mlp_tail.1 = (bf16[256,1024]{1,0:T(8,128)(2,1)}, bf16[6,256,1024]{2,1,0:T(8,128)(2,1)}, f32[256,1024]{1,0:T(8,128)}, bf16[256,256]{1,0:T(8,128)(2,1)}, bf16[256...) custom-call(s32[4]{0:T(128)} %pad_add_fusion.sc, ...), custom_call_target="tpu_custom_call" | custom-call | tf_op jit(solution)/shard_map/mlp_tail/pallas_call | solution.py:552
  140.8 2.4 collective-permute-start.16
  146.4 8.9 %rest_grads.1 = (bf16[640,1024]{1,0:T(8,128)(2,1)}, bf16[640,1024]{1,0:T(8,128)(2,1)}, bf16[640,1024]{1,0:T(8,128)(2,1)}, bf16[640,1024]{1,0:T(8,128)(2,1)}) custom-call(s32[4]{0:T(128)} %pad_add_fusion.sc, bf16[6,256,1024]{2,1,0:T(8,128)(2,1)} %get-tuple-element.160.acts.lo.ho, bf16[6,256,1024]{2,1,0:T(8,128)(2,1)} %copy-done, ...), custom_call_target="tpu_custom_call" | custom-call | tf_op jit(solution)/shard_map/rest_grads/pallas_call | solution.py:694
  156.6 7.7 %down_grads.1 = (bf16[512,1024]{1,0:T(8,128)(2,1)}, bf16[512,1024]{1,0:T(8,128)(2,1)}, bf16[512,1024]{1,0:T(8,128)(2,1)}, bf16[512,1024]{1,0:T(8,128)(2,1)}) custom-call(s32[4]{0:T(128)} %pad_add_fusion.sc, bf16[6,256,1024]{2,1,0:T(8,128)(2,1)} %get-tuple-element.160.acts.lo.ho, bf16[6,256,1024]{2,1,0:T(8,128)(2,1)} %copy-done, ...), custom_call_target="tpu_custom_call" | custom-call | tf_op jit(solution)/shard_map/down_grads/pallas_call | solution.py:646
  165.3 16.1 %attn_bwd.1 = (bf16[1024,1024]{1,0:T(8,128)(2,1)}, bf16[1024,768]{1,0:T(8,128)(2,1)}) custom-call(s32[4]{0:T(128)} %pad_add_fusion.sc, f32[4,8,256]{2,1,0:T(8,128)} %get-tuple-element.168.segr, bf16[8,272,1024]{2,1,0:T(8,128)(2,1)} %bitcast.38, bf16[4,1024,128]{2,1,0:T(8,128)(2,1)} %get-tuple-element.169.qm, bf16[1024,512]{1,0:T(8,128)(2,1)} %get-tuple-element.170.kv, ...), custom_call_target="tpu_custom_call" | custom-call | tf_op jit(solution)/shard_map/attn_bwd/pallas_call | solution.py:841
  181.4 7.5 %collective-permute-done.20 = bf16[512,1024]{1,0:T(8,128)(2,1)} collective-permute-done((bf16[512,1024]{1,0:T(8,128)(2,1)}, bf16[512,1024]{1,0:T(8,128)(2,1)}, u32[]{:S(2)}, u32[]{:S(2)}) %collective-permute-start.20) | collective-permute-done | bytes 1048608 | tf_op jit(solution)/shard_map/ppermute | solution.py:925
  189.0 1.6 add_convert_fusion
  193.0 5.5 %qkv_grads.1 = bf16[1024,896]{1,0:T(8,128)(2,1)} custom-call(s32[4]{0:T(128)} %pad_add_fusion.sc, bf16[4,256,1024]{2,1,0:T(8,128)(2,1)} %get-tuple-element.200.xall, bf16[1024,768]{1,0:T(8,128)(2,1)} %get-tuple-element.201.dall, f32[8,1024]{1,0:T(8,128)} %get-tuple-element.202.sums_m, f32[8,1024]{1,0:T(8,128)} %get-tuple-element.203.sums_a, ...), custom_call_target="tpu_custom_call" | custom-call | tf_op jit(solution)/shard_map/qkv_grads/pallas_call | solution.py:828
  198.5 2.0 add_convert_fusion.1
  200.5 19.2 %collective-permute-done.22 = bf16[640,1024]{1,0:T(8,128)(2,1)S(1)} collective-permute-done((bf16[640,1024]{1,0:T(8,128)(2,1)}, bf16[640,1024]{1,0:T(8,128)(2,1)S(1)}, u32[]{:S(2)}, u32[]{:S(2)}) %collective-permute-start.22) | collective-permute-done | bytes 1310752 | tf_op jit(solution)/shard_map/ppermute | solution.py:925
  224.0 1.7 collective-permute-start.26
  225.7 19.1 %collective-permute-done.26 = bf16[320,1024]{1,0:T(8,128)(2,1)} collective-permute-done((bf16[320,1024]{1,0:T(8,128)(2,1)S(1)}, bf16[320,1024]{1,0:T(8,128)(2,1)}, u32[]{:S(2)}, u32[]{:S(2)}) %collective-permute-start.26) | collective-permute-done | bytes 655392 | tf_op jit(solution)/shard_map/ppermute | solution.py:936
  245.1 1.8 add_convert_fusion.3
  246.8 3.8 %collective-permute-start.28 = (bf16[320,1024]{1,0:T(8,128)(2,1)S(1)}, bf16[320,1024]{1,0:T(8,128)(2,1)}, u32[]{:S(2)}, u32[]{:S(2)}) collective-permute-start(bf16[320,1024]{1,0:T(8,128)(2,1)S(1)} %add_convert_fusion.3), channel_id=1, source_target_pairs={{0,16},{8,24},{16,0},{24,8},{1,17},{9,25},{17,1},{25,9},{2,18},{10... | collective-permute-start | bytes 1966088 | tf_op jit(solution)/shard_map/ppermute | solution.py:936
  250.6 1.6 add_convert_fusion.7
  252.2 1.6 collective-permute-start.27
  253.8 23.7 %collective-permute-done.28 = bf16[320,1024]{1,0:T(8,128)(2,1)} collective-permute-done((bf16[320,1024]{1,0:T(8,128)(2,1)S(1)}, bf16[320,1024]{1,0:T(8,128)(2,1)}, u32[]{:S(2)}, u32[]{:S(2)}) %collective-permute-start.28) | collective-permute-done | bytes 655392 | tf_op jit(solution)/shard_map/ppermute | solution.py:936
  278.9 1.9 add_convert_fusion.6
  280.8 3.1 collective-permute-start.29
  283.9 2.6 reduce-scatter.5.cloned.1.call-done.refs_0_
  286.5 1.5 collective-permute-start.31
  288.0 2.4 collective-permute-start.32
  291.9 2.1 add_bitcast_fusion
  294.0 23.4 %collective-permute-done.29 = bf16[256,1024]{1,0:T(8,128)(2,1)S(1)} collective-permute-done((bf16[256,1024]{1,0:T(8,128)(2,1)S(1)}, bf16[256,1024]{1,0:T(8,128)(2,1)S(1)}, u32[]{:S(2)}, u32[]{:S(2)}) %collective-permute-start.29) | collective-permute-done | bytes 524320 | tf_op jit(solution)/shard_map/ppermute | solution.py:936
  317.4 5.3 %collective-permute-done.32.refs_2_ = bf16[128,896]{1,0:T(8,128)(2,1)S(1)} collective-permute-done((bf16[128,896]{1,0:T(8,128)(2,1)}, bf16[128,896]{1,0:T(8,128)(2,1)S(1)}, u32[]{:S(2)}, u32[]{:S(2)}) %collective-permute-start.32) | collective-permute-done | bytes 229408 | tf_op jit(solution)/shard_map/ppermute | solution.py:921
  323.5 4.3 %collective-permute-start.34 = (bf16[256,1024]{1,0:T(8,128)(2,1)S(1)}, bf16[256,1024]{1,0:T(8,128)(2,1)S(1)}, u32[]{:S(2)}, u32[]{:S(2)}) collective-permute-start(bf16[256,1024]{1,0:T(8,128)(2,1)S(1)} %add_convert_fusion.5), channel_id=1, source_target_pairs={{0,8},{8,0},{16,24},{24,16},{1,9},{9,1},{17,25},{25,17},{2,10},{10... | collective-permute-start | bytes 1572872 | tf_op jit(solution)/shard_map/ppermute | solution.py:936
  329.2 2.5 finish.1
  331.7 1.5 pad_maximum_fusion
  333.2 5.6 %collective-permute-done.34 = bf16[256,1024]{1,0:T(8,128)(2,1)S(1)} collective-permute-done((bf16[256,1024]{1,0:T(8,128)(2,1)S(1)}, bf16[256,1024]{1,0:T(8,128)(2,1)S(1)}, u32[]{:S(2)}, u32[]{:S(2)}) %collective-permute-start.34) | collective-permute-done | bytes 524320 | tf_op jit(solution)/shard_map/ppermute | solution.py:936
  338.9 1.6 maximum_convert_fusion.1
  (103 shorter events, 27.6 us)
Async XLA Ops:
  7.2 53.1 %all-gather.5.cloned.1.call-start = ((), (), s32[]{:S(2)}) async-start(), calls=%async_computation.4 | async-start | bytes 5013504 | tf_op jit(solution)/shard_map/all_gather | solution.py:1008
  10.4 108.0 %all-gather.7.cloned.1.call-start = ((), (), s32[]{:S(2)}) async-start(), calls=%async_computation.5 | async-start | bytes 9437184 | tf_op jit(solution)/shard_map/all_gather | solution.py:1017
  10.4 29.7 %collective-permute-start.2 = (bf16[272,1024]{1,0:T(8,128)(2,1)}, bf16[272,1024]{1,0:T(8,128)(2,1)S(1)}, u32[]{:S(2)}, u32[]{:S(2)}) collective-permute-start(bf16[272,1024]{1,0:T(8,128)(2,1)} %get-tuple-element.135.x0), channel_id=1, source_target_pairs={{0,16},{8,24},{16,0},{24,8},{1,17},{9,25},{17,1},{25,9},{2,18},{10... | collective-permute-start | bytes 1671176 | tf_op jit(solution)/shard_map/ppermute | solution.py:911
  14.5 35.0 %collective-permute-start.4 = (bf16[128,4096]{1,0:T(8,128)(2,1)}, bf16[128,4096]{1,0:T(8,128)(2,1)S(1)}, u32[]{:S(2)}, u32[]{:S(2)}) collective-permute-start(bf16[128,4096]{1,0:T(8,128)(2,1)} %refs_4_.1), channel_id=1, source_target_pairs={{0,2},{1,3},{2,0},{3,1},{4,6},{5,7},{6,4},{7,5},{8,10},{9,11},{10,... | collective-permute-start | bytes 3145736 | tf_op jit(solution)/shard_map/ppermute | solution.py:925
  16.0 35.6 %collective-permute-start.5 = (bf16[128,4096]{1,0:T(8,128)(2,1)}, bf16[128,4096]{1,0:T(8,128)(2,1)S(1)}, u32[]{:S(2)}, u32[]{:S(2)}) collective-permute-start(bf16[128,4096]{1,0:T(8,128)(2,1)} %refs_4_.1), channel_id=1, source_target_pairs={{0,4},{1,5},{2,6},{3,7},{4,0},{5,1},{6,2},{7,3},{8,12},{9,13},{10,... | collective-permute-start | bytes 3145736 | tf_op jit(solution)/shard_map/ppermute | solution.py:925
  17.6 23.9 %collective-permute-start = (bf16[272,1024]{1,0:T(8,128)(2,1)}, bf16[272,1024]{1,0:T(8,128)(2,1)S(1)}, u32[]{:S(2)}, u32[]{:S(2)}) collective-permute-start(bf16[272,1024]{1,0:T(8,128)(2,1)} %get-tuple-element.135.x0), channel_id=1, source_target_pairs={{0,8},{8,16},{16,24},{1,9},{9,17},{17,25},{2,10},{10,18},{18,26},{... | collective-permute-start | bytes 1671176 | tf_op jit(solution)/shard_map/ppermute | solution.py:909
  21.1 28.4 %collective-permute-start.1 = (bf16[272,1024]{1,0:T(8,128)(2,1)}, bf16[272,1024]{1,0:T(8,128)(2,1)S(1)}, u32[]{:S(2)}, u32[]{:S(2)}) collective-permute-start(bf16[272,1024]{1,0:T(8,128)(2,1)} %get-tuple-element.135.x0), channel_id=1, source_target_pairs={{8,0},{16,8},{24,16},{9,1},{17,9},{25,17},{10,2},{18,10},{26,18},{... | collective-permute-start | bytes 1671176 | tf_op jit(solution)/shard_map/ppermute | solution.py:910
  40.2 23.1 %copy-start.7 = (bf16[272,1024]{1,0:T(8,128)(2,1)}, bf16[272,1024]{1,0:T(8,128)(2,1)S(1)}, u32[]{:S(2)}) copy-start(bf16[272,1024]{1,0:T(8,128)(2,1)S(1)} %collective-permute-done.2.x2) | copy-start | bytes 1671172
  40.2 19.0 %collective-permute-start.3 = (bf16[272,1024]{1,0:T(8,128)(2,1)S(1)}, bf16[272,1024]{1,0:T(8,128)(2,1)}, u32[]{:S(2)}, u32[]{:S(2)}) collective-permute-start(bf16[272,1024]{1,0:T(8,128)(2,1)S(1)} %collective-permute-done.2.x2), channel_id=1, source_target_pairs={{8,0},{16,24},{9,1},{17,25},{10,2},{18,26},{11,3},{19,27},{12,4},{... | collective-permute-start | bytes 1671176 | tf_op jit(solution)/shard_map/ppermute | solution.py:916
  41.5 21.8 %copy-start.8 = (bf16[272,1024]{1,0:T(8,128)(2,1)}, bf16[272,1024]{1,0:T(8,128)(2,1)S(1)}, u32[]{:S(2)}) copy-start(bf16[272,1024]{1,0:T(8,128)(2,1)S(1)} %collective-permute-done.right) | copy-start | bytes 1671172
  49.5 43.9 %copy-start.2 = (bf16[128,4096]{1,0:T(8,128)(2,1)}, bf16[128,4096]{1,0:T(8,128)(2,1)S(1)}, u32[]{:S(2)}) copy-start(bf16[128,4096]{1,0:T(8,128)(2,1)S(1)} %collective-permute-done.4.refs_2_.refs_6_) | copy-start | bytes 3145732
  51.6 41.9 %copy-start.3 = (bf16[128,4096]{1,0:T(8,128)(2,1)}, bf16[128,4096]{1,0:T(8,128)(2,1)S(1)}, u32[]{:S(2)}) copy-start(bf16[128,4096]{1,0:T(8,128)(2,1)S(1)} %collective-permute-done.5.refs_4_.refs_8_) | copy-start | bytes 3145732
  60.3 184.7 %reduce-scatter.3.cloned.1.call-start = ((), (), s32[]{:S(2)}) async-start(), calls=%async_computation.2 | async-start | bytes 2621440 | tf_op jit(solution)/shard_map/reduce_scatter | solution.py:1078
  60.4 18.4 %collective-permute-start.10 = (bf16[128,2048]{1,0:T(8,128)(2,1)S(1)}, bf16[128,2048]{1,0:T(8,128)(2,1)}, u32[]{:S(2)}, u32[]{:S(2)}) collective-permute-start(bf16[128,2048]{1,0:T(8,128)(2,1)S(1)} %slice.29), channel_id=1, source_target_pairs={{0,2},{1,3},{2,0},{3,1},{4,6},{5,7},{6,4},{7,5},{8,10},{9,11},{10,... | collective-permute-start | bytes 1572872 | tf_op jit(solution)/shard_map/ppermute | solution.py:925
  61.8 19.5 %collective-permute-start.9 = (bf16[128,2048]{1,0:T(8,128)(2,1)}, bf16[128,2048]{1,0:T(8,128)(2,1)}, u32[]{:S(2)}, u32[]{:S(2)}) collective-permute-start(bf16[128,2048]{1,0:T(8,128)(2,1)} %slice.28), channel_id=1, source_target_pairs={{0,4},{1,5},{2,6},{3,7},{4,0},{5,1},{6,2},{7,3},{8,12},{9,13},{10,... | collective-permute-start | bytes 1572872 | tf_op jit(solution)/shard_map/ppermute | solution.py:925
  63.3 36.5 %collective-permute-start.11 = (bf16[128,4096]{1,0:T(8,128)(2,1)}, bf16[128,4096]{1,0:T(8,128)(2,1)}, u32[]{:S(2)}, u32[]{:S(2)}) collective-permute-start(bf16[128,4096]{1,0:T(8,128)(2,1)} %refs_4_.1), channel_id=1, source_target_pairs={{0,1},{1,0},{2,3},{3,2},{4,5},{5,4},{6,7},{7,6},{8,9},{9,8},{10,11... | collective-permute-start | bytes 3145736 | tf_op jit(solution)/shard_map/ppermute | solution.py:925
  81.3 7.0 %collective-permute-start.6 = (bf16[256,256]{1,0:T(8,128)(2,1)}, bf16[256,256]{1,0:T(8,128)(2,1)S(1)}, u32[]{:S(2)}, u32[]{:S(2)}) collective-permute-start(bf16[256,256]{1,0:T(8,128)(2,1)} %get-tuple-element.142), channel_id=1, source_target_pairs={{0,24},{8,0},{16,8},{24,16},{1,25},{9,1},{17,9},{25,17},{2,26},{10... | collective-permute-start | bytes 393224 | tf_op jit(solution)/shard_map/ppermute | solution.py:921
  81.3 12.1 %collective-permute-start.7 = (bf16[256,256]{1,0:T(8,128)(2,1)}, bf16[256,256]{1,0:T(8,128)(2,1)S(1)}, u32[]{:S(2)}, u32[]{:S(2)}) collective-permute-start(bf16[256,256]{1,0:T(8,128)(2,1)} %get-tuple-element.143), channel_id=1, source_target_pairs={{0,16},{8,24},{16,0},{24,8},{1,17},{9,25},{17,1},{25,9},{2,18},{10... | collective-permute-start | bytes 393224 | tf_op jit(solution)/shard_map/ppermute | solution.py:921
  84.2 9.2 %collective-permute-start.8 = (bf16[256,256]{1,0:T(8,128)(2,1)}, bf16[256,256]{1,0:T(8,128)(2,1)S(1)}, u32[]{:S(2)}, u32[]{:S(2)}) collective-permute-start(bf16[256,256]{1,0:T(8,128)(2,1)} %get-tuple-element.144), channel_id=1, source_target_pairs={{0,8},{8,16},{16,24},{24,0},{1,9},{9,17},{17,25},{25,1},{2,10},{10... | collective-permute-start | bytes 393224 | tf_op jit(solution)/shard_map/ppermute | solution.py:921
  85.5 14.3 %copy-start.1 = (bf16[128,4096]{1,0:T(8,128)(2,1)}, bf16[128,4096]{1,0:T(8,128)(2,1)S(1)}, u32[]{:S(2)}) copy-start(bf16[128,4096]{1,0:T(8,128)(2,1)S(1)} %pad_maximum_fusion.1.refs_6_.refs_10_) | copy-start | bytes 3145732
  93.5 6.3 %collective-permute-start.12 = (bf16[128,4096]{1,0:T(8,128)(2,1)S(1)}, bf16[128,4096]{1,0:T(8,128)(2,1)}, u32[]{:S(2)}, u32[]{:S(2)}) collective-permute-start(bf16[128,4096]{1,0:T(8,128)(2,1)S(1)} %collective-permute-done.4.refs_2_.refs_6_), channel_id=1, source_target_pairs={{0,1},{1,0},{2,3},{3,2},{4,5},{5,4},{6,7},{7,6},{8,9},{9,8},{10,11... | collective-permute-start | bytes 3145736 | tf_op jit(solution)/shard_map/ppermute | solution.py:925
  93.6 6.3 %collective-permute-start.13 = (bf16[128,4096]{1,0:T(8,128)(2,1)S(1)}, bf16[128,4096]{1,0:T(8,128)(2,1)}, u32[]{:S(2)}, u32[]{:S(2)}) collective-permute-start(bf16[128,4096]{1,0:T(8,128)(2,1)S(1)} %collective-permute-done.5.refs_4_.refs_8_), channel_id=1, source_target_pairs={{0,1},{1,0},{2,3},{3,2},{4,5},{5,4},{6,7},{7,6},{8,9},{9,8},{10,11... | collective-permute-start | bytes 3145736 | tf_op jit(solution)/shard_map/ppermute | solution.py:925
  94.0 5.8 %collective-permute-start.14 = (bf16[128,4096]{1,0:T(8,128)(2,1)S(1)}, bf16[128,4096]{1,0:T(8,128)(2,1)}, u32[]{:S(2)}, u32[]{:S(2)}) collective-permute-start(bf16[128,4096]{1,0:T(8,128)(2,1)S(1)} %pad_maximum_fusion.1.refs_6_.refs_10_), channel_id=1, source_target_pairs={{0,1},{1,0},{2,3},{3,2},{4,5},{5,4},{6,7},{7,6},{8,9},{9,8},{10,11... | collective-permute-start | bytes 3145736 | tf_op jit(solution)/shard_map/ppermute | solution.py:925
  109.5 35.2 %collective-permute-start.18 = (bf16[6,256,1024]{2,1,0:T(8,128)(2,1)}, bf16[6,256,1024]{2,1,0:T(8,128)(2,1)S(1)}, u32[]{:S(2)}, u32[]{:S(2)}) collective-permute-start(bf16[6,256,1024]{2,1,0:T(8,128)(2,1)} %get-tuple-element.160.acts.lo.ho), channel_id=1, source_target_pairs={{0,1},{1,0},{2,3},{3,2},{4,5},{5,4},{6,7},{7,6},{8,9},{9,8},{10,11... | collective-permute-start | bytes 9437192 | tf_op jit(solution)/shard_map/ppermute | solution.py:925
  139.0 6.1 %collective-permute-start.19 = (bf16[6,256,1024]{2,1,0:T(8,128)(2,1)}, bf16[6,256,1024]{2,1,0:T(8,128)(2,1)}, u32[]{:S(2)}, u32[]{:S(2)}) collective-permute-start(bf16[6,256,1024]{2,1,0:T(8,128)(2,1)} %get-tuple-element.178.go), channel_id=1, source_target_pairs={{0,1},{1,0},{2,3},{3,2},{4,5},{5,4},{6,7},{7,6},{8,9},{9,8},{10,11... | collective-permute-start | bytes 9437192 | tf_op jit(solution)/shard_map/ppermute | solution.py:925
  139.4 16.0 %collective-permute-start.15 = (bf16[256,256]{1,0:T(8,128)(2,1)}, bf16[256,256]{1,0:T(8,128)(2,1)S(1)}, u32[]{:S(2)}, u32[]{:S(2)}) collective-permute-start(bf16[256,256]{1,0:T(8,128)(2,1)} %get-tuple-element.175), channel_id=1, source_target_pairs={{0,8},{8,16},{16,24},{24,0},{1,9},{9,17},{17,25},{25,1},{2,10},{10... | collective-permute-start | bytes 393224 | tf_op jit(solution)/shard_map/ppermute | solution.py:921
  140.8 14.5 %collective-permute-start.16 = (bf16[256,256]{1,0:T(8,128)(2,1)}, bf16[256,256]{1,0:T(8,128)(2,1)S(1)}, u32[]{:S(2)}, u32[]{:S(2)}) collective-permute-start(bf16[256,256]{1,0:T(8,128)(2,1)} %get-tuple-element.176), channel_id=1, source_target_pairs={{0,16},{8,24},{16,0},{24,8},{1,17},{9,25},{17,1},{25,9},{2,18},{10... | collective-permute-start | bytes 393224 | tf_op jit(solution)/shard_map/ppermute | solution.py:921
  143.3 12.2 %collective-permute-start.17 = (bf16[256,256]{1,0:T(8,128)(2,1)}, bf16[256,256]{1,0:T(8,128)(2,1)S(1)}, u32[]{:S(2)}, u32[]{:S(2)}) collective-permute-start(bf16[256,256]{1,0:T(8,128)(2,1)} %get-tuple-element.177), channel_id=1, source_target_pairs={{0,24},{8,0},{16,8},{24,16},{1,25},{9,1},{17,9},{25,17},{2,26},{10... | collective-permute-start | bytes 393224 | tf_op jit(solution)/shard_map/ppermute | solution.py:921
  155.4 8.9 %copy-start.13 = (bf16[256,256]{1,0:T(8,128)(2,1)}, bf16[256,256]{1,0:T(8,128)(2,1)S(1)}, u32[]{:S(2)}) copy-start(bf16[256,256]{1,0:T(8,128)(2,1)S(1)} %collective-permute-done.15.g1) | copy-start | bytes 393220
  155.4 33.5 %collective-permute-start.21 = (bf16[640,1024]{1,0:T(8,128)(2,1)}, bf16[640,1024]{1,0:T(8,128)(2,1)S(1)}, u32[]{:S(2)}, u32[]{:S(2)}) collective-permute-start(bf16[640,1024]{1,0:T(8,128)(2,1)} %get-tuple-element.190), channel_id=1, source_target_pairs={{0,4},{1,5},{2,6},{3,7},{4,0},{5,1},{6,2},{7,3},{8,12},{9,13},{10,... | collective-permute-start | bytes 3932168 | tf_op jit(solution)/shard_map/ppermute | solution.py:925
  164.3 24.6 %collective-permute-start.20 = (bf16[512,1024]{1,0:T(8,128)(2,1)}, bf16[512,1024]{1,0:T(8,128)(2,1)}, u32[]{:S(2)}, u32[]{:S(2)}) collective-permute-start(bf16[512,1024]{1,0:T(8,128)(2,1)} %get-tuple-element.189), channel_id=1, source_target_pairs={{0,2},{1,3},{2,0},{3,1},{4,6},{5,7},{6,4},{7,5},{8,10},{9,11},{10,... | collective-permute-start | bytes 3145736 | tf_op jit(solution)/shard_map/ppermute | solution.py:925
  189.0 97.6 %reduce-scatter.5.cloned.1.call-start = ((), (), s32[]{:S(2)}) async-start(), calls=%async_computation.3 | async-start | bytes 2064384 | tf_op jit(solution)/shard_map/reduce_scatter | solution.py:1091
  190.6 29.1 %collective-permute-start.22 = (bf16[640,1024]{1,0:T(8,128)(2,1)}, bf16[640,1024]{1,0:T(8,128)(2,1)S(1)}, u32[]{:S(2)}, u32[]{:S(2)}) collective-permute-start(bf16[640,1024]{1,0:T(8,128)(2,1)} %add_convert_fusion), channel_id=1, source_target_pairs={{0,2},{1,3},{2,0},{3,1},{4,6},{5,7},{6,4},{7,5},{8,10},{9,11},{10,... | collective-permute-start | bytes 3932168 | tf_op jit(solution)/shard_map/ppermute | solution.py:925
  191.5 28.9 %collective-permute-start.23 = (bf16[640,1024]{1,0:T(8,128)(2,1)}, bf16[640,1024]{1,0:T(8,128)(2,1)}, u32[]{:S(2)}, u32[]{:S(2)}) collective-permute-start(bf16[640,1024]{1,0:T(8,128)(2,1)} %get-tuple-element.199), channel_id=1, source_target_pairs={{0,4},{1,5},{2,6},{3,7},{4,0},{5,1},{6,2},{7,3},{8,12},{9,13},{10,... | collective-permute-start | bytes 3932168 | tf_op jit(solution)/shard_map/ppermute | solution.py:925
  198.5 22.0 %copy-start.4 = (bf16[640,1024]{1,0:T(8,128)(2,1)S(1)}, bf16[640,1024]{1,0:T(8,128)(2,1)}, u32[]{:S(2)}) copy-start(bf16[640,1024]{1,0:T(8,128)(2,1)} %get-tuple-element.192) | copy-start | bytes 3932164
  200.5 21.4 %copy-start.19 = (bf16[512,1024]{1,0:T(8,128)(2,1)S(1)}, bf16[512,1024]{1,0:T(8,128)(2,1)}, u32[]{:S(2)}) copy-start(bf16[512,1024]{1,0:T(8,128)(2,1)} %get-tuple-element.211) | copy-start | bytes 3145732
  221.9 22.9 %collective-permute-start.24 = (bf16[512,1024]{1,0:T(8,128)(2,1)S(1)}, bf16[512,1024]{1,0:T(8,128)(2,1)}, u32[]{:S(2)}, u32[]{:S(2)}) collective-permute-start(bf16[512,1024]{1,0:T(8,128)(2,1)S(1)} %copy-done.19), channel_id=1, source_target_pairs={{0,2},{1,3},{2,0},{3,1},{4,6},{5,7},{6,4},{7,5},{8,10},{9,11},{10,... | collective-permute-start | bytes 3145736 | tf_op jit(solution)/shard_map/ppermute | solution.py:925
  223.1 21.9 %collective-permute-start.25 = (bf16[512,1024]{1,0:T(8,128)(2,1)S(1)}, bf16[512,1024]{1,0:T(8,128)(2,1)}, u32[]{:S(2)}, u32[]{:S(2)}) collective-permute-start(bf16[512,1024]{1,0:T(8,128)(2,1)S(1)} %add_convert_fusion.1), channel_id=1, source_target_pairs={{0,4},{1,5},{2,6},{3,7},{4,0},{5,1},{6,2},{7,3},{8,12},{9,13},{10,... | collective-permute-start | bytes 3145736 | tf_op jit(solution)/shard_map/ppermute | solution.py:925
  224.0 20.8 %collective-permute-start.26 = (bf16[320,1024]{1,0:T(8,128)(2,1)S(1)}, bf16[320,1024]{1,0:T(8,128)(2,1)}, u32[]{:S(2)}, u32[]{:S(2)}) collective-permute-start(bf16[320,1024]{1,0:T(8,128)(2,1)S(1)} %add_convert_fusion.4), channel_id=1, source_target_pairs={{0,8},{8,0},{16,24},{24,16},{1,9},{9,1},{17,25},{25,17},{2,10},{10... | collective-permute-start | bytes 1966088 | tf_op jit(solution)/shard_map/ppermute | solution.py:936
  246.8 30.6 %collective-permute-start.28 = (bf16[320,1024]{1,0:T(8,128)(2,1)S(1)}, bf16[320,1024]{1,0:T(8,128)(2,1)}, u32[]{:S(2)}, u32[]{:S(2)}) collective-permute-start(bf16[320,1024]{1,0:T(8,128)(2,1)S(1)} %add_convert_fusion.3), channel_id=1, source_target_pairs={{0,16},{8,24},{16,0},{24,8},{1,17},{9,25},{17,1},{25,9},{2,18},{10... | collective-permute-start | bytes 1966088 | tf_op jit(solution)/shard_map/ppermute | solution.py:936
  252.2 26.7 %collective-permute-start.27 = (bf16[256,1024]{1,0:T(8,128)(2,1)S(1)}, bf16[256,1024]{1,0:T(8,128)(2,1)}, u32[]{:S(2)}, u32[]{:S(2)}) collective-permute-start(bf16[256,1024]{1,0:T(8,128)(2,1)S(1)} %add_convert_fusion.7), channel_id=1, source_target_pairs={{0,8},{8,0},{16,24},{24,16},{1,9},{9,1},{17,25},{25,17},{2,10},{10... | collective-permute-start | bytes 1572872 | tf_op jit(solution)/shard_map/ppermute | solution.py:936
  253.8 38.1 %copy-start.6 = (f32[256,1024]{1,0:T(8,128)S(1)}, f32[256,1024]{1,0:T(8,128)}, u32[]{:S(2)}) copy-start(f32[256,1024]{1,0:T(8,128)} %get-tuple-element.167) | copy-start | bytes 3145732
  278.8 38.6 %collective-permute-start.30 = (bf16[320,1024]{1,0:T(8,128)(2,1)S(1)}, bf16[320,1024]{1,0:T(8,128)(2,1)S(1)}, u32[]{:S(2)}, u32[]{:S(2)}) collective-permute-start(bf16[320,1024]{1,0:T(8,128)(2,1)S(1)} %add_convert_fusion.2), channel_id=1, source_target_pairs={{0,8},{8,0},{16,24},{24,16},{1,9},{9,1},{17,25},{25,17},{2,10},{10... | collective-permute-start | bytes 1966088 | tf_op jit(solution)/shard_map/ppermute | solution.py:936
  280.8 36.7 %collective-permute-start.29 = (bf16[256,1024]{1,0:T(8,128)(2,1)S(1)}, bf16[256,1024]{1,0:T(8,128)(2,1)S(1)}, u32[]{:S(2)}, u32[]{:S(2)}) collective-permute-start(bf16[256,1024]{1,0:T(8,128)(2,1)S(1)} %add_convert_fusion.6), channel_id=1, source_target_pairs={{0,16},{8,24},{16,0},{24,8},{1,17},{9,25},{17,1},{25,9},{2,18},{10... | collective-permute-start | bytes 1572872 | tf_op jit(solution)/shard_map/ppermute | solution.py:936
  286.5 30.9 %collective-permute-start.31 = (bf16[128,896]{1,0:T(8,128)(2,1)}, bf16[128,896]{1,0:T(8,128)(2,1)S(1)}, u32[]{:S(2)}, u32[]{:S(2)}) collective-permute-start(bf16[128,896]{1,0:T(8,128)(2,1)} %reduce-scatter.5.cloned.1.call-done.refs_0_), channel_id=1, source_target_pairs={{0,8},{8,16},{16,24},{24,0},{1,9},{9,17},{17,25},{25,1},{2,10},{10... | collective-permute-start | bytes 688136 | tf_op jit(solution)/shard_map/ppermute | solution.py:921
  288.0 34.7 %collective-permute-start.32 = (bf16[128,896]{1,0:T(8,128)(2,1)}, bf16[128,896]{1,0:T(8,128)(2,1)S(1)}, u32[]{:S(2)}, u32[]{:S(2)}) collective-permute-start(bf16[128,896]{1,0:T(8,128)(2,1)} %reduce-scatter.5.cloned.1.call-done.refs_0_), channel_id=1, source_target_pairs={{0,16},{8,24},{16,0},{24,8},{1,17},{9,25},{17,1},{25,9},{2,18},{10... | collective-permute-start | bytes 688136 | tf_op jit(solution)/shard_map/ppermute | solution.py:921
  290.4 32.3 %collective-permute-start.33 = (bf16[128,896]{1,0:T(8,128)(2,1)}, bf16[128,896]{1,0:T(8,128)(2,1)S(1)}, u32[]{:S(2)}, u32[]{:S(2)}) collective-permute-start(bf16[128,896]{1,0:T(8,128)(2,1)} %reduce-scatter.5.cloned.1.call-done.refs_0_), channel_id=1, source_target_pairs={{0,24},{8,0},{16,8},{24,16},{1,25},{9,1},{17,9},{25,17},{2,26},{10... | collective-permute-start | bytes 688136 | tf_op jit(solution)/shard_map/ppermute | solution.py:921
  323.5 15.3 %collective-permute-start.34 = (bf16[256,1024]{1,0:T(8,128)(2,1)S(1)}, bf16[256,1024]{1,0:T(8,128)(2,1)S(1)}, u32[]{:S(2)}, u32[]{:S(2)}) collective-permute-start(bf16[256,1024]{1,0:T(8,128)(2,1)S(1)} %add_convert_fusion.5), channel_id=1, source_target_pairs={{0,8},{8,0},{16,24},{24,16},{1,9},{9,1},{17,25},{25,17},{2,10},{10... | collective-permute-start | bytes 1572872 | tf_op jit(solution)/shard_map/ppermute | solution.py:936
  (11 other events, 43.5 us)
Sparse Core Ops, SparseCore 0:
  10.5 49.6 all-gather.4
  62.1 56.2 all-gather.6
  189.1 47.7 reduce-scatter.2
  245.2 41.3 reduce-scatter.4

commit v5 on v4

--- a/solution.py
+++ b/solution.py
@@ -604,18 +604,15 @@
 REST = 640
 
 
-def step_shard(j, sc):
-    rel = jnp.where(j == 0, 3, jnp.where(j >= 3, 0, j))
-    return 2 * jnp.bitwise_xor(sc[1], rel) + sc[2]
-
-
 def product(left, right, res):
     for n in range(4):
         cols = slice(256 * n, 256 * n + 256)
         res[:, cols] = dot(left[...], right[:, cols]).astype(BF)
 
 
-def down_kernel(sc, ho, hp, go, gp, d3, d1, d2, d0, left, right, res):
+def down_kernel(count, sc, ho, hp, go, gp, *refs):
+    outs = refs[0:count]
+    left, right, res = refs[count:]
     s = pl.program_id(0)
 
     @pl.when(s == 0)
@@ -626,38 +623,39 @@
     left[:, 0:CHUNK] = jnp.transpose(ho[0])
     left[:, CHUNK:] = jnp.transpose(hp[0])
     product(left, right, res)
-    for n, out in enumerate((d3, d1, d2, d0)):
+    for n, out in enumerate(outs):
 
         @pl.when(s == n)
         def _():
             out[...] = res[...]
 
 
-def down_grads(scalars, acts, acts_p, grads, grads_p):
+def down_grads(scalars, acts, acts_p, grads, grads_p, distances):
     shape = jax.ShapeDtypeStruct
     full = lambda *s: pl.BlockSpec(s, lambda j, sc: (0,) * len(s))
+    first, count = distances[0], len(distances)
 
     def hid(j, sc):
-        f = step_shard(j, sc)
+        f = 2 * jnp.bitwise_xor(sc[1], first + j) + sc[2]
         return (f // 2, 0, f % 2)
 
     hidden = pl.BlockSpec((1, CHUNK, 512), hid)
     grad = pl.BlockSpec((1, CHUNK, 1024), lambda j, sc: (5, 0, 0))
     return pl.pallas_call(
-        down_kernel,
+        partial(down_kernel, count),
         name="down_grads",
         grid_spec=pltpu.PrefetchScalarGridSpec(
             num_scalar_prefetch=1,
-            grid=(4,),
+            grid=(count,),
             in_specs=[hidden, hidden, grad, grad],
-            out_specs=(full(512, 1024),) * 4,
+            out_specs=(full(512, 1024),) * count,
             scratch_shapes=[
                 pltpu.VMEM((512, 2 * CHUNK), BF),
                 pltpu.VMEM((2 * CHUNK, 1024), BF),
                 pltpu.VMEM((512, 1024), BF),
             ],
         ),
-        out_shape=(shape((512, 1024), BF),) * 4,
+        out_shape=(shape((512, 1024), BF),) * count,
         compiler_params=PARAMS,
     )(scalars, acts, acts_p, grads, grads_p)
 
@@ -1061,7 +1059,8 @@
     )
     gs = [g0] + [shift(g, k) for k, g in ((1, g1), (2, g2), (3, g3))]
     grads_p = swap(grads, 1)
-    d3, d1, d2, d0 = down_grads(scalars, acts, acts_p, grads, grads_p)
+    (d3,) = down_grads(scalars, acts, acts_p, grads, grads_p, (3,))
+    d0, d1, d2 = down_grads(scalars, acts, acts_p, grads, grads_p, (0, 1, 2))
     if plane:
         d_far = swap(d3, 2)
     r3, r1, r2, r0 = rest_grads(scalars, acts, acts_p, grads, grads_p)
@@ -1112,7 +1111,8 @@
     else:
         other = scalars.at[2].set(1)
         sums_w = (d3, d1, d2, d0, r3, r1, r2, r0)
-        second = down_grads(other, acts, acts_p, grads, grads_p)
+        e0, e1, e2, e3 = down_grads(other, acts, acts_p, grads, grads_p, (0, 1, 2, 3))
+        second = (e3, e1, e2, e0)
         second += rest_grads(other, acts, acts_p, grads, grads_p)
         rows_of = lambda t: ([t[3], t[1], t[2], t[0]], [t[7], t[5], t[6], t[4]])
         down_0, rest_0 = rows_of(sums_w)

time: 348 us -> 346 us (level)
  waiting for transfers between devices: 164 us -> 159 us
    pallas_call x1 -> x2, Pallas kernels: 7.71 us -> 10.3 us  [down_grads(): pl.pallas_call(partial(down_kernel, count), name='down_grads', grid_spec=...]
  transfers between devices with their start and end apart: 39 -> 39, of which waited for: 21 -> 23; matrix products, arithmetic and copies ran while one was open for 5% -> 5% of each run, Pallas kernels for 26% -> 27%
where the time goes in v5:
time: 346 us; the launch traced here: 345 us
  waiting for transfers between devices  159 us (46%)
  Pallas kernels  97 us (28%)
  starting transfers between devices  51.9 us (15%)
  other arithmetic  19.5 us (6%)
  between operations  14.2 us (4%)
  local copies, waits for them, and re-layouts  3.69 us (1%)
    ppermute x6, waiting for transfers between devices, neighbour(): return lax.ppermute(x, 'ctx', [(i, i ^ bits) for i in range(4)])  71.2 us
    ppermute x16, waiting for transfers between devices, swap(): lax.ppermute(x, 'fsdp', [(i, i ^ bits) for i in range(lax.axis_size('fsdp...  29.7 us
    pallas_call x1, Pallas kernels, mlp_tail(): pl.pallas_call(mlp_tail_kernel, name='mlp_tail', grid=(8,), in_specs=[SME...  20.8 us
    ppermute x1, waiting for transfers between devices, line_gather(): two = lax.ppermute(x, 'ctx', [(0, 2), (1, 3), (2, 0), (3, 1)])  17.8 us
    pallas_call x1, Pallas kernels, attn_bwd(): pl.pallas_call(attn_bwd_kernel, name='attn_bwd', out_shape=(shape((1024,...  16.1 us
    ppermute x6, starting transfers between devices, neighbour(): return lax.ppermute(x, 'ctx', [(i, i ^ bits) for i in range(4)])  15.6 us
    pallas_call x1, Pallas kernels, attn_fwd(): pl.pallas_call(attn_fwd_kernel, name='attn_fwd', out_shape=(shape((CHUNK,...  15.2 us
    ppermute x9, waiting for transfers between devices, shift(): return lax.ppermute(x, 'ctx', [(i, (i + k) % n) for i in range(n)])  13.8 us
  transfers between devices with their start and end apart: 39, of which 23 were waited for; matrix products, arithmetic and copies ran while one was open for 5% of the time, Pallas kernels for 27%

profile of v5, /device:TPU:0, one launch (start us, length us, event | category | flops | bytes accessed | tf_op | source)
XLA Modules:
  0.0 345.3 jit_solution(13477027998241879921)
XLA Ops:
  7.9 2.5 pack_inputs.1
  10.4 4.1 %collective-permute-start.2 = (bf16[272,1024]{1,0:T(8,128)(2,1)}, bf16[272,1024]{1,0:T(8,128)(2,1)S(1)}, u32[]{:S(2)}, u32[]{:S(2)}) collective-permute-start(bf16[272,1024]{1,0:T(8,128)(2,1)} %get-tuple-element.134.x0), channel_id=1, source_target_pairs={{0,16},{8,24},{16,0},{24,8},{1,17},{9,25},{17,1},{25,9},{2,18},{10... | collective-permute-start | bytes 1671176 | tf_op jit(solution)/shard_map/ppermute | solution.py:909
  16.0 1.5 collective-permute-start.5
  17.6 3.5 %collective-permute-start = (bf16[272,1024]{1,0:T(8,128)(2,1)}, bf16[272,1024]{1,0:T(8,128)(2,1)S(1)}, u32[]{:S(2)}, u32[]{:S(2)}) collective-permute-start(bf16[272,1024]{1,0:T(8,128)(2,1)} %get-tuple-element.134.x0), channel_id=1, source_target_pairs={{0,8},{8,16},{16,24},{1,9},{9,17},{17,25},{2,10},{10,18},{18,26},{... | collective-permute-start | bytes 1671176 | tf_op jit(solution)/shard_map/ppermute | solution.py:907
  22.4 17.8 %collective-permute-done.2.x2 = bf16[272,1024]{1,0:T(8,128)(2,1)S(1)} collective-permute-done((bf16[272,1024]{1,0:T(8,128)(2,1)}, bf16[272,1024]{1,0:T(8,128)(2,1)S(1)}, u32[]{:S(2)}, u32[]{:S(2)}) %collective-permute-start.2) | collective-permute-done | bytes 557088 | tf_op jit(solution)/shard_map/ppermute | solution.py:909
  41.5 8.0 %collective-permute-done.1.left = bf16[272,1024]{1,0:T(8,128)(2,1)S(1)} collective-permute-done((bf16[272,1024]{1,0:T(8,128)(2,1)}, bf16[272,1024]{1,0:T(8,128)(2,1)S(1)}, u32[]{:S(2)}, u32[]{:S(2)}) %collective-permute-start.1) | collective-permute-done | bytes 557088 | tf_op jit(solution)/shard_map/ppermute | solution.py:908
  49.5 2.1 collective-permute-done.5.refs_4_.refs_8_
  51.6 7.6 %collective-permute-done.3.far = bf16[272,1024]{1,0:T(8,128)(2,1)} collective-permute-done((bf16[272,1024]{1,0:T(8,128)(2,1)S(1)}, bf16[272,1024]{1,0:T(8,128)(2,1)}, u32[]{:S(2)}, u32[]{:S(2)}) %collective-permute-start.3) | collective-permute-done | bytes 557088 | tf_op jit(solution)/shard_map/ppermute | solution.py:914
  61.8 1.5 collective-permute-start.9
  63.3 15.2 %attn_fwd.1 = (bf16[256,256]{1,0:T(8,128)(2,1)}, bf16[256,256]{1,0:T(8,128)(2,1)}, bf16[256,256]{1,0:T(8,128)(2,1)}, bf16[256,256]{1,0:T(8,128)(2,1)}, f32[256,1...) custom-call(s32[4]{0:T(128)} %pad_add_fusion.sc, ...), custom_call_target="tpu_custom_call" | custom-call | tf_op jit(solution)/shard_map/attn_fwd/pallas_call | solution.py:223
  78.7 2.6 collective-permute-done.9
  81.3 2.9 collective-permute-start.7
  85.5 2.5 collective-permute-done.6.r1
  88.0 6.1 %collective-permute-done.7.r2 = bf16[256,256]{1,0:T(8,128)(2,1)S(1)} collective-permute-done((bf16[256,256]{1,0:T(8,128)(2,1)}, bf16[256,256]{1,0:T(8,128)(2,1)S(1)}, u32[]{:S(2)}, u32[]{:S(2)}) %collective-permute-start.7) | collective-permute-done | bytes 131104 | tf_op jit(solution)/shard_map/ppermute | solution.py:919
  94.9 5.6 %out_project.1 = (f32[256,1024]{1,0:T(8,128)}, bf16[256,1024]{1,0:T(8,128)(2,1)}, bf16[256,1024]{1,0:T(8,128)(2,1)}, f32[256,1024]{1,0:T(8,128)}, f32[256,128]{1...) custom-call(s32[4]{0:T(128)} %pad_add_fusion.sc, bf16[256,1024]{1,0:T(8,128)(2,1)} %bitcast.42, ...), custom_call_target="tpu_custom_call" | custom-call | tf_op jit(solution)/shard_map/out_project/pallas_call | solution.py:329
  100.6 9.7 %mlp_gate.1 = (bf16[6,256,1024]{2,1,0:T(8,128)(2,1)}, f32[256,4096]{1,0:T(8,128)}) custom-call(bf16[256,1024]{1,0:T(8,128)(2,1)} %get-tuple-element.153.low, bf16[256,1024]{1,0:T(8,128)(2,1)} %get-tuple-element.154.low_rel, bf16[256,1024]{1,0:T(8,128)(2,1)} %get-tuple-element.155.mixed, bf16[128,4096]{1,0:T(8,128)(2,1)} %refs_4_.1, ...), custom_call_target="tpu_custom_call" | custom-call | tf_op jit(solution)/shard_map/mlp_gate/pallas_call | solution.py:388
  110.5 7.9 %all-gather.7.cloned.1.call-done = bf16[4096,1024]{1,0:T(8,128)(2,1)} async-done(((bf16[512,1024]{1,0:T(8,128)(2,1)}), bf16[4096,1024]{1,0:T(8,128)(2,1)}) %all-gather.7.cloned.1.call-update) | async-done | bytes 8388624 | tf_op jit(solution)/shard_map/all_gather | solution.py:1015
  118.4 20.8 %mlp_tail.1 = (bf16[256,1024]{1,0:T(8,128)(2,1)}, bf16[6,256,1024]{2,1,0:T(8,128)(2,1)}, f32[256,1024]{1,0:T(8,128)}, bf16[256,256]{1,0:T(8,128)(2,1)}, bf16[256...) custom-call(s32[4]{0:T(128)} %pad_add_fusion.sc, ...), custom_call_target="tpu_custom_call" | custom-call | tf_op jit(solution)/shard_map/mlp_tail/pallas_call | solution.py:552
  141.0 2.4 collective-permute-start.16
  146.4 8.9 %rest_grads.1 = (bf16[640,1024]{1,0:T(8,128)(2,1)}, bf16[640,1024]{1,0:T(8,128)(2,1)}, bf16[640,1024]{1,0:T(8,128)(2,1)}, bf16[640,1024]{1,0:T(8,128)(2,1)}) custom-call(s32[4]{0:T(128)} %pad_add_fusion.sc, bf16[6,256,1024]{2,1,0:T(8,128)(2,1)} %get-tuple-element.159.acts.lo.ho, bf16[6,256,1024]{2,1,0:T(8,128)(2,1)} %copy-done, ...), custom_call_target="tpu_custom_call" | custom-call | tf_op jit(solution)/shard_map/rest_grads/pallas_call | solution.py:692
  156.6 3.8 %down_grads.2 = bf16[512,1024]{1,0:T(8,128)(2,1)} custom-call(s32[4]{0:T(128)} %pad_add_fusion.sc, bf16[6,256,1024]{2,1,0:T(8,128)(2,1)} %get-tuple-element.159.acts.lo.ho, bf16[6,256,1024]{2,1,0:T(8,128)(2,1)} %copy-done, bf16[6,256,1024]{2,1,0:T(8,128)(2,1)} %get-tuple-element.177.go, bf16[6,256,1024]{2,1,0:T(8,128)(2,1)} %collective-permute-done.19.gp), custom_call_target="tpu_custom_call" | custom-call | tf_op jit(solution)/shard_map/down_grads/pallas_call | solution.py:644
  161.4 16.1 %attn_bwd.1 = (bf16[1024,1024]{1,0:T(8,128)(2,1)}, bf16[1024,768]{1,0:T(8,128)(2,1)}) custom-call(s32[4]{0:T(128)} %pad_add_fusion.sc, f32[4,8,256]{2,1,0:T(8,128)} %get-tuple-element.167.segr, bf16[8,272,1024]{2,1,0:T(8,128)(2,1)} %bitcast.38, bf16[4,1024,128]{2,1,0:T(8,128)(2,1)} %get-tuple-element.168.qm, bf16[1024,512]{1,0:T(8,128)(2,1)} %get-tuple-element.169.kv, ...), custom_call_target="tpu_custom_call" | custom-call | tf_op jit(solution)/shard_map/attn_bwd/pallas_call | solution.py:839
  177.5 7.5 %collective-permute-done.20 = bf16[512,1024]{1,0:T(8,128)(2,1)} collective-permute-done((bf16[512,1024]{1,0:T(8,128)(2,1)}, bf16[512,1024]{1,0:T(8,128)(2,1)}, u32[]{:S(2)}, u32[]{:S(2)}) %collective-permute-start.20) | collective-permute-done | bytes 1048608 | tf_op jit(solution)/shard_map/ppermute | solution.py:923
  185.9 1.6 add_convert_fusion
  187.5 1.5 collective-permute-start.22
  189.6 6.5 %down_grads.3 = (bf16[512,1024]{1,0:T(8,128)(2,1)}, bf16[512,1024]{1,0:T(8,128)(2,1)}, bf16[512,1024]{1,0:T(8,128)(2,1)}) custom-call(s32[4]{0:T(128)} %pad_add_fusion.sc, bf16[6,256,1024]{2,1,0:T(8,128)(2,1)} %get-tuple-element.159.acts.lo.ho, bf16[6,256,1024]{2,1,0:T(8,128)(2,1)} %copy-done, bf16[6,256,1024]{2,1,0:T(8,128)(2,1)} %get-tuple-element.177.go, ...), custom_call_target="tpu_custom_call" | custom-call | tf_op jit(solution)/shard_map/down_grads/pallas_call | solution.py:644
  196.1 5.4 %qkv_grads.1 = bf16[1024,896]{1,0:T(8,128)(2,1)} custom-call(s32[4]{0:T(128)} %pad_add_fusion.sc, bf16[4,256,1024]{2,1,0:T(8,128)(2,1)} %get-tuple-element.198.xall, bf16[1024,768]{1,0:T(8,128)(2,1)} %get-tuple-element.199.dall, f32[8,1024]{1,0:T(8,128)} %get-tuple-element.200.sums_m, f32[8,1024]{1,0:T(8,128)} %get-tuple-element.201.sums_a, ...), custom_call_target="tpu_custom_call" | custom-call | tf_op jit(solution)/shard_map/qkv_grads/pallas_call | solution.py:826
  201.5 2.0 add_convert_fusion.1
  203.5 13.5 %collective-permute-done.22 = bf16[640,1024]{1,0:T(8,128)(2,1)S(1)} collective-permute-done((bf16[640,1024]{1,0:T(8,128)(2,1)}, bf16[640,1024]{1,0:T(8,128)(2,1)S(1)}, u32[]{:S(2)}, u32[]{:S(2)}) %collective-permute-start.22) | collective-permute-done | bytes 1310752 | tf_op jit(solution)/shard_map/ppermute | solution.py:923
  221.5 1.8 collective-permute-start.26
  223.3 18.2 %collective-permute-done.26 = bf16[320,1024]{1,0:T(8,128)(2,1)} collective-permute-done((bf16[320,1024]{1,0:T(8,128)(2,1)S(1)}, bf16[320,1024]{1,0:T(8,128)(2,1)}, u32[]{:S(2)}, u32[]{:S(2)}) %collective-permute-start.26) | collective-permute-done | bytes 655392 | tf_op jit(solution)/shard_map/ppermute | solution.py:934
  242.7 1.8 add_convert_fusion.3
  244.5 3.8 %collective-permute-start.28 = (bf16[320,1024]{1,0:T(8,128)(2,1)S(1)}, bf16[320,1024]{1,0:T(8,128)(2,1)}, u32[]{:S(2)}, u32[]{:S(2)}) collective-permute-start(bf16[320,1024]{1,0:T(8,128)(2,1)S(1)} %add_convert_fusion.3), channel_id=1, source_target_pairs={{0,16},{8,24},{16,0},{24,8},{1,17},{9,25},{17,1},{25,9},{2,18},{10... | collective-permute-start | bytes 1966088 | tf_op jit(solution)/shard_map/ppermute | solution.py:934
  248.3 1.6 add_convert_fusion.7
  249.9 1.6 collective-permute-start.27
  251.5 23.1 %collective-permute-done.28 = bf16[320,1024]{1,0:T(8,128)(2,1)} collective-permute-done((bf16[320,1024]{1,0:T(8,128)(2,1)S(1)}, bf16[320,1024]{1,0:T(8,128)(2,1)}, u32[]{:S(2)}, u32[]{:S(2)}) %collective-permute-start.28) | collective-permute-done | bytes 655392 | tf_op jit(solution)/shard_map/ppermute | solution.py:934
  276.4 1.9 add_convert_fusion.6
  278.3 3.7 %collective-permute-start.29 = (bf16[256,1024]{1,0:T(8,128)(2,1)S(1)}, bf16[256,1024]{1,0:T(8,128)(2,1)S(1)}, u32[]{:S(2)}, u32[]{:S(2)}) collective-permute-start(bf16[256,1024]{1,0:T(8,128)(2,1)S(1)} %add_convert_fusion.6), channel_id=1, source_target_pairs={{0,16},{8,24},{16,0},{24,8},{1,17},{9,25},{17,1},{25,9},{2,18},{10... | collective-permute-start | bytes 1572872 | tf_op jit(solution)/shard_map/ppermute | solution.py:934
  281.9 2.1 reduce-scatter.5.cloned.1.call-done.refs_0_
  285.5 2.4 collective-permute-start.32
  289.3 2.1 add_bitcast_fusion
  291.5 24.2 %collective-permute-done.29 = bf16[256,1024]{1,0:T(8,128)(2,1)S(1)} collective-permute-done((bf16[256,1024]{1,0:T(8,128)(2,1)S(1)}, bf16[256,1024]{1,0:T(8,128)(2,1)S(1)}, u32[]{:S(2)}, u32[]{:S(2)}) %collective-permute-start.29) | collective-permute-done | bytes 524320 | tf_op jit(solution)/shard_map/ppermute | solution.py:934
  315.7 5.1 %collective-permute-done.32.refs_2_ = bf16[128,896]{1,0:T(8,128)(2,1)S(1)} collective-permute-done((bf16[128,896]{1,0:T(8,128)(2,1)}, bf16[128,896]{1,0:T(8,128)(2,1)S(1)}, u32[]{:S(2)}, u32[]{:S(2)}) %collective-permute-start.32) | collective-permute-done | bytes 229408 | tf_op jit(solution)/shard_map/ppermute | solution.py:919
  321.5 4.4 %collective-permute-start.34 = (bf16[256,1024]{1,0:T(8,128)(2,1)S(1)}, bf16[256,1024]{1,0:T(8,128)(2,1)S(1)}, u32[]{:S(2)}, u32[]{:S(2)}) collective-permute-start(bf16[256,1024]{1,0:T(8,128)(2,1)S(1)} %add_convert_fusion.5), channel_id=1, source_target_pairs={{0,8},{8,0},{16,24},{24,16},{1,9},{9,1},{17,25},{25,17},{2,10},{10... | collective-permute-start | bytes 1572872 | tf_op jit(solution)/shard_map/ppermute | solution.py:934
  327.3 2.5 finish.1
  329.8 1.5 pad_maximum_fusion
  331.4 5.7 %collective-permute-done.34 = bf16[256,1024]{1,0:T(8,128)(2,1)S(1)} collective-permute-done((bf16[256,1024]{1,0:T(8,128)(2,1)S(1)}, bf16[256,1024]{1,0:T(8,128)(2,1)S(1)}, u32[]{:S(2)}, u32[]{:S(2)}) %collective-permute-start.34) | collective-permute-done | bytes 524320 | tf_op jit(solution)/shard_map/ppermute | solution.py:934
  337.2 1.6 maximum_convert_fusion.1
  (104 shorter events, 30.9 us)
Async XLA Ops:
  7.2 53.1 %all-gather.5.cloned.1.call-start = ((), (), s32[]{:S(2)}) async-start(), calls=%async_computation.4 | async-start | bytes 5013504 | tf_op jit(solution)/shard_map/all_gather | solution.py:1006
  10.4 108.0 %all-gather.7.cloned.1.call-start = ((), (), s32[]{:S(2)}) async-start(), calls=%async_computation.5 | async-start | bytes 9437184 | tf_op jit(solution)/shard_map/all_gather | solution.py:1015
  10.4 29.7 %collective-permute-start.2 = (bf16[272,1024]{1,0:T(8,128)(2,1)}, bf16[272,1024]{1,0:T(8,128)(2,1)S(1)}, u32[]{:S(2)}, u32[]{:S(2)}) collective-permute-start(bf16[272,1024]{1,0:T(8,128)(2,1)} %get-tuple-element.134.x0), channel_id=1, source_target_pairs={{0,16},{8,24},{16,0},{24,8},{1,17},{9,25},{17,1},{25,9},{2,18},{10... | collective-permute-start | bytes 1671176 | tf_op jit(solution)/shard_map/ppermute | solution.py:909
  14.5 35.0 %collective-permute-start.4 = (bf16[128,4096]{1,0:T(8,128)(2,1)}, bf16[128,4096]{1,0:T(8,128)(2,1)S(1)}, u32[]{:S(2)}, u32[]{:S(2)}) collective-permute-start(bf16[128,4096]{1,0:T(8,128)(2,1)} %refs_4_.1), channel_id=1, source_target_pairs={{0,2},{1,3},{2,0},{3,1},{4,6},{5,7},{6,4},{7,5},{8,10},{9,11},{10,... | collective-permute-start | bytes 3145736 | tf_op jit(solution)/shard_map/ppermute | solution.py:923
  16.0 35.6 %collective-permute-start.5 = (bf16[128,4096]{1,0:T(8,128)(2,1)}, bf16[128,4096]{1,0:T(8,128)(2,1)S(1)}, u32[]{:S(2)}, u32[]{:S(2)}) collective-permute-start(bf16[128,4096]{1,0:T(8,128)(2,1)} %refs_4_.1), channel_id=1, source_target_pairs={{0,4},{1,5},{2,6},{3,7},{4,0},{5,1},{6,2},{7,3},{8,12},{9,13},{10,... | collective-permute-start | bytes 3145736 | tf_op jit(solution)/shard_map/ppermute | solution.py:923
  17.6 23.9 %collective-permute-start = (bf16[272,1024]{1,0:T(8,128)(2,1)}, bf16[272,1024]{1,0:T(8,128)(2,1)S(1)}, u32[]{:S(2)}, u32[]{:S(2)}) collective-permute-start(bf16[272,1024]{1,0:T(8,128)(2,1)} %get-tuple-element.134.x0), channel_id=1, source_target_pairs={{0,8},{8,16},{16,24},{1,9},{9,17},{17,25},{2,10},{10,18},{18,26},{... | collective-permute-start | bytes 1671176 | tf_op jit(solution)/shard_map/ppermute | solution.py:907
  21.1 28.4 %collective-permute-start.1 = (bf16[272,1024]{1,0:T(8,128)(2,1)}, bf16[272,1024]{1,0:T(8,128)(2,1)S(1)}, u32[]{:S(2)}, u32[]{:S(2)}) collective-permute-start(bf16[272,1024]{1,0:T(8,128)(2,1)} %get-tuple-element.134.x0), channel_id=1, source_target_pairs={{8,0},{16,8},{24,16},{9,1},{17,9},{25,17},{10,2},{18,10},{26,18},{... | collective-permute-start | bytes 1671176 | tf_op jit(solution)/shard_map/ppermute | solution.py:908
  40.2 23.1 %copy-start.7 = (bf16[272,1024]{1,0:T(8,128)(2,1)}, bf16[272,1024]{1,0:T(8,128)(2,1)S(1)}, u32[]{:S(2)}) copy-start(bf16[272,1024]{1,0:T(8,128)(2,1)S(1)} %collective-permute-done.2.x2) | copy-start | bytes 1671172
  40.2 19.0 %collective-permute-start.3 = (bf16[272,1024]{1,0:T(8,128)(2,1)S(1)}, bf16[272,1024]{1,0:T(8,128)(2,1)}, u32[]{:S(2)}, u32[]{:S(2)}) collective-permute-start(bf16[272,1024]{1,0:T(8,128)(2,1)S(1)} %collective-permute-done.2.x2), channel_id=1, source_target_pairs={{8,0},{16,24},{9,1},{17,25},{10,2},{18,26},{11,3},{19,27},{12,4},{... | collective-permute-start | bytes 1671176 | tf_op jit(solution)/shard_map/ppermute | solution.py:914
  41.5 21.8 %copy-start.8 = (bf16[272,1024]{1,0:T(8,128)(2,1)}, bf16[272,1024]{1,0:T(8,128)(2,1)S(1)}, u32[]{:S(2)}) copy-start(bf16[272,1024]{1,0:T(8,128)(2,1)S(1)} %collective-permute-done.right) | copy-start | bytes 1671172
  49.5 44.7 %copy-start.2 = (bf16[128,4096]{1,0:T(8,128)(2,1)}, bf16[128,4096]{1,0:T(8,128)(2,1)S(1)}, u32[]{:S(2)}) copy-start(bf16[128,4096]{1,0:T(8,128)(2,1)S(1)} %collective-permute-done.4.refs_2_.refs_6_) | copy-start | bytes 3145732
  51.6 42.7 %copy-start.3 = (bf16[128,4096]{1,0:T(8,128)(2,1)}, bf16[128,4096]{1,0:T(8,128)(2,1)S(1)}, u32[]{:S(2)}) copy-start(bf16[128,4096]{1,0:T(8,128)(2,1)S(1)} %collective-permute-done.5.refs_4_.refs_8_) | copy-start | bytes 3145732
  60.3 182.4 %reduce-scatter.3.cloned.1.call-start = ((), (), s32[]{:S(2)}) async-start(), calls=%async_computation.2 | async-start | bytes 2621440 | tf_op jit(solution)/shard_map/reduce_scatter | solution.py:1077
  60.4 18.4 %collective-permute-start.10 = (bf16[128,2048]{1,0:T(8,128)(2,1)S(1)}, bf16[128,2048]{1,0:T(8,128)(2,1)}, u32[]{:S(2)}, u32[]{:S(2)}) collective-permute-start(bf16[128,2048]{1,0:T(8,128)(2,1)S(1)} %slice.29), channel_id=1, source_target_pairs={{0,2},{1,3},{2,0},{3,1},{4,6},{5,7},{6,4},{7,5},{8,10},{9,11},{10,... | collective-permute-start | bytes 1572872 | tf_op jit(solution)/shard_map/ppermute | solution.py:923
  61.8 19.5 %collective-permute-start.9 = (bf16[128,2048]{1,0:T(8,128)(2,1)}, bf16[128,2048]{1,0:T(8,128)(2,1)}, u32[]{:S(2)}, u32[]{:S(2)}) collective-permute-start(bf16[128,2048]{1,0:T(8,128)(2,1)} %slice.28), channel_id=1, source_target_pairs={{0,4},{1,5},{2,6},{3,7},{4,0},{5,1},{6,2},{7,3},{8,12},{9,13},{10,... | collective-permute-start | bytes 1572872 | tf_op jit(solution)/shard_map/ppermute | solution.py:923
  63.3 37.2 %collective-permute-start.11 = (bf16[128,4096]{1,0:T(8,128)(2,1)}, bf16[128,4096]{1,0:T(8,128)(2,1)}, u32[]{:S(2)}, u32[]{:S(2)}) collective-permute-start(bf16[128,4096]{1,0:T(8,128)(2,1)} %refs_4_.1), channel_id=1, source_target_pairs={{0,1},{1,0},{2,3},{3,2},{4,5},{5,4},{6,7},{7,6},{8,9},{9,8},{10,11... | collective-permute-start | bytes 3145736 | tf_op jit(solution)/shard_map/ppermute | solution.py:923
  81.3 6.7 %collective-permute-start.6 = (bf16[256,256]{1,0:T(8,128)(2,1)}, bf16[256,256]{1,0:T(8,128)(2,1)S(1)}, u32[]{:S(2)}, u32[]{:S(2)}) collective-permute-start(bf16[256,256]{1,0:T(8,128)(2,1)} %get-tuple-element.141), channel_id=1, source_target_pairs={{0,24},{8,0},{16,8},{24,16},{1,25},{9,1},{17,9},{25,17},{2,26},{10... | collective-permute-start | bytes 393224 | tf_op jit(solution)/shard_map/ppermute | solution.py:919
  81.3 12.8 %collective-permute-start.7 = (bf16[256,256]{1,0:T(8,128)(2,1)}, bf16[256,256]{1,0:T(8,128)(2,1)S(1)}, u32[]{:S(2)}, u32[]{:S(2)}) collective-permute-start(bf16[256,256]{1,0:T(8,128)(2,1)} %get-tuple-element.142), channel_id=1, source_target_pairs={{0,16},{8,24},{16,0},{24,8},{1,17},{9,25},{17,1},{25,9},{2,18},{10... | collective-permute-start | bytes 393224 | tf_op jit(solution)/shard_map/ppermute | solution.py:919
  84.2 10.0 %collective-permute-start.8 = (bf16[256,256]{1,0:T(8,128)(2,1)}, bf16[256,256]{1,0:T(8,128)(2,1)S(1)}, u32[]{:S(2)}, u32[]{:S(2)}) collective-permute-start(bf16[256,256]{1,0:T(8,128)(2,1)} %get-tuple-element.143), channel_id=1, source_target_pairs={{0,8},{8,16},{16,24},{24,0},{1,9},{9,17},{17,25},{25,1},{2,10},{10... | collective-permute-start | bytes 393224 | tf_op jit(solution)/shard_map/ppermute | solution.py:919
  85.5 15.0 %copy-start.1 = (bf16[128,4096]{1,0:T(8,128)(2,1)}, bf16[128,4096]{1,0:T(8,128)(2,1)S(1)}, u32[]{:S(2)}) copy-start(bf16[128,4096]{1,0:T(8,128)(2,1)S(1)} %pad_maximum_fusion.1.refs_6_.refs_10_) | copy-start | bytes 3145732
  94.2 6.3 %collective-permute-start.12 = (bf16[128,4096]{1,0:T(8,128)(2,1)S(1)}, bf16[128,4096]{1,0:T(8,128)(2,1)}, u32[]{:S(2)}, u32[]{:S(2)}) collective-permute-start(bf16[128,4096]{1,0:T(8,128)(2,1)S(1)} %collective-permute-done.4.refs_2_.refs_6_), channel_id=1, source_target_pairs={{0,1},{1,0},{2,3},{3,2},{4,5},{5,4},{6,7},{7,6},{8,9},{9,8},{10,11... | collective-permute-start | bytes 3145736 | tf_op jit(solution)/shard_map/ppermute | solution.py:923
  94.3 6.3 %collective-permute-start.13 = (bf16[128,4096]{1,0:T(8,128)(2,1)S(1)}, bf16[128,4096]{1,0:T(8,128)(2,1)}, u32[]{:S(2)}, u32[]{:S(2)}) collective-permute-start(bf16[128,4096]{1,0:T(8,128)(2,1)S(1)} %collective-permute-done.5.refs_4_.refs_8_), channel_id=1, source_target_pairs={{0,1},{1,0},{2,3},{3,2},{4,5},{5,4},{6,7},{7,6},{8,9},{9,8},{10,11... | collective-permute-start | bytes 3145736 | tf_op jit(solution)/shard_map/ppermute | solution.py:923
  94.8 5.8 %collective-permute-start.14 = (bf16[128,4096]{1,0:T(8,128)(2,1)S(1)}, bf16[128,4096]{1,0:T(8,128)(2,1)}, u32[]{:S(2)}, u32[]{:S(2)}) collective-permute-start(bf16[128,4096]{1,0:T(8,128)(2,1)S(1)} %pad_maximum_fusion.1.refs_6_.refs_10_), channel_id=1, source_target_pairs={{0,1},{1,0},{2,3},{3,2},{4,5},{5,4},{6,7},{7,6},{8,9},{9,8},{10,11... | collective-permute-start | bytes 3145736 | tf_op jit(solution)/shard_map/ppermute | solution.py:923
  110.2 34.6 %collective-permute-start.18 = (bf16[6,256,1024]{2,1,0:T(8,128)(2,1)}, bf16[6,256,1024]{2,1,0:T(8,128)(2,1)S(1)}, u32[]{:S(2)}, u32[]{:S(2)}) collective-permute-start(bf16[6,256,1024]{2,1,0:T(8,128)(2,1)} %get-tuple-element.159.acts.lo.ho), channel_id=1, source_target_pairs={{0,1},{1,0},{2,3},{3,2},{4,5},{5,4},{6,7},{7,6},{8,9},{9,8},{10,11... | collective-permute-start | bytes 9437192 | tf_op jit(solution)/shard_map/ppermute | solution.py:923
  139.2 6.1 %collective-permute-start.19 = (bf16[6,256,1024]{2,1,0:T(8,128)(2,1)}, bf16[6,256,1024]{2,1,0:T(8,128)(2,1)}, u32[]{:S(2)}, u32[]{:S(2)}) collective-permute-start(bf16[6,256,1024]{2,1,0:T(8,128)(2,1)} %get-tuple-element.177.go), channel_id=1, source_target_pairs={{0,1},{1,0},{2,3},{3,2},{4,5},{5,4},{6,7},{7,6},{8,9},{9,8},{10,11... | collective-permute-start | bytes 9437192 | tf_op jit(solution)/shard_map/ppermute | solution.py:923
  139.5 15.9 %collective-permute-start.15 = (bf16[256,256]{1,0:T(8,128)(2,1)}, bf16[256,256]{1,0:T(8,128)(2,1)S(1)}, u32[]{:S(2)}, u32[]{:S(2)}) collective-permute-start(bf16[256,256]{1,0:T(8,128)(2,1)} %get-tuple-element.174), channel_id=1, source_target_pairs={{0,8},{8,16},{16,24},{24,0},{1,9},{9,17},{17,25},{25,1},{2,10},{10... | collective-permute-start | bytes 393224 | tf_op jit(solution)/shard_map/ppermute | solution.py:919
  141.0 14.4 %collective-permute-start.16 = (bf16[256,256]{1,0:T(8,128)(2,1)}, bf16[256,256]{1,0:T(8,128)(2,1)S(1)}, u32[]{:S(2)}, u32[]{:S(2)}) collective-permute-start(bf16[256,256]{1,0:T(8,128)(2,1)} %get-tuple-element.175), channel_id=1, source_target_pairs={{0,16},{8,24},{16,0},{24,8},{1,17},{9,25},{17,1},{25,9},{2,18},{10... | collective-permute-start | bytes 393224 | tf_op jit(solution)/shard_map/ppermute | solution.py:919
  143.4 12.0 %collective-permute-start.17 = (bf16[256,256]{1,0:T(8,128)(2,1)}, bf16[256,256]{1,0:T(8,128)(2,1)S(1)}, u32[]{:S(2)}, u32[]{:S(2)}) collective-permute-start(bf16[256,256]{1,0:T(8,128)(2,1)} %get-tuple-element.176), channel_id=1, source_target_pairs={{0,24},{8,0},{16,8},{24,16},{1,25},{9,1},{17,9},{25,17},{2,26},{10... | collective-permute-start | bytes 393224 | tf_op jit(solution)/shard_map/ppermute | solution.py:919
  155.5 30.4 %collective-permute-start.21 = (bf16[640,1024]{1,0:T(8,128)(2,1)}, bf16[640,1024]{1,0:T(8,128)(2,1)S(1)}, u32[]{:S(2)}, u32[]{:S(2)}) collective-permute-start(bf16[640,1024]{1,0:T(8,128)(2,1)} %get-tuple-element.188), channel_id=1, source_target_pairs={{0,4},{1,5},{2,6},{3,7},{4,0},{5,1},{6,2},{7,3},{8,12},{9,13},{10,... | collective-permute-start | bytes 3932168 | tf_op jit(solution)/shard_map/ppermute | solution.py:923
  160.4 24.6 %collective-permute-start.20 = (bf16[512,1024]{1,0:T(8,128)(2,1)}, bf16[512,1024]{1,0:T(8,128)(2,1)}, u32[]{:S(2)}, u32[]{:S(2)}) collective-permute-start(bf16[512,1024]{1,0:T(8,128)(2,1)} %down_grads.2), channel_id=1, source_target_pairs={{0,2},{1,3},{2,0},{3,1},{4,6},{5,7},{6,4},{7,5},{8,10},{9,11},{10,... | collective-permute-start | bytes 3145736 | tf_op jit(solution)/shard_map/ppermute | solution.py:923
  177.5 8.4 %copy-start.5 = (bf16[640,1024]{1,0:T(8,128)(2,1)S(1)}, bf16[640,1024]{1,0:T(8,128)(2,1)}, u32[]{:S(2)}) copy-start(bf16[640,1024]{1,0:T(8,128)(2,1)} %get-tuple-element.191) | copy-start | bytes 3932164
  185.8 98.2 %reduce-scatter.5.cloned.1.call-start = ((), (), s32[]{:S(2)}) async-start(), calls=%async_computation.3 | async-start | bytes 2064384 | tf_op jit(solution)/shard_map/reduce_scatter | solution.py:1090
  187.5 29.5 %collective-permute-start.22 = (bf16[640,1024]{1,0:T(8,128)(2,1)}, bf16[640,1024]{1,0:T(8,128)(2,1)S(1)}, u32[]{:S(2)}, u32[]{:S(2)}) collective-permute-start(bf16[640,1024]{1,0:T(8,128)(2,1)} %add_convert_fusion), channel_id=1, source_target_pairs={{0,2},{1,3},{2,0},{3,1},{4,6},{5,7},{6,4},{7,5},{8,10},{9,11},{10,... | collective-permute-start | bytes 3932168 | tf_op jit(solution)/shard_map/ppermute | solution.py:923
  189.0 29.3 %collective-permute-start.23 = (bf16[640,1024]{1,0:T(8,128)(2,1)}, bf16[640,1024]{1,0:T(8,128)(2,1)}, u32[]{:S(2)}, u32[]{:S(2)}) collective-permute-start(bf16[640,1024]{1,0:T(8,128)(2,1)} %get-tuple-element.197), channel_id=1, source_target_pairs={{0,4},{1,5},{2,6},{3,7},{4,0},{5,1},{6,2},{7,3},{8,12},{9,13},{10,... | collective-permute-start | bytes 3932168 | tf_op jit(solution)/shard_map/ppermute | solution.py:923
  201.5 16.9 %copy-start.4 = (bf16[640,1024]{1,0:T(8,128)(2,1)S(1)}, bf16[640,1024]{1,0:T(8,128)(2,1)}, u32[]{:S(2)}) copy-start(bf16[640,1024]{1,0:T(8,128)(2,1)} %get-tuple-element.190) | copy-start | bytes 3932164
  203.5 16.3 %copy-start.19 = (bf16[512,1024]{1,0:T(8,128)(2,1)S(1)}, bf16[512,1024]{1,0:T(8,128)(2,1)}, u32[]{:S(2)}) copy-start(bf16[512,1024]{1,0:T(8,128)(2,1)} %get-tuple-element.209) | copy-start | bytes 3145732
  219.8 22.6 %collective-permute-start.24 = (bf16[512,1024]{1,0:T(8,128)(2,1)S(1)}, bf16[512,1024]{1,0:T(8,128)(2,1)}, u32[]{:S(2)}, u32[]{:S(2)}) collective-permute-start(bf16[512,1024]{1,0:T(8,128)(2,1)S(1)} %copy-done.19), channel_id=1, source_target_pairs={{0,2},{1,3},{2,0},{3,1},{4,6},{5,7},{6,4},{7,5},{8,10},{9,11},{10,... | collective-permute-start | bytes 3145736 | tf_op jit(solution)/shard_map/ppermute | solution.py:923
  220.4 22.3 %collective-permute-start.25 = (bf16[512,1024]{1,0:T(8,128)(2,1)S(1)}, bf16[512,1024]{1,0:T(8,128)(2,1)}, u32[]{:S(2)}, u32[]{:S(2)}) collective-permute-start(bf16[512,1024]{1,0:T(8,128)(2,1)S(1)} %add_convert_fusion.1), channel_id=1, source_target_pairs={{0,4},{1,5},{2,6},{3,7},{4,0},{5,1},{6,2},{7,3},{8,12},{9,13},{10,... | collective-permute-start | bytes 3145736 | tf_op jit(solution)/shard_map/ppermute | solution.py:923
  221.5 20.0 %collective-permute-start.26 = (bf16[320,1024]{1,0:T(8,128)(2,1)S(1)}, bf16[320,1024]{1,0:T(8,128)(2,1)}, u32[]{:S(2)}, u32[]{:S(2)}) collective-permute-start(bf16[320,1024]{1,0:T(8,128)(2,1)S(1)} %add_convert_fusion.4), channel_id=1, source_target_pairs={{0,8},{8,0},{16,24},{24,16},{1,9},{9,1},{17,25},{25,17},{2,10},{10... | collective-permute-start | bytes 1966088 | tf_op jit(solution)/shard_map/ppermute | solution.py:934
  244.5 30.1 %collective-permute-start.28 = (bf16[320,1024]{1,0:T(8,128)(2,1)S(1)}, bf16[320,1024]{1,0:T(8,128)(2,1)}, u32[]{:S(2)}, u32[]{:S(2)}) collective-permute-start(bf16[320,1024]{1,0:T(8,128)(2,1)S(1)} %add_convert_fusion.3), channel_id=1, source_target_pairs={{0,16},{8,24},{16,0},{24,8},{1,17},{9,25},{17,1},{25,9},{2,18},{10... | collective-permute-start | bytes 1966088 | tf_op jit(solution)/shard_map/ppermute | solution.py:934
  249.9 26.5 %collective-permute-start.27 = (bf16[256,1024]{1,0:T(8,128)(2,1)S(1)}, bf16[256,1024]{1,0:T(8,128)(2,1)}, u32[]{:S(2)}, u32[]{:S(2)}) collective-permute-start(bf16[256,1024]{1,0:T(8,128)(2,1)S(1)} %add_convert_fusion.7), channel_id=1, source_target_pairs={{0,8},{8,0},{16,24},{24,16},{1,9},{9,1},{17,25},{25,17},{2,10},{10... | collective-permute-start | bytes 1572872 | tf_op jit(solution)/shard_map/ppermute | solution.py:934
  251.5 37.8 %copy-start.6 = (f32[256,1024]{1,0:T(8,128)S(1)}, f32[256,1024]{1,0:T(8,128)}, u32[]{:S(2)}) copy-start(f32[256,1024]{1,0:T(8,128)} %get-tuple-element.166) | copy-start | bytes 3145732
  276.0 39.7 %collective-permute-start.30 = (bf16[320,1024]{1,0:T(8,128)(2,1)S(1)}, bf16[320,1024]{1,0:T(8,128)(2,1)S(1)}, u32[]{:S(2)}, u32[]{:S(2)}) collective-permute-start(bf16[320,1024]{1,0:T(8,128)(2,1)S(1)} %add_convert_fusion.2), channel_id=1, source_target_pairs={{0,8},{8,0},{16,24},{24,16},{1,9},{9,1},{17,25},{25,17},{2,10},{10... | collective-permute-start | bytes 1966088 | tf_op jit(solution)/shard_map/ppermute | solution.py:934
  278.3 37.4 %collective-permute-start.29 = (bf16[256,1024]{1,0:T(8,128)(2,1)S(1)}, bf16[256,1024]{1,0:T(8,128)(2,1)S(1)}, u32[]{:S(2)}, u32[]{:S(2)}) collective-permute-start(bf16[256,1024]{1,0:T(8,128)(2,1)S(1)} %add_convert_fusion.6), channel_id=1, source_target_pairs={{0,16},{8,24},{16,0},{24,8},{1,17},{9,25},{17,1},{25,9},{2,18},{10... | collective-permute-start | bytes 1572872 | tf_op jit(solution)/shard_map/ppermute | solution.py:934
  284.0 31.6 %collective-permute-start.31 = (bf16[128,896]{1,0:T(8,128)(2,1)}, bf16[128,896]{1,0:T(8,128)(2,1)S(1)}, u32[]{:S(2)}, u32[]{:S(2)}) collective-permute-start(bf16[128,896]{1,0:T(8,128)(2,1)} %reduce-scatter.5.cloned.1.call-done.refs_0_), channel_id=1, source_target_pairs={{0,8},{8,16},{16,24},{24,0},{1,9},{9,17},{17,25},{25,1},{2,10},{10... | collective-permute-start | bytes 688136 | tf_op jit(solution)/shard_map/ppermute | solution.py:919
  285.5 35.2 %collective-permute-start.32 = (bf16[128,896]{1,0:T(8,128)(2,1)}, bf16[128,896]{1,0:T(8,128)(2,1)S(1)}, u32[]{:S(2)}, u32[]{:S(2)}) collective-permute-start(bf16[128,896]{1,0:T(8,128)(2,1)} %reduce-scatter.5.cloned.1.call-done.refs_0_), channel_id=1, source_target_pairs={{0,16},{8,24},{16,0},{24,8},{1,17},{9,25},{17,1},{25,9},{2,18},{10... | collective-permute-start | bytes 688136 | tf_op jit(solution)/shard_map/ppermute | solution.py:919
  287.9 32.9 %collective-permute-start.33 = (bf16[128,896]{1,0:T(8,128)(2,1)}, bf16[128,896]{1,0:T(8,128)(2,1)S(1)}, u32[]{:S(2)}, u32[]{:S(2)}) collective-permute-start(bf16[128,896]{1,0:T(8,128)(2,1)} %reduce-scatter.5.cloned.1.call-done.refs_0_), channel_id=1, source_target_pairs={{0,24},{8,0},{16,8},{24,16},{1,25},{9,1},{17,9},{25,17},{2,26},{10... | collective-permute-start | bytes 688136 | tf_op jit(solution)/shard_map/ppermute | solution.py:919
  321.5 15.6 %collective-permute-start.34 = (bf16[256,1024]{1,0:T(8,128)(2,1)S(1)}, bf16[256,1024]{1,0:T(8,128)(2,1)S(1)}, u32[]{:S(2)}, u32[]{:S(2)}) collective-permute-start(bf16[256,1024]{1,0:T(8,128)(2,1)S(1)} %add_convert_fusion.5), channel_id=1, source_target_pairs={{0,8},{8,0},{16,24},{24,16},{1,9},{9,1},{17,25},{25,17},{2,10},{10... | collective-permute-start | bytes 1572872 | tf_op jit(solution)/shard_map/ppermute | solution.py:934
  (11 other events, 33.6 us)
Sparse Core Ops, SparseCore 0:
  10.5 49.6 all-gather.4
  62.1 56.2 all-gather.6
  186.0 46.5 reduce-scatter.2
  242.9 41.1 reduce-scatter.4

commit v6 on v5

--- a/solution.py
+++ b/solution.py
@@ -397,8 +397,8 @@
     )(low, low_rel, mixed, *ups, pack)
 
 
-def mlp_tail_kernel(sc, acts, down_cols, down_rows, slope, small, valid, inv, *refs):
-    far = refs[0 : SHARDS + 4]
+def mlp_tail_kernel(sc, acts, slope, small, valid, inv, *refs):
+    far = refs[0 : SHARDS + 5]
     (
         out,
         grads,
@@ -422,12 +422,16 @@
         cot,
         scaled,
         wout,
+        rows_d,
         sems,
-    ) = refs[SHARDS + 4 :]
+    ) = refs[SHARDS + 5 :]
     s = pl.program_id(0)
     z = sc[0]
-    targets = [normed, cot, scaled, wout] + [held.at[n] for n in range(SHARDS)]
-    sources = [far[0], far[1], far[2], far[3].at[:, 0:ROWS, :]] + list(far[4:])
+    halves = [(slice(None), slice(None), slice(512 * n, 512 * n + 512)) for n in range(2)]
+    targets = [rows_d.at[h] for h in halves] + [normed, cot, scaled, wout]
+    targets += [held.at[n] for n in range(SHARDS)]
+    sources = [far[0].at[h] for h in halves]
+    sources += [far[1], far[2], far[3], far[4].at[:, 0:ROWS, :]] + list(far[5:])
     copies = [
         pltpu.make_async_copy(src, dst, sems.at[n])
         for n, (src, dst) in enumerate(zip(sources, targets))
@@ -443,17 +447,19 @@
         for copy in copies:
             copy.start()
 
+    for n in range(2):
+        pl.when(s == n)(copies[n].wait)
+
     @pl.when(s < 2)
     def _():
         hidden = jnp.concatenate([acts[b] for b in range(4)], axis=1)
         for n in range(2):
             cols = pl.ds(pl.multiple_of(jnp.minimum(s, 1) * 512 + 256 * n, 256), 256)
-            part = down_cols[:, :, 256 * n : 256 * n + 256].reshape(4096, 256)
-            acc[:, cols] = dot(hidden, part)
+            acc[:, cols] = dot(hidden, rows_d[:, :, cols].reshape(4096, 256))
 
     @pl.when(s == 1)
     def _():
-        for copy in copies[0:2]:
+        for copy in copies[2:4]:
             copy.wait()
         bias, gain, shift_by = vec(small, 0, 640, 128), vec(small, 1, 0, 128), vec(small, 1, 128, 128)
 
@@ -481,7 +487,7 @@
     @pl.when((s >= 2) & (s < 6))
     def _():
         j = jnp.clip(s - 2, 0, 3)
-        pre[...] = dot(gm[...], down_rows[...].reshape(1024, 1024), ((1,), (1,)))
+        pre[...] = dot(gm[...], rows_d[pl.ds(2 * j, 2)].reshape(1024, 1024), ((1,), (1,)))
         for n in range(2):
             cols = slice(512 * n, 512 * n + 512)
             total_ub = jnp.zeros((8, 512), F32)
@@ -499,7 +505,7 @@
     @pl.when(s == 6)
     def _():
         grads[0] = gm[...]
-        for copy in copies[2:]:
+        for copy in copies[4:]:
             copy.wait()
 
     @pl.when(s >= 6)
@@ -556,14 +562,12 @@
         in_specs=[
             SMEM_SPEC,
             full(4, CHUNK, 1024),
-            pl.BlockSpec((SHARDS, 512, 512), lambda s: (0, 0, jnp.minimum(s, 1))),
-            pl.BlockSpec((2, 512, 1024), lambda s: (block(s), 0, 0)),
             pl.BlockSpec((CHUNK, 1024), lambda s: (0, block(s))),
             SMALL_SPEC,
             full(CHUNK, 128),
             full(CHUNK, 128),
         ]
-        + [pl.BlockSpec(memory_space=pl.ANY)] * (SHARDS + 4),
+        + [pl.BlockSpec(memory_space=pl.ANY)] * (SHARDS + 5),
         out_specs=(
             full(CHUNK, 1024),
             pl.BlockSpec((1, CHUNK, 1024), grads_at),
@@ -595,10 +599,11 @@
             pltpu.VMEM((CHUNK, 1024), BF),
             pltpu.VMEM((CHUNK, 1024), F32),
             pltpu.VMEM((SHARDS, ROWS, 1024), BF),
-            pltpu.SemaphoreType.DMA((SHARDS + 4,)),
+            pltpu.VMEM((SHARDS, 512, 1024), BF),
+            pltpu.SemaphoreType.DMA((SHARDS + 6,)),
         ],
         compiler_params=PARAMS,
-    )(scalars, acts, down, down, slope, pack, valid, inv, normed, cot, scaled, pack, *ups)
+    )(scalars, acts, slope, pack, valid, inv, down, normed, cot, scaled, pack, *ups)
 
 
 REST = 640

time: 346 us -> 345 us (level)
  no operation moved by 1% of the time
where the time goes in v6:
time: 345 us; the launch traced here: 344 us
  waiting for transfers between devices  159 us (46%)
  Pallas kernels  95.6 us (28%)
  starting transfers between devices  51.9 us (15%)
  other arithmetic  19.5 us (6%)
  between operations  14.2 us (4%)
  local copies, waits for them, and re-layouts  3.71 us (1%)
    ppermute x6, waiting for transfers between devices, neighbour(): return lax.ppermute(x, 'ctx', [(i, i ^ bits) for i in range(4)])  71.1 us
    ppermute x16, waiting for transfers between devices, swap(): lax.ppermute(x, 'fsdp', [(i, i ^ bits) for i in range(lax.axis_size('fsdp...  29.6 us
    pallas_call x1, Pallas kernels, mlp_tail(): pl.pallas_call(mlp_tail_kernel, name='mlp_tail', grid=(8,), in_specs=[SME...  19.4 us
    ppermute x1, waiting for transfers between devices, line_gather(): two = lax.ppermute(x, 'ctx', [(0, 2), (1, 3), (2, 0), (3, 1)])  17.8 us
    pallas_call x1, Pallas kernels, attn_bwd(): pl.pallas_call(attn_bwd_kernel, name='attn_bwd', out_shape=(shape((1024,...  16.1 us
    ppermute x6, starting transfers between devices, neighbour(): return lax.ppermute(x, 'ctx', [(i, i ^ bits) for i in range(4)])  15.7 us
    pallas_call x1, Pallas kernels, attn_fwd(): pl.pallas_call(attn_fwd_kernel, name='attn_fwd', out_shape=(shape((CHUNK,...  15.2 us
    ppermute x9, waiting for transfers between devices, shift(): return lax.ppermute(x, 'ctx', [(i, (i + k) % n) for i in range(n)])  13.8 us
  transfers between devices with their start and end apart: 39, of which 23 were waited for; matrix products, arithmetic and copies ran while one was open for 5% of the time, Pallas kernels for 27%

profile of v6, /device:TPU:0, one launch (start us, length us, event | category | flops | bytes accessed | tf_op | source)
XLA Modules:
  0.0 343.9 jit_solution(9982490524085700641)
XLA Ops:
  7.9 2.5 pack_inputs.1
  10.4 4.1 %collective-permute-start.2 = (bf16[272,1024]{1,0:T(8,128)(2,1)}, bf16[272,1024]{1,0:T(8,128)(2,1)S(1)}, u32[]{:S(2)}, u32[]{:S(2)}) collective-permute-start(bf16[272,1024]{1,0:T(8,128)(2,1)} %get-tuple-element.134.x0), channel_id=1, source_target_pairs={{0,16},{8,24},{16,0},{24,8},{1,17},{9,25},{17,1},{25,9},{2,18},{10... | collective-permute-start | bytes 1671176 | tf_op jit(solution)/shard_map/ppermute | solution.py:914
  14.5 1.5 collective-permute-start.4
  16.0 1.5 collective-permute-start.5
  17.6 3.5 %collective-permute-start = (bf16[272,1024]{1,0:T(8,128)(2,1)}, bf16[272,1024]{1,0:T(8,128)(2,1)S(1)}, u32[]{:S(2)}, u32[]{:S(2)}) collective-permute-start(bf16[272,1024]{1,0:T(8,128)(2,1)} %get-tuple-element.134.x0), channel_id=1, source_target_pairs={{0,8},{8,16},{16,24},{1,9},{9,17},{17,25},{2,10},{10,18},{18,26},{... | collective-permute-start | bytes 1671176 | tf_op jit(solution)/shard_map/ppermute | solution.py:912
  22.4 17.8 %collective-permute-done.2.x2 = bf16[272,1024]{1,0:T(8,128)(2,1)S(1)} collective-permute-done((bf16[272,1024]{1,0:T(8,128)(2,1)}, bf16[272,1024]{1,0:T(8,128)(2,1)S(1)}, u32[]{:S(2)}, u32[]{:S(2)}) %collective-permute-start.2) | collective-permute-done | bytes 557088 | tf_op jit(solution)/shard_map/ppermute | solution.py:914
  41.5 8.0 %collective-permute-done.1.left = bf16[272,1024]{1,0:T(8,128)(2,1)S(1)} collective-permute-done((bf16[272,1024]{1,0:T(8,128)(2,1)}, bf16[272,1024]{1,0:T(8,128)(2,1)S(1)}, u32[]{:S(2)}, u32[]{:S(2)}) %collective-permute-start.1) | collective-permute-done | bytes 557088 | tf_op jit(solution)/shard_map/ppermute | solution.py:913
  49.5 2.1 collective-permute-done.5.refs_4_.refs_9_
  51.6 7.6 %collective-permute-done.3.far = bf16[272,1024]{1,0:T(8,128)(2,1)} collective-permute-done((bf16[272,1024]{1,0:T(8,128)(2,1)S(1)}, bf16[272,1024]{1,0:T(8,128)(2,1)}, u32[]{:S(2)}, u32[]{:S(2)}) %collective-permute-start.3) | collective-permute-done | bytes 557088 | tf_op jit(solution)/shard_map/ppermute | solution.py:919
  61.8 1.5 collective-permute-start.9
  63.3 15.2 %attn_fwd.1 = (bf16[256,256]{1,0:T(8,128)(2,1)}, bf16[256,256]{1,0:T(8,128)(2,1)}, bf16[256,256]{1,0:T(8,128)(2,1)}, bf16[256,256]{1,0:T(8,128)(2,1)}, f32[256,1...) custom-call(s32[4]{0:T(128)} %pad_add_fusion.sc, ...), custom_call_target="tpu_custom_call" | custom-call | tf_op jit(solution)/shard_map/attn_fwd/pallas_call | solution.py:223
  78.7 2.6 collective-permute-done.9
  81.3 2.9 collective-permute-start.7
  85.5 2.5 collective-permute-done.6.r1
  88.0 6.1 %collective-permute-done.7.r2 = bf16[256,256]{1,0:T(8,128)(2,1)S(1)} collective-permute-done((bf16[256,256]{1,0:T(8,128)(2,1)}, bf16[256,256]{1,0:T(8,128)(2,1)S(1)}, u32[]{:S(2)}, u32[]{:S(2)}) %collective-permute-start.7) | collective-permute-done | bytes 131104 | tf_op jit(solution)/shard_map/ppermute | solution.py:924
  94.9 5.6 %out_project.1 = (f32[256,1024]{1,0:T(8,128)}, bf16[256,1024]{1,0:T(8,128)(2,1)}, bf16[256,1024]{1,0:T(8,128)(2,1)}, f32[256,1024]{1,0:T(8,128)}, f32[256,128]{1...) custom-call(s32[4]{0:T(128)} %pad_add_fusion.sc, bf16[256,1024]{1,0:T(8,128)(2,1)} %bitcast.41, ...), custom_call_target="tpu_custom_call" | custom-call | tf_op jit(solution)/shard_map/out_project/pallas_call | solution.py:329
  100.6 9.7 %mlp_gate.1 = (bf16[6,256,1024]{2,1,0:T(8,128)(2,1)}, f32[256,4096]{1,0:T(8,128)}) custom-call(bf16[256,1024]{1,0:T(8,128)(2,1)} %get-tuple-element.153.low, bf16[256,1024]{1,0:T(8,128)(2,1)} %get-tuple-element.154.low_rel, bf16[256,1024]{1,0:T(8,128)(2,1)} %get-tuple-element.155.mixed, bf16[128,4096]{1,0:T(8,128)(2,1)} %refs_5_.1, ...), custom_call_target="tpu_custom_call" | custom-call | tf_op jit(solution)/shard_map/mlp_gate/pallas_call | solution.py:388
  110.5 7.9 %all-gather.7.cloned.1.call-done = bf16[4096,1024]{1,0:T(8,128)(2,1)} async-done(((bf16[512,1024]{1,0:T(8,128)(2,1)}), bf16[4096,1024]{1,0:T(8,128)(2,1)}) %all-gather.7.cloned.1.call-update) | async-done | bytes 8388624 | tf_op jit(solution)/shard_map/all_gather | solution.py:1020
  118.4 19.4 %mlp_tail.1 = (bf16[256,1024]{1,0:T(8,128)(2,1)}, bf16[6,256,1024]{2,1,0:T(8,128)(2,1)}, f32[256,1024]{1,0:T(8,128)}, bf16[256,256]{1,0:T(8,128)(2,1)}, bf16[256...) custom-call(s32[4]{0:T(128)} %pad_add_fusion.sc, ...), custom_call_target="tpu_custom_call" | custom-call | tf_op jit(solution)/shard_map/mlp_tail/pallas_call | solution.py:558
  139.6 2.4 collective-permute-start.16
  145.0 8.9 %rest_grads.1 = (bf16[640,1024]{1,0:T(8,128)(2,1)}, bf16[640,1024]{1,0:T(8,128)(2,1)}, bf16[640,1024]{1,0:T(8,128)(2,1)}, bf16[640,1024]{1,0:T(8,128)(2,1)}) custom-call(s32[4]{0:T(128)} %pad_add_fusion.sc, bf16[6,256,1024]{2,1,0:T(8,128)(2,1)} %get-tuple-element.159.acts.lo.ho, bf16[6,256,1024]{2,1,0:T(8,128)(2,1)} %copy-done, ...), custom_call_target="tpu_custom_call" | custom-call | tf_op jit(solution)/shard_map/rest_grads/pallas_call | solution.py:697
  155.2 3.8 %down_grads.2 = bf16[512,1024]{1,0:T(8,128)(2,1)} custom-call(s32[4]{0:T(128)} %pad_add_fusion.sc, bf16[6,256,1024]{2,1,0:T(8,128)(2,1)} %get-tuple-element.159.acts.lo.ho, bf16[6,256,1024]{2,1,0:T(8,128)(2,1)} %copy-done, bf16[6,256,1024]{2,1,0:T(8,128)(2,1)} %get-tuple-element.177.go, bf16[6,256,1024]{2,1,0:T(8,128)(2,1)} %collective-permute-done.19.gp), custom_call_target="tpu_custom_call" | custom-call | tf_op jit(solution)/shard_map/down_grads/pallas_call | solution.py:649
  160.0 16.1 %attn_bwd.1 = (bf16[1024,1024]{1,0:T(8,128)(2,1)}, bf16[1024,768]{1,0:T(8,128)(2,1)}) custom-call(s32[4]{0:T(128)} %pad_add_fusion.sc, f32[4,8,256]{2,1,0:T(8,128)} %get-tuple-element.167.segr, bf16[8,272,1024]{2,1,0:T(8,128)(2,1)} %bitcast.38, bf16[4,1024,128]{2,1,0:T(8,128)(2,1)} %get-tuple-element.168.qm, bf16[1024,512]{1,0:T(8,128)(2,1)} %get-tuple-element.169.kv, ...), custom_call_target="tpu_custom_call" | custom-call | tf_op jit(solution)/shard_map/attn_bwd/pallas_call | solution.py:844
  176.1 7.5 %collective-permute-done.20 = bf16[512,1024]{1,0:T(8,128)(2,1)} collective-permute-done((bf16[512,1024]{1,0:T(8,128)(2,1)}, bf16[512,1024]{1,0:T(8,128)(2,1)}, u32[]{:S(2)}, u32[]{:S(2)}) %collective-permute-start.20) | collective-permute-done | bytes 1048608 | tf_op jit(solution)/shard_map/ppermute | solution.py:928
  184.5 1.6 add_convert_fusion
  188.1 6.5 %down_grads.3 = (bf16[512,1024]{1,0:T(8,128)(2,1)}, bf16[512,1024]{1,0:T(8,128)(2,1)}, bf16[512,1024]{1,0:T(8,128)(2,1)}) custom-call(s32[4]{0:T(128)} %pad_add_fusion.sc, bf16[6,256,1024]{2,1,0:T(8,128)(2,1)} %get-tuple-element.159.acts.lo.ho, bf16[6,256,1024]{2,1,0:T(8,128)(2,1)} %copy-done, bf16[6,256,1024]{2,1,0:T(8,128)(2,1)} %get-tuple-element.177.go, ...), custom_call_target="tpu_custom_call" | custom-call | tf_op jit(solution)/shard_map/down_grads/pallas_call | solution.py:649
  194.7 5.3 %qkv_grads.1 = bf16[1024,896]{1,0:T(8,128)(2,1)} custom-call(s32[4]{0:T(128)} %pad_add_fusion.sc, bf16[4,256,1024]{2,1,0:T(8,128)(2,1)} %get-tuple-element.198.xall, bf16[1024,768]{1,0:T(8,128)(2,1)} %get-tuple-element.199.dall, f32[8,1024]{1,0:T(8,128)} %get-tuple-element.200.sums_m, f32[8,1024]{1,0:T(8,128)} %get-tuple-element.201.sums_a, ...), custom_call_target="tpu_custom_call" | custom-call | tf_op jit(solution)/shard_map/qkv_grads/pallas_call | solution.py:831
  200.0 2.0 add_convert_fusion.1
  202.1 13.5 %collective-permute-done.22 = bf16[640,1024]{1,0:T(8,128)(2,1)S(1)} collective-permute-done((bf16[640,1024]{1,0:T(8,128)(2,1)}, bf16[640,1024]{1,0:T(8,128)(2,1)S(1)}, u32[]{:S(2)}, u32[]{:S(2)}) %collective-permute-start.22) | collective-permute-done | bytes 1310752 | tf_op jit(solution)/shard_map/ppermute | solution.py:928
  220.1 1.8 collective-permute-start.26
  221.9 18.1 %collective-permute-done.26 = bf16[320,1024]{1,0:T(8,128)(2,1)} collective-permute-done((bf16[320,1024]{1,0:T(8,128)(2,1)S(1)}, bf16[320,1024]{1,0:T(8,128)(2,1)}, u32[]{:S(2)}, u32[]{:S(2)}) %collective-permute-start.26) | collective-permute-done | bytes 655392 | tf_op jit(solution)/shard_map/ppermute | solution.py:939
  241.3 1.8 add_convert_fusion.3
  243.1 3.8 %collective-permute-start.28 = (bf16[320,1024]{1,0:T(8,128)(2,1)S(1)}, bf16[320,1024]{1,0:T(8,128)(2,1)}, u32[]{:S(2)}, u32[]{:S(2)}) collective-permute-start(bf16[320,1024]{1,0:T(8,128)(2,1)S(1)} %add_convert_fusion.3), channel_id=1, source_target_pairs={{0,16},{8,24},{16,0},{24,8},{1,17},{9,25},{17,1},{25,9},{2,18},{10... | collective-permute-start | bytes 1966088 | tf_op jit(solution)/shard_map/ppermute | solution.py:939
  246.9 1.6 add_convert_fusion.7
  248.5 1.5 collective-permute-start.27
  250.1 23.2 %collective-permute-done.28 = bf16[320,1024]{1,0:T(8,128)(2,1)} collective-permute-done((bf16[320,1024]{1,0:T(8,128)(2,1)S(1)}, bf16[320,1024]{1,0:T(8,128)(2,1)}, u32[]{:S(2)}, u32[]{:S(2)}) %collective-permute-start.28) | collective-permute-done | bytes 655392 | tf_op jit(solution)/shard_map/ppermute | solution.py:939
  275.0 1.9 add_convert_fusion.6
  276.9 3.6 %collective-permute-start.29 = (bf16[256,1024]{1,0:T(8,128)(2,1)S(1)}, bf16[256,1024]{1,0:T(8,128)(2,1)S(1)}, u32[]{:S(2)}, u32[]{:S(2)}) collective-permute-start(bf16[256,1024]{1,0:T(8,128)(2,1)S(1)} %add_convert_fusion.6), channel_id=1, source_target_pairs={{0,16},{8,24},{16,0},{24,8},{1,17},{9,25},{17,1},{25,9},{2,18},{10... | collective-permute-start | bytes 1572872 | tf_op jit(solution)/shard_map/ppermute | solution.py:939
  280.5 2.2 reduce-scatter.5.cloned.1.call-done.refs_0_
  284.1 2.4 collective-permute-start.32
  288.0 2.1 add_bitcast_fusion
  290.1 24.0 %collective-permute-done.29 = bf16[256,1024]{1,0:T(8,128)(2,1)S(1)} collective-permute-done((bf16[256,1024]{1,0:T(8,128)(2,1)S(1)}, bf16[256,1024]{1,0:T(8,128)(2,1)S(1)}, u32[]{:S(2)}, u32[]{:S(2)}) %collective-permute-start.29) | collective-permute-done | bytes 524320 | tf_op jit(solution)/shard_map/ppermute | solution.py:939
  314.2 5.1 %collective-permute-done.32.refs_2_ = bf16[128,896]{1,0:T(8,128)(2,1)S(1)} collective-permute-done((bf16[128,896]{1,0:T(8,128)(2,1)}, bf16[128,896]{1,0:T(8,128)(2,1)S(1)}, u32[]{:S(2)}, u32[]{:S(2)}) %collective-permute-start.32) | collective-permute-done | bytes 229408 | tf_op jit(solution)/shard_map/ppermute | solution.py:924
  320.1 4.4 %collective-permute-start.34 = (bf16[256,1024]{1,0:T(8,128)(2,1)S(1)}, bf16[256,1024]{1,0:T(8,128)(2,1)S(1)}, u32[]{:S(2)}, u32[]{:S(2)}) collective-permute-start(bf16[256,1024]{1,0:T(8,128)(2,1)S(1)} %add_convert_fusion.5), channel_id=1, source_target_pairs={{0,8},{8,0},{16,24},{24,16},{1,9},{9,1},{17,25},{25,17},{2,10},{10... | collective-permute-start | bytes 1572872 | tf_op jit(solution)/shard_map/ppermute | solution.py:939
  325.9 2.5 finish.1
  328.4 1.5 pad_maximum_fusion
  330.0 5.8 %collective-permute-done.34 = bf16[256,1024]{1,0:T(8,128)(2,1)S(1)} collective-permute-done((bf16[256,1024]{1,0:T(8,128)(2,1)S(1)}, bf16[256,1024]{1,0:T(8,128)(2,1)S(1)}, u32[]{:S(2)}, u32[]{:S(2)}) %collective-permute-start.34) | collective-permute-done | bytes 524320 | tf_op jit(solution)/shard_map/ppermute | solution.py:939
  335.8 1.6 maximum_convert_fusion.1
  (104 shorter events, 30.8 us)
Async XLA Ops:
  7.2 53.1 %all-gather.5.cloned.1.call-start = ((), (), s32[]{:S(2)}) async-start(), calls=%async_computation.4 | async-start | bytes 5013504 | tf_op jit(solution)/shard_map/all_gather | solution.py:1011
  10.4 108.0 %all-gather.7.cloned.1.call-start = ((), (), s32[]{:S(2)}) async-start(), calls=%async_computation.5 | async-start | bytes 9437184 | tf_op jit(solution)/shard_map/all_gather | solution.py:1020
  10.4 29.7 %collective-permute-start.2 = (bf16[272,1024]{1,0:T(8,128)(2,1)}, bf16[272,1024]{1,0:T(8,128)(2,1)S(1)}, u32[]{:S(2)}, u32[]{:S(2)}) collective-permute-start(bf16[272,1024]{1,0:T(8,128)(2,1)} %get-tuple-element.134.x0), channel_id=1, source_target_pairs={{0,16},{8,24},{16,0},{24,8},{1,17},{9,25},{17,1},{25,9},{2,18},{10... | collective-permute-start | bytes 1671176 | tf_op jit(solution)/shard_map/ppermute | solution.py:914
  14.5 35.0 %collective-permute-start.4 = (bf16[128,4096]{1,0:T(8,128)(2,1)}, bf16[128,4096]{1,0:T(8,128)(2,1)S(1)}, u32[]{:S(2)}, u32[]{:S(2)}) collective-permute-start(bf16[128,4096]{1,0:T(8,128)(2,1)} %refs_5_.1), channel_id=1, source_target_pairs={{0,2},{1,3},{2,0},{3,1},{4,6},{5,7},{6,4},{7,5},{8,10},{9,11},{10,... | collective-permute-start | bytes 3145736 | tf_op jit(solution)/shard_map/ppermute | solution.py:928
  16.0 35.6 %collective-permute-start.5 = (bf16[128,4096]{1,0:T(8,128)(2,1)}, bf16[128,4096]{1,0:T(8,128)(2,1)S(1)}, u32[]{:S(2)}, u32[]{:S(2)}) collective-permute-start(bf16[128,4096]{1,0:T(8,128)(2,1)} %refs_5_.1), channel_id=1, source_target_pairs={{0,4},{1,5},{2,6},{3,7},{4,0},{5,1},{6,2},{7,3},{8,12},{9,13},{10,... | collective-permute-start | bytes 3145736 | tf_op jit(solution)/shard_map/ppermute | solution.py:928
  17.6 23.9 %collective-permute-start = (bf16[272,1024]{1,0:T(8,128)(2,1)}, bf16[272,1024]{1,0:T(8,128)(2,1)S(1)}, u32[]{:S(2)}, u32[]{:S(2)}) collective-permute-start(bf16[272,1024]{1,0:T(8,128)(2,1)} %get-tuple-element.134.x0), channel_id=1, source_target_pairs={{0,8},{8,16},{16,24},{1,9},{9,17},{17,25},{2,10},{10,18},{18,26},{... | collective-permute-start | bytes 1671176 | tf_op jit(solution)/shard_map/ppermute | solution.py:912
  21.1 28.4 %collective-permute-start.1 = (bf16[272,1024]{1,0:T(8,128)(2,1)}, bf16[272,1024]{1,0:T(8,128)(2,1)S(1)}, u32[]{:S(2)}, u32[]{:S(2)}) collective-permute-start(bf16[272,1024]{1,0:T(8,128)(2,1)} %get-tuple-element.134.x0), channel_id=1, source_target_pairs={{8,0},{16,8},{24,16},{9,1},{17,9},{25,17},{10,2},{18,10},{26,18},{... | collective-permute-start | bytes 1671176 | tf_op jit(solution)/shard_map/ppermute | solution.py:913
  40.2 23.1 %copy-start.7 = (bf16[272,1024]{1,0:T(8,128)(2,1)}, bf16[272,1024]{1,0:T(8,128)(2,1)S(1)}, u32[]{:S(2)}) copy-start(bf16[272,1024]{1,0:T(8,128)(2,1)S(1)} %collective-permute-done.2.x2) | copy-start | bytes 1671172
  40.2 19.0 %collective-permute-start.3 = (bf16[272,1024]{1,0:T(8,128)(2,1)S(1)}, bf16[272,1024]{1,0:T(8,128)(2,1)}, u32[]{:S(2)}, u32[]{:S(2)}) collective-permute-start(bf16[272,1024]{1,0:T(8,128)(2,1)S(1)} %collective-permute-done.2.x2), channel_id=1, source_target_pairs={{8,0},{16,24},{9,1},{17,25},{10,2},{18,26},{11,3},{19,27},{12,4},{... | collective-permute-start | bytes 1671176 | tf_op jit(solution)/shard_map/ppermute | solution.py:919
  41.5 21.8 %copy-start.8 = (bf16[272,1024]{1,0:T(8,128)(2,1)}, bf16[272,1024]{1,0:T(8,128)(2,1)S(1)}, u32[]{:S(2)}) copy-start(bf16[272,1024]{1,0:T(8,128)(2,1)S(1)} %collective-permute-done.right) | copy-start | bytes 1671172
  49.5 44.7 %copy-start.2 = (bf16[128,4096]{1,0:T(8,128)(2,1)}, bf16[128,4096]{1,0:T(8,128)(2,1)S(1)}, u32[]{:S(2)}) copy-start(bf16[128,4096]{1,0:T(8,128)(2,1)S(1)} %collective-permute-done.4.refs_2_.refs_7_) | copy-start | bytes 3145732
  51.6 42.7 %copy-start.3 = (bf16[128,4096]{1,0:T(8,128)(2,1)}, bf16[128,4096]{1,0:T(8,128)(2,1)S(1)}, u32[]{:S(2)}) copy-start(bf16[128,4096]{1,0:T(8,128)(2,1)S(1)} %collective-permute-done.5.refs_4_.refs_9_) | copy-start | bytes 3145732
  60.3 181.0 %reduce-scatter.3.cloned.1.call-start = ((), (), s32[]{:S(2)}) async-start(), calls=%async_computation.2 | async-start | bytes 2621440 | tf_op jit(solution)/shard_map/reduce_scatter | solution.py:1082
  60.4 18.4 %collective-permute-start.10 = (bf16[128,2048]{1,0:T(8,128)(2,1)S(1)}, bf16[128,2048]{1,0:T(8,128)(2,1)}, u32[]{:S(2)}, u32[]{:S(2)}) collective-permute-start(bf16[128,2048]{1,0:T(8,128)(2,1)S(1)} %slice.29), channel_id=1, source_target_pairs={{0,2},{1,3},{2,0},{3,1},{4,6},{5,7},{6,4},{7,5},{8,10},{9,11},{10,... | collective-permute-start | bytes 1572872 | tf_op jit(solution)/shard_map/ppermute | solution.py:928
  61.8 19.5 %collective-permute-start.9 = (bf16[128,2048]{1,0:T(8,128)(2,1)}, bf16[128,2048]{1,0:T(8,128)(2,1)}, u32[]{:S(2)}, u32[]{:S(2)}) collective-permute-start(bf16[128,2048]{1,0:T(8,128)(2,1)} %slice.28), channel_id=1, source_target_pairs={{0,4},{1,5},{2,6},{3,7},{4,0},{5,1},{6,2},{7,3},{8,12},{9,13},{10,... | collective-permute-start | bytes 1572872 | tf_op jit(solution)/shard_map/ppermute | solution.py:928
  63.3 37.2 %collective-permute-start.11 = (bf16[128,4096]{1,0:T(8,128)(2,1)}, bf16[128,4096]{1,0:T(8,128)(2,1)}, u32[]{:S(2)}, u32[]{:S(2)}) collective-permute-start(bf16[128,4096]{1,0:T(8,128)(2,1)} %refs_5_.1), channel_id=1, source_target_pairs={{0,1},{1,0},{2,3},{3,2},{4,5},{5,4},{6,7},{7,6},{8,9},{9,8},{10,11... | collective-permute-start | bytes 3145736 | tf_op jit(solution)/shard_map/ppermute | solution.py:928
  81.3 6.7 %collective-permute-start.6 = (bf16[256,256]{1,0:T(8,128)(2,1)}, bf16[256,256]{1,0:T(8,128)(2,1)S(1)}, u32[]{:S(2)}, u32[]{:S(2)}) collective-permute-start(bf16[256,256]{1,0:T(8,128)(2,1)} %get-tuple-element.141), channel_id=1, source_target_pairs={{0,24},{8,0},{16,8},{24,16},{1,25},{9,1},{17,9},{25,17},{2,26},{10... | collective-permute-start | bytes 393224 | tf_op jit(solution)/shard_map/ppermute | solution.py:924
  81.3 12.8 %collective-permute-start.7 = (bf16[256,256]{1,0:T(8,128)(2,1)}, bf16[256,256]{1,0:T(8,128)(2,1)S(1)}, u32[]{:S(2)}, u32[]{:S(2)}) collective-permute-start(bf16[256,256]{1,0:T(8,128)(2,1)} %get-tuple-element.142), channel_id=1, source_target_pairs={{0,16},{8,24},{16,0},{24,8},{1,17},{9,25},{17,1},{25,9},{2,18},{10... | collective-permute-start | bytes 393224 | tf_op jit(solution)/shard_map/ppermute | solution.py:924
  84.2 10.0 %collective-permute-start.8 = (bf16[256,256]{1,0:T(8,128)(2,1)}, bf16[256,256]{1,0:T(8,128)(2,1)S(1)}, u32[]{:S(2)}, u32[]{:S(2)}) collective-permute-start(bf16[256,256]{1,0:T(8,128)(2,1)} %get-tuple-element.143), channel_id=1, source_target_pairs={{0,8},{8,16},{16,24},{24,0},{1,9},{9,17},{17,25},{25,1},{2,10},{10... | collective-permute-start | bytes 393224 | tf_op jit(solution)/shard_map/ppermute | solution.py:924
  85.5 15.0 %copy-start.1 = (bf16[128,4096]{1,0:T(8,128)(2,1)}, bf16[128,4096]{1,0:T(8,128)(2,1)S(1)}, u32[]{:S(2)}) copy-start(bf16[128,4096]{1,0:T(8,128)(2,1)S(1)} %pad_maximum_fusion.1.refs_6_.refs_11_) | copy-start | bytes 3145732
  94.2 6.3 %collective-permute-start.12 = (bf16[128,4096]{1,0:T(8,128)(2,1)S(1)}, bf16[128,4096]{1,0:T(8,128)(2,1)}, u32[]{:S(2)}, u32[]{:S(2)}) collective-permute-start(bf16[128,4096]{1,0:T(8,128)(2,1)S(1)} %collective-permute-done.4.refs_2_.refs_7_), channel_id=1, source_target_pairs={{0,1},{1,0},{2,3},{3,2},{4,5},{5,4},{6,7},{7,6},{8,9},{9,8},{10,11... | collective-permute-start | bytes 3145736 | tf_op jit(solution)/shard_map/ppermute | solution.py:928
  94.3 6.3 %collective-permute-start.13 = (bf16[128,4096]{1,0:T(8,128)(2,1)S(1)}, bf16[128,4096]{1,0:T(8,128)(2,1)}, u32[]{:S(2)}, u32[]{:S(2)}) collective-permute-start(bf16[128,4096]{1,0:T(8,128)(2,1)S(1)} %collective-permute-done.5.refs_4_.refs_9_), channel_id=1, source_target_pairs={{0,1},{1,0},{2,3},{3,2},{4,5},{5,4},{6,7},{7,6},{8,9},{9,8},{10,11... | collective-permute-start | bytes 3145736 | tf_op jit(solution)/shard_map/ppermute | solution.py:928
  94.8 5.8 %collective-permute-start.14 = (bf16[128,4096]{1,0:T(8,128)(2,1)S(1)}, bf16[128,4096]{1,0:T(8,128)(2,1)}, u32[]{:S(2)}, u32[]{:S(2)}) collective-permute-start(bf16[128,4096]{1,0:T(8,128)(2,1)S(1)} %pad_maximum_fusion.1.refs_6_.refs_11_), channel_id=1, source_target_pairs={{0,1},{1,0},{2,3},{3,2},{4,5},{5,4},{6,7},{7,6},{8,9},{9,8},{10,11... | collective-permute-start | bytes 3145736 | tf_op jit(solution)/shard_map/ppermute | solution.py:928
  110.2 33.2 %collective-permute-start.18 = (bf16[6,256,1024]{2,1,0:T(8,128)(2,1)}, bf16[6,256,1024]{2,1,0:T(8,128)(2,1)S(1)}, u32[]{:S(2)}, u32[]{:S(2)}) collective-permute-start(bf16[6,256,1024]{2,1,0:T(8,128)(2,1)} %get-tuple-element.159.acts.lo.ho), channel_id=1, source_target_pairs={{0,1},{1,0},{2,3},{3,2},{4,5},{5,4},{6,7},{7,6},{8,9},{9,8},{10,11... | collective-permute-start | bytes 9437192 | tf_op jit(solution)/shard_map/ppermute | solution.py:928
  137.8 6.1 %collective-permute-start.19 = (bf16[6,256,1024]{2,1,0:T(8,128)(2,1)}, bf16[6,256,1024]{2,1,0:T(8,128)(2,1)}, u32[]{:S(2)}, u32[]{:S(2)}) collective-permute-start(bf16[6,256,1024]{2,1,0:T(8,128)(2,1)} %get-tuple-element.177.go), channel_id=1, source_target_pairs={{0,1},{1,0},{2,3},{3,2},{4,5},{5,4},{6,7},{7,6},{8,9},{9,8},{10,11... | collective-permute-start | bytes 9437192 | tf_op jit(solution)/shard_map/ppermute | solution.py:928
  138.1 15.9 %collective-permute-start.15 = (bf16[256,256]{1,0:T(8,128)(2,1)}, bf16[256,256]{1,0:T(8,128)(2,1)S(1)}, u32[]{:S(2)}, u32[]{:S(2)}) collective-permute-start(bf16[256,256]{1,0:T(8,128)(2,1)} %get-tuple-element.174), channel_id=1, source_target_pairs={{0,8},{8,16},{16,24},{24,0},{1,9},{9,17},{17,25},{25,1},{2,10},{10... | collective-permute-start | bytes 393224 | tf_op jit(solution)/shard_map/ppermute | solution.py:924
  139.6 14.4 %collective-permute-start.16 = (bf16[256,256]{1,0:T(8,128)(2,1)}, bf16[256,256]{1,0:T(8,128)(2,1)S(1)}, u32[]{:S(2)}, u32[]{:S(2)}) collective-permute-start(bf16[256,256]{1,0:T(8,128)(2,1)} %get-tuple-element.175), channel_id=1, source_target_pairs={{0,16},{8,24},{16,0},{24,8},{1,17},{9,25},{17,1},{25,9},{2,18},{10... | collective-permute-start | bytes 393224 | tf_op jit(solution)/shard_map/ppermute | solution.py:924
  142.0 12.0 %collective-permute-start.17 = (bf16[256,256]{1,0:T(8,128)(2,1)}, bf16[256,256]{1,0:T(8,128)(2,1)S(1)}, u32[]{:S(2)}, u32[]{:S(2)}) collective-permute-start(bf16[256,256]{1,0:T(8,128)(2,1)} %get-tuple-element.176), channel_id=1, source_target_pairs={{0,24},{8,0},{16,8},{24,16},{1,25},{9,1},{17,9},{25,17},{2,26},{10... | collective-permute-start | bytes 393224 | tf_op jit(solution)/shard_map/ppermute | solution.py:924
  154.0 30.4 %collective-permute-start.21 = (bf16[640,1024]{1,0:T(8,128)(2,1)}, bf16[640,1024]{1,0:T(8,128)(2,1)S(1)}, u32[]{:S(2)}, u32[]{:S(2)}) collective-permute-start(bf16[640,1024]{1,0:T(8,128)(2,1)} %get-tuple-element.188), channel_id=1, source_target_pairs={{0,4},{1,5},{2,6},{3,7},{4,0},{5,1},{6,2},{7,3},{8,12},{9,13},{10,... | collective-permute-start | bytes 3932168 | tf_op jit(solution)/shard_map/ppermute | solution.py:928
  159.0 24.6 %collective-permute-start.20 = (bf16[512,1024]{1,0:T(8,128)(2,1)}, bf16[512,1024]{1,0:T(8,128)(2,1)}, u32[]{:S(2)}, u32[]{:S(2)}) collective-permute-start(bf16[512,1024]{1,0:T(8,128)(2,1)} %down_grads.2), channel_id=1, source_target_pairs={{0,2},{1,3},{2,0},{3,1},{4,6},{5,7},{6,4},{7,5},{8,10},{9,11},{10,... | collective-permute-start | bytes 3145736 | tf_op jit(solution)/shard_map/ppermute | solution.py:928
  176.1 8.4 %copy-start.5 = (bf16[640,1024]{1,0:T(8,128)(2,1)S(1)}, bf16[640,1024]{1,0:T(8,128)(2,1)}, u32[]{:S(2)}) copy-start(bf16[640,1024]{1,0:T(8,128)(2,1)} %get-tuple-element.191) | copy-start | bytes 3932164
  184.4 98.2 %reduce-scatter.5.cloned.1.call-start = ((), (), s32[]{:S(2)}) async-start(), calls=%async_computation.3 | async-start | bytes 2064384 | tf_op jit(solution)/shard_map/reduce_scatter | solution.py:1095
  186.1 29.5 %collective-permute-start.22 = (bf16[640,1024]{1,0:T(8,128)(2,1)}, bf16[640,1024]{1,0:T(8,128)(2,1)S(1)}, u32[]{:S(2)}, u32[]{:S(2)}) collective-permute-start(bf16[640,1024]{1,0:T(8,128)(2,1)} %add_convert_fusion), channel_id=1, source_target_pairs={{0,2},{1,3},{2,0},{3,1},{4,6},{5,7},{6,4},{7,5},{8,10},{9,11},{10,... | collective-permute-start | bytes 3932168 | tf_op jit(solution)/shard_map/ppermute | solution.py:928
  187.6 29.3 %collective-permute-start.23 = (bf16[640,1024]{1,0:T(8,128)(2,1)}, bf16[640,1024]{1,0:T(8,128)(2,1)}, u32[]{:S(2)}, u32[]{:S(2)}) collective-permute-start(bf16[640,1024]{1,0:T(8,128)(2,1)} %get-tuple-element.197), channel_id=1, source_target_pairs={{0,4},{1,5},{2,6},{3,7},{4,0},{5,1},{6,2},{7,3},{8,12},{9,13},{10,... | collective-permute-start | bytes 3932168 | tf_op jit(solution)/shard_map/ppermute | solution.py:928
  200.0 16.9 %copy-start.4 = (bf16[640,1024]{1,0:T(8,128)(2,1)S(1)}, bf16[640,1024]{1,0:T(8,128)(2,1)}, u32[]{:S(2)}) copy-start(bf16[640,1024]{1,0:T(8,128)(2,1)} %get-tuple-element.190) | copy-start | bytes 3932164
  202.1 16.3 %copy-start.19 = (bf16[512,1024]{1,0:T(8,128)(2,1)S(1)}, bf16[512,1024]{1,0:T(8,128)(2,1)}, u32[]{:S(2)}) copy-start(bf16[512,1024]{1,0:T(8,128)(2,1)} %get-tuple-element.209) | copy-start | bytes 3145732
  218.3 22.6 %collective-permute-start.24 = (bf16[512,1024]{1,0:T(8,128)(2,1)S(1)}, bf16[512,1024]{1,0:T(8,128)(2,1)}, u32[]{:S(2)}, u32[]{:S(2)}) collective-permute-start(bf16[512,1024]{1,0:T(8,128)(2,1)S(1)} %copy-done.19), channel_id=1, source_target_pairs={{0,2},{1,3},{2,0},{3,1},{4,6},{5,7},{6,4},{7,5},{8,10},{9,11},{10,... | collective-permute-start | bytes 3145736 | tf_op jit(solution)/shard_map/ppermute | solution.py:928
  219.0 22.3 %collective-permute-start.25 = (bf16[512,1024]{1,0:T(8,128)(2,1)S(1)}, bf16[512,1024]{1,0:T(8,128)(2,1)}, u32[]{:S(2)}, u32[]{:S(2)}) collective-permute-start(bf16[512,1024]{1,0:T(8,128)(2,1)S(1)} %add_convert_fusion.1), channel_id=1, source_target_pairs={{0,4},{1,5},{2,6},{3,7},{4,0},{5,1},{6,2},{7,3},{8,12},{9,13},{10,... | collective-permute-start | bytes 3145736 | tf_op jit(solution)/shard_map/ppermute | solution.py:928
  220.1 20.0 %collective-permute-start.26 = (bf16[320,1024]{1,0:T(8,128)(2,1)S(1)}, bf16[320,1024]{1,0:T(8,128)(2,1)}, u32[]{:S(2)}, u32[]{:S(2)}) collective-permute-start(bf16[320,1024]{1,0:T(8,128)(2,1)S(1)} %add_convert_fusion.4), channel_id=1, source_target_pairs={{0,8},{8,0},{16,24},{24,16},{1,9},{9,1},{17,25},{25,17},{2,10},{10... | collective-permute-start | bytes 1966088 | tf_op jit(solution)/shard_map/ppermute | solution.py:939
  243.1 30.2 %collective-permute-start.28 = (bf16[320,1024]{1,0:T(8,128)(2,1)S(1)}, bf16[320,1024]{1,0:T(8,128)(2,1)}, u32[]{:S(2)}, u32[]{:S(2)}) collective-permute-start(bf16[320,1024]{1,0:T(8,128)(2,1)S(1)} %add_convert_fusion.3), channel_id=1, source_target_pairs={{0,16},{8,24},{16,0},{24,8},{1,17},{9,25},{17,1},{25,9},{2,18},{10... | collective-permute-start | bytes 1966088 | tf_op jit(solution)/shard_map/ppermute | solution.py:939
  248.5 26.5 %collective-permute-start.27 = (bf16[256,1024]{1,0:T(8,128)(2,1)S(1)}, bf16[256,1024]{1,0:T(8,128)(2,1)}, u32[]{:S(2)}, u32[]{:S(2)}) collective-permute-start(bf16[256,1024]{1,0:T(8,128)(2,1)S(1)} %add_convert_fusion.7), channel_id=1, source_target_pairs={{0,8},{8,0},{16,24},{24,16},{1,9},{9,1},{17,25},{25,17},{2,10},{10... | collective-permute-start | bytes 1572872 | tf_op jit(solution)/shard_map/ppermute | solution.py:939
  250.1 37.9 %copy-start.6 = (f32[256,1024]{1,0:T(8,128)S(1)}, f32[256,1024]{1,0:T(8,128)}, u32[]{:S(2)}) copy-start(f32[256,1024]{1,0:T(8,128)} %get-tuple-element.166) | copy-start | bytes 3145732
  274.6 39.6 %collective-permute-start.30 = (bf16[320,1024]{1,0:T(8,128)(2,1)S(1)}, bf16[320,1024]{1,0:T(8,128)(2,1)S(1)}, u32[]{:S(2)}, u32[]{:S(2)}) collective-permute-start(bf16[320,1024]{1,0:T(8,128)(2,1)S(1)} %add_convert_fusion.2), channel_id=1, source_target_pairs={{0,8},{8,0},{16,24},{24,16},{1,9},{9,1},{17,25},{25,17},{2,10},{10... | collective-permute-start | bytes 1966088 | tf_op jit(solution)/shard_map/ppermute | solution.py:939
  276.9 37.3 %collective-permute-start.29 = (bf16[256,1024]{1,0:T(8,128)(2,1)S(1)}, bf16[256,1024]{1,0:T(8,128)(2,1)S(1)}, u32[]{:S(2)}, u32[]{:S(2)}) collective-permute-start(bf16[256,1024]{1,0:T(8,128)(2,1)S(1)} %add_convert_fusion.6), channel_id=1, source_target_pairs={{0,16},{8,24},{16,0},{24,8},{1,17},{9,25},{17,1},{25,9},{2,18},{10... | collective-permute-start | bytes 1572872 | tf_op jit(solution)/shard_map/ppermute | solution.py:939
  282.7 31.5 %collective-permute-start.31 = (bf16[128,896]{1,0:T(8,128)(2,1)}, bf16[128,896]{1,0:T(8,128)(2,1)S(1)}, u32[]{:S(2)}, u32[]{:S(2)}) collective-permute-start(bf16[128,896]{1,0:T(8,128)(2,1)} %reduce-scatter.5.cloned.1.call-done.refs_0_), channel_id=1, source_target_pairs={{0,8},{8,16},{16,24},{24,0},{1,9},{9,17},{17,25},{25,1},{2,10},{10... | collective-permute-start | bytes 688136 | tf_op jit(solution)/shard_map/ppermute | solution.py:924
  284.1 35.2 %collective-permute-start.32 = (bf16[128,896]{1,0:T(8,128)(2,1)}, bf16[128,896]{1,0:T(8,128)(2,1)S(1)}, u32[]{:S(2)}, u32[]{:S(2)}) collective-permute-start(bf16[128,896]{1,0:T(8,128)(2,1)} %reduce-scatter.5.cloned.1.call-done.refs_0_), channel_id=1, source_target_pairs={{0,16},{8,24},{16,0},{24,8},{1,17},{9,25},{17,1},{25,9},{2,18},{10... | collective-permute-start | bytes 688136 | tf_op jit(solution)/shard_map/ppermute | solution.py:924
  286.5 32.8 %collective-permute-start.33 = (bf16[128,896]{1,0:T(8,128)(2,1)}, bf16[128,896]{1,0:T(8,128)(2,1)S(1)}, u32[]{:S(2)}, u32[]{:S(2)}) collective-permute-start(bf16[128,896]{1,0:T(8,128)(2,1)} %reduce-scatter.5.cloned.1.call-done.refs_0_), channel_id=1, source_target_pairs={{0,24},{8,0},{16,8},{24,16},{1,25},{9,1},{17,9},{25,17},{2,26},{10... | collective-permute-start | bytes 688136 | tf_op jit(solution)/shard_map/ppermute | solution.py:924
  320.1 15.7 %collective-permute-start.34 = (bf16[256,1024]{1,0:T(8,128)(2,1)S(1)}, bf16[256,1024]{1,0:T(8,128)(2,1)S(1)}, u32[]{:S(2)}, u32[]{:S(2)}) collective-permute-start(bf16[256,1024]{1,0:T(8,128)(2,1)S(1)} %add_convert_fusion.5), channel_id=1, source_target_pairs={{0,8},{8,0},{16,24},{24,16},{1,9},{9,1},{17,25},{25,17},{2,10},{10... | collective-permute-start | bytes 1572872 | tf_op jit(solution)/shard_map/ppermute | solution.py:939
  (11 other events, 33.7 us)
Sparse Core Ops, SparseCore 0:
  10.5 49.6 all-gather.4
  62.1 56.2 all-gather.6
  184.6 46.4 reduce-scatter.2
  241.4 41.1 reduce-scatter.4
